TPU v7x, 32 devices: a whole 2x2x4 slice. The times are simulated.
32 devices in a mesh: dp: 8 (over z, core), tensor: 4 (over y, x).
Axes of the slice: x: 2, y: 2, z: 4, core: 2. Of those that a mesh axis runs over, the one named last changes fastest.
Arguments:
- tokens: bfloat16 [8192, 2048], P(('dp', 'tensor')), may hold values from -6 to 6
- positions: int32 [8192], P('dp'), may hold values from 0 to 4095, as said below
- input_gain: float32 [2048], replicated, may hold values from 0.25 to 1.75
- middle_gain: float32 [2048], replicated, may hold values from 0.25 to 1.75
- query_gain: float32 [128], replicated, may hold values from 0.25 to 1.75
- key_gain: float32 [128], replicated, may hold values from 0.25 to 1.75
- query_weight: bfloat16 [2048, 2048], P('dp', 'tensor'), may hold values from -0.125 to 0.125
- key_matrix: bfloat16 [2048, 1024], P('dp', 'tensor'), may hold values from -0.125 to 0.125
- value_matrix: bfloat16 [2048, 1024], P('dp', 'tensor'), may hold values from -0.125 to 0.125
- output_weight: bfloat16 [2048, 2048], P('dp', 'tensor'), may hold values from -2 to 2
- gate_weight: bfloat16 [2048, 6144], P('dp', 'tensor'), may hold values from -0.125 to 0.125
- up_weight: bfloat16 [2048, 6144], P('dp', 'tensor'), may hold values from -0.125 to 0.125
- down_weight: bfloat16 [2048, 6144], P('dp', 'tensor'), may hold values from -0.078125 to 0.078125
- layer_cotangent: bfloat16 [8192, 2048], P(('dp', 'tensor')), may hold values from -6 to 6
Outputs:
- layer_output: float32 [8192, 2048], P(('dp', 'tensor'))
- tokens_grad: float32 [8192, 2048], P(('dp', 'tensor'))
- input_gain_grad: float32 [2048], replicated
- middle_gain_grad: float32 [2048], replicated
- query_gain_grad: float32 [128], replicated
- key_gain_grad: float32 [128], replicated
- query_weight_grad: float32 [2048, 2048], P('dp', 'tensor')
- key_weight_grad: float32 [2048, 1024], P('dp', 'tensor')
- value_weight_grad: float32 [2048, 1024], P('dp', 'tensor')
- output_weight_grad: float32 [2048, 2048], P('dp', 'tensor')
- gate_weight_grad: float32 [2048, 6144], P('dp', 'tensor')
- up_weight_grad: float32 [2048, 6144], P('dp', 'tensor')
- down_weight_grad: float32 [2048, 6144], P('dp', 'tensor')
Inputs may be any that keep to these rules, and one draw needn't show every extreme that they name: Within each sequence of 1024 tokens the positions rise from token to token by 1 to 4; some sequence starts at 0 and some sequence ends at 4095.
All inputs are finite; a program needn't handle non-finite values.
Results may differ from a plain program's by a relative error of at most 0.024.
Values may be sent and summed in bfloat16 or wider, within the bound.
No kernel may reach another device: no remote copies, remote signals or barrier semaphores. Data moves between devices by JAX's collectives and lax.ppermute only.
A program may use at most 192 MiB of HBM per device.

v0:
```python
import math

import jax
import jax.numpy as jnp
from jax import lax
from jax.sharding import PartitionSpec as P

SEQUENCE_LENGTH = 1024


epsilon = 1e-06
masked = -1e30


def matmul(left, right):
    return jnp.dot(left, right, preferred_element_type=jnp.float32)


def contract_first(left, right):
    return lax.dot_general(
        left, right, (((0,), (0,)), ((), ())), preferred_element_type=jnp.float32
    )


def contract_last(left, right):
    return lax.dot_general(
        left, right, (((1,), (1,)), ((), ())), preferred_element_type=jnp.float32
    )


def rotate(value_rows):
    halfway = value_rows.shape[-1] // 2
    return jnp.concatenate([-value_rows[..., halfway:], value_rows[..., :halfway]], axis=-1)


def unrotate(value_rows):
    halfway = value_rows.shape[-1] // 2
    return jnp.concatenate([value_rows[..., halfway:], -value_rows[..., :halfway]], axis=-1)


def tables(positions, width):
    frequency = jnp.exp(
        jnp.arange(width // 2, dtype=jnp.float32) * (-2.0 * math.log(1000000.0) / width)
    )
    angles = positions.astype(jnp.float32)[:, None] * frequency[None, :]
    cosine = jnp.cos(angles)
    sine_table = jnp.sin(angles)
    return (
        jnp.concatenate([cosine, cosine], axis=-1)[:, None, :],
        jnp.concatenate([sine_table, sine_table], axis=-1)[:, None, :],
    )


def inverse_rms(value_rows):
    return lax.rsqrt(jnp.mean(value_rows * value_rows, axis=-1, keepdims=True) + epsilon)


def norm_backward(upstream, scaled, inverse, gain):
    inner = upstream * gain
    return inverse * (inner - scaled * jnp.mean(inner * scaled, axis=-1, keepdims=True))


def scores_block(query_block, key_block, row_offset, score_scale):
    scores = (
        jnp.einsum("qhgd,khd->hgqk", query_block, key_block, preferred_element_type=jnp.float32)
        * score_scale
    )
    shape = (query_block.shape[0], key_block.shape[0])
    row_index = row_offset + lax.broadcasted_iota(jnp.int32, shape, 0)
    column_index = lax.broadcasted_iota(jnp.int32, shape, 1)
    return jnp.where(column_index <= row_index, scores, masked)


def shards(
    tokens,
    positions,
    input_gain,
    middle_gain,
    query_gain,
    key_gain,
    query_weight,
    key_matrix,
    value_matrix,
    output_weight,
    gate_weight,
    up_weight,
    down_weight,
    layer_cotangent,
):
    head_size = query_gain.shape[0]
    query_heads = query_weight.shape[1] // head_size
    key_heads = key_matrix.shape[1] // head_size
    grouping = query_heads // key_heads
    group_rows = positions.shape[0]
    block_rows = min(512, SEQUENCE_LENGTH)
    blocks = group_rows // block_rows
    score_scale = head_size ** (-0.5)
    inputs = tokens.astype(jnp.float32)
    inverse_in = inverse_rms(inputs)
    scaled_in = inputs * inverse_in
    normed_rows = lax.all_gather(
        (scaled_in * input_gain).astype(jnp.bfloat16), "tensor", axis=0, tiled=True
    )
    wide_query, wide_key, wide_value, wide_output, wide_gating, wide_upward, wide_down = (
        lax.all_gather(query_weight, "dp", axis=0, tiled=True),
        lax.all_gather(key_matrix, "dp", axis=0, tiled=True),
        lax.all_gather(value_matrix, "dp", axis=0, tiled=True),
        lax.all_gather(output_weight, "dp", axis=0, tiled=True),
        lax.all_gather(gate_weight, "dp", axis=0, tiled=True),
        lax.all_gather(up_weight, "dp", axis=0, tiled=True),
        lax.all_gather(down_weight, "dp", axis=0, tiled=True),
    )
    cosine, sine_table = tables(positions, head_size)
    query_raw = matmul(normed_rows, wide_query).reshape(group_rows, query_heads, head_size)
    raw_key_rows = matmul(normed_rows, wide_key).reshape(group_rows, key_heads, head_size)
    value_rows = (
        matmul(normed_rows, wide_value)
        .astype(jnp.bfloat16)
        .reshape(group_rows, key_heads, head_size)
    )
    query_inverse = inverse_rms(query_raw)
    query_scaled = query_raw * query_inverse
    query_normed = query_scaled * query_gain
    query_rows = (query_normed * cosine + rotate(query_normed) * sine_table).astype(jnp.bfloat16)
    query_rows = query_rows.reshape(group_rows, key_heads, grouping, head_size)
    key_inverse = inverse_rms(raw_key_rows)
    key_scaled = raw_key_rows * key_inverse
    key_normed = key_scaled * key_gain
    key_rows = (key_normed * cosine + rotate(key_normed) * sine_table).astype(jnp.bfloat16)

    def forward_block(block_index):
        first_row = block_index * block_rows
        first_key = first_row // SEQUENCE_LENGTH * SEQUENCE_LENGTH
        query_block = lax.dynamic_slice_in_dim(query_rows, first_row, block_rows, 0)
        scores = scores_block(query_block, key_rows, first_row - first_key, score_scale)
        highest_score = jnp.max(scores, axis=-1, keepdims=True)
        log_total = highest_score + jnp.log(
            jnp.sum(jnp.exp(scores - highest_score), axis=-1, keepdims=True)
        )
        shares = jnp.exp(scores - log_total).astype(jnp.bfloat16)
        attended_rows = jnp.einsum(
            "hgqk,khd->qhgd", shares, value_rows, preferred_element_type=jnp.float32
        )
        return (attended_rows.astype(jnp.bfloat16), log_total)

    attended_rows, log_totals = lax.map(forward_block, jnp.arange(blocks, dtype=jnp.int32))
    attended_rows = attended_rows.reshape(group_rows, query_heads * head_size)
    branch = lax.psum_scatter(
        contract_last(attended_rows, wide_output).astype(jnp.bfloat16),
        "tensor",
        scatter_dimension=0,
        tiled=True,
    ).astype(jnp.float32)
    middle = inputs + branch
    inverse_mid = inverse_rms(middle)
    scaled_mid = middle * inverse_mid
    normed_middle = lax.all_gather(
        (scaled_mid * middle_gain).astype(jnp.bfloat16), "tensor", axis=0, tiled=True
    )
    gating = matmul(normed_middle, wide_gating)
    upward = matmul(normed_middle, wide_upward)
    gate_sigmoid = jax.nn.sigmoid(gating)
    silu_gate = gating * gate_sigmoid
    active = (silu_gate * upward).astype(jnp.bfloat16)
    layer_output = middle + lax.psum_scatter(
        contract_last(active, wide_down).astype(jnp.bfloat16),
        "tensor",
        scatter_dimension=0,
        tiled=True,
    ).astype(jnp.float32)
    cotangent = lax.all_gather(layer_cotangent, "tensor", axis=0, tiled=True)
    wide_query, wide_key, wide_value, wide_output, wide_gating, wide_upward, wide_down = (
        lax.all_gather(query_weight, "dp", axis=0, tiled=True),
        lax.all_gather(key_matrix, "dp", axis=0, tiled=True),
        lax.all_gather(value_matrix, "dp", axis=0, tiled=True),
        lax.all_gather(output_weight, "dp", axis=0, tiled=True),
        lax.all_gather(gate_weight, "dp", axis=0, tiled=True),
        lax.all_gather(up_weight, "dp", axis=0, tiled=True),
        lax.all_gather(down_weight, "dp", axis=0, tiled=True),
    )
    down_term = contract_first(cotangent, active)
    active_grad = matmul(cotangent, wide_down)
    gate_grad = (
        active_grad * upward * gate_sigmoid * (1.0 + gating * (1.0 - gate_sigmoid))
    ).astype(jnp.bfloat16)
    upward_grad = (active_grad * silu_gate).astype(jnp.bfloat16)
    gate_term = contract_first(normed_middle, gate_grad)
    upward_term = contract_first(normed_middle, upward_grad)
    middle_partial = contract_last(gate_grad, wide_gating) + contract_last(upward_grad, wide_upward)
    middle_normed_grad = lax.psum_scatter(
        middle_partial.astype(jnp.bfloat16), "tensor", scatter_dimension=0, tiled=True
    ).astype(jnp.float32)
    middle_gain_term = jnp.sum(middle_normed_grad * scaled_mid, axis=0)
    middle_grad = layer_cotangent.astype(jnp.float32) + norm_backward(
        middle_normed_grad, scaled_mid, inverse_mid, middle_gain
    )
    branch_grad = lax.all_gather(middle_grad.astype(jnp.bfloat16), "tensor", axis=0, tiled=True)
    output_term = contract_first(branch_grad, attended_rows)
    attended_grad = matmul(branch_grad, wide_output).astype(jnp.bfloat16)
    attended_grad = attended_grad.reshape(group_rows, key_heads, grouping, head_size)

    def backward_block(carried, block_index):
        key_total, value_total = carried
        first_row = block_index * block_rows
        first_key = first_row // SEQUENCE_LENGTH * SEQUENCE_LENGTH
        query_block = lax.dynamic_slice_in_dim(query_rows, first_row, block_rows, 0)
        grad_block = lax.dynamic_slice_in_dim(attended_grad, first_row, block_rows, 0)
        scores = scores_block(query_block, key_rows, first_row - first_key, score_scale)
        shares = jnp.exp(scores - log_totals[block_index])
        shares_low = shares.astype(jnp.bfloat16)
        share_grad = jnp.einsum(
            "qhgd,khd->hgqk", grad_block, value_rows, preferred_element_type=jnp.float32
        )
        score_grad = (
            shares * (share_grad - jnp.sum(share_grad * shares, axis=-1, keepdims=True))
        ).astype(jnp.bfloat16)
        query_part = (
            jnp.einsum("hgqk,khd->qhgd", score_grad, key_rows, preferred_element_type=jnp.float32)
            * score_scale
        )
        key_part = (
            jnp.einsum(
                "hgqk,qhgd->khd", score_grad, query_block, preferred_element_type=jnp.float32
            )
            * score_scale
        )
        value_part = jnp.einsum(
            "hgqk,qhgd->khd", shares_low, grad_block, preferred_element_type=jnp.float32
        )
        key_total = key_total + key_part
        value_total = value_total + value_part
        return ((key_total, value_total), query_part)

    blank_grads = jnp.zeros((group_rows, key_heads, head_size), jnp.float32)
    (keys_grad, values_grad), queries_grad = lax.scan(
        backward_block, (blank_grads, blank_grads), jnp.arange(blocks, dtype=jnp.int32)
    )
    queries_grad = queries_grad.reshape(group_rows, query_heads, head_size)
    query_normed_grad = queries_grad * cosine + unrotate(queries_grad * sine_table)
    query_gain_term = jnp.sum(query_normed_grad * query_scaled, axis=(0, 1))
    query_raw_grad = norm_backward(
        query_normed_grad, query_scaled, query_inverse, query_gain
    ).astype(jnp.bfloat16)
    query_raw_grad = query_raw_grad.reshape(group_rows, query_heads * head_size)
    key_normed_grad = keys_grad * cosine + unrotate(keys_grad * sine_table)
    key_gain_term = jnp.sum(key_normed_grad * key_scaled, axis=(0, 1))
    key_raw_grad = norm_backward(key_normed_grad, key_scaled, key_inverse, key_gain).astype(
        jnp.bfloat16
    )
    key_raw_grad = key_raw_grad.reshape(group_rows, key_heads * head_size)
    value_raw_grad = values_grad.astype(jnp.bfloat16).reshape(group_rows, key_heads * head_size)
    query_term = contract_first(normed_rows, query_raw_grad)
    key_term = contract_first(normed_rows, key_raw_grad)
    value_term = contract_first(normed_rows, value_raw_grad)
    input_partial = (
        contract_last(query_raw_grad, wide_query)
        + contract_last(key_raw_grad, wide_key)
        + contract_last(value_raw_grad, wide_value)
    )
    input_normed_grad = lax.psum_scatter(
        input_partial.astype(jnp.bfloat16), "tensor", scatter_dimension=0, tiled=True
    ).astype(jnp.float32)
    input_gain_term = jnp.sum(input_normed_grad * scaled_in, axis=0)
    tokens_grad = middle_grad + norm_backward(input_normed_grad, scaled_in, inverse_in, input_gain)
    query_sum, key_sum, value_sum, output_sum, gate_sum, upward_sum, down_sum = (
        lax.psum_scatter(
            query_term.astype(jnp.bfloat16), "dp", scatter_dimension=0, tiled=True
        ).astype(jnp.float32),
        lax.psum_scatter(
            key_term.astype(jnp.bfloat16), "dp", scatter_dimension=0, tiled=True
        ).astype(jnp.float32),
        lax.psum_scatter(
            value_term.astype(jnp.bfloat16), "dp", scatter_dimension=0, tiled=True
        ).astype(jnp.float32),
        lax.psum_scatter(
            output_term.astype(jnp.bfloat16), "dp", scatter_dimension=0, tiled=True
        ).astype(jnp.float32),
        lax.psum_scatter(
            gate_term.astype(jnp.bfloat16), "dp", scatter_dimension=0, tiled=True
        ).astype(jnp.float32),
        lax.psum_scatter(
            upward_term.astype(jnp.bfloat16), "dp", scatter_dimension=0, tiled=True
        ).astype(jnp.float32),
        lax.psum_scatter(
            down_term.astype(jnp.bfloat16), "dp", scatter_dimension=0, tiled=True
        ).astype(jnp.float32),
    )
    input_gain_sum, middle_gain_sum, query_gain_sum, key_gain_sum = lax.psum(
        (input_gain_term, middle_gain_term, query_gain_term, key_gain_term), ("dp", "tensor")
    )
    return (
        layer_output,
        tokens_grad,
        input_gain_sum,
        middle_gain_sum,
        query_gain_sum,
        key_gain_sum,
        query_sum,
        key_sum,
        value_sum,
        output_sum,
        gate_sum,
        upward_sum,
        down_sum,
    )


def solution(mesh):
    placed = (
        P(("dp", "tensor"), None),
        P("dp"),
        P(),
        P(),
        P(),
        P(),
        P("dp", "tensor"),
        P("dp", "tensor"),
        P("dp", "tensor"),
        P("dp", "tensor"),
        P("dp", "tensor"),
        P("dp", "tensor"),
        P("dp", "tensor"),
        P(("dp", "tensor"), None),
    )
    return jax.shard_map(
        shards,
        mesh=mesh,
        in_specs=placed,
        out_specs=(
            P(("dp", "tensor"), None),
            P(("dp", "tensor"), None),
            P(),
            P(),
            P(),
            P(),
            P("dp", "tensor"),
            P("dp", "tensor"),
            P("dp", "tensor"),
            P("dp", "tensor"),
            P("dp", "tensor"),
            P("dp", "tensor"),
            P("dp", "tensor"),
        ),
        check_vma=False,
    )
```

profile of v0, /device:TPU:0, one launch (start us, length us, event | category | flops | bytes accessed | tf_op | source)
XLA Modules:
  0.0 1160.9 jit_solution(6719207721562460313)
XLA Ops:
  9.5 2.5 fusion.69
  16.8 17.7 %all-gather.16.cloned.1.call-done = bf16[2048,256]{1,0:T(8,128)(2,1)} async-done(((bf16[256,256]{1,0:T(8,128)(2,1)}), bf16[2048,256]{1,0:T(8,128)(2,1)}) %all-gather.16.cloned.1.call-update) | async-done | bytes 1048592 | tf_op jit(solution)/shard_map/all_gather | solution.py:106
  34.5 54.8 %all-gather.12.cloned.1.call-done = bf16[1024,2048]{1,0:T(8,128)(2,1)} async-done(((bf16[256,2048]{1,0:T(8,128)(2,1)}), bf16[1024,2048]{1,0:T(8,128)(2,1)}) %all-gather.12.cloned.1.call-update) | async-done | bytes 4194320 | tf_op jit(solution)/shard_map/all_gather | solution.py:101
  89.2 3.8 multiply_reduce_fusion.6
  96.5 23.5 %all-gather.14.cloned.1.call-done = bf16[2048,512]{1,0:T(8,128)(2,1)} async-done(((bf16[256,512]{1,0:T(8,128)(2,1)}), bf16[2048,512]{1,0:T(8,128)(2,1)}) %all-gather.14.cloned.1.call-update) | async-done | bytes 2097168 | tf_op jit(solution)/shard_map/all_gather | solution.py:105
  120.0 6.6 multiply_reduce_fusion.3
  129.8 3.2 copy.45
  134.9 3.4 copy.44
  138.3 4.8 all-gather.18.cloned.1.call-done
  143.1 3.8 convolution_convert_fusion.10
  147.1 3.5 fusion.77
  150.6 19.8 %while.31 = (s32[]{:T(128)}, bf16[2,512,2,2,128]{4,3,2,1,0:T(2,128)(2,1)}, f32[2,2,2,512,1]{3,2,1,4,0:T(2,128)S(1)}, s32[2]{0:T(128)S(1)}, bf16[1024,2,2,128]{3,...) while((s32[]{:T(128)}, ...), condition=%wide.region_6.7_spmd, body=%wide.region_3.6_spmd.sunk | while | flops 1097595392 | bytes 38867372 | solution.py:146
  173.3 6.4 convolution_convert_fusion.4
  180.5 51.6 %reduce-scatter.12.cloned.1.call-done = bf16[256,2048]{1,0:T(8,128)(2,1)} async-done(((bf16[1024,2048]{1,0:T(8,128)(2,1)}), bf16[256,2048]{1,0:T(8,128)(2,1)}) %reduce-scatter.12.cloned.1.call-update) | async-done | bytes 1048592 | tf_op jit(solution)/shard_map/reduce_scatter | solution.py:148
  233.7 2.6 multiply_convert_fusion.3
  238.4 60.1 %all-gather.24.cloned.1.call-done = bf16[2048,1536]{1,0:T(8,128)(2,1)} async-done(((bf16[256,1536]{1,0:T(8,128)(2,1)}), bf16[2048,1536]{1,0:T(8,128)(2,1)}) %all-gather.24.cloned.1.call-update) | async-done | bytes 6291472 | tf_op jit(solution)/shard_map/all_gather | solution.py:109
  298.5 54.0 %all-gather.22.cloned.1.call-done = bf16[1024,2048]{1,0:T(8,128)(2,1)} async-done(((bf16[256,2048]{1,0:T(8,128)(2,1)}), bf16[1024,2048]{1,0:T(8,128)(2,1)}) %all-gather.22.cloned.1.call-update) | async-done | bytes 4194320 | tf_op jit(solution)/shard_map/all_gather | solution.py:157
  352.5 11.8 %fusion.85 = f32[1024,1536]{1,0:T(8,128)} fusion(bf16[1024,2048]{1,0:T(8,128)(2,1)} %all-gather.22.cloned.1.call-done, bf16[2048,1536]{1,0:T(8,128)(2,1)} %all-gather.24.cloned.1.call-done), kind=kOutput, calls=%fused_computation.158 | convolution fusion | flops 6442450944 | bytes 16777216 | tf_op jit(solution)/shard_map/dot_general | solution.py:16
  364.3 54.7 %all-gather.26.cloned.1.call-done = bf16[2048,1536]{1,0:T(8,128)(2,1)} async-done(((bf16[256,1536]{1,0:T(8,128)(2,1)}), bf16[2048,1536]{1,0:T(8,128)(2,1)}) %all-gather.26.cloned.1.call-update) | async-done | bytes 6291472 | tf_op jit(solution)/shard_map/all_gather | solution.py:110
  419.0 11.7 %fusion.86 = f32[1024,1536]{1,0:T(8,128)} fusion(bf16[1024,2048]{1,0:T(8,128)(2,1)} %all-gather.22.cloned.1.call-done, bf16[2048,1536]{1,0:T(8,128)(2,1)} %all-gather.26.cloned.1.call-done), kind=kOutput, calls=%fused_computation.159 | convolution fusion | flops 6442450944 | bytes 16777216 | tf_op jit(solution)/shard_map/dot_general | solution.py:16
  430.7 41.5 %all-gather.30.cloned.1.call-done = bf16[1024,2048]{1,0:T(8,128)(2,1)} async-done(((bf16[256,2048]{1,0:T(8,128)(2,1)}), bf16[1024,2048]{1,0:T(8,128)(2,1)}) %all-gather.30.cloned.1.call-update) | async-done | bytes 4194320 | tf_op jit(solution)/shard_map/all_gather | solution.py:171
  472.2 66.5 %all-gather.28.cloned.1.call-done = bf16[2048,1536]{1,0:T(8,128)(2,1)} async-done(((bf16[256,1536]{1,0:T(8,128)(2,1)}), bf16[2048,1536]{1,0:T(8,128)(2,1)}) %all-gather.28.cloned.1.call-update) | async-done | bytes 6291472 | tf_op jit(solution)/shard_map/all_gather | solution.py:111
  538.8 16.4 %multiply_convert_fusion = (bf16[1024,1536]{1,0:T(8,128)(2,1)}, bf16[1024,1536]{1,0:T(8,128)(2,1)S(1)}, bf16[1024,1536]{1,0:T(8,128)(2,1)}) fusion(f32[1024,1536]{1,0:T(8,128)} %fusion.85, f32[1024,1536]{1,0:T(8,128)} %fusion.86, bf16[1024,2048]{1,0:T(8,128)(2,1)} %all-gather.30.cloned.1.call-done, bf16[2048,1536]{1,0:T(8,128)(2,1)} %all-gather.28.cloned.1.call-done), kind=kOutput, calls=%fused_computation.67 | convolution fusion | flops 6466043904 | bytes 32505856 | tf_op jit(solution)/shard_map/dot_general | solution.py:16
  555.1 10.0 fusion.87
  565.2 10.6 add_convert_fusion.1
  575.9 51.5 %reduce-scatter.16.cloned.1.call-done = bf16[256,2048]{1,0:T(8,128)(2,1)} async-done(((bf16[1024,2048]{1,0:T(8,128)(2,1)}), bf16[256,2048]{1,0:T(8,128)(2,1)}) %reduce-scatter.16.cloned.1.call-update) | async-done | bytes 1048592 | tf_op jit(solution)/shard_map/reduce_scatter | solution.py:190
  627.4 3.2 fusion.68
  632.8 11.6 convolution_convert_fusion.2
  644.4 11.5 convolution_convert_fusion.1
  656.0 11.5 fusion.54
  667.6 17.9 %all-gather.32.cloned.1.call-done = bf16[1024,2048]{1,0:T(8,128)(2,1)} async-done(((bf16[256,2048]{1,0:T(8,128)(2,1)}), bf16[1024,2048]{1,0:T(8,128)(2,1)}) %all-gather.32.cloned.1.call-update) | async-done | bytes 4194320 | tf_op jit(solution)/shard_map/all_gather | solution.py:197
  685.5 6.2 convolution_convert_fusion.9
  691.8 64.2 %while.32 = (s32[]{:T(128)}, f32[1024,2,128]{0,2,1:T(8,128)S(1)}, f32[1024,2,128]{0,2,1:T(8,128)}, f32[2,512,2,2,128]{4,1,3,2,0:T(8,128)}, s32[2]{0:T(128)S(1)},...) while((s32[]{:T(128)}, f32[1024,2,128]{0,2,1:T(8,128)S(1)}, ...), condition=%wide.region_14.15_spmd.clone, body=%wide.region_12.14_spmd.clone.sunk | while | flops 2717907456 | bytes 149484608 | solution.py:235
  693.4 4.5 fusion.164
  699.9 7.5 fusion.165
  714.1 3.4 fusion.167
  718.9 4.7 fusion.168
  725.3 4.5 fusion.164
  731.8 7.5 fusion.165
  746.0 3.4 fusion.167
  750.7 5.1 fusion.168
  762.2 5.3 convolution_convert_fusion.7
  767.6 5.9 convolution_convert_fusion.5
  773.6 4.1 multiply_cosine_fusion.1
  778.7 4.0 reshape.223
  782.7 3.1 copy.57
  785.8 4.2 copy.55
  791.8 2.7 fusion.83
  798.4 7.1 multiply_reduce_fusion
  807.5 2.9 copy.58
  815.5 3.7 convolution_convert_fusion.6
  823.9 3.4 add_convert_fusion
  827.4 11.1 convolution_convert_fusion.3
  841.0 2.6 convert_element_type.181
  843.6 54.7 %reduce-scatter.32.cloned.1.call-done = bf16[256,1536]{0,1:T(8,128)(2,1)} async-done(((bf16[2048,1536]{0,1:T(8,128)(2,1)}), bf16[256,1536]{0,1:T(8,128)(2,1)}) %reduce-scatter.32.cloned.1.call-update) | async-done | bytes 786448 | tf_op jit(solution)/shard_map/reduce_scatter | solution.py:284
  898.3 2.5 copy.62
  900.8 30.4 %reduce-scatter.22.cloned.1.call-done = bf16[256,256]{1,0:T(8,128)(2,1)} async-done(((bf16[2048,256]{1,0:T(8,128)(2,1)}), bf16[256,256]{1,0:T(8,128)(2,1)}) %reduce-scatter.22.cloned.1.call-update) | async-done | bytes 131088 | tf_op jit(solution)/shard_map/reduce_scatter | solution.py:269
  932.8 31.1 %reduce-scatter.24.cloned.1.call-done = bf16[256,256]{1,0:T(8,128)(2,1)} async-done(((bf16[2048,256]{1,0:T(8,128)(2,1)}), bf16[256,256]{1,0:T(8,128)(2,1)}) %reduce-scatter.24.cloned.1.call-update) | async-done | bytes 131088 | tf_op jit(solution)/shard_map/reduce_scatter | solution.py:272
  965.6 34.7 %reduce-scatter.26.cloned.1.call-done = bf16[256,512]{1,0:T(8,128)(2,1)} async-done(((bf16[2048,512]{1,0:T(8,128)(2,1)}), bf16[256,512]{1,0:T(8,128)(2,1)}) %reduce-scatter.26.cloned.1.call-update) | async-done | bytes 262160 | tf_op jit(solution)/shard_map/reduce_scatter | solution.py:275
  1002.1 35.4 %reduce-scatter.20.cloned.1.call-done = bf16[256,512]{1,0:T(8,128)(2,1)} async-done(((bf16[2048,512]{1,0:T(8,128)(2,1)}), bf16[256,512]{1,0:T(8,128)(2,1)}) %reduce-scatter.20.cloned.1.call-update) | async-done | bytes 262160 | tf_op jit(solution)/shard_map/reduce_scatter | solution.py:266
  1039.3 52.6 %reduce-scatter.18.cloned.1.call-done = bf16[256,2048]{1,0:T(8,128)(2,1)} async-done(((bf16[1024,2048]{1,0:T(8,128)(2,1)}), bf16[256,2048]{1,0:T(8,128)(2,1)}) %reduce-scatter.18.cloned.1.call-update) | async-done | bytes 1048592 | tf_op jit(solution)/shard_map/reduce_scatter | solution.py:260
  1093.9 40.0 %all-reduce = (f32[2048]{0:T(1024)}, f32[2048]{0:T(1024)}, f32[128]{0:T(128)}, f32[128]{0:T(128)}) all-reduce(f32[2048]{0:T(1024)S(1)} %get-tuple-element.334, f32[2048]{0:T(1024)S(1)} %copy-done.39, f32[128]{0:T(128)S(1)} %get-tuple-element.330, f32[128]{0:T(128)S(1)} %get-tuple-element.336), channel_id=1, replica_groups=mesh['dp'=8,'tensor'=4] {'dp','tensor'}, use_global_device_ids=true, to_apply=%region_20.21 | all-reduce | flops 4352 | bytes 34816 | tf_op jit(solution)/shard_map/psum | solution.py:288
  1133.9 14.2 %reduce-scatter.14.cloned.1.call-done = bf16[256,2048]{1,0:T(8,128)(2,1)} async-done(((bf16[1024,2048]{1,0:T(8,128)(2,1)}), bf16[256,2048]{1,0:T(8,128)(2,1)}) %reduce-scatter.14.cloned.1.call-update) | async-done | bytes 1048592 | tf_op jit(solution)/shard_map/reduce_scatter | solution.py:165
  1148.1 5.8 fusion.64
  (268 shorter events, 97.8 us)
Async XLA Ops:
  7.2 6.9 copy-start.50
  7.2 27.3 %all-gather.16.cloned.1.call-start = ((), (), s32[]{:S(2)}) async-start(), calls=%async_computation.13 | async-start | bytes 1179648 | tf_op jit(solution)/shard_map/all_gather | solution.py:106
  7.9 81.3 %all-gather.12.cloned.1.call-start = ((), (), s32[]{:S(2)}) async-start(), calls=%async_computation.11 | async-start | bytes 5242880 | tf_op jit(solution)/shard_map/all_gather | solution.py:101
  9.5 4.5 copy-start.42
  12.0 107.9 %all-gather.14.cloned.1.call-start = ((), (), s32[]{:S(2)}) async-start(), calls=%async_computation.12 | async-start | bytes 2359296 | tf_op jit(solution)/shard_map/all_gather | solution.py:105
  12.8 130.3 %all-gather.18.cloned.1.call-start = ((), (), s32[]{:S(2)}) async-start(), calls=%async_computation.14 | async-start | bytes 1179648 | tf_op jit(solution)/shard_map/all_gather | solution.py:107
  13.3 159.9 %all-gather.20.cloned.1.call-start = ((), (), s32[]{:S(2)}) async-start(), calls=%async_computation.15 | async-start | bytes 2359296 | tf_op jit(solution)/shard_map/all_gather | solution.py:108
  13.9 218.1 %reduce-scatter.12.cloned.1.call-start = ((), (), s32[]{:S(2)}) async-start(), calls=%async_computation.16 | async-start | bytes 5242880 | tf_op jit(solution)/shard_map/reduce_scatter | solution.py:148
  16.3 130.8 %copy-start.17 = (f32[1024,128]{1,0:T(8,128)}, f32[1024,128]{1,0:T(8,128)S(1)}, u32[]{:S(2)}) copy-start(f32[1024,128]{1,0:T(8,128)S(1)} %get-tuple-element.403) | copy-start | bytes 1572868
  16.5 76.8 %copy-start.15 = (f32[1024,128]{0,1:T(8,128)}, f32[1024,128]{0,1:T(8,128)S(1)}, u32[]{:S(2)}) copy-start(f32[1024,128]{0,1:T(8,128)S(1)} %copy.47) | copy-start | bytes 1572868
  16.7 76.6 %copy-start.19 = (f32[1024,128]{0,1:T(8,128)}, f32[1024,128]{0,1:T(8,128)S(1)}, u32[]{:S(2)}) copy-start(f32[1024,128]{0,1:T(8,128)S(1)} %copy.48) | copy-start | bytes 1572868
  16.8 76.3 %copy-start.48 = (f32[128]{0:T(128)S(1)}, f32[128]{0:T(128)}, u32[]{:S(2)}) copy-start(f32[128]{0:T(128)} %param.23) | copy-start | bytes 1540
  96.5 30.1 %copy-start.46 = (f32[128]{0:T(128)S(1)}, f32[128]{0:T(128)}, u32[]{:S(2)}) copy-start(f32[128]{0:T(128)} %param.22) | copy-start | bytes 1540
  126.6 3.2 copy-start.30
  179.6 52.4 %copy-start.2 = (bf16[256,2048]{1,0:T(8,128)(2,1)S(1)}, bf16[256,2048]{1,0:T(8,128)(2,1)}, u32[]{:S(2)}) copy-start(bf16[256,2048]{1,0:T(8,128)(2,1)} %param.18) | copy-start | bytes 3145732
  179.6 54.0 %copy-start.34 = (f32[2048]{0:T(1024)S(1)}, f32[2048]{0:T(1024)}, u32[]{:S(2)}) copy-start(f32[2048]{0:T(1024)} %param.21) | copy-start | bytes 24580
  179.7 118.9 %all-gather.24.cloned.1.call-start = ((), (), s32[]{:S(2)}) async-start(), calls=%async_computation.18 | async-start | bytes 7077888 | tf_op jit(solution)/shard_map/all_gather | solution.py:109
  180.4 172.1 %all-gather.22.cloned.1.call-start = ((), (), s32[]{:S(2)}) async-start(), calls=%async_computation.17 | async-start | bytes 5242880 | tf_op jit(solution)/shard_map/all_gather | solution.py:157
  233.7 396.9 %copy-start.40 = (f32[256]{0:T(256)}, f32[256]{0:T(256)S(1)}, u32[]{:S(2)}) copy-start(f32[256]{0:T(256)S(1)} %add_rsqrt_fusion.2) | copy-start | bytes 3076
  236.3 182.7 %all-gather.26.cloned.1.call-start = ((), (), s32[]{:S(2)}) async-start(), calls=%async_computation.19 | async-start | bytes 7077888 | tf_op jit(solution)/shard_map/all_gather | solution.py:110
  237.0 235.2 %all-gather.30.cloned.1.call-start = ((), (), s32[]{:S(2)}) async-start(), calls=%async_computation.22 | async-start | bytes 5242880 | tf_op jit(solution)/shard_map/all_gather | solution.py:171
  237.6 301.2 %all-gather.28.cloned.1.call-start = ((), (), s32[]{:S(2)}) async-start(), calls=%async_computation.20 | async-start | bytes 7077888 | tf_op jit(solution)/shard_map/all_gather | solution.py:111
  238.4 389.0 %reduce-scatter.16.cloned.1.call-start = ((), (), s32[]{:S(2)}) async-start(), calls=%async_computation.23 | async-start | bytes 5242880 | tf_op jit(solution)/shard_map/reduce_scatter | solution.py:190
  555.1 10.0 copy-start.57
  555.1 10.0 copy-start.53
  575.8 109.7 %all-gather.32.cloned.1.call-start = ((), (), s32[]{:S(2)}) async-start(), calls=%async_computation.24 | async-start | bytes 5242880 | tf_op jit(solution)/shard_map/all_gather | solution.py:197
  627.4 3.2 copy-start.5
  627.4 3.2 copy-start.12
  627.4 3.2 copy-start.13
  632.7 205.8 %reduce-scatter.28.cloned.1.call-start = ((), (), s32[]{:S(2)}) async-start(), calls=%async_computation.30 | async-start | bytes 7077888 | tf_op jit(solution)/shard_map/reduce_scatter | solution.py:278
  644.3 196.7 %reduce-scatter.30.cloned.1.call-start = ((), (), s32[]{:S(2)}) async-start(), calls=%async_computation.31 | async-start | bytes 7077888 | tf_op jit(solution)/shard_map/reduce_scatter | solution.py:281
  655.9 242.3 %reduce-scatter.32.cloned.1.call-start = ((), (), s32[]{:S(2)}) async-start(), calls=%async_computation.32 | async-start | bytes 7077888 | tf_op jit(solution)/shard_map/reduce_scatter | solution.py:284
  667.5 263.7 %reduce-scatter.22.cloned.1.call-start = ((), (), s32[]{:S(2)}) async-start(), calls=%async_computation.27 | async-start | bytes 1179648 | tf_op jit(solution)/shard_map/reduce_scatter | solution.py:269
  699.9 7.5 slice-start
  699.9 7.5 slice-start.1
  714.1 4.8 copy-start
  731.7 7.5 slice-start
  731.8 7.5 slice-start.1
  746.0 4.7 copy-start
  762.0 201.9 %reduce-scatter.24.cloned.1.call-start = ((), (), s32[]{:S(2)}) async-start(), calls=%async_computation.28 | async-start | bytes 1179648 | tf_op jit(solution)/shard_map/reduce_scatter | solution.py:272
  762.2 5.3 copy-start.20
  762.2 5.4 copy-start.27
  767.5 6.1 copy-start.38
  767.5 6.1 copy-start.52
  767.5 232.7 %reduce-scatter.26.cloned.1.call-start = ((), (), s32[]{:S(2)}) async-start(), calls=%async_computation.29 | async-start | bytes 2359296 | tf_op jit(solution)/shard_map/reduce_scatter | solution.py:275
  773.5 5.2 copy-start.47
  773.5 9.2 copy-start.31
  773.5 264.0 %reduce-scatter.20.cloned.1.call-start = ((), (), s32[]{:S(2)}) async-start(), calls=%async_computation.26 | async-start | bytes 2359296 | tf_op jit(solution)/shard_map/reduce_scatter | solution.py:266
  785.8 4.2 copy-start.18
  798.4 7.2 copy-start.10
  798.4 7.2 copy-start.11
  810.4 2.9 copy-start.14
  815.5 3.7 copy-start.24
  815.5 4.0 copy-start.22
  819.3 272.6 %reduce-scatter.18.cloned.1.call-start = ((), (), s32[]{:S(2)}) async-start(), calls=%async_computation.25 | async-start | bytes 5242880 | tf_op jit(solution)/shard_map/reduce_scatter | solution.py:260
  827.3 320.8 %reduce-scatter.14.cloned.1.call-start = ((), (), s32[]{:S(2)}) async-start(), calls=%async_computation.21 | async-start | bytes 5242880 | tf_op jit(solution)/shard_map/reduce_scatter | solution.py:165
  841.0 250.9 %copy-start.3 = (bf16[256,2048]{1,0:T(8,128)(2,1)S(1)}, bf16[256,2048]{1,0:T(8,128)(2,1)}, u32[]{:S(2)}) copy-start(bf16[256,2048]{1,0:T(8,128)(2,1)} %param.18) | copy-start | bytes 3145732
  841.0 250.9 %copy-start.36 = (f32[2048]{0:T(1024)S(1)}, f32[2048]{0:T(1024)}, u32[]{:S(2)}) copy-start(f32[2048]{0:T(1024)} %param.20) | copy-start | bytes 24580
  841.0 250.9 %copy-start.43 = (f32[256]{0:T(256)S(1)}, f32[256]{0:T(256)}, u32[]{:S(2)}) copy-start(f32[256]{0:T(256)} %copy-done.42) | copy-start | bytes 3076
  843.6 250.3 %copy-start.39 = (f32[2048]{0:T(1024)S(1)}, f32[2048]{0:T(1024)}, u32[]{:S(2)}) copy-start(f32[2048]{0:T(1024)} %get-tuple-element.332) | copy-start | bytes 24580
  843.6 304.5 %copy-start.6 = (bf16[256,2048]{1,0:T(8,128)(2,1)S(1)}, bf16[256,2048]{1,0:T(8,128)(2,1)}, u32[]{:S(2)}) copy-start(bf16[256,2048]{1,0:T(8,128)(2,1)} %reduce-scatter.12.cloned.1.call-done) | copy-start | bytes 3145732
  843.6 304.5 %copy-start.35 = (f32[2048]{0:T(1024)S(1)}, f32[2048]{0:T(1024)}, u32[]{:S(2)}) copy-start(f32[2048]{0:T(1024)} %param.21) | copy-start | bytes 24580
  843.6 304.5 %copy-start.41 = (f32[256]{0:T(256)S(1)}, f32[256]{0:T(256)}, u32[]{:S(2)}) copy-start(f32[256]{0:T(256)} %copy-done.40) | copy-start | bytes 3076
  843.6 304.5 %copy-start.45 = (f32[256]{0:T(256)S(1)}, f32[256]{0:T(256)}, u32[]{:S(2)}) copy-start(f32[256]{0:T(256)} %copy-done.44) | copy-start | bytes 3076
  (24 other events, 44.7 us)
Sparse Core Ops, SparseCore 0:
  9.6 24.7 all-gather.15
  36.9 52.3 all-gather.11
  90.8 29.0 all-gather.13
  121.4 21.5 all-gather.17
  144.5 28.7 all-gather.19
  179.8 52.1 reduce-scatter.11
  233.8 64.7 all-gather.23
  301.1 51.3 all-gather.21
  354.2 64.7 all-gather.25
  420.9 51.3 all-gather.29
  474.0 64.7 all-gather.27
  576.0 51.3 reduce-scatter.15
  632.8 52.6 all-gather.31
  687.7 69.7 reduce-scatter.27
  759.7 68.1 reduce-scatter.29
  830.1 68.1 reduce-scatter.31
  900.4 30.7 reduce-scatter.21
  933.4 30.5 reduce-scatter.23
  966.3 33.9 reduce-scatter.25
  1003.0 34.4 reduce-scatter.19
  1040.4 51.3 reduce-scatter.17
  1095.1 52.9 reduce-scatter.13
where the time goes:
time: 1170 us; the launch traced here: 1160 us
  waiting for transfers between devices  757 us (65%)
  matrix products  211 us (18%)
  other arithmetic  76.2 us (7%)
  local copies, waits for them, and re-layouts  53.5 us (5%)
  blocking collectives  40 us (3%)
  between operations  15.3 us (1%)
    all_gather x1, waiting for transfers between devices, shards(): lax.all_gather(down_weight, 'dp', axis=0, tiled=True)  66.5 us
    dot_general x7, matrix products, matmul(): return jnp.dot(left, right, preferred_element_type=jnp.float32)  60.2 us
    all_gather x1, waiting for transfers between devices, shards(): lax.all_gather(gate_weight, 'dp', axis=0, tiled=True)  60.1 us
    all_gather x1, waiting for transfers between devices, shards(): lax.all_gather((scaled_in * input_gain).astype(jnp.bfloat16), 'tensor', a...  54.8 us
    all_gather x1, waiting for transfers between devices, shards(): lax.all_gather(up_weight, 'dp', axis=0, tiled=True)  54.7 us
    reduce_scatter x1, waiting for transfers between devices, shards(): lax.psum_scatter(down_term.astype(jnp.bfloat16), 'dp', scatter_dimension=...  54.7 us
    all_gather x1, waiting for transfers between devices, shards(): lax.all_gather((scaled_mid * middle_gain).astype(jnp.bfloat16), 'tensor',...  54 us
    reduce_scatter x1, waiting for transfers between devices, shards(): lax.psum_scatter(input_partial.astype(jnp.bfloat16), 'tensor', scatter_di...  52.6 us
  transfers between devices with their start and end apart: 22, of which 20 were waited for; matrix products, arithmetic and copies ran while one was open for 23% of the time, Pallas kernels for 0%

commit v1 on v0

v1 whole, which is shorter than its diff:
```python
import math

import jax
import jax.numpy as jnp
from jax import lax
from jax.experimental import pallas as pl
from jax.experimental.pallas import tpu as pltpu
from jax.sharding import PartitionSpec as P

SEQUENCE_LENGTH = 1024


epsilon = 1e-06
masked = -1e30


def matmul(left, right):
    return jnp.dot(left, right, preferred_element_type=jnp.float32)


def contract_first(left, right):
    return lax.dot_general(
        left, right, (((0,), (0,)), ((), ())), preferred_element_type=jnp.float32
    )


def contract_last(left, right):
    return lax.dot_general(
        left, right, (((1,), (1,)), ((), ())), preferred_element_type=jnp.float32
    )


def tables(positions, width):
    frequency = jnp.exp(
        jnp.arange(width // 2, dtype=jnp.float32) * (-2.0 * math.log(1000000.0) / width)
    )
    angles = positions.astype(jnp.float32)[:, None] * frequency[None, :]
    cosine = jnp.cos(angles)
    sine = jnp.sin(angles)
    return (
        jnp.concatenate([cosine, cosine], axis=-1),
        jnp.concatenate([-sine, sine], axis=-1),
    )


def inverse_rms(value_rows):
    return lax.rsqrt(jnp.mean(value_rows * value_rows, axis=-1, keepdims=True) + epsilon)


def norm_backward(upstream, scaled, inverse, gain):
    inner = upstream * gain
    return inverse * (inner - scaled * jnp.mean(inner * scaled, axis=-1, keepdims=True))


class Links:
    def __init__(self, dp_size, tensor_size):
        self.dp_size = dp_size
        self.tensor_size = tensor_size

    def across(self, value, bit):
        return lax.ppermute(
            value, "tensor", [(place, place ^ bit) for place in range(self.tensor_size)]
        )

    def relative_tokens(self, values):
        count = values.shape[0] // self.tensor_size
        place = lax.axis_index("tensor")
        return jnp.concatenate(
            [
                lax.dynamic_slice_in_dim(values, (place ^ other) * count, count, 0)
                for other in range(self.tensor_size)
            ],
            axis=0,
        )

    def gather_tokens(self, block):
        if self.tensor_size != 4:
            bit = 1
            while bit < self.tensor_size:
                block = jnp.concatenate([block, self.across(block, bit)], axis=0)
                bit *= 2
            return block
        half = block.shape[0] // 2
        by_x = self.across(block, 1)
        by_y = self.across(block, 2)
        corner_low = self.across(by_y[:half], 1)
        corner_high = self.across(by_x[half:], 2)
        return jnp.concatenate([block, by_x, by_y, corner_low, corner_high], axis=0)

    def scatter_tokens(self, partial):
        if self.tensor_size != 4:
            bit = self.tensor_size // 2
            while bit:
                middle = partial.shape[0] // 2
                arrived = self.across(partial[middle:], bit).astype(jnp.float32)
                total = partial[:middle].astype(jnp.float32) + arrived
                partial = total.astype(partial.dtype)
                bit //= 2
            return total
        count = partial.shape[0] // self.tensor_size
        half = count // 2

        def piece(block, high):
            start = block * count + high * half
            return partial[start : start + half]

        wide = jnp.float32
        low_own = self.across(piece(1, 0), 1)
        low_pass = self.across(piece(3, 0), 1)
        high_own = self.across(piece(2, 1), 2)
        high_pass = self.across(piece(3, 1), 2)
        low_last = self.across(
            (piece(2, 0).astype(wide) + low_pass.astype(wide)).astype(partial.dtype), 2
        )
        high_last = self.across(
            (piece(1, 1).astype(wide) + high_pass.astype(wide)).astype(partial.dtype), 1
        )
        low = piece(0, 0).astype(wide) + low_own.astype(wide) + low_last.astype(wide)
        high = piece(0, 1).astype(wide) + high_own.astype(wide) + high_last.astype(wide)
        return jnp.concatenate([low, high], axis=0)

    def gather_weight(self, shard):
        return lax.all_gather(shard, "dp", axis=0, tiled=True)

    def scatter_weight(self, partial):
        return lax.psum_scatter(partial, "dp", scatter_dimension=0, tiled=True)

    def total(self, value):
        bit = 1
        while bit < self.tensor_size:
            value = value + self.across(value, bit)
            bit *= 2
        bit = 1
        while bit < self.dp_size:
            value = value + lax.ppermute(
                value, "dp", [(place, place ^ bit) for place in range(self.dp_size)]
            )
            bit *= 2
        return value


def product(left, right, left_axis, right_axis):
    return lax.dot_general(
        left,
        right,
        (((left_axis,), (right_axis,)), ((), ())),
        preferred_element_type=jnp.float32,
    )


class Attention:
    def __init__(self, rows, head_size, query_heads, key_heads, blocks):
        self.rows = rows
        self.head_size = head_size
        self.query_heads = query_heads
        self.key_heads = key_heads
        self.grouping = query_heads // key_heads
        self.blocks = blocks
        self.block = rows // blocks
        self.scale = head_size ** (-0.5)

    def outside(self, place, index):
        return pl.ds(pl.multiple_of((index ^ place) * self.block, self.block), self.block)

    def inside(self, index):
        return slice(index * self.block, (index + 1) * self.block)

    def head(self, index):
        return slice(index * self.head_size, (index + 1) * self.head_size)

    def turn(self, rows):
        return pltpu.roll(rows, self.head_size // 2, axis=1)

    def forward_kernel(
        self, place_ref, raw_query, raw_key, raw_value, cosine, sine, query_gain, key_gain,
        query, key, value, attended, totals,
    ):
        place = place_ref[0]

        def prepared(raw, gain, where):
            normed = raw * inverse_rms(raw) * gain
            turned = normed * cosine[where, :] + self.turn(normed) * sine[where, :]
            return turned.astype(jnp.bfloat16)

        for index in range(self.blocks):
            there, here = self.outside(place, index), self.inside(index)
            key[here, :] = prepared(raw_key[there, :], key_gain[...], there)
            value[here, :] = raw_value[there, :].astype(jnp.bfloat16)
            for member in range(self.grouping):
                query[here, self.head(member)] = prepared(
                    raw_query[there, self.head(member)], query_gain[...], there
                )
        for member in range(self.grouping):
            for index in range(self.blocks):
                span = (index + 1) * self.block
                scores = self.scale * product(
                    query[self.inside(index), self.head(member)], key[:span, :], 1, 1
                )
                row = index * self.block + lax.broadcasted_iota(jnp.int32, scores.shape, 0)
                column = lax.broadcasted_iota(jnp.int32, scores.shape, 1)
                scores = jnp.where(column <= row, scores, masked)
                highest = jnp.max(scores, axis=1, keepdims=True)
                powers = jnp.exp(scores - highest)
                total = jnp.sum(powers, axis=1, keepdims=True)
                shares = (powers * (1.0 / total)).astype(jnp.bfloat16)
                attended[self.outside(place, index), self.head(member)] = product(
                    shares, value[:span, :], 1, 0
                ).astype(jnp.bfloat16)
                log_total = jnp.broadcast_to(
                    highest + jnp.log(total), (self.block, self.head_size)
                )
                totals[0, member : member + 1, self.inside(index)] = log_total.T[:1, :]

    def forward(self, place, raw, cosine, sine, query_gain, key_gain):
        rows, size, group = self.rows, self.head_size, self.grouping
        wide = group * size
        first_key, first_value = self.query_heads, self.query_heads + self.key_heads
        whole = lambda h, p: (0, 0)
        by_head = lambda h, p: (0, h)
        low = jnp.bfloat16
        return pl.pallas_call(
            self.forward_kernel,
            name="attention_forward",
            grid_spec=pltpu.PrefetchScalarGridSpec(
                num_scalar_prefetch=1,
                grid=(self.key_heads,),
                in_specs=[
                    pl.BlockSpec((rows, wide), by_head),
                    pl.BlockSpec((rows, size), lambda h, p: (0, first_key + h)),
                    pl.BlockSpec((rows, size), lambda h, p: (0, first_value + h)),
                    pl.BlockSpec((rows, size), whole),
                    pl.BlockSpec((rows, size), whole),
                    pl.BlockSpec((1, size), whole),
                    pl.BlockSpec((1, size), whole),
                ],
                out_specs=[
                    pl.BlockSpec((rows, wide), by_head),
                    pl.BlockSpec((rows, size), by_head),
                    pl.BlockSpec((rows, size), by_head),
                    pl.BlockSpec((rows, wide), by_head),
                    pl.BlockSpec((1, group, rows), lambda h, p: (h, 0, 0)),
                ],
            ),
            out_shape=[
                jax.ShapeDtypeStruct((rows, self.query_heads * size), low),
                jax.ShapeDtypeStruct((rows, self.key_heads * size), low),
                jax.ShapeDtypeStruct((rows, self.key_heads * size), low),
                jax.ShapeDtypeStruct((rows, self.query_heads * size), low),
                jax.ShapeDtypeStruct((self.key_heads, group, rows), jnp.float32),
            ],
        )(place, raw, raw, raw, cosine, sine, query_gain[None, :], key_gain[None, :])

    def backward_kernel(
        self, place_ref, raw_query, raw_key, cosine, sine, query_gain, key_gain,
        query, key, value, totals, upstream,
        raw_grad, query_gain_grad, key_gain_grad, key_total, value_total,
    ):
        place = place_ref[0]
        current = pl.program_id(0)
        size, group = self.head_size, self.grouping

        @pl.when(current == 0)
        def _():
            query_gain_grad[...] = jnp.zeros_like(query_gain_grad)
            key_gain_grad[...] = jnp.zeros_like(key_gain_grad)

        def store(where, head, grad):
            column = pl.multiple_of(head * size, size)
            raw_grad[where, pl.ds(column, size)] = grad.astype(jnp.bfloat16)

        def through_norm(raw, grad, gain, where, gain_grad):
            inverse = inverse_rms(raw)
            scaled = raw * inverse
            normed_grad = grad * cosine[where, :] - self.turn(grad) * sine[where, :]
            gain_grad[...] += jnp.sum(normed_grad * scaled, axis=0, keepdims=True)
            return norm_backward(normed_grad, scaled, inverse, gain)

        for member in range(group):
            for index in reversed(range(self.blocks)):
                here, there = self.inside(index), self.outside(place, index)
                span = (index + 1) * self.block
                query_block = query[here, self.head(member)]
                grad_block = upstream[there, self.head(member)]
                scores = self.scale * product(key[:span, :], query_block, 1, 1)
                row = index * self.block + lax.broadcasted_iota(jnp.int32, scores.shape, 1)
                column = lax.broadcasted_iota(jnp.int32, scores.shape, 0)
                scores = jnp.where(column <= row, scores, masked)
                shares = jnp.exp(scores - totals[0, member : member + 1, here])
                share_grad = product(value[:span, :], grad_block, 1, 1)
                inner = jnp.sum(share_grad * shares, axis=0, keepdims=True)
                score_grad = (shares * (share_grad - inner)).astype(jnp.bfloat16)
                value_part = product(shares.astype(jnp.bfloat16), grad_block, 1, 0)
                key_part = product(score_grad, query_block, 1, 0)
                if member == 0 and index == self.blocks - 1:
                    value_total[...] = value_part
                    key_total[...] = key_part
                else:
                    value_total[:span, :] += value_part
                    key_total[:span, :] += key_part
                query_grad = self.scale * product(score_grad, key[:span, :], 0, 0)
                store(
                    there,
                    current * group + member,
                    through_norm(
                        raw_query[there, self.head(member)],
                        query_grad,
                        query_gain[...],
                        there,
                        query_gain_grad,
                    ),
                )
        for index in range(self.blocks):
            here, there = self.inside(index), self.outside(place, index)
            store(
                there,
                self.query_heads + current,
                through_norm(
                    raw_key[there, :],
                    self.scale * key_total[here, :],
                    key_gain[...],
                    there,
                    key_gain_grad,
                ),
            )
            store(there, self.query_heads + self.key_heads + current, value_total[here, :])

    def backward(
        self, place, raw, cosine, sine, query_gain, key_gain, query, key, value, totals, upstream
    ):
        rows, size, group = self.rows, self.head_size, self.grouping
        wide = group * size
        first_key = self.query_heads
        whole = lambda h, p: (0, 0)
        by_head = lambda h, p: (0, h)
        columns = (self.query_heads + 2 * self.key_heads) * size
        return pl.pallas_call(
            self.backward_kernel,
            name="attention_backward",
            grid_spec=pltpu.PrefetchScalarGridSpec(
                num_scalar_prefetch=1,
                grid=(self.key_heads,),
                in_specs=[
                    pl.BlockSpec((rows, wide), by_head),
                    pl.BlockSpec((rows, size), lambda h, p: (0, first_key + h)),
                    pl.BlockSpec((rows, size), whole),
                    pl.BlockSpec((rows, size), whole),
                    pl.BlockSpec((1, size), whole),
                    pl.BlockSpec((1, size), whole),
                    pl.BlockSpec((rows, wide), by_head),
                    pl.BlockSpec((rows, size), by_head),
                    pl.BlockSpec((rows, size), by_head),
                    pl.BlockSpec((1, group, rows), lambda h, p: (h, 0, 0)),
                    pl.BlockSpec((rows, wide), by_head),
                ],
                out_specs=[
                    pl.BlockSpec((rows, columns), whole),
                    pl.BlockSpec((1, size), whole),
                    pl.BlockSpec((1, size), whole),
                ],
                scratch_shapes=[
                    pltpu.VMEM((rows, size), jnp.float32),
                    pltpu.VMEM((rows, size), jnp.float32),
                ],
            ),
            out_shape=[
                jax.ShapeDtypeStruct((rows, columns), jnp.bfloat16),
                jax.ShapeDtypeStruct((1, size), jnp.float32),
                jax.ShapeDtypeStruct((1, size), jnp.float32),
            ],
        )(
            place, raw, raw, cosine, sine, query_gain[None, :], key_gain[None, :],
            query, key, value, totals, upstream,
        )


def shards(
    links,
    tokens,
    positions,
    input_gain,
    middle_gain,
    query_gain,
    key_gain,
    query_weight,
    key_matrix,
    value_matrix,
    output_weight,
    gate_weight,
    up_weight,
    down_weight,
    layer_cotangent,
):
    head_size = query_gain.shape[0]
    query_heads = query_weight.shape[1] // head_size
    key_heads = key_matrix.shape[1] // head_size
    query_width = query_heads * head_size
    key_width = key_heads * head_size
    group_rows = positions.shape[0]
    assert group_rows == SEQUENCE_LENGTH
    attention = Attention(group_rows, head_size, query_heads, key_heads, links.tensor_size)
    place = lax.axis_index("tensor").astype(jnp.int32)[None]
    hidden = gate_weight.shape[1]
    wide_attention = links.gather_weight(
        jnp.concatenate([query_weight, key_matrix, value_matrix], axis=1)
    )
    wide_output = links.gather_weight(output_weight)
    wide_feed = links.gather_weight(jnp.concatenate([gate_weight, up_weight], axis=1))
    wide_down = links.gather_weight(down_weight)

    positions = links.relative_tokens(positions)
    inputs = tokens.astype(jnp.float32)
    inverse_in = inverse_rms(inputs)
    scaled_in = inputs * inverse_in
    normed_rows = links.gather_tokens((scaled_in * input_gain).astype(jnp.bfloat16))
    own_cotangent, normed_rows = lax.optimization_barrier((layer_cotangent, normed_rows))
    cotangent = links.gather_tokens(own_cotangent)

    cosine, sine = tables(positions, head_size)
    raw_rows = matmul(normed_rows, wide_attention)
    query_rows, key_rows, value_rows, attended_rows, log_totals = attention.forward(
        place, raw_rows, cosine, sine, query_gain, key_gain
    )
    branch = links.scatter_tokens(contract_last(attended_rows, wide_output).astype(jnp.bfloat16))
    middle = inputs + branch
    inverse_mid = inverse_rms(middle)
    scaled_mid = middle * inverse_mid
    normed_middle = links.gather_tokens((scaled_mid * middle_gain).astype(jnp.bfloat16))
    feed = matmul(normed_middle, wide_feed)
    gating, upward = feed[:, :hidden], feed[:, hidden:]
    gate_sigmoid = jax.nn.sigmoid(gating)
    silu_gate = gating * gate_sigmoid
    active = (silu_gate * upward).astype(jnp.bfloat16)
    down_term = contract_first(cotangent, active).astype(jnp.bfloat16)
    active, down_term = lax.optimization_barrier((active, down_term))
    down_sum = links.scatter_weight(down_term)
    cotangent, down_term = lax.optimization_barrier((cotangent, down_term))
    active_grad = matmul(cotangent, wide_down)
    gate_grad = (
        active_grad * upward * gate_sigmoid * (1.0 + gating * (1.0 - gate_sigmoid))
    ).astype(jnp.bfloat16)
    upward_grad = (active_grad * silu_gate).astype(jnp.bfloat16)
    feed_grad = jnp.concatenate([gate_grad, upward_grad], axis=1)
    middle_partial = contract_last(feed_grad, wide_feed)
    middle_normed_grad = links.scatter_tokens(middle_partial.astype(jnp.bfloat16))
    feed_term = contract_first(normed_middle, feed_grad).astype(jnp.bfloat16)
    feed_term, down_sum = lax.optimization_barrier((feed_term, down_sum))
    feed_sum = links.scatter_weight(feed_term)
    layer_output = middle + links.scatter_tokens(
        contract_last(active, wide_down).astype(jnp.bfloat16)
    )
    middle_gain_term = jnp.sum(middle_normed_grad * scaled_mid, axis=0)
    middle_grad = own_cotangent.astype(jnp.float32) + norm_backward(
        middle_normed_grad, scaled_mid, inverse_mid, middle_gain
    )
    low_middle_grad, feed_term = lax.optimization_barrier(
        (middle_grad.astype(jnp.bfloat16), feed_term)
    )
    branch_grad = links.gather_tokens(low_middle_grad)
    output_term = contract_first(branch_grad, attended_rows).astype(jnp.bfloat16)
    output_term, feed_sum = lax.optimization_barrier((output_term, feed_sum))
    output_sum = links.scatter_weight(output_term)
    branch_grad, output_term = lax.optimization_barrier((branch_grad, output_term))
    attended_grad = matmul(branch_grad, wide_output).astype(jnp.bfloat16)
    raw_grad, query_gain_term, key_gain_term = attention.backward(
        place,
        raw_rows,
        cosine,
        sine,
        query_gain,
        key_gain,
        query_rows,
        key_rows,
        value_rows,
        log_totals,
        attended_grad,
    )
    input_normed_grad = links.scatter_tokens(
        contract_last(raw_grad, wide_attention).astype(jnp.bfloat16)
    )
    attention_sum = links.scatter_weight(contract_first(normed_rows, raw_grad).astype(jnp.bfloat16))
    input_gain_term = jnp.sum(input_normed_grad * scaled_in, axis=0)
    tokens_grad = middle_grad + norm_backward(input_normed_grad, scaled_in, inverse_in, input_gain)
    other_terms = links.total(
        jnp.concatenate([middle_gain_term, query_gain_term[0], key_gain_term[0]])
    )
    width = tokens.shape[1]
    attention_sum, output_sum, feed_sum, down_sum = (
        summed.astype(jnp.float32) for summed in (attention_sum, output_sum, feed_sum, down_sum)
    )
    return (
        layer_output,
        tokens_grad,
        links.total(input_gain_term),
        other_terms[:width],
        other_terms[width : width + head_size],
        other_terms[width + head_size :],
        attention_sum[:, :query_width],
        attention_sum[:, query_width : query_width + key_width],
        attention_sum[:, query_width + key_width :],
        output_sum,
        feed_sum[:, :hidden],
        feed_sum[:, hidden:],
        down_sum,
    )


def solution(mesh):
    links = Links(mesh.shape["dp"], mesh.shape["tensor"])
    placed = (
        P(("dp", "tensor"), None),
        P("dp"),
        P(),
        P(),
        P(),
        P(),
        P("dp", "tensor"),
        P("dp", "tensor"),
        P("dp", "tensor"),
        P("dp", "tensor"),
        P("dp", "tensor"),
        P("dp", "tensor"),
        P("dp", "tensor"),
        P(("dp", "tensor"), None),
    )
    return jax.shard_map(
        lambda *arrays: shards(links, *arrays),
        mesh=mesh,
        in_specs=placed,
        out_specs=(
            P(("dp", "tensor"), None),
            P(("dp", "tensor"), None),
            P(),
            P(),
            P(),
            P(),
            P("dp", "tensor"),
            P("dp", "tensor"),
            P("dp", "tensor"),
            P("dp", "tensor"),
            P("dp", "tensor"),
            P("dp", "tensor"),
            P("dp", "tensor"),
        ),
        check_vma=False,
    )
```

time: 1170 us -> 627 us (0.54)
  waiting for transfers between devices: 757 us -> 321 us
  matrix products: 211 us -> 126 us
  starting transfers between devices: 1.06 us -> 68.3 us
  other arithmetic: 76.2 us -> 30.7 us
  blocking collectives: 40 us -> 0 us
  Pallas kernels: 0 us -> 30.4 us
  local copies, waits for them, and re-layouts: 53.5 us -> 29.5 us
    all_gather x11 -> x4, waiting for transfers between devices: 396 us -> 41 us  [gather_weight(): return lax.all_gather(shard, 'dp', axis=0, tiled=True)]
    reduce_scatter x11 -> x4, waiting for transfers between devices: 356 us -> 34.8 us  [scatter_weight(): return lax.psum_scatter(partial, 'dp', scatter_dimension=0, tiled=True)]
    ppermute x0 -> x50, waiting for transfers between devices: none -> 244 us  [the longest x44 239 us: across(): lax.ppermute(value, 'tensor', [(place, place ^ bit) for place in range(se...]
    ppermute x0 -> x50, starting transfers between devices: none -> 67.8 us  [the longest x44 55.3 us: across(): lax.ppermute(value, 'tensor', [(place, place ^ bit) for place in range(se...]
    dot_general x14 -> x0, matrix products: 53.3 us -> none  [the longest x2 15 us: backward_block(): jnp.einsum('qhgd,khd->hgqk', grad_block, value_rows, preferred_element_ty...]
    psum x1 -> x0, blocking collectives: 40 us -> none  [shards(): lax.psum((input_gain_term, middle_gain_term, query_gain_term, key_gain_te...]
    pallas_call x0 -> x2, Pallas kernels: none -> 30.4 us  [the longest x1 16.1 us: backward(): pl.pallas_call(self.backward_kernel, name='attention_backward', grid_spec...]
    convert_element_type x15 -> x7, other arithmetic: 27.3 us -> 5.58 us  [the longest x2 3.13 us: shards(): summed.astype(jnp.float32)]
  transfers between devices with their start and end apart: 22 -> 58, of which waited for: 20 -> 40; matrix products, arithmetic and copies ran while one was open for 23% -> 27% of each run, Pallas kernels for 0% -> 5%
where the time goes in v1:
time: 627 us; the launch traced here: 621 us
  waiting for transfers between devices  321 us (51%)
  matrix products  126 us (20%)
  starting transfers between devices  68.3 us (11%)
  other arithmetic  30.7 us (5%)
  Pallas kernels  30.4 us (5%)
  local copies, waits for them, and re-layouts  29.5 us (5%)
  between operations  15.2 us (2%)
    ppermute x44, waiting for transfers between devices, across(): lax.ppermute(value, 'tensor', [(place, place ^ bit) for place in range(se...  239 us
    ppermute x44, starting transfers between devices, across(): lax.ppermute(value, 'tensor', [(place, place ^ bit) for place in range(se...  55.3 us
    dot_general x4, matrix products, matmul(): return jnp.dot(left, right, preferred_element_type=jnp.float32)  47.1 us
    all_gather x4, waiting for transfers between devices, gather_weight(): return lax.all_gather(shard, 'dp', axis=0, tiled=True)  41 us
    dot_general x4, matrix products, contract_first(): lax.dot_general(left, right, (((0,), (0,)), ((), ())), preferred_element_...  40.8 us
    dot_general x4, matrix products, contract_last(): lax.dot_general(left, right, (((1,), (1,)), ((), ())), preferred_element_...  38.2 us
    reduce_scatter x4, waiting for transfers between devices, scatter_weight(): return lax.psum_scatter(partial, 'dp', scatter_dimension=0, tiled=True)  34.8 us
    unnamed x64, local copies, waits for them, and re-layouts  19.8 us
  transfers between devices with their start and end apart: 58, of which 40 were waited for; matrix products, arithmetic and copies ran while one was open for 27% of the time, Pallas kernels for 5%

profile of v1, /device:TPU:0, one launch (start us, length us, event | category | flops | bytes accessed | tf_op | source)
XLA Modules:
  0.0 620.8 jit_solution(16737503843338924786)
XLA Ops:
  7.2 2.0 pad_maximum_fusion.8
  10.1 2.7 pad_maximum_fusion.7
  14.8 3.0 collective-permute-start.1
  19.4 1.9 fusion.14
  21.3 19.9 %collective-permute-done.1 = bf16[256,2048]{1,0:T(8,128)(2,1)S(1)} collective-permute-done((bf16[256,2048]{1,0:T(8,128)(2,1)}, bf16[256,2048]{1,0:T(8,128)(2,1)S(1)}, u32[]{:S(2)}, u32[]{:S(2)}) %collective-permute-start.1) | collective-permute-done | bytes 1048608 | tf_op jit(solution)/shard_map/ppermute | solution.py:61
  41.2 1.8 collective-permute-start.2
  48.1 6.4 %collective-permute-done.2 = bf16[128,2048]{1,0:T(8,128)(2,1)S(1)} collective-permute-done((bf16[128,2048]{1,0:T(8,128)(2,1)S(1)}, bf16[128,2048]{1,0:T(8,128)(2,1)S(1)}, u32[]{:S(2)}, u32[]{:S(2)}) %collective-permute-start.2) | collective-permute-done | bytes 524320 | tf_op jit(solution)/shard_map/ppermute | solution.py:61
  55.3 1.7 collective-permute-done.3
  57.9 2.3 all-gather.5.cloned.1.call-done
  60.1 10.0 %fusion.28.raw_query.raw_key.raw_value = f32[1024,1024]{1,0:T(8,128)} fusion(bf16[1024,2048]{1,0:T(8,128)(2,1)} %constant_dynamic-update-slice_fusion, bf16[2048,1024]{1,0:T(8,128)(2,1)} %all-gather.5.cloned.1.call-done), kind=kOutput, calls=%fused_computation.100 | convolution fusion | flops 4294967296 | bytes 12582912 | tf_op jit(solution)/shard_map/dot_general | solution.py:18
  70.2 14.3 %attention_forward.1 = (bf16[1024,512]{1,0:T(8,128)(2,1)}, bf16[1024,256]{1,0:T(8,128)(2,1)}, bf16[1024,256]{1,0:T(8,128)(2,1)}, bf16[1024,512]{1,0:T(8,128)(2,1)}, f32[2,2,1024]{2,1,0:T(2,128)}) custom-call(s32[1]{0:T(128)} %bitcast.place_ref, f32[1024,1024]{1,0:T(8,128)} %fusion.28.raw_query.raw_key.raw_value, ...), custom_call_target="tpu_custom_call" | custom-call | tf_op jit(solution)/shard_map/attention_forward/pallas_call | solution.py:221
  84.5 5.0 all-gather.7.cloned.1.call-done
  89.5 4.3 convolution_convert_fusion.3
  97.6 11.3 %collective-permute-done.5 = bf16[128,2048]{1,0:T(8,128)(2,1)S(1)} collective-permute-done((bf16[128,2048]{1,0:T(8,128)(2,1)S(1)}, bf16[128,2048]{1,0:T(8,128)(2,1)S(1)}, u32[]{:S(2)}, u32[]{:S(2)}) %collective-permute-start.5) | collective-permute-done | bytes 524320 | tf_op jit(solution)/shard_map/ppermute | solution.py:61
  111.1 8.3 %collective-permute-done.4 = bf16[128,2048]{1,0:T(8,128)(2,1)S(1)} collective-permute-done((bf16[128,2048]{1,0:T(8,128)(2,1)S(1)}, bf16[128,2048]{1,0:T(8,128)(2,1)S(1)}, u32[]{:S(2)}, u32[]{:S(2)}) %collective-permute-start.4) | collective-permute-done | bytes 524320 | tf_op jit(solution)/shard_map/ppermute | solution.py:61
  119.4 4.5 collective-permute-done.6
  129.0 6.2 collective-permute-done.7
  135.2 5.0 collective-permute-done.9
  145.9 11.8 %collective-permute-done.15 = bf16[256,2048]{1,0:T(8,128)(2,1)S(1)} collective-permute-done((bf16[256,2048]{1,0:T(8,128)(2,1)}, bf16[256,2048]{1,0:T(8,128)(2,1)S(1)}, u32[]{:S(2)}, u32[]{:S(2)}) %collective-permute-start.15) | collective-permute-done | bytes 1048608 | tf_op jit(solution)/shard_map/ppermute | solution.py:61
  162.9 9.7 %collective-permute-done.16 = bf16[128,2048]{1,0:T(8,128)(2,1)S(1)} collective-permute-done((bf16[128,2048]{1,0:T(8,128)(2,1)S(1)}, bf16[128,2048]{1,0:T(8,128)(2,1)S(1)}, u32[]{:S(2)}, u32[]{:S(2)}) %collective-permute-start.16) | collective-permute-done | bytes 524320 | tf_op jit(solution)/shard_map/ppermute | solution.py:61
  172.6 7.5 %collective-permute-done.11 = bf16[256,2048]{1,0:T(8,128)(2,1)S(1)} collective-permute-done((bf16[256,2048]{1,0:T(8,128)(2,1)S(1)}, bf16[256,2048]{1,0:T(8,128)(2,1)S(1)}, u32[]{:S(2)}, u32[]{:S(2)}) %collective-permute-start.11) | collective-permute-done | bytes 1048608 | tf_op jit(solution)/shard_map/ppermute | solution.py:61
  181.7 7.4 %collective-permute-done.17 = bf16[128,2048]{1,0:T(8,128)(2,1)S(1)} collective-permute-done((bf16[128,2048]{1,0:T(8,128)(2,1)S(1)}, bf16[128,2048]{1,0:T(8,128)(2,1)S(1)}, u32[]{:S(2)}, u32[]{:S(2)}) %collective-permute-start.17) | collective-permute-done | bytes 524320 | tf_op jit(solution)/shard_map/ppermute | solution.py:61
  189.2 5.9 collective-permute-done.10
  198.8 3.5 collective-permute-done.12
  205.2 2.8 all-gather.9.cloned.1.call-done
  208.0 17.4 %fusion.29 = f32[1024,3072]{1,0:T(8,128)S(1)} fusion(bf16[1024,2048]{1,0:T(8,128)(2,1)} %constant_dynamic-update-slice_fusion.5, bf16[2048,3072]{1,0:T(8,128)(2,1)} %all-gather.9.cloned.1.call-done), kind=kOutput, calls=%fused_computation.101 | convolution fusion | flops 12884901888 | bytes 29360128 | tf_op jit(solution)/shard_map/dot_general | solution.py:18
  225.4 2.0 multiply_convert_fusion.2
  227.3 3.8 copy-done.2
  232.8 8.7 %convolution_convert_fusion.1 = bf16[2048,1536]{1,0:T(8,128)(2,1)} fusion(bf16[1024,2048]{1,0:T(8,128)(2,1)S(1)} %copy-done.11, bf16[1024,1536]{1,0:T(8,128)(2,1)S(1)} %multiply_convert_fusion.2), kind=kOutput, calls=%fused_computation.1 | convolution fusion | flops 6445596672 | bytes 13631488 | tf_op jit(solution)/shard_map/dot_general | solution.py:22
  241.5 31.0 %all-gather.11.cloned.1.call-done = bf16[2048,1536]{1,0:T(8,128)(2,1)} async-done(((bf16[256,1536]{1,0:T(8,128)(2,1)}), bf16[2048,1536]{1,0:T(8,128)(2,1)}) %all-gather.11.cloned.1.call-update) | async-done | bytes 6291472 | tf_op jit(solution)/shard_map/all_gather | solution.py:123
  272.5 14.3 %multiply_convert_fusion.1 = (bf16[1024,1536]{1,0:T(8,128)(2,1)S(1)}, bf16[1024,1536]{1,0:T(8,128)(2,1)S(1)}) fusion(f32[1024,3072]{1,0:T(8,128)} %copy-done.2, bf16[1024,2048]{1,0:T(8,128)(2,1)} %copy-done.10, bf16[2048,1536]{1,0:T(8,128)(2,1)} %all-gather.11.cloned.1.call-done), kind=kOutput, calls=%fused_computation.4 | convolution fusion | flops 6462898176 | bytes 29360128 | tf_op jit(solution)/shard_map/dot_general | solution.py:18
  289.4 18.9 %convolution_convert_fusion = bf16[2048,3072]{1,0:T(8,128)(2,1)} fusion(bf16[1024,2048]{1,0:T(8,128)(2,1)} %constant_dynamic-update-slice_fusion.5, bf16[1024,1536]{1,0:T(8,128)(2,1)S(1)} %get-tuple-element.64, bf16[1024,1536]{1,0:T(8,128)(2,1)S(1)} %get-tuple-element.63), kind=kOutput, calls=%fused_computation | convolution fusion | flops 12903776256 | bytes 23068672 | tf_op jit(solution)/shard_map/dot_general | solution.py:22
  308.3 34.8 %reduce-scatter.5.cloned.1.call-done = bf16[256,1536]{1,0:T(8,128)(2,1)} async-done(((bf16[2048,1536]{1,0:T(8,128)(2,1)}), bf16[256,1536]{1,0:T(8,128)(2,1)}) %reduce-scatter.5.cloned.1.call-update) | async-done | bytes 786448 | tf_op jit(solution)/shard_map/reduce_scatter | solution.py:126
  343.2 17.8 %fusion.2 = bf16[1024,2048]{1,0:T(8,128)(2,1)S(1)} fusion(bf16[2048,3072]{1,0:T(8,128)(2,1)} %all-gather.9.cloned.1.call-done, bf16[1024,1536]{1,0:T(8,128)(2,1)} %copy-done.24, bf16[1024,1536]{1,0:T(8,128)(2,1)} %copy-done.23), kind=kOutput, calls=%fused_computation.10 | convolution fusion | flops 12899581952 | bytes 23068672 | tf_op jit(solution)/shard_map/dot_general | solution.py:28
  362.9 8.9 %convolution_convert_fusion.2 = bf16[1024,2048]{1,0:T(8,128)(2,1)S(1)} fusion(bf16[1024,1536]{1,0:T(8,128)(2,1)S(1)} %copy-done.7, bf16[2048,1536]{1,0:T(8,128)(2,1)} %all-gather.11.cloned.1.call-done), kind=kOutput, calls=%fused_computation.9 | convolution fusion | flops 6444548096 | bytes 13631488 | tf_op jit(solution)/shard_map/dot_general | solution.py:28
  377.7 9.1 %collective-permute-done.19 = bf16[128,2048]{1,0:T(8,128)(2,1)S(1)} collective-permute-done((bf16[128,2048]{1,0:T(8,128)(2,1)S(1)}, bf16[128,2048]{1,0:T(8,128)(2,1)S(1)}, u32[]{:S(2)}, u32[]{:S(2)}) %collective-permute-start.19) | collective-permute-done | bytes 524320 | tf_op jit(solution)/shard_map/ppermute | solution.py:61
  388.5 9.6 %collective-permute-done.24 = bf16[128,2048]{1,0:T(8,128)(2,1)S(1)} collective-permute-done((bf16[128,2048]{1,0:T(8,128)(2,1)S(1)}, bf16[128,2048]{1,0:T(8,128)(2,1)S(1)}, u32[]{:S(2)}, u32[]{:S(2)}) %collective-permute-start.24) | collective-permute-done | bytes 524320 | tf_op jit(solution)/shard_map/ppermute | solution.py:61
  402.1 4.4 collective-permute-done.18
  407.9 14.7 %collective-permute-done.22 = bf16[128,2048]{1,0:T(8,128)(2,1)S(1)} collective-permute-done((bf16[128,2048]{1,0:T(8,128)(2,1)S(1)}, bf16[128,2048]{1,0:T(8,128)(2,1)S(1)}, u32[]{:S(2)}, u32[]{:S(2)}) %collective-permute-start.22) | collective-permute-done | bytes 524320 | tf_op jit(solution)/shard_map/ppermute | solution.py:61
  422.6 18.6 %collective-permute-done.20 = bf16[128,2048]{1,0:T(8,128)(2,1)S(1)} collective-permute-done((bf16[128,2048]{1,0:T(8,128)(2,1)S(1)}, bf16[128,2048]{1,0:T(8,128)(2,1)S(1)}, u32[]{:S(2)}, u32[]{:S(2)}) %collective-permute-start.20) | collective-permute-done | bytes 524320 | tf_op jit(solution)/shard_map/ppermute | solution.py:61
  444.0 7.9 %collective-permute-done.23 = bf16[128,2048]{1,0:T(8,128)(2,1)S(1)} collective-permute-done((bf16[128,2048]{1,0:T(8,128)(2,1)S(1)}, bf16[128,2048]{1,0:T(8,128)(2,1)S(1)}, u32[]{:S(2)}, u32[]{:S(2)}) %collective-permute-start.23) | collective-permute-done | bytes 524320 | tf_op jit(solution)/shard_map/ppermute | solution.py:61
  452.1 4.0 fusion.18
  459.0 18.7 %collective-permute-done.31 = bf16[256,2048]{1,0:T(8,128)(2,1)S(1)} collective-permute-done((bf16[256,2048]{1,0:T(8,128)(2,1)S(1)}, bf16[256,2048]{1,0:T(8,128)(2,1)S(1)}, u32[]{:S(2)}, u32[]{:S(2)}) %collective-permute-start.31) | collective-permute-done | bytes 1048608 | tf_op jit(solution)/shard_map/ppermute | solution.py:61
  477.8 2.1 collective-permute-start.32
  482.3 6.9 %collective-permute-done.32 = bf16[128,2048]{1,0:T(8,128)(2,1)S(1)} collective-permute-done((bf16[128,2048]{1,0:T(8,128)(2,1)S(1)}, bf16[128,2048]{1,0:T(8,128)(2,1)S(1)}, u32[]{:S(2)}, u32[]{:S(2)}) %collective-permute-start.32) | collective-permute-done | bytes 524320 | tf_op jit(solution)/shard_map/ppermute | solution.py:61
  490.9 2.0 copy-done.9
  492.9 3.7 convolution_convert_fusion.6
  497.0 5.5 convolution_convert_fusion.7.upstream
  502.5 16.1 %attention_backward.1 = (bf16[1024,1024]{1,0:T(8,128)(2,1)}, f32[1,128]{1,0:T(1,128)}, f32[1,128]{1,0:T(1,128)}) custom-call(s32[1]{0:T(128)} %bitcast.place_ref, f32[1024,1024]{1,0:T(8,128)} %fusion.28.raw_query.raw_key.raw_value, f32[1024,1024]{1,0:T(8,128)} %fusion.28.raw_query.raw_key.raw_value, f32[1024,128]{1,0:T(8,128)} %get-tuple-element.103.cosine, ...), custom_call_target="tpu_custom_call" | custom-call | tf_op jit(solution)/shard_map/attention_backward/pallas_call | solution.py:336
  518.5 9.5 %convolution_convert_fusion.4 = bf16[2048,1024]{1,0:T(8,128)(2,1)} fusion(bf16[1024,2048]{1,0:T(8,128)(2,1)} %constant_dynamic-update-slice_fusion, bf16[1024,1024]{1,0:T(8,128)(2,1)} %get-tuple-element.46), kind=kOutput, calls=%fused_computation.12 | convolution fusion | flops 4297064448 | bytes 10485760 | tf_op jit(solution)/shard_map/dot_general | solution.py:22
  529.6 7.2 %convolution_convert_fusion.5 = bf16[1024,2048]{1,0:T(8,128)(2,1)S(1)} fusion(bf16[1024,1024]{1,0:T(8,128)(2,1)S(1)} %copy-done.21, bf16[2048,1024]{1,0:T(8,128)(2,1)} %all-gather.5.cloned.1.call-done), kind=kOutput, calls=%fused_computation.13 | convolution fusion | flops 4297064448 | bytes 10485760 | tf_op jit(solution)/shard_map/dot_general | solution.py:28
  539.5 11.8 %collective-permute-done.35 = bf16[128,2048]{1,0:T(8,128)(2,1)S(1)} collective-permute-done((bf16[128,2048]{1,0:T(8,128)(2,1)S(1)}, bf16[128,2048]{1,0:T(8,128)(2,1)S(1)}, u32[]{:S(2)}, u32[]{:S(2)}) %collective-permute-start.35) | collective-permute-done | bytes 524320 | tf_op jit(solution)/shard_map/ppermute | solution.py:61
  551.5 2.0 collective-permute-start.37
  553.6 3.4 collective-permute-done.34
  556.9 8.2 %collective-permute-done.36 = bf16[128,2048]{1,0:T(8,128)(2,1)S(1)} collective-permute-done((bf16[128,2048]{1,0:T(8,128)(2,1)S(1)}, bf16[128,2048]{1,0:T(8,128)(2,1)S(1)}, u32[]{:S(2)}, u32[]{:S(2)}) %collective-permute-start.36) | collective-permute-done | bytes 524320 | tf_op jit(solution)/shard_map/ppermute | solution.py:61
  567.8 7.2 %collective-permute-done.45 = f32[2304]{0:T(1024)S(1)} collective-permute-done((f32[2304]{0:T(1024)S(1)}, f32[2304]{0:T(1024)S(1)}, u32[]{:S(2)}, u32[]{:S(2)}) %collective-permute-start.45) | collective-permute-done | bytes 9248 | tf_op jit(solution)/shard_map/ppermute | solution.py:61
  575.3 3.4 collective-permute-done.46
  579.9 10.0 %collective-permute-start.48 = (f32[2304]{0:T(1024)S(1)}, f32[2304]{0:T(1024)S(1)}, u32[]{:S(2)}, u32[]{:S(2)}) collective-permute-start(f32[2304]{0:T(1024)S(1)} %add.199), channel_id=1, source_target_pairs={{0,8},{4,12},{8,0},{12,4},{16,24},{20,28},{24,16},{28,20},{1,9},{5... | collective-permute-start | bytes 27656 | tf_op jit(solution)/shard_map/ppermute | solution.py:135
  596.0 2.1 fusion.24
  600.0 3.0 collective-permute-done.43
  604.5 1.9 fusion.11
  608.2 1.8 convert_element_type.281
  610.0 1.8 slice.245
  611.8 1.8 fusion.25
  (204 shorter events, 90.8 us)
Async XLA Ops:
  7.2 52.9 %all-gather.5.cloned.1.call-start = ((), (), s32[]{:S(2)}) async-start(), calls=%async_computation.4 | async-start | bytes 4718592 | tf_op jit(solution)/shard_map/all_gather | solution.py:123
  9.3 80.2 %all-gather.7.cloned.1.call-start = ((), (), s32[]{:S(2)}) async-start(), calls=%async_computation.5 | async-start | bytes 2359296 | tf_op jit(solution)/shard_map/all_gather | solution.py:123
  10.1 197.9 %all-gather.9.cloned.1.call-start = ((), (), s32[]{:S(2)}) async-start(), calls=%async_computation.6 | async-start | bytes 14155776 | tf_op jit(solution)/shard_map/all_gather | solution.py:123
  12.8 259.7 %all-gather.11.cloned.1.call-start = ((), (), s32[]{:S(2)}) async-start(), calls=%async_computation.7 | async-start | bytes 7077888 | tf_op jit(solution)/shard_map/all_gather | solution.py:123
  14.8 26.3 %collective-permute-start.1 = (bf16[256,2048]{1,0:T(8,128)(2,1)}, bf16[256,2048]{1,0:T(8,128)(2,1)S(1)}, u32[]{:S(2)}, u32[]{:S(2)}) collective-permute-start(bf16[256,2048]{1,0:T(8,128)(2,1)} %get-tuple-element.62), channel_id=1, source_target_pairs={{0,2},{1,3},{2,0},{3,1},{4,6},{5,7},{6,4},{7,5},{8,10},{9,11},{10,... | collective-permute-start | bytes 3145736 | tf_op jit(solution)/shard_map/ppermute | solution.py:61
  17.8 26.5 %collective-permute-start = (bf16[256,2048]{1,0:T(8,128)(2,1)}, bf16[256,2048]{1,0:T(8,128)(2,1)S(1)}, u32[]{:S(2)}, u32[]{:S(2)}) collective-permute-start(bf16[256,2048]{1,0:T(8,128)(2,1)} %get-tuple-element.62), channel_id=1, source_target_pairs={{0,1},{1,0},{2,3},{3,2},{4,5},{5,4},{6,7},{7,6},{8,9},{9,8},{10,11... | collective-permute-start | bytes 3145736 | tf_op jit(solution)/shard_map/ppermute | solution.py:61
  41.2 13.3 %collective-permute-start.2 = (bf16[128,2048]{1,0:T(8,128)(2,1)S(1)}, bf16[128,2048]{1,0:T(8,128)(2,1)S(1)}, u32[]{:S(2)}, u32[]{:S(2)}) collective-permute-start(bf16[128,2048]{1,0:T(8,128)(2,1)S(1)} %slice.200), channel_id=1, source_target_pairs={{0,1},{1,0},{2,3},{3,2},{4,5},{5,4},{6,7},{7,6},{8,9},{9,8},{10,11... | collective-permute-start | bytes 1572872 | tf_op jit(solution)/shard_map/ppermute | solution.py:61
  44.3 12.7 %collective-permute-start.3 = (bf16[128,2048]{1,0:T(8,128)(2,1)S(1)}, bf16[128,2048]{1,0:T(8,128)(2,1)S(1)}, u32[]{:S(2)}, u32[]{:S(2)}) collective-permute-start(bf16[128,2048]{1,0:T(8,128)(2,1)S(1)} %slice.201), channel_id=1, source_target_pairs={{0,2},{1,3},{2,0},{3,1},{4,6},{5,7},{6,4},{7,5},{8,10},{9,11},{10,... | collective-permute-start | bytes 1572872 | tf_op jit(solution)/shard_map/ppermute | solution.py:61
  93.8 31.6 %copy-start.5 = (bf16[1024,2048]{1,0:T(8,128)(2,1)}, bf16[1024,2048]{1,0:T(8,128)(2,1)S(1)}, u32[]{:S(2)}) copy-start(bf16[1024,2048]{1,0:T(8,128)(2,1)S(1)} %convolution_convert_fusion.3) | copy-start | bytes 12582916
  94.0 14.8 %collective-permute-start.5 = (bf16[128,2048]{1,0:T(8,128)(2,1)S(1)}, bf16[128,2048]{1,0:T(8,128)(2,1)S(1)}, u32[]{:S(2)}, u32[]{:S(2)}) collective-permute-start(bf16[128,2048]{1,0:T(8,128)(2,1)S(1)} %get-tuple-element.88), channel_id=1, source_target_pairs={{0,1},{1,0},{2,3},{3,2},{4,5},{5,4},{6,7},{7,6},{8,9},{9,8},{10,11... | collective-permute-start | bytes 1572872 | tf_op jit(solution)/shard_map/ppermute | solution.py:61
  95.6 23.8 %collective-permute-start.4 = (bf16[128,2048]{1,0:T(8,128)(2,1)S(1)}, bf16[128,2048]{1,0:T(8,128)(2,1)S(1)}, u32[]{:S(2)}, u32[]{:S(2)}) collective-permute-start(bf16[128,2048]{1,0:T(8,128)(2,1)S(1)} %get-tuple-element.85), channel_id=1, source_target_pairs={{0,1},{1,0},{2,3},{3,2},{4,5},{5,4},{6,7},{7,6},{8,9},{9,8},{10,11... | collective-permute-start | bytes 1572872 | tf_op jit(solution)/shard_map/ppermute | solution.py:61
  96.1 23.3 %collective-permute-start.8 = (bf16[128,2048]{1,0:T(8,128)(2,1)S(1)}, bf16[128,2048]{1,0:T(8,128)(2,1)S(1)}, u32[]{:S(2)}, u32[]{:S(2)}) collective-permute-start(bf16[128,2048]{1,0:T(8,128)(2,1)S(1)} %get-tuple-element.86), channel_id=1, source_target_pairs={{0,2},{1,3},{2,0},{3,1},{4,6},{5,7},{6,4},{7,5},{8,10},{9,11},{10,... | collective-permute-start | bytes 1572872 | tf_op jit(solution)/shard_map/ppermute | solution.py:61
  109.0 14.9 %collective-permute-start.6 = (bf16[128,2048]{1,0:T(8,128)(2,1)S(1)}, bf16[128,2048]{1,0:T(8,128)(2,1)S(1)}, u32[]{:S(2)}, u32[]{:S(2)}) collective-permute-start(bf16[128,2048]{1,0:T(8,128)(2,1)S(1)} %add_convert_fusion.7), channel_id=1, source_target_pairs={{0,2},{1,3},{2,0},{3,1},{4,6},{5,7},{6,4},{7,5},{8,10},{9,11},{10,... | collective-permute-start | bytes 1572872 | tf_op jit(solution)/shard_map/ppermute | solution.py:61
  110.5 24.6 %collective-permute-start.7 = (bf16[128,2048]{1,0:T(8,128)(2,1)S(1)}, bf16[128,2048]{1,0:T(8,128)(2,1)S(1)}, u32[]{:S(2)}, u32[]{:S(2)}) collective-permute-start(bf16[128,2048]{1,0:T(8,128)(2,1)S(1)} %get-tuple-element.87), channel_id=1, source_target_pairs={{0,2},{1,3},{2,0},{3,1},{4,6},{5,7},{6,4},{7,5},{8,10},{9,11},{10,... | collective-permute-start | bytes 1572872 | tf_op jit(solution)/shard_map/ppermute | solution.py:61
  125.3 14.9 %collective-permute-start.9 = (bf16[128,2048]{1,0:T(8,128)(2,1)S(1)}, bf16[128,2048]{1,0:T(8,128)(2,1)S(1)}, u32[]{:S(2)}, u32[]{:S(2)}) collective-permute-start(bf16[128,2048]{1,0:T(8,128)(2,1)S(1)} %get-tuple-element.84), channel_id=1, source_target_pairs={{0,1},{1,0},{2,3},{3,2},{4,5},{5,4},{6,7},{7,6},{8,9},{9,8},{10,11... | collective-permute-start | bytes 1572872 | tf_op jit(solution)/shard_map/ppermute | solution.py:61
  126.8 216.3 %reduce-scatter.5.cloned.1.call-start = ((), (), s32[]{:S(2)}) async-start(), calls=%async_computation.8 | async-start | bytes 7077888 | tf_op jit(solution)/shard_map/reduce_scatter | solution.py:126
  126.9 30.8 %collective-permute-start.15 = (bf16[256,2048]{1,0:T(8,128)(2,1)}, bf16[256,2048]{1,0:T(8,128)(2,1)S(1)}, u32[]{:S(2)}, u32[]{:S(2)}) collective-permute-start(bf16[256,2048]{1,0:T(8,128)(2,1)} %param.27), channel_id=1, source_target_pairs={{0,2},{1,3},{2,0},{3,1},{4,6},{5,7},{6,4},{7,5},{8,10},{9,11},{10,... | collective-permute-start | bytes 3145736 | tf_op jit(solution)/shard_map/ppermute | solution.py:61
  128.4 32.7 %collective-permute-start.14 = (bf16[256,2048]{1,0:T(8,128)(2,1)}, bf16[256,2048]{1,0:T(8,128)(2,1)S(1)}, u32[]{:S(2)}, u32[]{:S(2)}) collective-permute-start(bf16[256,2048]{1,0:T(8,128)(2,1)} %param.27), channel_id=1, source_target_pairs={{0,1},{1,0},{2,3},{3,2},{4,5},{5,4},{6,7},{7,6},{8,9},{9,8},{10,11... | collective-permute-start | bytes 3145736 | tf_op jit(solution)/shard_map/ppermute | solution.py:61
  144.4 35.7 %collective-permute-start.11 = (bf16[256,2048]{1,0:T(8,128)(2,1)S(1)}, bf16[256,2048]{1,0:T(8,128)(2,1)S(1)}, u32[]{:S(2)}, u32[]{:S(2)}) collective-permute-start(bf16[256,2048]{1,0:T(8,128)(2,1)S(1)} %get-tuple-element.58), channel_id=1, source_target_pairs={{0,2},{1,3},{2,0},{3,1},{4,6},{5,7},{6,4},{7,5},{8,10},{9,11},{10,... | collective-permute-start | bytes 3145736 | tf_op jit(solution)/shard_map/ppermute | solution.py:61
  157.7 14.9 %collective-permute-start.16 = (bf16[128,2048]{1,0:T(8,128)(2,1)S(1)}, bf16[128,2048]{1,0:T(8,128)(2,1)S(1)}, u32[]{:S(2)}, u32[]{:S(2)}) collective-permute-start(bf16[128,2048]{1,0:T(8,128)(2,1)S(1)} %slice.214), channel_id=1, source_target_pairs={{0,1},{1,0},{2,3},{3,2},{4,5},{5,4},{6,7},{7,6},{8,9},{9,8},{10,11... | collective-permute-start | bytes 1572872 | tf_op jit(solution)/shard_map/ppermute | solution.py:61
  159.2 35.9 %collective-permute-start.10 = (bf16[256,2048]{1,0:T(8,128)(2,1)S(1)}, bf16[256,2048]{1,0:T(8,128)(2,1)S(1)}, u32[]{:S(2)}, u32[]{:S(2)}) collective-permute-start(bf16[256,2048]{1,0:T(8,128)(2,1)S(1)} %get-tuple-element.58), channel_id=1, source_target_pairs={{0,1},{1,0},{2,3},{3,2},{4,5},{5,4},{6,7},{7,6},{8,9},{9,8},{10,11... | collective-permute-start | bytes 3145736 | tf_op jit(solution)/shard_map/ppermute | solution.py:61
  161.1 28.0 %collective-permute-start.17 = (bf16[128,2048]{1,0:T(8,128)(2,1)S(1)}, bf16[128,2048]{1,0:T(8,128)(2,1)S(1)}, u32[]{:S(2)}, u32[]{:S(2)}) collective-permute-start(bf16[128,2048]{1,0:T(8,128)(2,1)S(1)} %slice.215), channel_id=1, source_target_pairs={{0,2},{1,3},{2,0},{3,1},{4,6},{5,7},{6,4},{7,5},{8,10},{9,11},{10,... | collective-permute-start | bytes 1572872 | tf_op jit(solution)/shard_map/ppermute | solution.py:61
  180.1 22.2 %collective-permute-start.12 = (bf16[128,2048]{1,0:T(8,128)(2,1)S(1)}, bf16[128,2048]{1,0:T(8,128)(2,1)S(1)}, u32[]{:S(2)}, u32[]{:S(2)}) collective-permute-start(bf16[128,2048]{1,0:T(8,128)(2,1)S(1)} %slice.210), channel_id=1, source_target_pairs={{0,1},{1,0},{2,3},{3,2},{4,5},{5,4},{6,7},{7,6},{8,9},{9,8},{10,11... | collective-permute-start | bytes 1572872 | tf_op jit(solution)/shard_map/ppermute | solution.py:61
  195.1 9.2 %collective-permute-start.13 = (bf16[128,2048]{1,0:T(8,128)(2,1)S(1)}, bf16[128,2048]{1,0:T(8,128)(2,1)S(1)}, u32[]{:S(2)}, u32[]{:S(2)}) collective-permute-start(bf16[128,2048]{1,0:T(8,128)(2,1)S(1)} %slice.211), channel_id=1, source_target_pairs={{0,2},{1,3},{2,0},{3,1},{4,6},{5,7},{6,4},{7,5},{8,10},{9,11},{10,... | collective-permute-start | bytes 1572872 | tf_op jit(solution)/shard_map/ppermute | solution.py:61
  241.5 255.2 %reduce-scatter.7.cloned.1.call-start = ((), (), s32[]{:S(2)}) async-start(), calls=%async_computation.9 | async-start | bytes 14155776 | tf_op jit(solution)/shard_map/reduce_scatter | solution.py:126
  343.1 265.0 %reduce-scatter.11.cloned.1.call-start = ((), (), s32[]{:S(2)}) async-start(), calls=%async_computation.11 | async-start | bytes 2359296 | tf_op jit(solution)/shard_map/reduce_scatter | solution.py:126
  361.2 14.4 %collective-permute-start.25 = (bf16[128,2048]{1,0:T(8,128)(2,1)S(1)}, bf16[128,2048]{1,0:T(8,128)(2,1)S(1)}, u32[]{:S(2)}, u32[]{:S(2)}) collective-permute-start(bf16[128,2048]{1,0:T(8,128)(2,1)S(1)} %get-tuple-element.76), channel_id=1, source_target_pairs={{0,1},{1,0},{2,3},{3,2},{4,5},{5,4},{6,7},{7,6},{8,9},{9,8},{10,11... | collective-permute-start | bytes 1572872 | tf_op jit(solution)/shard_map/ppermute | solution.py:61
  371.9 14.9 %collective-permute-start.19 = (bf16[128,2048]{1,0:T(8,128)(2,1)S(1)}, bf16[128,2048]{1,0:T(8,128)(2,1)S(1)}, u32[]{:S(2)}, u32[]{:S(2)}) collective-permute-start(bf16[128,2048]{1,0:T(8,128)(2,1)S(1)} %get-tuple-element.82), channel_id=1, source_target_pairs={{0,1},{1,0},{2,3},{3,2},{4,5},{5,4},{6,7},{7,6},{8,9},{9,8},{10,11... | collective-permute-start | bytes 1572872 | tf_op jit(solution)/shard_map/ppermute | solution.py:61
  373.5 24.6 %collective-permute-start.24 = (bf16[128,2048]{1,0:T(8,128)(2,1)S(1)}, bf16[128,2048]{1,0:T(8,128)(2,1)S(1)}, u32[]{:S(2)}, u32[]{:S(2)}) collective-permute-start(bf16[128,2048]{1,0:T(8,128)(2,1)S(1)} %get-tuple-element.73), channel_id=1, source_target_pairs={{0,1},{1,0},{2,3},{3,2},{4,5},{5,4},{6,7},{7,6},{8,9},{9,8},{10,11... | collective-permute-start | bytes 1572872 | tf_op jit(solution)/shard_map/ppermute | solution.py:61
  374.0 25.6 %collective-permute-start.28 = (bf16[128,2048]{1,0:T(8,128)(2,1)S(1)}, bf16[128,2048]{1,0:T(8,128)(2,1)S(1)}, u32[]{:S(2)}, u32[]{:S(2)}) collective-permute-start(bf16[128,2048]{1,0:T(8,128)(2,1)S(1)} %get-tuple-element.74), channel_id=1, source_target_pairs={{0,2},{1,3},{2,0},{3,1},{4,6},{5,7},{6,4},{7,5},{8,10},{9,11},{10,... | collective-permute-start | bytes 1572872 | tf_op jit(solution)/shard_map/ppermute | solution.py:61
  375.7 24.5 %collective-permute-start.26 = (bf16[128,2048]{1,0:T(8,128)(2,1)S(1)}, bf16[128,2048]{1,0:T(8,128)(2,1)S(1)}, u32[]{:S(2)}, u32[]{:S(2)}) collective-permute-start(bf16[128,2048]{1,0:T(8,128)(2,1)S(1)} %add_convert_fusion.3), channel_id=1, source_target_pairs={{0,2},{1,3},{2,0},{3,1},{4,6},{5,7},{6,4},{7,5},{8,10},{9,11},{10,... | collective-permute-start | bytes 1572872 | tf_op jit(solution)/shard_map/ppermute | solution.py:61
  376.3 66.9 %collective-permute-start.27 = (bf16[128,2048]{1,0:T(8,128)(2,1)S(1)}, bf16[128,2048]{1,0:T(8,128)(2,1)S(1)}, u32[]{:S(2)}, u32[]{:S(2)}) collective-permute-start(bf16[128,2048]{1,0:T(8,128)(2,1)S(1)} %get-tuple-element.75), channel_id=1, source_target_pairs={{0,2},{1,3},{2,0},{3,1},{4,6},{5,7},{6,4},{7,5},{8,10},{9,11},{10,... | collective-permute-start | bytes 1572872 | tf_op jit(solution)/shard_map/ppermute | solution.py:61
  386.9 19.6 %collective-permute-start.18 = (bf16[128,2048]{1,0:T(8,128)(2,1)S(1)}, bf16[128,2048]{1,0:T(8,128)(2,1)S(1)}, u32[]{:S(2)}, u32[]{:S(2)}) collective-permute-start(bf16[128,2048]{1,0:T(8,128)(2,1)S(1)} %get-tuple-element.79), channel_id=1, source_target_pairs={{0,1},{1,0},{2,3},{3,2},{4,5},{5,4},{6,7},{7,6},{8,9},{9,8},{10,11... | collective-permute-start | bytes 1572872 | tf_op jit(solution)/shard_map/ppermute | solution.py:61
  398.1 24.5 %collective-permute-start.22 = (bf16[128,2048]{1,0:T(8,128)(2,1)S(1)}, bf16[128,2048]{1,0:T(8,128)(2,1)S(1)}, u32[]{:S(2)}, u32[]{:S(2)}) collective-permute-start(bf16[128,2048]{1,0:T(8,128)(2,1)S(1)} %get-tuple-element.80), channel_id=1, source_target_pairs={{0,2},{1,3},{2,0},{3,1},{4,6},{5,7},{6,4},{7,5},{8,10},{9,11},{10,... | collective-permute-start | bytes 1572872 | tf_op jit(solution)/shard_map/ppermute | solution.py:61
  399.6 44.4 %collective-permute-start.21 = (bf16[128,2048]{1,0:T(8,128)(2,1)S(1)}, bf16[128,2048]{1,0:T(8,128)(2,1)S(1)}, u32[]{:S(2)}, u32[]{:S(2)}) collective-permute-start(bf16[128,2048]{1,0:T(8,128)(2,1)S(1)} %get-tuple-element.81), channel_id=1, source_target_pairs={{0,2},{1,3},{2,0},{3,1},{4,6},{5,7},{6,4},{7,5},{8,10},{9,11},{10,... | collective-permute-start | bytes 1572872 | tf_op jit(solution)/shard_map/ppermute | solution.py:61
  400.1 41.1 %collective-permute-start.20 = (bf16[128,2048]{1,0:T(8,128)(2,1)S(1)}, bf16[128,2048]{1,0:T(8,128)(2,1)S(1)}, u32[]{:S(2)}, u32[]{:S(2)}) collective-permute-start(bf16[128,2048]{1,0:T(8,128)(2,1)S(1)} %add_convert_fusion.5), channel_id=1, source_target_pairs={{0,2},{1,3},{2,0},{3,1},{4,6},{5,7},{6,4},{7,5},{8,10},{9,11},{10,... | collective-permute-start | bytes 1572872 | tf_op jit(solution)/shard_map/ppermute | solution.py:61
  406.5 36.7 %collective-permute-start.29 = (bf16[128,2048]{1,0:T(8,128)(2,1)S(1)}, bf16[128,2048]{1,0:T(8,128)(2,1)S(1)}, u32[]{:S(2)}, u32[]{:S(2)}) collective-permute-start(bf16[128,2048]{1,0:T(8,128)(2,1)S(1)} %get-tuple-element.72), channel_id=1, source_target_pairs={{0,1},{1,0},{2,3},{3,2},{4,5},{5,4},{6,7},{7,6},{8,9},{9,8},{10,11... | collective-permute-start | bytes 1572872 | tf_op jit(solution)/shard_map/ppermute | solution.py:61
  441.6 10.2 %collective-permute-start.23 = (bf16[128,2048]{1,0:T(8,128)(2,1)S(1)}, bf16[128,2048]{1,0:T(8,128)(2,1)S(1)}, u32[]{:S(2)}, u32[]{:S(2)}) collective-permute-start(bf16[128,2048]{1,0:T(8,128)(2,1)S(1)} %get-tuple-element.78), channel_id=1, source_target_pairs={{0,1},{1,0},{2,3},{3,2},{4,5},{5,4},{6,7},{7,6},{8,9},{9,8},{10,11... | collective-permute-start | bytes 1572872 | tf_op jit(solution)/shard_map/ppermute | solution.py:61
  456.1 21.7 %collective-permute-start.31 = (bf16[256,2048]{1,0:T(8,128)(2,1)S(1)}, bf16[256,2048]{1,0:T(8,128)(2,1)S(1)}, u32[]{:S(2)}, u32[]{:S(2)}) collective-permute-start(bf16[256,2048]{1,0:T(8,128)(2,1)S(1)} %get-tuple-element.43), channel_id=1, source_target_pairs={{0,2},{1,3},{2,0},{3,1},{4,6},{5,7},{6,4},{7,5},{8,10},{9,11},{10,... | collective-permute-start | bytes 3145736 | tf_op jit(solution)/shard_map/ppermute | solution.py:61
  457.6 24.0 %collective-permute-start.30 = (bf16[256,2048]{1,0:T(8,128)(2,1)S(1)}, bf16[256,2048]{1,0:T(8,128)(2,1)S(1)}, u32[]{:S(2)}, u32[]{:S(2)}) collective-permute-start(bf16[256,2048]{1,0:T(8,128)(2,1)S(1)} %get-tuple-element.43), channel_id=1, source_target_pairs={{0,1},{1,0},{2,3},{3,2},{4,5},{5,4},{6,7},{7,6},{8,9},{9,8},{10,11... | collective-permute-start | bytes 3145736 | tf_op jit(solution)/shard_map/ppermute | solution.py:61
  477.8 11.3 %collective-permute-start.32 = (bf16[128,2048]{1,0:T(8,128)(2,1)S(1)}, bf16[128,2048]{1,0:T(8,128)(2,1)S(1)}, u32[]{:S(2)}, u32[]{:S(2)}) collective-permute-start(bf16[128,2048]{1,0:T(8,128)(2,1)S(1)} %slice.232), channel_id=1, source_target_pairs={{0,1},{1,0},{2,3},{3,2},{4,5},{5,4},{6,7},{7,6},{8,9},{9,8},{10,11... | collective-permute-start | bytes 1572872 | tf_op jit(solution)/shard_map/ppermute | solution.py:61
  481.6 9.2 %collective-permute-start.33 = (bf16[128,2048]{1,0:T(8,128)(2,1)S(1)}, bf16[128,2048]{1,0:T(8,128)(2,1)S(1)}, u32[]{:S(2)}, u32[]{:S(2)}) collective-permute-start(bf16[128,2048]{1,0:T(8,128)(2,1)S(1)} %slice.233), channel_id=1, source_target_pairs={{0,2},{1,3},{2,0},{3,1},{4,6},{5,7},{6,4},{7,5},{8,10},{9,11},{10,... | collective-permute-start | bytes 1572872 | tf_op jit(solution)/shard_map/ppermute | solution.py:61
  496.7 113.2 %reduce-scatter.9.cloned.1.call-start = ((), (), s32[]{:S(2)}) async-start(), calls=%async_computation.10 | async-start | bytes 4718592 | tf_op jit(solution)/shard_map/reduce_scatter | solution.py:126
  537.0 14.3 %collective-permute-start.35 = (bf16[128,2048]{1,0:T(8,128)(2,1)S(1)}, bf16[128,2048]{1,0:T(8,128)(2,1)S(1)}, u32[]{:S(2)}, u32[]{:S(2)}) collective-permute-start(bf16[128,2048]{1,0:T(8,128)(2,1)S(1)} %get-tuple-element.70), channel_id=1, source_target_pairs={{0,1},{1,0},{2,3},{3,2},{4,5},{5,4},{6,7},{7,6},{8,9},{9,8},{10,11... | collective-permute-start | bytes 1572872 | tf_op jit(solution)/shard_map/ppermute | solution.py:61
  538.7 18.3 %collective-permute-start.34 = (bf16[128,2048]{1,0:T(8,128)(2,1)S(1)}, bf16[128,2048]{1,0:T(8,128)(2,1)S(1)}, u32[]{:S(2)}, u32[]{:S(2)}) collective-permute-start(bf16[128,2048]{1,0:T(8,128)(2,1)S(1)} %get-tuple-element.67), channel_id=1, source_target_pairs={{0,1},{1,0},{2,3},{3,2},{4,5},{5,4},{6,7},{7,6},{8,9},{9,8},{10,11... | collective-permute-start | bytes 1572872 | tf_op jit(solution)/shard_map/ppermute | solution.py:61
  539.1 50.9 %copy-start.1 = (bf16[256,2048]{1,0:T(8,128)(2,1)S(1)}, bf16[256,2048]{1,0:T(8,128)(2,1)}, u32[]{:S(2)}) copy-start(bf16[256,2048]{1,0:T(8,128)(2,1)} %param.14) | copy-start | bytes 3145732
  539.1 50.9 %copy-start.14 = (f32[2048]{0:T(1024)S(1)}, f32[2048]{0:T(1024)}, u32[]{:S(2)}) copy-start(f32[2048]{0:T(1024)} %param.16) | copy-start | bytes 24580
  539.1 50.9 %copy-start.16 = (f32[256]{0:T(256)S(1)}, f32[256]{0:T(256)}, u32[]{:S(2)}) copy-start(f32[256]{0:T(256)} %copy-done.15) | copy-start | bytes 3076
  539.1 17.8 %collective-permute-start.38 = (bf16[128,2048]{1,0:T(8,128)(2,1)S(1)}, bf16[128,2048]{1,0:T(8,128)(2,1)S(1)}, u32[]{:S(2)}, u32[]{:S(2)}) collective-permute-start(bf16[128,2048]{1,0:T(8,128)(2,1)S(1)} %get-tuple-element.68), channel_id=1, source_target_pairs={{0,2},{1,3},{2,0},{3,1},{4,6},{5,7},{6,4},{7,5},{8,10},{9,11},{10,... | collective-permute-start | bytes 1572872 | tf_op jit(solution)/shard_map/ppermute | solution.py:61
  551.5 13.7 %collective-permute-start.36 = (bf16[128,2048]{1,0:T(8,128)(2,1)S(1)}, bf16[128,2048]{1,0:T(8,128)(2,1)S(1)}, u32[]{:S(2)}, u32[]{:S(2)}) collective-permute-start(bf16[128,2048]{1,0:T(8,128)(2,1)S(1)} %add_convert_fusion.1), channel_id=1, source_target_pairs={{0,2},{1,3},{2,0},{3,1},{4,6},{5,7},{6,4},{7,5},{8,10},{9,11},{10,... | collective-permute-start | bytes 1572872 | tf_op jit(solution)/shard_map/ppermute | solution.py:61
  551.5 40.2 %copy-start.8 = (bf16[256,1536]{1,0:T(8,128)(2,1)S(1)}, bf16[256,1536]{1,0:T(8,128)(2,1)}, u32[]{:S(2)}) copy-start(bf16[256,1536]{1,0:T(8,128)(2,1)} %reduce-scatter.5.cloned.1.call-done) | copy-start | bytes 2359300
  551.5 38.3 %collective-permute-start.37 = (bf16[128,2048]{1,0:T(8,128)(2,1)S(1)}, bf16[128,2048]{1,0:T(8,128)(2,1)S(1)}, u32[]{:S(2)}, u32[]{:S(2)}) collective-permute-start(bf16[128,2048]{1,0:T(8,128)(2,1)S(1)} %get-tuple-element.69), channel_id=1, source_target_pairs={{0,2},{1,3},{2,0},{3,1},{4,6},{5,7},{6,4},{7,5},{8,10},{9,11},{10,... | collective-permute-start | bytes 1572872 | tf_op jit(solution)/shard_map/ppermute | solution.py:61
  565.6 30.4 %copy-start.4 = (bf16[256,3072]{1,0:T(8,128)(2,1)S(1)}, bf16[256,3072]{1,0:T(8,128)(2,1)}, u32[]{:S(2)}) copy-start(bf16[256,3072]{1,0:T(8,128)(2,1)} %reduce-scatter.7.cloned.1.call-done) | copy-start | bytes 4718596
  565.6 24.2 %collective-permute-start.39 = (bf16[128,2048]{1,0:T(8,128)(2,1)S(1)}, bf16[128,2048]{1,0:T(8,128)(2,1)S(1)}, u32[]{:S(2)}, u32[]{:S(2)}) collective-permute-start(bf16[128,2048]{1,0:T(8,128)(2,1)S(1)} %get-tuple-element.66), channel_id=1, source_target_pairs={{0,1},{1,0},{2,3},{3,2},{4,5},{5,4},{6,7},{7,6},{8,9},{9,8},{10,11... | collective-permute-start | bytes 1572872 | tf_op jit(solution)/shard_map/ppermute | solution.py:61
  566.7 8.3 %collective-permute-start.45 = (f32[2304]{0:T(1024)S(1)}, f32[2304]{0:T(1024)S(1)}, u32[]{:S(2)}, u32[]{:S(2)}) collective-permute-start(f32[2304]{0:T(1024)S(1)} %pad_maximum_fusion.11), channel_id=1, source_target_pairs={{0,1},{1,0},{2,3},{3,2},{4,5},{5,4},{6,7},{7,6},{8,9},{9,8},{10,11... | collective-permute-start | bytes 27656 | tf_op jit(solution)/shard_map/ppermute | solution.py:61
  575.0 3.7 collective-permute-start.46
  578.7 1.2 collective-permute-start.47
  579.9 13.2 %collective-permute-start.48 = (f32[2304]{0:T(1024)S(1)}, f32[2304]{0:T(1024)S(1)}, u32[]{:S(2)}, u32[]{:S(2)}) collective-permute-start(f32[2304]{0:T(1024)S(1)} %add.199), channel_id=1, source_target_pairs={{0,8},{4,12},{8,0},{12,4},{16,24},{20,28},{24,16},{28,20},{1,9},{5... | collective-permute-start | bytes 27656 | tf_op jit(solution)/shard_map/ppermute | solution.py:135
  590.8 3.7 collective-permute-start.40
  593.1 5.0 collective-permute-start.49
  594.5 3.7 collective-permute-start.41
  598.1 1.2 collective-permute-start.42
  599.3 3.7 collective-permute-start.43
  603.0 4.5 collective-permute-start.44
  (19 other events, 170.6 us)
Sparse Core Ops, SparseCore 0:
  10.2 49.8 all-gather.4
  61.7 27.6 all-gather.6
  91.7 116.2 all-gather.8
  209.5 62.9 all-gather.10
  274.6 68.4 reduce-scatter.4
  345.3 127.5 reduce-scatter.6
  496.8 41.1 reduce-scatter.10
  540.4 48.6 reduce-scatter.8

commit v2 on v1

--- a/solution.py
+++ b/solution.py
@@ -56,6 +56,22 @@
     def __init__(self, dp_size, tensor_size):
         self.dp_size = dp_size
         self.tensor_size = tensor_size
+        self.chips = dp_size // 2
+        self.swap = [(place, place ^ 1) for place in range(dp_size)]
+
+    def shifted(self, value, step):
+        return lax.ppermute(
+            value,
+            "dp",
+            [
+                (2 * chip + core, 2 * ((chip + step) % self.chips) + core)
+                for chip in range(self.chips)
+                for core in range(2)
+            ],
+        )
+
+    def other_core(self, value):
+        return lax.ppermute(value, "dp", self.swap)
 
     def across(self, value, bit):
         return lax.ppermute(
@@ -73,7 +89,12 @@
             axis=0,
         )
 
-    def gather_tokens(self, block):
+    def gather_first(self, block):
+        if self.tensor_size != 4:
+            return block, block
+        return self.across(block, 1), self.across(block, 2)
+
+    def gather_second(self, block, first):
         if self.tensor_size != 4:
             bit = 1
             while bit < self.tensor_size:
@@ -81,43 +102,57 @@
                 bit *= 2
             return block
         half = block.shape[0] // 2
-        by_x = self.across(block, 1)
-        by_y = self.across(block, 2)
+        by_x, by_y = first
         corner_low = self.across(by_y[:half], 1)
         corner_high = self.across(by_x[half:], 2)
         return jnp.concatenate([block, by_x, by_y, corner_low, corner_high], axis=0)
 
+    def gather_tokens(self, block):
+        return self.gather_second(block, self.gather_first(block))
+
     def scatter_tokens(self, partial):
+        return self.scatter_second(partial, self.scatter_first(partial))
+
+    def half_block(self, partial, block, high):
+        half = partial.shape[0] // (2 * self.tensor_size)
+        start = 2 * block * half + high * half
+        return partial[start : start + half]
+
+    def scatter_first(self, partial):
         if self.tensor_size != 4:
+            return (partial,)
+        return (
+            self.across(self.half_block(partial, 3, 0), 1),
+            self.across(self.half_block(partial, 3, 1), 2),
+            self.across(self.half_block(partial, 1, 0), 1),
+            self.across(self.half_block(partial, 2, 1), 2),
+        )
+
+    def scatter_second(self, partial, first):
+        wide = jnp.float32
+        if self.tensor_size != 4:
+            (partial,) = first
             bit = self.tensor_size // 2
             while bit:
                 middle = partial.shape[0] // 2
-                arrived = self.across(partial[middle:], bit).astype(jnp.float32)
-                total = partial[:middle].astype(jnp.float32) + arrived
+                arrived = self.across(partial[middle:], bit).astype(wide)
+                total = partial[:middle].astype(wide) + arrived
                 partial = total.astype(partial.dtype)
                 bit //= 2
             return total
-        count = partial.shape[0] // self.tensor_size
-        half = count // 2
-
-        def piece(block, high):
-            start = block * count + high * half
-            return partial[start : start + half]
-
-        wide = jnp.float32
-        low_own = self.across(piece(1, 0), 1)
-        low_pass = self.across(piece(3, 0), 1)
-        high_own = self.across(piece(2, 1), 2)
-        high_pass = self.across(piece(3, 1), 2)
-        low_last = self.across(
-            (piece(2, 0).astype(wide) + low_pass.astype(wide)).astype(partial.dtype), 2
+        low_pass, high_pass, low_own, high_own = first
+
+        def passed(block, high, arrived):
+            total = self.half_block(partial, block, high).astype(wide) + arrived.astype(wide)
+            return total.astype(partial.dtype)
+
+        low_last = self.across(passed(2, 0, low_pass), 2)
+        high_last = self.across(passed(1, 1, high_pass), 1)
+        low = self.half_block(partial, 0, 0).astype(wide) + low_own.astype(wide)
+        high = self.half_block(partial, 0, 1).astype(wide) + high_own.astype(wide)
+        return jnp.concatenate(
+            [low + low_last.astype(wide), high + high_last.astype(wide)], axis=0
         )
-        high_last = self.across(
-            (piece(1, 1).astype(wide) + high_pass.astype(wide)).astype(partial.dtype), 1
-        )
-        low = piece(0, 0).astype(wide) + low_own.astype(wide) + low_last.astype(wide)
-        high = piece(0, 1).astype(wide) + high_own.astype(wide) + high_last.astype(wide)
-        return jnp.concatenate([low, high], axis=0)
 
     def gather_weight(self, shard):
         return lax.all_gather(shard, "dp", axis=0, tiled=True)
@@ -125,18 +160,22 @@
     def scatter_weight(self, partial):
         return lax.psum_scatter(partial, "dp", scatter_dimension=0, tiled=True)
 
-    def total(self, value):
+    def total_tensor(self, value):
         bit = 1
         while bit < self.tensor_size:
             value = value + self.across(value, bit)
             bit *= 2
-        bit = 1
-        while bit < self.dp_size:
-            value = value + lax.ppermute(
-                value, "dp", [(place, place ^ bit) for place in range(self.dp_size)]
-            )
-            bit *= 2
         return value
+
+    def total_dp(self, value):
+        chip = lax.axis_index("dp") // 2
+        value = value + self.other_core(value)
+        parts = jnp.stack([value] + [self.shifted(value, step) for step in range(1, self.chips)])
+        total = None
+        for target in range(self.chips):
+            part = lax.dynamic_index_in_dim(parts, (chip - target) % self.chips, 0, keepdims=False)
+            total = part if total is None else total + part
+        return total
 
 
 def product(left, right, left_axis, right_axis):
@@ -158,6 +197,14 @@
         self.blocks = blocks
         self.block = rows // blocks
         self.scale = head_size ** (-0.5)
+
+    def cost(self, products):
+        scores = self.query_heads * self.rows * self.rows
+        return pl.CostEstimate(
+            flops=products * 2 * scores * 2 * self.head_size,
+            transcendentals=scores,
+            bytes_accessed=16 * self.query_heads * self.rows * self.head_size,
+        )
 
     def outside(self, place, index):
         return pl.ds(pl.multiple_of((index ^ place) * self.block, self.block), self.block)
@@ -221,6 +268,7 @@
         return pl.pallas_call(
             self.forward_kernel,
             name="attention_forward",
+            cost_estimate=self.cost(2),
             grid_spec=pltpu.PrefetchScalarGridSpec(
                 num_scalar_prefetch=1,
                 grid=(self.key_heads,),
@@ -336,6 +384,7 @@
         return pl.pallas_call(
             self.backward_kernel,
             name="attention_backward",
+            cost_estimate=self.cost(5),
             grid_spec=pltpu.PrefetchScalarGridSpec(
                 num_scalar_prefetch=1,
                 grid=(self.key_heads,),
@@ -400,10 +449,11 @@
     attention = Attention(group_rows, head_size, query_heads, key_heads, links.tensor_size)
     place = lax.axis_index("tensor").astype(jnp.int32)[None]
     hidden = gate_weight.shape[1]
-    wide_attention = links.gather_weight(
-        jnp.concatenate([query_weight, key_matrix, value_matrix], axis=1)
-    )
-    wide_output = links.gather_weight(output_weight)
+    wide_mixing = links.gather_weight(
+        jnp.concatenate([query_weight, key_matrix, value_matrix, output_weight], axis=1)
+    )
+    wide_attention = wide_mixing[:, : query_width + 2 * key_width]
+    wide_output = wide_mixing[:, query_width + 2 * key_width :]
     wide_feed = links.gather_weight(jnp.concatenate([gate_weight, up_weight], axis=1))
     wide_down = links.gather_weight(down_weight)
 
@@ -412,15 +462,20 @@
     inverse_in = inverse_rms(inputs)
     scaled_in = inputs * inverse_in
     normed_rows = links.gather_tokens((scaled_in * input_gain).astype(jnp.bfloat16))
-    own_cotangent, normed_rows = lax.optimization_barrier((layer_cotangent, normed_rows))
-    cotangent = links.gather_tokens(own_cotangent)
+    own_cotangent = layer_cotangent
+    cotangent_first = links.gather_first(own_cotangent)
+    normed_rows, cotangent_first = lax.optimization_barrier((normed_rows, cotangent_first))
+    cotangent = links.gather_second(own_cotangent, cotangent_first)
 
     cosine, sine = tables(positions, head_size)
     raw_rows = matmul(normed_rows, wide_attention)
     query_rows, key_rows, value_rows, attended_rows, log_totals = attention.forward(
         place, raw_rows, cosine, sine, query_gain, key_gain
     )
-    branch = links.scatter_tokens(contract_last(attended_rows, wide_output).astype(jnp.bfloat16))
+    attended_rows, cotangent = lax.optimization_barrier((attended_rows, cotangent))
+    branch_partial = contract_last(attended_rows, wide_output).astype(jnp.bfloat16)
+    branch_first = links.scatter_first(branch_partial)
+    branch = links.scatter_second(branch_partial, branch_first)
     middle = inputs + branch
     inverse_mid = inverse_rms(middle)
     scaled_mid = middle * inverse_mid
@@ -441,24 +496,25 @@
     upward_grad = (active_grad * silu_gate).astype(jnp.bfloat16)
     feed_grad = jnp.concatenate([gate_grad, upward_grad], axis=1)
     middle_partial = contract_last(feed_grad, wide_feed)
-    middle_normed_grad = links.scatter_tokens(middle_partial.astype(jnp.bfloat16))
+    middle_partial = middle_partial.astype(jnp.bfloat16)
+    feed_grad, middle_partial = lax.optimization_barrier((feed_grad, middle_partial))
+    middle_first = links.scatter_first(middle_partial)
     feed_term = contract_first(normed_middle, feed_grad).astype(jnp.bfloat16)
-    feed_term, down_sum = lax.optimization_barrier((feed_term, down_sum))
+    feed_term, middle_first, down_sum = lax.optimization_barrier(
+        (feed_term, middle_first, down_sum)
+    )
     feed_sum = links.scatter_weight(feed_term)
-    layer_output = middle + links.scatter_tokens(
-        contract_last(active, wide_down).astype(jnp.bfloat16)
-    )
+    middle_normed_grad = links.scatter_second(middle_partial, middle_first)
+    feed_partial = contract_last(active, wide_down).astype(jnp.bfloat16)
+    middle_normed_grad, feed_partial = lax.optimization_barrier((middle_normed_grad, feed_partial))
     middle_gain_term = jnp.sum(middle_normed_grad * scaled_mid, axis=0)
     middle_grad = own_cotangent.astype(jnp.float32) + norm_backward(
         middle_normed_grad, scaled_mid, inverse_mid, middle_gain
     )
-    low_middle_grad, feed_term = lax.optimization_barrier(
-        (middle_grad.astype(jnp.bfloat16), feed_term)
-    )
-    branch_grad = links.gather_tokens(low_middle_grad)
+    branch_grad = links.gather_tokens(middle_grad.astype(jnp.bfloat16))
+    feed_partial, branch_grad = lax.optimization_barrier((feed_partial, branch_grad))
+    feed_first = links.scatter_first(feed_partial)
     output_term = contract_first(branch_grad, attended_rows).astype(jnp.bfloat16)
-    output_term, feed_sum = lax.optimization_barrier((output_term, feed_sum))
-    output_sum = links.scatter_weight(output_term)
     branch_grad, output_term = lax.optimization_barrier((branch_grad, output_term))
     attended_grad = matmul(branch_grad, wide_output).astype(jnp.bfloat16)
     raw_grad, query_gain_term, key_gain_term = attention.backward(
@@ -474,33 +530,47 @@
         log_totals,
         attended_grad,
     )
-    input_normed_grad = links.scatter_tokens(
-        contract_last(raw_grad, wide_attention).astype(jnp.bfloat16)
-    )
-    attention_sum = links.scatter_weight(contract_first(normed_rows, raw_grad).astype(jnp.bfloat16))
-    input_gain_term = jnp.sum(input_normed_grad * scaled_in, axis=0)
+    raw_grad, feed_first = lax.optimization_barrier((raw_grad, feed_first))
+    input_partial = contract_last(raw_grad, wide_attention).astype(jnp.bfloat16)
+    input_first = links.scatter_first(input_partial)
+    raw_grad, input_partial = lax.optimization_barrier((raw_grad, input_partial))
+    attention_term = contract_first(normed_rows, raw_grad).astype(jnp.bfloat16)
+    mixing_term = jnp.concatenate([attention_term, output_term], axis=1)
+    mixing_term, feed_sum, passed = lax.optimization_barrier(
+        (mixing_term, feed_sum, input_first[:2])
+    )
+    input_first = passed + input_first[2:]
+    mixing_sum = links.scatter_weight(mixing_term)
+    feed_branch = links.scatter_second(feed_partial, feed_first)
+    input_first, feed_branch = lax.optimization_barrier((input_first, feed_branch))
+    input_gain_term = (
+        jnp.sum(input_partial.astype(jnp.float32) * normed_rows.astype(jnp.float32), axis=0)
+        / input_gain
+    )
+    terms = jnp.concatenate(
+        [input_gain_term, middle_gain_term, query_gain_term[0], key_gain_term[0]]
+    )
+    input_normed_grad = links.scatter_second(input_partial, input_first)
+    terms, input_normed_grad = lax.optimization_barrier((terms, input_normed_grad))
+    layer_output = middle + feed_branch
     tokens_grad = middle_grad + norm_backward(input_normed_grad, scaled_in, inverse_in, input_gain)
-    other_terms = links.total(
-        jnp.concatenate([middle_gain_term, query_gain_term[0], key_gain_term[0]])
-    )
+    terms = links.total_dp(links.total_tensor(terms))
     width = tokens.shape[1]
-    attention_sum, output_sum, feed_sum, down_sum = (
-        summed.astype(jnp.float32) for summed in (attention_sum, output_sum, feed_sum, down_sum)
-    )
+    mixing_sum, feed_sum = mixing_sum.astype(jnp.float32), feed_sum.astype(jnp.float32)
     return (
         layer_output,
         tokens_grad,
-        links.total(input_gain_term),
-        other_terms[:width],
-        other_terms[width : width + head_size],
-        other_terms[width + head_size :],
-        attention_sum[:, :query_width],
-        attention_sum[:, query_width : query_width + key_width],
-        attention_sum[:, query_width + key_width :],
-        output_sum,
+        terms[:width],
+        terms[width : 2 * width],
+        terms[2 * width : 2 * width + head_size],
+        terms[2 * width + head_size :],
+        mixing_sum[:, :query_width],
+        mixing_sum[:, query_width : query_width + key_width],
+        mixing_sum[:, query_width + key_width : query_width + 2 * key_width],
+        mixing_sum[:, query_width + 2 * key_width :],
         feed_sum[:, :hidden],
         feed_sum[:, hidden:],
-        down_sum,
+        down_sum.astype(jnp.float32),
     )
 
 

time: 627 us -> 567 us (0.904)
  waiting for transfers between devices: 321 us -> 230 us
  other arithmetic: 30.7 us -> 51.9 us
  local copies, waits for them, and re-layouts: 29.5 us -> 49.7 us
  starting transfers between devices: 68.3 us -> 55.4 us
    ppermute x44 -> x42, waiting for transfers between devices: 239 us -> 198 us  [across(): lax.ppermute(value, 'tensor', [(place, place ^ bit) for place in range(se...]
    reduce_scatter x4 -> x3, waiting for transfers between devices: 34.8 us -> 9.68 us  [scatter_weight(): return lax.psum_scatter(partial, 'dp', scatter_dimension=0, tiled=True)]
    all_gather x4 -> x3, waiting for transfers between devices: 41 us -> 19.6 us  [gather_weight(): return lax.all_gather(shard, 'dp', axis=0, tiled=True)]
    add x18 -> x12, other arithmetic: 5.2 us -> 15.1 us  [the longest x4 7.99 us: scatter_second(): low + low_last.astype(wide)]
    ppermute x44 -> x42, starting transfers between devices: 55.3 us -> 45.8 us  [across(): lax.ppermute(value, 'tensor', [(place, place ^ bit) for place in range(se...]
    slice x16, local copies, waits for them, and re-layouts: 5.76 us -> 13.5 us  [the longest x4 6.87 us: half_block(): return partial[start:start + half]]
    unnamed x64 -> x91, local copies, waits for them, and re-layouts: 19.8 us -> 27.5 us
    concatenate x2 -> x7, other arithmetic: 2.02 us -> 8.32 us  [the longest x1 3.39 us: shards(): mixing_term = jnp.concatenate([attention_term, output_term], axis=1)]
  transfers between devices with their start and end apart: 58 -> 52, of which waited for: 40 -> 33; matrix products, arithmetic and copies ran while one was open for 27% -> 38% of each run, Pallas kernels for 5% -> 5%
where the time goes in v2:
time: 567 us; the launch traced here: 560 us
  waiting for transfers between devices  230 us (41%)
  matrix products  127 us (22%)
  starting transfers between devices  55.4 us (10%)
  other arithmetic  51.9 us (9%)
  local copies, waits for them, and re-layouts  49.7 us (9%)
  Pallas kernels  30.7 us (5%)
  between operations  15.4 us (3%)
    ppermute x42, waiting for transfers between devices, across(): lax.ppermute(value, 'tensor', [(place, place ^ bit) for place in range(se...  198 us
    dot_general x4, matrix products, matmul(): return jnp.dot(left, right, preferred_element_type=jnp.float32)  48.4 us
    ppermute x42, starting transfers between devices, across(): lax.ppermute(value, 'tensor', [(place, place ^ bit) for place in range(se...  45.8 us
    dot_general x4, matrix products, contract_last(): lax.dot_general(left, right, (((1,), (1,)), ((), ())), preferred_element_...  40.1 us
    dot_general x4, matrix products, contract_first(): lax.dot_general(left, right, (((0,), (0,)), ((), ())), preferred_element_...  38.6 us
    unnamed x91, local copies, waits for them, and re-layouts  27.5 us
    all_gather x3, waiting for transfers between devices, gather_weight(): return lax.all_gather(shard, 'dp', axis=0, tiled=True)  19.6 us
    pallas_call x1, Pallas kernels, backward(): pl.pallas_call(self.backward_kernel, name='attention_backward', cost_esti...  16.3 us
  transfers between devices with their start and end apart: 52, of which 33 were waited for; matrix products, arithmetic and copies ran while one was open for 38% of the time, Pallas kernels for 5%

profile of v2, /device:TPU:0, one launch (start us, length us, event | category | flops | bytes accessed | tf_op | source)
XLA Modules:
  0.0 560.1 jit_solution(16921571572265130684)
XLA Ops:
  7.2 2.2 pad_maximum_fusion.6
  9.5 2.7 pad_maximum_fusion.5
  14.3 3.0 collective-permute-start.1
  19.5 1.9 fusion.19
  21.4 20.2 %collective-permute-done.1 = bf16[256,2048]{1,0:T(8,128)(2,1)} collective-permute-done((bf16[256,2048]{1,0:T(8,128)(2,1)}, bf16[256,2048]{1,0:T(8,128)(2,1)}, u32[]{:S(2)}, u32[]{:S(2)}) %collective-permute-start.1) | collective-permute-done | bytes 1048608 | tf_op jit(solution)/shard_map/ppermute | solution.py:77
  42.7 2.1 collective-permute-start.2
  48.5 2.3 constant_dynamic-update-slice_fusion.3
  50.8 2.3 constant_dynamic-update-slice_fusion.2
  53.1 22.7 %collective-permute-done.2 = bf16[128,2048]{1,0:T(8,128)(2,1)S(1)} collective-permute-done((bf16[128,2048]{1,0:T(8,128)(2,1)S(1)}, bf16[128,2048]{1,0:T(8,128)(2,1)S(1)}, u32[]{:S(2)}, u32[]{:S(2)}) %collective-permute-start.2) | collective-permute-done | bytes 524320 | tf_op jit(solution)/shard_map/ppermute | solution.py:77
  83.1 2.3 constant_dynamic-update-slice_fusion.7
  85.4 5.8 %collective-permute-done.6 = bf16[128,2048]{1,0:T(8,128)(2,1)S(1)} collective-permute-done((bf16[128,2048]{1,0:T(8,128)(2,1)S(1)}, bf16[128,2048]{1,0:T(8,128)(2,1)S(1)}, u32[]{:S(2)}, u32[]{:S(2)}) %collective-permute-start.6) | collective-permute-done | bytes 524320 | tf_op jit(solution)/shard_map/ppermute | solution.py:77
  94.7 10.0 %fusion.2.raw_query.raw_key.raw_value = f32[1024,1024]{1,0:T(8,128)} fusion(bf16[1024,2048]{1,0:T(8,128)(2,1)} %constant_dynamic-update-slice_fusion, bf16[2048,1536]{1,0:T(8,128)(2,1)} %all-gather.4.cloned.1.call-done), kind=kOutput, calls=%fused_computation.16 | convolution fusion | flops 4294967296 | bytes 12582912 | tf_op jit(solution)/shard_map/dot_general | solution.py:18
  104.7 14.4 %attention_forward.1 = (bf16[1024,512]{1,0:T(8,128)(2,1)}, bf16[1024,256]{1,0:T(8,128)(2,1)}, bf16[1024,256]{1,0:T(8,128)(2,1)}, bf16[1024,512]{1,0:T(8,128)(2,1)}, f32[2,2,1024]{2,1,0:T(2,128)}) custom-call(s32[1]{0:T(128)} %bitcast.place_ref, f32[1024,1024]{1,0:T(8,128)} %fusion.2.raw_query.raw_key.raw_value, ...), custom_call_target="tpu_custom_call" | custom-call | flops 4294967296 | bytes 8388608 | tf_op jit(solution)/shard_map/attention_forward/pallas_call | solution.py:268
  119.1 4.3 convolution_convert_fusion.4
  127.2 12.3 %collective-permute-done.9 = bf16[128,2048]{1,0:T(8,128)(2,1)S(1)} collective-permute-done((bf16[128,2048]{1,0:T(8,128)(2,1)S(1)}, bf16[128,2048]{1,0:T(8,128)(2,1)S(1)}, u32[]{:S(2)}, u32[]{:S(2)}) %collective-permute-start.9) | collective-permute-done | bytes 524320 | tf_op jit(solution)/shard_map/ppermute | solution.py:77
  141.9 5.4 collective-permute-done.8
  147.3 7.2 %collective-permute-done.10 = bf16[128,2048]{1,0:T(8,128)(2,1)} collective-permute-done((bf16[128,2048]{1,0:T(8,128)(2,1)S(1)}, bf16[128,2048]{1,0:T(8,128)(2,1)}, u32[]{:S(2)}, u32[]{:S(2)}) %collective-permute-start.10) | collective-permute-done | bytes 524320 | tf_op jit(solution)/shard_map/ppermute | solution.py:77
  154.5 2.0 convert_add_fusion.8
  156.9 3.1 collective-permute-done.11
  160.0 11.1 %collective-permute-done.13 = bf16[128,2048]{1,0:T(8,128)(2,1)S(1)} collective-permute-done((bf16[128,2048]{1,0:T(8,128)(2,1)S(1)}, bf16[128,2048]{1,0:T(8,128)(2,1)S(1)}, u32[]{:S(2)}, u32[]{:S(2)}) %collective-permute-start.13) | collective-permute-done | bytes 524320 | tf_op jit(solution)/shard_map/ppermute | solution.py:77
  175.0 19.7 %collective-permute-done.15 = bf16[256,2048]{1,0:T(8,128)(2,1)S(1)} collective-permute-done((bf16[256,2048]{1,0:T(8,128)(2,1)S(1)}, bf16[256,2048]{1,0:T(8,128)(2,1)S(1)}, u32[]{:S(2)}, u32[]{:S(2)}) %collective-permute-start.15) | collective-permute-done | bytes 1048608 | tf_op jit(solution)/shard_map/ppermute | solution.py:77
  197.8 6.2 %collective-permute-done.16 = bf16[128,2048]{1,0:T(8,128)(2,1)S(1)} collective-permute-done((bf16[128,2048]{1,0:T(8,128)(2,1)S(1)}, bf16[128,2048]{1,0:T(8,128)(2,1)S(1)}, u32[]{:S(2)}, u32[]{:S(2)}) %collective-permute-start.16) | collective-permute-done | bytes 524320 | tf_op jit(solution)/shard_map/ppermute | solution.py:77
  205.7 17.2 %fusion.32 = f32[1024,3072]{1,0:T(8,128)S(1)} fusion(bf16[1024,2048]{1,0:T(8,128)(2,1)} %constant_dynamic-update-slice_fusion.10, bf16[2048,3072]{1,0:T(8,128)(2,1)} %all-gather.6.cloned.1.call-done), kind=kOutput, calls=%fused_computation.107 | convolution fusion | flops 12884901888 | bytes 29360128 | tf_op jit(solution)/shard_map/dot_general | solution.py:18
  222.9 2.0 multiply_convert_fusion.2
  224.9 2.6 copy-done.8
  229.2 11.2 %convolution_convert_fusion.1 = bf16[2048,1536]{1,0:T(8,128)(2,1)} fusion(bf16[1024,2048]{1,0:T(8,128)(2,1)} %constant_dynamic-update-slice_fusion.5, bf16[1024,1536]{1,0:T(8,128)(2,1)S(1)} %multiply_convert_fusion.2), kind=kOutput, calls=%fused_computation.2 | convolution fusion | flops 6445596672 | bytes 13631488 | tf_op jit(solution)/shard_map/dot_general | solution.py:22
  240.4 19.6 %all-gather.8.cloned.1.call-done = bf16[2048,1536]{1,0:T(8,128)(2,1)} async-done(((bf16[256,1536]{1,0:T(8,128)(2,1)}), bf16[2048,1536]{1,0:T(8,128)(2,1)}) %all-gather.8.cloned.1.call-update) | async-done | bytes 6291472 | tf_op jit(solution)/shard_map/all_gather | solution.py:158
  260.1 14.9 %multiply_convert_fusion.1 = (bf16[1024,1536]{1,0:T(8,128)(2,1)S(1)}, bf16[1024,1536]{1,0:T(8,128)(2,1)S(1)}) fusion(f32[1024,3072]{1,0:T(8,128)} %copy-done.8, bf16[1024,2048]{1,0:T(8,128)(2,1)} %constant_dynamic-update-slice_fusion.5, bf16[2048,1536]{1,0:T(8,128)(2,1)} %all-gather.8.cloned.1.call-done), kind=kOutput, calls=%fused_computation.6 | convolution fusion | flops 6462898176 | bytes 29360128 | tf_op jit(solution)/shard_map/dot_general | solution.py:18
  278.6 19.5 %convolution_convert_fusion.2 = bf16[1024,2048]{1,0:T(8,128)(2,1)} fusion(bf16[2048,3072]{1,0:T(8,128)(2,1)} %all-gather.6.cloned.1.call-done, bf16[1024,1536]{1,0:T(8,128)(2,1)} %copy-done.18, bf16[1024,1536]{1,0:T(8,128)(2,1)} %copy-done.17), kind=kOutput, calls=%fused_computation.10 | convolution fusion | flops 12899581952 | bytes 23068672 | tf_op jit(solution)/shard_map/dot_general | solution.py:28
  298.2 2.9 fusion.25
  305.1 18.4 %convolution_convert_fusion = bf16[2048,3072]{1,0:T(8,128)(2,1)} fusion(bf16[1024,2048]{1,0:T(8,128)(2,1)} %constant_dynamic-update-slice_fusion.10, bf16[1024,3072]{1,0:T(8,128)(2,1)S(1)} %pad_maximum_fusion), kind=kOutput, calls=%fused_computation | convolution fusion | flops 12891193344 | bytes 23068672 | tf_op jit(solution)/shard_map/dot_general | solution.py:22
  323.6 3.2 collective-permute-done.20
  327.9 2.8 reduce-scatter.4.cloned.1.call-done
  333.8 10.1 %collective-permute-done.22 = bf16[128,2048]{1,0:T(8,128)(2,1)S(1)} collective-permute-done((bf16[128,2048]{1,0:T(8,128)(2,1)S(1)}, bf16[128,2048]{1,0:T(8,128)(2,1)S(1)}, u32[]{:S(2)}, u32[]{:S(2)}) %collective-permute-start.22) | collective-permute-done | bytes 524320 | tf_op jit(solution)/shard_map/ppermute | solution.py:77
  343.9 1.9 convert_add_fusion.6
  347.3 8.8 %convolution_convert_fusion.3 = bf16[1024,2048]{1,0:T(8,128)(2,1)S(1)} fusion(bf16[1024,1536]{1,0:T(8,128)(2,1)S(1)} %copy-done.20, bf16[2048,1536]{1,0:T(8,128)(2,1)} %all-gather.8.cloned.1.call-done), kind=kOutput, calls=%fused_computation.11 | convolution fusion | flops 6444548096 | bytes 13631488 | tf_op jit(solution)/shard_map/dot_general | solution.py:28
  356.5 3.1 convert_add_fusion.5
  364.0 18.9 %collective-permute-done.25 = bf16[256,2048]{1,0:T(8,128)(2,1)S(1)} collective-permute-done((bf16[256,2048]{1,0:T(8,128)(2,1)S(1)}, bf16[256,2048]{1,0:T(8,128)(2,1)S(1)}, u32[]{:S(2)}, u32[]{:S(2)}) %collective-permute-start.25) | collective-permute-done | bytes 1048608 | tf_op jit(solution)/shard_map/ppermute | solution.py:77
  382.9 1.9 collective-permute-start.26
  384.9 2.0 collective-permute-done.24
  387.4 7.6 %collective-permute-done.26 = bf16[128,2048]{1,0:T(8,128)(2,1)S(1)} collective-permute-done((bf16[128,2048]{1,0:T(8,128)(2,1)S(1)}, bf16[128,2048]{1,0:T(8,128)(2,1)S(1)}, u32[]{:S(2)}, u32[]{:S(2)}) %collective-permute-start.26) | collective-permute-done | bytes 524320 | tf_op jit(solution)/shard_map/ppermute | solution.py:77
  396.2 3.8 convolution_convert_fusion.7
  405.4 4.0 copy.27
  409.4 6.2 %fusion.16.upstream = bf16[1024,512]{1,0:T(8,128)(2,1)} fusion(bf16[1024,2048]{1,0:T(8,128)(2,1)} %copy-done.23, bf16[2048,1536]{1,0:T(8,128)(2,1)} %all-gather.4.cloned.1.call-done), kind=kOutput, calls=%fused_computation.43 | convolution fusion | flops 2148007936 | bytes 7340032 | tf_op jit(solution)/shard_map/dot_general | solution.py:18
  415.6 16.3 %attention_backward.1 = (bf16[1024,1024]{1,0:T(8,128)(2,1)}, f32[1,128]{1,0:T(1,128)}, f32[1,128]{1,0:T(1,128)}) custom-call(s32[1]{0:T(128)} %bitcast.place_ref, f32[1024,1024]{1,0:T(8,128)} %fusion.2.raw_query.raw_key.raw_value, f32[1024,1024]{1,0:T(8,128)} %fusion.2.raw_query.raw_key.raw_value, f32[1024,128]{1,0:T(8,128)} %get-tuple-element.177.cosine, ...), custom_call_target="tpu_custom_call" | custom-call | flops 10737418240 | bytes 8388608 | tf_op jit(solution)/shard_map/attention_backward/pallas_call | solution.py:384
  432.0 7.5 %convolution_convert_fusion.6 = bf16[1024,2048]{1,0:T(8,128)(2,1)S(1)} fusion(bf16[1024,1024]{1,0:T(8,128)(2,1)} %get-tuple-element.87, bf16[2048,1536]{1,0:T(8,128)(2,1)} %all-gather.4.cloned.1.call-done), kind=kOutput, calls=%fused_computation.14 | convolution fusion | flops 4297064448 | bytes 10485760 | tf_op jit(solution)/shard_map/dot_general | solution.py:28
  439.5 2.0 copy-done.6
  444.5 5.3 convolution_convert_fusion.5
  449.8 3.4 pad_maximum_fusion.1
  453.6 6.9 %reduce-scatter.6.cloned.1.call-done = bf16[256,3072]{1,0:T(8,128)(2,1)} async-done(((bf16[2048,3072]{1,0:T(8,128)(2,1)}), bf16[256,3072]{1,0:T(8,128)(2,1)}) %reduce-scatter.6.cloned.1.call-update) | async-done | bytes 1572880 | tf_op jit(solution)/shard_map/reduce_scatter | solution.py:161
  463.5 10.1 %collective-permute-done.36 = bf16[128,2048]{1,0:T(8,128)(2,1)S(1)} collective-permute-done((bf16[128,2048]{1,0:T(8,128)(2,1)S(1)}, bf16[128,2048]{1,0:T(8,128)(2,1)S(1)}, u32[]{:S(2)}, u32[]{:S(2)}) %collective-permute-start.36) | collective-permute-done | bytes 524320 | tf_op jit(solution)/shard_map/ppermute | solution.py:77
  473.5 2.0 convert_add_fusion.4
  479.1 11.4 %collective-permute-done.37 = bf16[128,2048]{1,0:T(8,128)(2,1)S(1)} collective-permute-done((bf16[128,2048]{1,0:T(8,128)(2,1)S(1)}, bf16[128,2048]{1,0:T(8,128)(2,1)S(1)}, u32[]{:S(2)}, u32[]{:S(2)}) %collective-permute-start.37) | collective-permute-done | bytes 524320 | tf_op jit(solution)/shard_map/ppermute | solution.py:77
  493.3 4.1 collective-permute-done.34
  497.5 2.1 add_convert_fusion.1
  501.1 2.6 convert_element_type.287
  503.7 5.9 %collective-permute-done.38 = bf16[128,2048]{1,0:T(8,128)(2,1)} collective-permute-done((bf16[128,2048]{1,0:T(8,128)(2,1)}, bf16[128,2048]{1,0:T(8,128)(2,1)}, u32[]{:S(2)}, u32[]{:S(2)}) %collective-permute-start.38) | collective-permute-done | bytes 524320 | tf_op jit(solution)/shard_map/ppermute | solution.py:77
  509.6 2.1 convert_add_fusion.2
  513.3 4.0 multiply_reduce_fusion
  517.4 3.9 collective-permute-done.39
  524.2 2.1 fusion.27
  528.5 1.8 collective-permute-done.41
  531.5 8.7 %collective-permute-start.45 = (f32[4352]{0:T(1024)S(1)}, f32[4352]{0:T(1024)S(1)}, u32[]{:S(2)}, u32[]{:S(2)}) collective-permute-start(f32[4352]{0:T(1024)S(1)} %add.213), channel_id=1, source_target_pairs={{0,24},{4,28},{8,0},{12,4},{16,8},{20,12},{24,16},{28,20},{1,25},{... | collective-permute-start | bytes 52232 | tf_op jit(solution)/shard_map/ppermute | solution.py:63
  540.8 3.1 fusion.11
  (223 shorter events, 93.8 us)
Async XLA Ops:
  7.2 87.5 %all-gather.4.cloned.1.call-start = ((), (), s32[]{:S(2)}) async-start(), calls=%async_computation.3 | async-start | bytes 7077888 | tf_op jit(solution)/shard_map/all_gather | solution.py:158
  9.5 196.2 %all-gather.6.cloned.1.call-start = ((), (), s32[]{:S(2)}) async-start(), calls=%async_computation.4 | async-start | bytes 14155776 | tf_op jit(solution)/shard_map/all_gather | solution.py:158
  12.3 247.8 %all-gather.8.cloned.1.call-start = ((), (), s32[]{:S(2)}) async-start(), calls=%async_computation.5 | async-start | bytes 7077888 | tf_op jit(solution)/shard_map/all_gather | solution.py:158
  14.3 27.3 %collective-permute-start.1 = (bf16[256,2048]{1,0:T(8,128)(2,1)}, bf16[256,2048]{1,0:T(8,128)(2,1)}, u32[]{:S(2)}, u32[]{:S(2)}) collective-permute-start(bf16[256,2048]{1,0:T(8,128)(2,1)} %get-tuple-element.131), channel_id=1, source_target_pairs={{0,2},{1,3},{2,0},{3,1},{4,6},{5,7},{6,4},{7,5},{8,10},{9,11},{10,... | collective-permute-start | bytes 3145736 | tf_op jit(solution)/shard_map/ppermute | solution.py:77
  17.3 28.5 %collective-permute-start = (bf16[256,2048]{1,0:T(8,128)(2,1)}, bf16[256,2048]{1,0:T(8,128)(2,1)}, u32[]{:S(2)}, u32[]{:S(2)}) collective-permute-start(bf16[256,2048]{1,0:T(8,128)(2,1)} %get-tuple-element.131), channel_id=1, source_target_pairs={{0,1},{1,0},{2,3},{3,2},{4,5},{5,4},{6,7},{7,6},{8,9},{9,8},{10,11... | collective-permute-start | bytes 3145736 | tf_op jit(solution)/shard_map/ppermute | solution.py:77
  18.8 58.7 %collective-permute-start.4 = (bf16[256,2048]{1,0:T(8,128)(2,1)S(1)}, bf16[256,2048]{1,0:T(8,128)(2,1)S(1)}, u32[]{:S(2)}, u32[]{:S(2)}) collective-permute-start(bf16[256,2048]{1,0:T(8,128)(2,1)S(1)} %copy-done.9), channel_id=1, source_target_pairs={{0,1},{1,0},{2,3},{3,2},{4,5},{5,4},{6,7},{7,6},{8,9},{9,8},{10,11... | collective-permute-start | bytes 3145736 | tf_op jit(solution)/shard_map/ppermute | solution.py:77
  19.3 58.2 %collective-permute-start.5 = (bf16[256,2048]{1,0:T(8,128)(2,1)S(1)}, bf16[256,2048]{1,0:T(8,128)(2,1)}, u32[]{:S(2)}, u32[]{:S(2)}) collective-permute-start(bf16[256,2048]{1,0:T(8,128)(2,1)S(1)} %copy-done.9), channel_id=1, source_target_pairs={{0,2},{1,3},{2,0},{3,1},{4,6},{5,7},{6,4},{7,5},{8,10},{9,11},{10,... | collective-permute-start | bytes 3145736 | tf_op jit(solution)/shard_map/ppermute | solution.py:77
  42.7 33.2 %collective-permute-start.2 = (bf16[128,2048]{1,0:T(8,128)(2,1)S(1)}, bf16[128,2048]{1,0:T(8,128)(2,1)S(1)}, u32[]{:S(2)}, u32[]{:S(2)}) collective-permute-start(bf16[128,2048]{1,0:T(8,128)(2,1)S(1)} %slice.232), channel_id=1, source_target_pairs={{0,1},{1,0},{2,3},{3,2},{4,5},{5,4},{6,7},{7,6},{8,9},{9,8},{10,11... | collective-permute-start | bytes 1572872 | tf_op jit(solution)/shard_map/ppermute | solution.py:77
  46.9 29.8 %collective-permute-start.3 = (bf16[128,2048]{1,0:T(8,128)(2,1)S(1)}, bf16[128,2048]{1,0:T(8,128)(2,1)S(1)}, u32[]{:S(2)}, u32[]{:S(2)}) collective-permute-start(bf16[128,2048]{1,0:T(8,128)(2,1)S(1)} %slice.233), channel_id=1, source_target_pairs={{0,2},{1,3},{2,0},{3,1},{4,6},{5,7},{6,4},{7,5},{8,10},{9,11},{10,... | collective-permute-start | bytes 1572872 | tf_op jit(solution)/shard_map/ppermute | solution.py:77
  78.6 12.7 %collective-permute-start.6 = (bf16[128,2048]{1,0:T(8,128)(2,1)S(1)}, bf16[128,2048]{1,0:T(8,128)(2,1)S(1)}, u32[]{:S(2)}, u32[]{:S(2)}) collective-permute-start(bf16[128,2048]{1,0:T(8,128)(2,1)S(1)} %slice.177), channel_id=1, source_target_pairs={{0,1},{1,0},{2,3},{3,2},{4,5},{5,4},{6,7},{7,6},{8,9},{9,8},{10,11... | collective-permute-start | bytes 1572872 | tf_op jit(solution)/shard_map/ppermute | solution.py:77
  81.5 12.4 %collective-permute-start.7 = (bf16[128,2048]{1,0:T(8,128)(2,1)S(1)}, bf16[128,2048]{1,0:T(8,128)(2,1)S(1)}, u32[]{:S(2)}, u32[]{:S(2)}) collective-permute-start(bf16[128,2048]{1,0:T(8,128)(2,1)S(1)} %slice.178), channel_id=1, source_target_pairs={{0,2},{1,3},{2,0},{3,1},{4,6},{5,7},{6,4},{7,5},{8,10},{9,11},{10,... | collective-permute-start | bytes 1572872 | tf_op jit(solution)/shard_map/ppermute | solution.py:77
  123.4 16.1 %copy-start.16 = (bf16[1024,2048]{1,0:T(8,128)(2,1)}, bf16[1024,2048]{1,0:T(8,128)(2,1)S(1)}, u32[]{:S(2)}) copy-start(bf16[1024,2048]{1,0:T(8,128)(2,1)S(1)} %convolution_convert_fusion.4) | copy-start | bytes 12582916
  124.6 14.9 %collective-permute-start.9 = (bf16[128,2048]{1,0:T(8,128)(2,1)S(1)}, bf16[128,2048]{1,0:T(8,128)(2,1)S(1)}, u32[]{:S(2)}, u32[]{:S(2)}) collective-permute-start(bf16[128,2048]{1,0:T(8,128)(2,1)S(1)} %get-tuple-element.157), channel_id=1, source_target_pairs={{0,1},{1,0},{2,3},{3,2},{4,5},{5,4},{6,7},{7,6},{8,9},{9,8},{10,11... | collective-permute-start | bytes 1572872 | tf_op jit(solution)/shard_map/ppermute | solution.py:77
  125.2 22.0 %collective-permute-start.8 = (bf16[128,2048]{1,0:T(8,128)(2,1)}, bf16[128,2048]{1,0:T(8,128)(2,1)S(1)}, u32[]{:S(2)}, u32[]{:S(2)}) collective-permute-start(bf16[128,2048]{1,0:T(8,128)(2,1)} %get-tuple-element.154), channel_id=1, source_target_pairs={{0,1},{1,0},{2,3},{3,2},{4,5},{5,4},{6,7},{7,6},{8,9},{9,8},{10,11... | collective-permute-start | bytes 1572872 | tf_op jit(solution)/shard_map/ppermute | solution.py:77
  126.7 20.6 %collective-permute-start.12 = (bf16[128,2048]{1,0:T(8,128)(2,1)S(1)}, bf16[128,2048]{1,0:T(8,128)(2,1)}, u32[]{:S(2)}, u32[]{:S(2)}) collective-permute-start(bf16[128,2048]{1,0:T(8,128)(2,1)S(1)} %get-tuple-element.155), channel_id=1, source_target_pairs={{0,2},{1,3},{2,0},{3,1},{4,6},{5,7},{6,4},{7,5},{8,10},{9,11},{10,... | collective-permute-start | bytes 1572872 | tf_op jit(solution)/shard_map/ppermute | solution.py:77
  139.6 14.8 %collective-permute-start.10 = (bf16[128,2048]{1,0:T(8,128)(2,1)S(1)}, bf16[128,2048]{1,0:T(8,128)(2,1)}, u32[]{:S(2)}, u32[]{:S(2)}) collective-permute-start(bf16[128,2048]{1,0:T(8,128)(2,1)S(1)} %add_convert_fusion.7), channel_id=1, source_target_pairs={{0,2},{1,3},{2,0},{3,1},{4,6},{5,7},{6,4},{7,5},{8,10},{9,11},{10,... | collective-permute-start | bytes 1572872 | tf_op jit(solution)/shard_map/ppermute | solution.py:77
  140.3 190.4 %reduce-scatter.4.cloned.1.call-start = ((), (), s32[]{:S(2)}) async-start(), calls=%async_computation.6 | async-start | bytes 7077888 | tf_op jit(solution)/shard_map/reduce_scatter | solution.py:161
  140.4 19.6 %collective-permute-start.11 = (bf16[128,2048]{1,0:T(8,128)(2,1)S(1)}, bf16[128,2048]{1,0:T(8,128)(2,1)S(1)}, u32[]{:S(2)}, u32[]{:S(2)}) collective-permute-start(bf16[128,2048]{1,0:T(8,128)(2,1)S(1)} %get-tuple-element.156), channel_id=1, source_target_pairs={{0,2},{1,3},{2,0},{3,1},{4,6},{5,7},{6,4},{7,5},{8,10},{9,11},{10,... | collective-permute-start | bytes 1572872 | tf_op jit(solution)/shard_map/ppermute | solution.py:77
  156.4 16.4 %copy-start.24 = (f32[2048]{0:T(1024)S(1)}, f32[2048]{0:T(1024)}, u32[]{:S(2)}) copy-start(f32[2048]{0:T(1024)} %param.17) | copy-start | bytes 24580
  156.5 14.6 %collective-permute-start.13 = (bf16[128,2048]{1,0:T(8,128)(2,1)S(1)}, bf16[128,2048]{1,0:T(8,128)(2,1)S(1)}, u32[]{:S(2)}, u32[]{:S(2)}) collective-permute-start(bf16[128,2048]{1,0:T(8,128)(2,1)S(1)} %get-tuple-element.153), channel_id=1, source_target_pairs={{0,1},{1,0},{2,3},{3,2},{4,5},{5,4},{6,7},{7,6},{8,9},{9,8},{10,11... | collective-permute-start | bytes 1572872 | tf_op jit(solution)/shard_map/ppermute | solution.py:77
  172.8 23.9 %copy-start = (f32[256,2048]{1,0:T(8,128)}, f32[256,2048]{1,0:T(8,128)S(1)}, u32[]{:S(2)}) copy-start(f32[256,2048]{1,0:T(8,128)S(1)} %get-tuple-element.129) | copy-start | bytes 6291460
  172.8 23.9 %copy-start.28 = (f32[256]{0:T(256)}, f32[256]{0:T(256)S(1)}, u32[]{:S(2)}) copy-start(f32[256]{0:T(256)S(1)} %add_rsqrt_fusion) | copy-start | bytes 3076
  174.3 20.4 %collective-permute-start.15 = (bf16[256,2048]{1,0:T(8,128)(2,1)S(1)}, bf16[256,2048]{1,0:T(8,128)(2,1)S(1)}, u32[]{:S(2)}, u32[]{:S(2)}) collective-permute-start(bf16[256,2048]{1,0:T(8,128)(2,1)S(1)} %get-tuple-element.127), channel_id=1, source_target_pairs={{0,2},{1,3},{2,0},{3,1},{4,6},{5,7},{6,4},{7,5},{8,10},{9,11},{10,... | collective-permute-start | bytes 3145736 | tf_op jit(solution)/shard_map/ppermute | solution.py:77
  174.3 20.5 %collective-permute-start.14 = (bf16[256,2048]{1,0:T(8,128)(2,1)S(1)}, bf16[256,2048]{1,0:T(8,128)(2,1)S(1)}, u32[]{:S(2)}, u32[]{:S(2)}) collective-permute-start(bf16[256,2048]{1,0:T(8,128)(2,1)S(1)} %get-tuple-element.127), channel_id=1, source_target_pairs={{0,1},{1,0},{2,3},{3,2},{4,5},{5,4},{6,7},{7,6},{8,9},{9,8},{10,11... | collective-permute-start | bytes 3145736 | tf_op jit(solution)/shard_map/ppermute | solution.py:77
  194.8 9.2 %collective-permute-start.16 = (bf16[128,2048]{1,0:T(8,128)(2,1)S(1)}, bf16[128,2048]{1,0:T(8,128)(2,1)S(1)}, u32[]{:S(2)}, u32[]{:S(2)}) collective-permute-start(bf16[128,2048]{1,0:T(8,128)(2,1)S(1)} %slice.244), channel_id=1, source_target_pairs={{0,1},{1,0},{2,3},{3,2},{4,5},{5,4},{6,7},{7,6},{8,9},{9,8},{10,11... | collective-permute-start | bytes 1572872 | tf_op jit(solution)/shard_map/ppermute | solution.py:77
  194.9 10.0 %collective-permute-start.17 = (bf16[128,2048]{1,0:T(8,128)(2,1)S(1)}, bf16[128,2048]{1,0:T(8,128)(2,1)S(1)}, u32[]{:S(2)}, u32[]{:S(2)}) collective-permute-start(bf16[128,2048]{1,0:T(8,128)(2,1)S(1)} %slice.245), channel_id=1, source_target_pairs={{0,2},{1,3},{2,0},{3,1},{4,6},{5,7},{6,4},{7,5},{8,10},{9,11},{10,... | collective-permute-start | bytes 1572872 | tf_op jit(solution)/shard_map/ppermute | solution.py:77
  240.4 220.1 %reduce-scatter.6.cloned.1.call-start = ((), (), s32[]{:S(2)}) async-start(), calls=%async_computation.7 | async-start | bytes 14155776 | tf_op jit(solution)/shard_map/reduce_scatter | solution.py:161
  301.1 22.5 %collective-permute-start.18 = (bf16[128,2048]{1,0:T(8,128)(2,1)}, bf16[128,2048]{1,0:T(8,128)(2,1)}, u32[]{:S(2)}, u32[]{:S(2)}) collective-permute-start(bf16[128,2048]{1,0:T(8,128)(2,1)} %get-tuple-element.151), channel_id=1, source_target_pairs={{0,1},{1,0},{2,3},{3,2},{4,5},{5,4},{6,7},{7,6},{8,9},{9,8},{10,11... | collective-permute-start | bytes 1572872 | tf_op jit(solution)/shard_map/ppermute | solution.py:77
  302.5 21.0 %collective-permute-start.19 = (bf16[128,2048]{1,0:T(8,128)(2,1)}, bf16[128,2048]{1,0:T(8,128)(2,1)}, u32[]{:S(2)}, u32[]{:S(2)}) collective-permute-start(bf16[128,2048]{1,0:T(8,128)(2,1)} %get-tuple-element.150), channel_id=1, source_target_pairs={{0,2},{1,3},{2,0},{3,1},{4,6},{5,7},{6,4},{7,5},{8,10},{9,11},{10,... | collective-permute-start | bytes 1572872 | tf_op jit(solution)/shard_map/ppermute | solution.py:77
  304.0 22.7 %collective-permute-start.20 = (bf16[128,2048]{1,0:T(8,128)(2,1)}, bf16[128,2048]{1,0:T(8,128)(2,1)}, u32[]{:S(2)}, u32[]{:S(2)}) collective-permute-start(bf16[128,2048]{1,0:T(8,128)(2,1)} %get-tuple-element.149), channel_id=1, source_target_pairs={{0,1},{1,0},{2,3},{3,2},{4,5},{5,4},{6,7},{7,6},{8,9},{9,8},{10,11... | collective-permute-start | bytes 1572872 | tf_op jit(solution)/shard_map/ppermute | solution.py:77
  304.6 23.3 %collective-permute-start.21 = (bf16[128,2048]{1,0:T(8,128)(2,1)}, bf16[128,2048]{1,0:T(8,128)(2,1)}, u32[]{:S(2)}, u32[]{:S(2)}) collective-permute-start(bf16[128,2048]{1,0:T(8,128)(2,1)} %get-tuple-element.148), channel_id=1, source_target_pairs={{0,2},{1,3},{2,0},{3,1},{4,6},{5,7},{6,4},{7,5},{8,10},{9,11},{10,... | collective-permute-start | bytes 1572872 | tf_op jit(solution)/shard_map/ppermute | solution.py:77
  330.7 16.6 %copy-start.20 = (bf16[1024,1536]{1,0:T(8,128)(2,1)S(1)}, bf16[1024,1536]{1,0:T(8,128)(2,1)}, u32[]{:S(2)}) copy-start(bf16[1024,1536]{1,0:T(8,128)(2,1)} %copy-done.19) | copy-start | bytes 9437188
  330.7 216.3 %reduce-scatter.8.cloned.1.call-start = ((), (), s32[]{:S(2)}) async-start(), calls=%async_computation.8 | async-start | bytes 7077888 | tf_op jit(solution)/shard_map/reduce_scatter | solution.py:161
  332.3 11.6 %collective-permute-start.22 = (bf16[128,2048]{1,0:T(8,128)(2,1)S(1)}, bf16[128,2048]{1,0:T(8,128)(2,1)S(1)}, u32[]{:S(2)}, u32[]{:S(2)}) collective-permute-start(bf16[128,2048]{1,0:T(8,128)(2,1)S(1)} %add_convert_fusion.5), channel_id=1, source_target_pairs={{0,2},{1,3},{2,0},{3,1},{4,6},{5,7},{6,4},{7,5},{8,10},{9,11},{10,... | collective-permute-start | bytes 1572872 | tf_op jit(solution)/shard_map/ppermute | solution.py:77
  345.8 10.7 %collective-permute-start.23 = (bf16[128,2048]{1,0:T(8,128)(2,1)S(1)}, bf16[128,2048]{1,0:T(8,128)(2,1)S(1)}, u32[]{:S(2)}, u32[]{:S(2)}) collective-permute-start(bf16[128,2048]{1,0:T(8,128)(2,1)S(1)} %get-tuple-element.147), channel_id=1, source_target_pairs={{0,1},{1,0},{2,3},{3,2},{4,5},{5,4},{6,7},{7,6},{8,9},{9,8},{10,11... | collective-permute-start | bytes 1572872 | tf_op jit(solution)/shard_map/ppermute | solution.py:77
  356.1 43.8 %copy-start.15 = (bf16[1024,2048]{1,0:T(8,128)(2,1)}, bf16[1024,2048]{1,0:T(8,128)(2,1)S(1)}, u32[]{:S(2)}) copy-start(bf16[1024,2048]{1,0:T(8,128)(2,1)S(1)} %convolution_convert_fusion.3) | copy-start | bytes 12582916
  361.6 34.6 %copy-start.35 = (bf16[1024,512]{1,0:T(8,128)(2,1)S(1)}, bf16[1024,512]{1,0:T(8,128)(2,1)}, u32[]{:S(2)}) copy-start(bf16[1024,512]{1,0:T(8,128)(2,1)} %get-tuple-element.65) | copy-start | bytes 3145732
  361.6 21.3 %collective-permute-start.25 = (bf16[256,2048]{1,0:T(8,128)(2,1)S(1)}, bf16[256,2048]{1,0:T(8,128)(2,1)S(1)}, u32[]{:S(2)}, u32[]{:S(2)}) collective-permute-start(bf16[256,2048]{1,0:T(8,128)(2,1)S(1)} %get-tuple-element.125), channel_id=1, source_target_pairs={{0,2},{1,3},{2,0},{3,1},{4,6},{5,7},{6,4},{7,5},{8,10},{9,11},{10,... | collective-permute-start | bytes 3145736 | tf_op jit(solution)/shard_map/ppermute | solution.py:77
  363.1 23.7 %collective-permute-start.24 = (bf16[256,2048]{1,0:T(8,128)(2,1)S(1)}, bf16[256,2048]{1,0:T(8,128)(2,1)S(1)}, u32[]{:S(2)}, u32[]{:S(2)}) collective-permute-start(bf16[256,2048]{1,0:T(8,128)(2,1)S(1)} %get-tuple-element.125), channel_id=1, source_target_pairs={{0,1},{1,0},{2,3},{3,2},{4,5},{5,4},{6,7},{7,6},{8,9},{9,8},{10,11... | collective-permute-start | bytes 3145736 | tf_op jit(solution)/shard_map/ppermute | solution.py:77
  382.9 12.0 %collective-permute-start.26 = (bf16[128,2048]{1,0:T(8,128)(2,1)S(1)}, bf16[128,2048]{1,0:T(8,128)(2,1)S(1)}, u32[]{:S(2)}, u32[]{:S(2)}) collective-permute-start(bf16[128,2048]{1,0:T(8,128)(2,1)S(1)} %slice.248), channel_id=1, source_target_pairs={{0,1},{1,0},{2,3},{3,2},{4,5},{5,4},{6,7},{7,6},{8,9},{9,8},{10,11... | collective-permute-start | bytes 1572872 | tf_op jit(solution)/shard_map/ppermute | solution.py:77
  386.9 9.2 %collective-permute-start.27 = (bf16[128,2048]{1,0:T(8,128)(2,1)S(1)}, bf16[128,2048]{1,0:T(8,128)(2,1)S(1)}, u32[]{:S(2)}, u32[]{:S(2)}) collective-permute-start(bf16[128,2048]{1,0:T(8,128)(2,1)S(1)} %slice.249), channel_id=1, source_target_pairs={{0,2},{1,3},{2,0},{3,1},{4,6},{5,7},{6,4},{7,5},{8,10},{9,11},{10,... | collective-permute-start | bytes 1572872 | tf_op jit(solution)/shard_map/ppermute | solution.py:77
  401.4 30.6 %collective-permute-start.28 = (bf16[128,2048]{1,0:T(8,128)(2,1)}, bf16[128,2048]{1,0:T(8,128)(2,1)}, u32[]{:S(2)}, u32[]{:S(2)}) collective-permute-start(bf16[128,2048]{1,0:T(8,128)(2,1)} %get-tuple-element.145), channel_id=1, source_target_pairs={{0,1},{1,0},{2,3},{3,2},{4,5},{5,4},{6,7},{7,6},{8,9},{9,8},{10,11... | collective-permute-start | bytes 1572872 | tf_op jit(solution)/shard_map/ppermute | solution.py:77
  402.5 29.4 %collective-permute-start.29 = (bf16[128,2048]{1,0:T(8,128)(2,1)}, bf16[128,2048]{1,0:T(8,128)(2,1)}, u32[]{:S(2)}, u32[]{:S(2)}) collective-permute-start(bf16[128,2048]{1,0:T(8,128)(2,1)} %get-tuple-element.144), channel_id=1, source_target_pairs={{0,2},{1,3},{2,0},{3,1},{4,6},{5,7},{6,4},{7,5},{8,10},{9,11},{10,... | collective-permute-start | bytes 1572872 | tf_op jit(solution)/shard_map/ppermute | solution.py:77
  402.6 29.4 %collective-permute-start.30 = (bf16[128,2048]{1,0:T(8,128)(2,1)}, bf16[128,2048]{1,0:T(8,128)(2,1)}, u32[]{:S(2)}, u32[]{:S(2)}) collective-permute-start(bf16[128,2048]{1,0:T(8,128)(2,1)} %get-tuple-element.143), channel_id=1, source_target_pairs={{0,1},{1,0},{2,3},{3,2},{4,5},{5,4},{6,7},{7,6},{8,9},{9,8},{10,11... | collective-permute-start | bytes 1572872 | tf_op jit(solution)/shard_map/ppermute | solution.py:77
  403.6 28.3 %collective-permute-start.31 = (bf16[128,2048]{1,0:T(8,128)(2,1)}, bf16[128,2048]{1,0:T(8,128)(2,1)}, u32[]{:S(2)}, u32[]{:S(2)}) collective-permute-start(bf16[128,2048]{1,0:T(8,128)(2,1)} %get-tuple-element.142), channel_id=1, source_target_pairs={{0,2},{1,3},{2,0},{3,1},{4,6},{5,7},{6,4},{7,5},{8,10},{9,11},{10,... | collective-permute-start | bytes 1572872 | tf_op jit(solution)/shard_map/ppermute | solution.py:77
  442.9 10.3 %collective-permute-start.32 = (bf16[128,2048]{1,0:T(8,128)(2,1)}, bf16[128,2048]{1,0:T(8,128)(2,1)}, u32[]{:S(2)}, u32[]{:S(2)}) collective-permute-start(bf16[128,2048]{1,0:T(8,128)(2,1)} %get-tuple-element.141), channel_id=1, source_target_pairs={{0,1},{1,0},{2,3},{3,2},{4,5},{5,4},{6,7},{7,6},{8,9},{9,8},{10,11... | collective-permute-start | bytes 1572872 | tf_op jit(solution)/shard_map/ppermute | solution.py:77
  444.1 9.5 %collective-permute-start.33 = (bf16[128,2048]{1,0:T(8,128)(2,1)}, bf16[128,2048]{1,0:T(8,128)(2,1)}, u32[]{:S(2)}, u32[]{:S(2)}) collective-permute-start(bf16[128,2048]{1,0:T(8,128)(2,1)} %get-tuple-element.140), channel_id=1, source_target_pairs={{0,2},{1,3},{2,0},{3,1},{4,6},{5,7},{6,4},{7,5},{8,10},{9,11},{10,... | collective-permute-start | bytes 1572872 | tf_op jit(solution)/shard_map/ppermute | solution.py:77
  460.5 16.6 %copy-start.22 = (bf16[128,2048]{1,0:T(8,128)(2,1)S(1)}, bf16[128,2048]{1,0:T(8,128)(2,1)}, u32[]{:S(2)}) copy-start(bf16[128,2048]{1,0:T(8,128)(2,1)} %get-tuple-element.139) | copy-start | bytes 1572868
  460.5 17.1 %copy-start.21 = (bf16[128,2048]{1,0:T(8,128)(2,1)S(1)}, bf16[128,2048]{1,0:T(8,128)(2,1)}, u32[]{:S(2)}) copy-start(bf16[128,2048]{1,0:T(8,128)(2,1)} %get-tuple-element.138) | copy-start | bytes 1572868
  461.9 11.6 %collective-permute-start.36 = (bf16[128,2048]{1,0:T(8,128)(2,1)S(1)}, bf16[128,2048]{1,0:T(8,128)(2,1)S(1)}, u32[]{:S(2)}, u32[]{:S(2)}) collective-permute-start(bf16[128,2048]{1,0:T(8,128)(2,1)S(1)} %add_convert_fusion.3), channel_id=1, source_target_pairs={{0,2},{1,3},{2,0},{3,1},{4,6},{5,7},{6,4},{7,5},{8,10},{9,11},{10,... | collective-permute-start | bytes 1572872 | tf_op jit(solution)/shard_map/ppermute | solution.py:77
  475.5 14.9 %collective-permute-start.37 = (bf16[128,2048]{1,0:T(8,128)(2,1)S(1)}, bf16[128,2048]{1,0:T(8,128)(2,1)S(1)}, u32[]{:S(2)}, u32[]{:S(2)}) collective-permute-start(bf16[128,2048]{1,0:T(8,128)(2,1)S(1)} %get-tuple-element.137), channel_id=1, source_target_pairs={{0,1},{1,0},{2,3},{3,2},{4,5},{5,4},{6,7},{7,6},{8,9},{9,8},{10,11... | collective-permute-start | bytes 1572872 | tf_op jit(solution)/shard_map/ppermute | solution.py:77
  477.0 20.4 %collective-permute-start.34 = (bf16[128,2048]{1,0:T(8,128)(2,1)S(1)}, bf16[128,2048]{1,0:T(8,128)(2,1)}, u32[]{:S(2)}, u32[]{:S(2)}) collective-permute-start(bf16[128,2048]{1,0:T(8,128)(2,1)S(1)} %copy-done.22), channel_id=1, source_target_pairs={{0,1},{1,0},{2,3},{3,2},{4,5},{5,4},{6,7},{7,6},{8,9},{9,8},{10,11... | collective-permute-start | bytes 1572872 | tf_op jit(solution)/shard_map/ppermute | solution.py:77
  477.6 19.9 %collective-permute-start.35 = (bf16[128,2048]{1,0:T(8,128)(2,1)S(1)}, bf16[128,2048]{1,0:T(8,128)(2,1)}, u32[]{:S(2)}, u32[]{:S(2)}) collective-permute-start(bf16[128,2048]{1,0:T(8,128)(2,1)S(1)} %copy-done.21), channel_id=1, source_target_pairs={{0,2},{1,3},{2,0},{3,1},{4,6},{5,7},{6,4},{7,5},{8,10},{9,11},{10,... | collective-permute-start | bytes 1572872 | tf_op jit(solution)/shard_map/ppermute | solution.py:77
  499.6 10.0 %collective-permute-start.38 = (bf16[128,2048]{1,0:T(8,128)(2,1)}, bf16[128,2048]{1,0:T(8,128)(2,1)}, u32[]{:S(2)}, u32[]{:S(2)}) collective-permute-start(bf16[128,2048]{1,0:T(8,128)(2,1)} %add_convert_fusion.1), channel_id=1, source_target_pairs={{0,2},{1,3},{2,0},{3,1},{4,6},{5,7},{6,4},{7,5},{8,10},{9,11},{10,... | collective-permute-start | bytes 1572872 | tf_op jit(solution)/shard_map/ppermute | solution.py:77
  501.1 12.2 %copy-start.7 = (bf16[1024,2048]{1,0:T(8,128)(2,1)S(1)}, bf16[1024,2048]{1,0:T(8,128)(2,1)}, u32[]{:S(2)}) copy-start(bf16[1024,2048]{1,0:T(8,128)(2,1)} %copy-done.6) | copy-start | bytes 12582916
  511.8 9.5 %collective-permute-start.39 = (bf16[128,2048]{1,0:T(8,128)(2,1)S(1)}, bf16[128,2048]{1,0:T(8,128)(2,1)S(1)}, u32[]{:S(2)}, u32[]{:S(2)}) collective-permute-start(bf16[128,2048]{1,0:T(8,128)(2,1)S(1)} %get-tuple-element.135), channel_id=1, source_target_pairs={{0,1},{1,0},{2,3},{3,2},{4,5},{5,4},{6,7},{7,6},{8,9},{9,8},{10,11... | collective-permute-start | bytes 1572872 | tf_op jit(solution)/shard_map/ppermute | solution.py:77
  522.7 18.2 %copy-start.3 = (f32[256,2048]{1,0:T(8,128)S(1)}, f32[256,2048]{1,0:T(8,128)}, u32[]{:S(2)}) copy-start(f32[256,2048]{1,0:T(8,128)} %copy-done.2) | copy-start | bytes 6291460
  522.7 18.1 %copy-start.11 = (f32[256,2048]{1,0:T(8,128)S(1)}, f32[256,2048]{1,0:T(8,128)}, u32[]{:S(2)}) copy-start(f32[256,2048]{1,0:T(8,128)} %pad_maximum_fusion.3) | copy-start | bytes 6291460
  522.7 3.8 collective-permute-start.40
  526.5 3.8 collective-permute-start.41
  530.3 1.2 collective-permute-start.42
  531.5 12.4 %collective-permute-start.45 = (f32[4352]{0:T(1024)S(1)}, f32[4352]{0:T(1024)S(1)}, u32[]{:S(2)}, u32[]{:S(2)}) collective-permute-start(f32[4352]{0:T(1024)S(1)} %add.213), channel_id=1, source_target_pairs={{0,24},{4,28},{8,0},{12,4},{16,8},{20,12},{24,16},{28,20},{1,25},{... | collective-permute-start | bytes 52232 | tf_op jit(solution)/shard_map/ppermute | solution.py:63
  540.2 4.7 collective-permute-start.44
  540.2 5.6 collective-permute-start.43
  (25 other events, 121.6 us)
Sparse Core Ops, SparseCore 0:
  10.3 67.4 all-gather.3
  80.0 115.3 all-gather.5
  197.0 62.9 all-gather.7
  262.2 68.4 reduce-scatter.3
  332.9 127.5 reduce-scatter.5
  462.6 68.1 reduce-scatter.7

commit v3 on v2

--- a/solution.py
+++ b/solution.py
@@ -185,6 +185,21 @@
         (((left_axis,), (right_axis,)), ((), ())),
         preferred_element_type=jnp.float32,
     )
+
+
+def split_columns(rows, widths):
+    def kernel(source, *targets):
+        start = 0
+        for target in targets:
+            width = target.shape[1]
+            target[...] = source[:, start : start + width].astype(jnp.float32)
+            start += width
+
+    return pl.pallas_call(
+        kernel,
+        name="split_columns",
+        out_shape=[jax.ShapeDtypeStruct((rows.shape[0], width), jnp.float32) for width in widths],
+    )(rows)
 
 
 class Attention:
@@ -531,18 +546,17 @@
         attended_grad,
     )
     raw_grad, feed_first = lax.optimization_barrier((raw_grad, feed_first))
+    attention_term = contract_first(normed_rows, raw_grad).astype(jnp.bfloat16)
+    feed_first, attention_term = lax.optimization_barrier((feed_first, attention_term))
+    feed_branch = links.scatter_second(feed_partial, feed_first)
+    raw_grad, attention_term = lax.optimization_barrier((raw_grad, attention_term))
     input_partial = contract_last(raw_grad, wide_attention).astype(jnp.bfloat16)
+    mixing_term = jnp.concatenate([attention_term, output_term], axis=1)
+    mixing_term, feed_sum, feed_branch, input_partial = lax.optimization_barrier(
+        (mixing_term, feed_sum, feed_branch, input_partial)
+    )
+    mixing_sum = links.scatter_weight(mixing_term)
     input_first = links.scatter_first(input_partial)
-    raw_grad, input_partial = lax.optimization_barrier((raw_grad, input_partial))
-    attention_term = contract_first(normed_rows, raw_grad).astype(jnp.bfloat16)
-    mixing_term = jnp.concatenate([attention_term, output_term], axis=1)
-    mixing_term, feed_sum, passed = lax.optimization_barrier(
-        (mixing_term, feed_sum, input_first[:2])
-    )
-    input_first = passed + input_first[2:]
-    mixing_sum = links.scatter_weight(mixing_term)
-    feed_branch = links.scatter_second(feed_partial, feed_first)
-    input_first, feed_branch = lax.optimization_barrier((input_first, feed_branch))
     input_gain_term = (
         jnp.sum(input_partial.astype(jnp.float32) * normed_rows.astype(jnp.float32), axis=0)
         / input_gain
@@ -556,7 +570,10 @@
     tokens_grad = middle_grad + norm_backward(input_normed_grad, scaled_in, inverse_in, input_gain)
     terms = links.total_dp(links.total_tensor(terms))
     width = tokens.shape[1]
-    mixing_sum, feed_sum = mixing_sum.astype(jnp.float32), feed_sum.astype(jnp.float32)
+    feed_sum = feed_sum.astype(jnp.float32)
+    query_sum, key_sum, value_sum, output_sum = split_columns(
+        mixing_sum, (query_width, key_width, key_width, query_width)
+    )
     return (
         layer_output,
         tokens_grad,
@@ -564,10 +581,10 @@
         terms[width : 2 * width],
         terms[2 * width : 2 * width + head_size],
         terms[2 * width + head_size :],
-        mixing_sum[:, :query_width],
-        mixing_sum[:, query_width : query_width + key_width],
-        mixing_sum[:, query_width + key_width : query_width + 2 * key_width],
-        mixing_sum[:, query_width + 2 * key_width :],
+        query_sum,
+        key_sum,
+        value_sum,
+        output_sum,
         feed_sum[:, :hidden],
         feed_sum[:, hidden:],
         down_sum.astype(jnp.float32),

time: 567 us -> 557 us (0.982)
  local copies, waits for them, and re-layouts: 49.7 us -> 39 us
  waiting for transfers between devices: 230 us -> 223 us
    ppermute x42, waiting for transfers between devices: 198 us -> 190 us  [across(): lax.ppermute(value, 'tensor', [(place, place ^ bit) for place in range(se...]
    unnamed x91 -> x77, local copies, waits for them, and re-layouts: 27.5 us -> 21.5 us
  transfers between devices with their start and end apart: 52 -> 52, of which waited for: 33 -> 32; matrix products, arithmetic and copies ran while one was open for 38% -> 38% of each run, Pallas kernels for 5% -> 6%
where the time goes in v3:
time: 557 us; the launch traced here: 550 us
  waiting for transfers between devices  223 us (40%)
  matrix products  129 us (23%)
  starting transfers between devices  56.8 us (10%)
  other arithmetic  53 us (10%)
  local copies, waits for them, and re-layouts  39 us (7%)
  Pallas kernels  33 us (6%)
  between operations  15.3 us (3%)
    ppermute x42, waiting for transfers between devices, across(): lax.ppermute(value, 'tensor', [(place, place ^ bit) for place in range(se...  190 us
    dot_general x4, matrix products, matmul(): return jnp.dot(left, right, preferred_element_type=jnp.float32)  47.1 us
    ppermute x42, starting transfers between devices, across(): lax.ppermute(value, 'tensor', [(place, place ^ bit) for place in range(se...  44.7 us
    dot_general x4, matrix products, contract_last(): lax.dot_general(left, right, (((1,), (1,)), ((), ())), preferred_element_...  41.1 us
    dot_general x4, matrix products, contract_first(): lax.dot_general(left, right, (((0,), (0,)), ((), ())), preferred_element_...  41 us
    unnamed x77, local copies, waits for them, and re-layouts  21.5 us
    all_gather x3, waiting for transfers between devices, gather_weight(): return lax.all_gather(shard, 'dp', axis=0, tiled=True)  19.6 us
    pallas_call x1, Pallas kernels, backward(): pl.pallas_call(self.backward_kernel, name='attention_backward', cost_esti...  16.3 us
  transfers between devices with their start and end apart: 52, of which 32 were waited for; matrix products, arithmetic and copies ran while one was open for 38% of the time, Pallas kernels for 6%

profile of v3, /device:TPU:0, one launch (start us, length us, event | category | flops | bytes accessed | tf_op | source)
XLA Modules:
  0.0 549.7 jit_solution(14512531303111484132)
XLA Ops:
  7.2 2.2 pad_maximum_fusion.6
  9.5 2.7 pad_maximum_fusion.5
  14.3 3.0 collective-permute-start.1
  19.5 1.9 fusion.19
  21.4 20.2 %collective-permute-done.1 = bf16[256,2048]{1,0:T(8,128)(2,1)} collective-permute-done((bf16[256,2048]{1,0:T(8,128)(2,1)}, bf16[256,2048]{1,0:T(8,128)(2,1)}, u32[]{:S(2)}, u32[]{:S(2)}) %collective-permute-start.1) | collective-permute-done | bytes 1048608 | tf_op jit(solution)/shard_map/ppermute | solution.py:77
  42.7 2.1 collective-permute-start.2
  48.5 2.3 constant_dynamic-update-slice_fusion.3
  50.8 2.3 constant_dynamic-update-slice_fusion.2
  53.1 22.7 %collective-permute-done.2 = bf16[128,2048]{1,0:T(8,128)(2,1)S(1)} collective-permute-done((bf16[128,2048]{1,0:T(8,128)(2,1)S(1)}, bf16[128,2048]{1,0:T(8,128)(2,1)S(1)}, u32[]{:S(2)}, u32[]{:S(2)}) %collective-permute-start.2) | collective-permute-done | bytes 524320 | tf_op jit(solution)/shard_map/ppermute | solution.py:77
  83.2 2.3 constant_dynamic-update-slice_fusion.7
  85.5 5.8 %collective-permute-done.6 = bf16[128,2048]{1,0:T(8,128)(2,1)S(1)} collective-permute-done((bf16[128,2048]{1,0:T(8,128)(2,1)S(1)}, bf16[128,2048]{1,0:T(8,128)(2,1)S(1)}, u32[]{:S(2)}, u32[]{:S(2)}) %collective-permute-start.6) | collective-permute-done | bytes 524320 | tf_op jit(solution)/shard_map/ppermute | solution.py:77
  94.7 10.0 %fusion.2.raw_query.raw_key.raw_value = f32[1024,1024]{1,0:T(8,128)} fusion(bf16[1024,2048]{1,0:T(8,128)(2,1)} %constant_dynamic-update-slice_fusion, bf16[2048,1536]{1,0:T(8,128)(2,1)} %all-gather.4.cloned.1.call-done), kind=kOutput, calls=%fused_computation.16 | convolution fusion | flops 4294967296 | bytes 12582912 | tf_op jit(solution)/shard_map/dot_general | solution.py:18
  104.7 14.4 %attention_forward.1 = (bf16[1024,512]{1,0:T(8,128)(2,1)}, bf16[1024,256]{1,0:T(8,128)(2,1)}, bf16[1024,256]{1,0:T(8,128)(2,1)}, bf16[1024,512]{1,0:T(8,128)(2,1)}, f32[2,2,1024]{2,1,0:T(2,128)}) custom-call(s32[1]{0:T(128)} %bitcast.place_ref, f32[1024,1024]{1,0:T(8,128)} %fusion.2.raw_query.raw_key.raw_value, ...), custom_call_target="tpu_custom_call" | custom-call | flops 4294967296 | bytes 8388608 | tf_op jit(solution)/shard_map/attention_forward/pallas_call | solution.py:283
  119.1 4.3 convolution_convert_fusion.4
  127.2 12.3 %collective-permute-done.9 = bf16[128,2048]{1,0:T(8,128)(2,1)S(1)} collective-permute-done((bf16[128,2048]{1,0:T(8,128)(2,1)S(1)}, bf16[128,2048]{1,0:T(8,128)(2,1)S(1)}, u32[]{:S(2)}, u32[]{:S(2)}) %collective-permute-start.9) | collective-permute-done | bytes 524320 | tf_op jit(solution)/shard_map/ppermute | solution.py:77
  141.9 5.4 collective-permute-done.8
  147.3 7.2 %collective-permute-done.10 = bf16[128,2048]{1,0:T(8,128)(2,1)} collective-permute-done((bf16[128,2048]{1,0:T(8,128)(2,1)S(1)}, bf16[128,2048]{1,0:T(8,128)(2,1)}, u32[]{:S(2)}, u32[]{:S(2)}) %collective-permute-start.10) | collective-permute-done | bytes 524320 | tf_op jit(solution)/shard_map/ppermute | solution.py:77
  154.5 2.0 convert_add_fusion.8
  156.9 3.1 collective-permute-done.11
  160.0 11.1 %collective-permute-done.13 = bf16[128,2048]{1,0:T(8,128)(2,1)S(1)} collective-permute-done((bf16[128,2048]{1,0:T(8,128)(2,1)S(1)}, bf16[128,2048]{1,0:T(8,128)(2,1)S(1)}, u32[]{:S(2)}, u32[]{:S(2)}) %collective-permute-start.13) | collective-permute-done | bytes 524320 | tf_op jit(solution)/shard_map/ppermute | solution.py:77
  175.0 19.8 %collective-permute-done.15 = bf16[256,2048]{1,0:T(8,128)(2,1)S(1)} collective-permute-done((bf16[256,2048]{1,0:T(8,128)(2,1)S(1)}, bf16[256,2048]{1,0:T(8,128)(2,1)S(1)}, u32[]{:S(2)}, u32[]{:S(2)}) %collective-permute-start.15) | collective-permute-done | bytes 1048608 | tf_op jit(solution)/shard_map/ppermute | solution.py:77
  197.7 6.3 %collective-permute-done.16 = bf16[128,2048]{1,0:T(8,128)(2,1)S(1)} collective-permute-done((bf16[128,2048]{1,0:T(8,128)(2,1)S(1)}, bf16[128,2048]{1,0:T(8,128)(2,1)S(1)}, u32[]{:S(2)}, u32[]{:S(2)}) %collective-permute-start.16) | collective-permute-done | bytes 524320 | tf_op jit(solution)/shard_map/ppermute | solution.py:77
  205.7 17.2 %fusion.30 = f32[1024,3072]{1,0:T(8,128)S(1)} fusion(bf16[1024,2048]{1,0:T(8,128)(2,1)} %constant_dynamic-update-slice_fusion.10, bf16[2048,3072]{1,0:T(8,128)(2,1)} %all-gather.6.cloned.1.call-done), kind=kOutput, calls=%fused_computation.105 | convolution fusion | flops 12884901888 | bytes 29360128 | tf_op jit(solution)/shard_map/dot_general | solution.py:18
  223.0 2.0 multiply_convert_fusion.2
  224.9 2.6 copy-done.7
  229.2 11.2 %convolution_convert_fusion.1 = bf16[2048,1536]{1,0:T(8,128)(2,1)} fusion(bf16[1024,2048]{1,0:T(8,128)(2,1)} %constant_dynamic-update-slice_fusion.5, bf16[1024,1536]{1,0:T(8,128)(2,1)S(1)} %multiply_convert_fusion.2), kind=kOutput, calls=%fused_computation.2 | convolution fusion | flops 6445596672 | bytes 13631488 | tf_op jit(solution)/shard_map/dot_general | solution.py:22
  240.5 19.6 %all-gather.8.cloned.1.call-done = bf16[2048,1536]{1,0:T(8,128)(2,1)} async-done(((bf16[256,1536]{1,0:T(8,128)(2,1)}), bf16[2048,1536]{1,0:T(8,128)(2,1)}) %all-gather.8.cloned.1.call-update) | async-done | bytes 6291472 | tf_op jit(solution)/shard_map/all_gather | solution.py:158
  260.1 14.9 %multiply_convert_fusion.1 = (bf16[1024,1536]{1,0:T(8,128)(2,1)S(1)}, bf16[1024,1536]{1,0:T(8,128)(2,1)S(1)}) fusion(f32[1024,3072]{1,0:T(8,128)} %copy-done.7, bf16[1024,2048]{1,0:T(8,128)(2,1)} %constant_dynamic-update-slice_fusion.5, bf16[2048,1536]{1,0:T(8,128)(2,1)} %all-gather.8.cloned.1.call-done), kind=kOutput, calls=%fused_computation.6 | convolution fusion | flops 6462898176 | bytes 29360128 | tf_op jit(solution)/shard_map/dot_general | solution.py:18
  278.6 19.5 %convolution_convert_fusion.2 = bf16[1024,2048]{1,0:T(8,128)(2,1)} fusion(bf16[2048,3072]{1,0:T(8,128)(2,1)} %all-gather.6.cloned.1.call-done, bf16[1024,1536]{1,0:T(8,128)(2,1)} %copy-done.15, bf16[1024,1536]{1,0:T(8,128)(2,1)} %copy-done.14), kind=kOutput, calls=%fused_computation.10 | convolution fusion | flops 12899581952 | bytes 23068672 | tf_op jit(solution)/shard_map/dot_general | solution.py:28
  298.1 2.9 fusion.25
  305.0 18.4 %convolution_convert_fusion = bf16[2048,3072]{1,0:T(8,128)(2,1)} fusion(bf16[1024,2048]{1,0:T(8,128)(2,1)} %constant_dynamic-update-slice_fusion.10, bf16[1024,3072]{1,0:T(8,128)(2,1)S(1)} %pad_maximum_fusion), kind=kOutput, calls=%fused_computation | convolution fusion | flops 12891193344 | bytes 23068672 | tf_op jit(solution)/shard_map/dot_general | solution.py:22
  323.5 3.1 collective-permute-done.20
  327.8 2.9 reduce-scatter.4.cloned.1.call-done
  333.8 10.1 %collective-permute-done.22 = bf16[128,2048]{1,0:T(8,128)(2,1)S(1)} collective-permute-done((bf16[128,2048]{1,0:T(8,128)(2,1)S(1)}, bf16[128,2048]{1,0:T(8,128)(2,1)S(1)}, u32[]{:S(2)}, u32[]{:S(2)}) %collective-permute-start.22) | collective-permute-done | bytes 524320 | tf_op jit(solution)/shard_map/ppermute | solution.py:77
  343.9 1.9 convert_add_fusion.6
  347.3 8.8 %convolution_convert_fusion.3 = bf16[1024,2048]{1,0:T(8,128)(2,1)S(1)} fusion(bf16[1024,1536]{1,0:T(8,128)(2,1)S(1)} %copy-done.17, bf16[2048,1536]{1,0:T(8,128)(2,1)} %all-gather.8.cloned.1.call-done), kind=kOutput, calls=%fused_computation.11 | convolution fusion | flops 6444548096 | bytes 13631488 | tf_op jit(solution)/shard_map/dot_general | solution.py:28
  356.5 3.1 convert_add_fusion.5
  364.0 18.9 %collective-permute-done.25 = bf16[256,2048]{1,0:T(8,128)(2,1)S(1)} collective-permute-done((bf16[256,2048]{1,0:T(8,128)(2,1)S(1)}, bf16[256,2048]{1,0:T(8,128)(2,1)S(1)}, u32[]{:S(2)}, u32[]{:S(2)}) %collective-permute-start.25) | collective-permute-done | bytes 1048608 | tf_op jit(solution)/shard_map/ppermute | solution.py:77
  384.8 2.0 collective-permute-done.24
  387.3 7.6 %collective-permute-done.26 = bf16[128,2048]{1,0:T(8,128)(2,1)S(1)} collective-permute-done((bf16[128,2048]{1,0:T(8,128)(2,1)S(1)}, bf16[128,2048]{1,0:T(8,128)(2,1)S(1)}, u32[]{:S(2)}, u32[]{:S(2)}) %collective-permute-start.26) | collective-permute-done | bytes 524320 | tf_op jit(solution)/shard_map/ppermute | solution.py:77
  396.2 3.9 convolution_convert_fusion.7
  405.4 4.9 fusion.16.upstream
  410.4 16.3 %attention_backward.1 = (bf16[1024,1024]{1,0:T(8,128)(2,1)}, f32[1,128]{1,0:T(1,128)}, f32[1,128]{1,0:T(1,128)}) custom-call(s32[1]{0:T(128)} %bitcast.place_ref, f32[1024,1024]{1,0:T(8,128)} %fusion.2.raw_query.raw_key.raw_value, f32[1024,1024]{1,0:T(8,128)} %fusion.2.raw_query.raw_key.raw_value, f32[1024,128]{1,0:T(8,128)} %get-tuple-element.168.cosine, ...), custom_call_target="tpu_custom_call" | custom-call | flops 10737418240 | bytes 8388608 | tf_op jit(solution)/shard_map/attention_backward/pallas_call | solution.py:399
  426.7 7.6 %convolution_convert_fusion.6 = bf16[2048,1024]{1,0:T(8,128)(2,1)S(1)} fusion(bf16[1024,2048]{1,0:T(8,128)(2,1)} %constant_dynamic-update-slice_fusion, bf16[1024,1024]{1,0:T(8,128)(2,1)} %get-tuple-element.103), kind=kOutput, calls=%fused_computation.14 | convolution fusion | flops 4297064448 | bytes 10485760 | tf_op jit(solution)/shard_map/dot_general | solution.py:22
  436.1 8.5 %convolution_convert_fusion.5 = bf16[1024,2048]{1,0:T(8,128)(2,1)} fusion(bf16[1024,1024]{1,0:T(8,128)(2,1)S(1)} %copy-done.31, bf16[2048,1536]{1,0:T(8,128)(2,1)} %all-gather.4.cloned.1.call-done), kind=kOutput, calls=%fused_computation.13 | convolution fusion | flops 4297064448 | bytes 10485760 | tf_op jit(solution)/shard_map/dot_general | solution.py:28
  444.9 3.2 convert_add_fusion.4
  449.3 3.1 pad_maximum_fusion.1
  452.5 5.2 collective-permute-done.33
  459.2 2.7 pad_maximum_fusion.3
  462.0 2.7 fusion.23
  468.0 11.5 %collective-permute-done.35 = bf16[128,2048]{1,0:T(8,128)(2,1)S(1)} collective-permute-done((bf16[128,2048]{1,0:T(8,128)(2,1)S(1)}, bf16[128,2048]{1,0:T(8,128)(2,1)S(1)}, u32[]{:S(2)}, u32[]{:S(2)}) %collective-permute-start.35) | collective-permute-done | bytes 524320 | tf_op jit(solution)/shard_map/ppermute | solution.py:77
  479.6 2.0 add_convert_fusion.1
  482.8 2.6 convert_element_type.283
  486.2 7.2 %collective-permute-done.36 = bf16[128,2048]{1,0:T(8,128)(2,1)} collective-permute-done((bf16[128,2048]{1,0:T(8,128)(2,1)}, bf16[128,2048]{1,0:T(8,128)(2,1)}, u32[]{:S(2)}, u32[]{:S(2)}) %collective-permute-start.36) | collective-permute-done | bytes 524320 | tf_op jit(solution)/shard_map/ppermute | solution.py:77
  493.4 2.1 convert_add_fusion.2
  497.1 4.0 multiply_reduce_fusion
  501.1 3.7 collective-permute-done.39
  506.8 2.1 fusion.27
  514.1 6.3 %collective-permute-start.45 = (f32[4352]{0:T(1024)S(1)}, f32[4352]{0:T(1024)S(1)}, u32[]{:S(2)}, u32[]{:S(2)}) collective-permute-start(f32[4352]{0:T(1024)S(1)} %add.213), channel_id=1, source_target_pairs={{0,24},{4,28},{8,0},{12,4},{16,8},{20,12},{24,16},{28,20},{1,25},{... | collective-permute-start | bytes 52232 | tf_op jit(solution)/shard_map/ppermute | solution.py:63
  520.3 5.1 collective-permute-start.44
  525.9 3.1 fusion.11
  529.5 2.2 collective-permute-done.43
  533.0 7.2 %reduce-scatter.8.cloned.1.call-done.source = bf16[256,1536]{1,0:T(8,128)(2,1)} async-done(((bf16[2048,1536]{1,0:T(8,128)(2,1)}), bf16[256,1536]{1,0:T(8,128)(2,1)}) %reduce-scatter.8.cloned.1.call-update) | async-done | bytes 786448 | tf_op jit(solution)/shard_map/reduce_scatter | solution.py:161
  540.2 2.3 split_columns.1
  (207 shorter events, 84.8 us)
Async XLA Ops:
  7.2 87.5 %all-gather.4.cloned.1.call-start = ((), (), s32[]{:S(2)}) async-start(), calls=%async_computation.3 | async-start | bytes 7077888 | tf_op jit(solution)/shard_map/all_gather | solution.py:158
  9.4 9.9 %copy-start.27 = (s32[1024]{0:T(1024)S(1)}, s32[1024]{0:T(1024)}, u32[]{:S(2)}) copy-start(s32[1024]{0:T(1024)} %param.15) | copy-start | bytes 12292
  9.5 196.3 %all-gather.6.cloned.1.call-start = ((), (), s32[]{:S(2)}) async-start(), calls=%async_computation.4 | async-start | bytes 14155776 | tf_op jit(solution)/shard_map/all_gather | solution.py:158
  12.3 247.8 %all-gather.8.cloned.1.call-start = ((), (), s32[]{:S(2)}) async-start(), calls=%async_computation.5 | async-start | bytes 7077888 | tf_op jit(solution)/shard_map/all_gather | solution.py:158
  14.3 27.3 %collective-permute-start.1 = (bf16[256,2048]{1,0:T(8,128)(2,1)}, bf16[256,2048]{1,0:T(8,128)(2,1)}, u32[]{:S(2)}, u32[]{:S(2)}) collective-permute-start(bf16[256,2048]{1,0:T(8,128)(2,1)} %get-tuple-element.126), channel_id=1, source_target_pairs={{0,2},{1,3},{2,0},{3,1},{4,6},{5,7},{6,4},{7,5},{8,10},{9,11},{10,... | collective-permute-start | bytes 3145736 | tf_op jit(solution)/shard_map/ppermute | solution.py:77
  17.3 28.5 %collective-permute-start = (bf16[256,2048]{1,0:T(8,128)(2,1)}, bf16[256,2048]{1,0:T(8,128)(2,1)}, u32[]{:S(2)}, u32[]{:S(2)}) collective-permute-start(bf16[256,2048]{1,0:T(8,128)(2,1)} %get-tuple-element.126), channel_id=1, source_target_pairs={{0,1},{1,0},{2,3},{3,2},{4,5},{5,4},{6,7},{7,6},{8,9},{9,8},{10,11... | collective-permute-start | bytes 3145736 | tf_op jit(solution)/shard_map/ppermute | solution.py:77
  18.8 58.7 %collective-permute-start.4 = (bf16[256,2048]{1,0:T(8,128)(2,1)S(1)}, bf16[256,2048]{1,0:T(8,128)(2,1)S(1)}, u32[]{:S(2)}, u32[]{:S(2)}) collective-permute-start(bf16[256,2048]{1,0:T(8,128)(2,1)S(1)} %copy-done.8), channel_id=1, source_target_pairs={{0,1},{1,0},{2,3},{3,2},{4,5},{5,4},{6,7},{7,6},{8,9},{9,8},{10,11... | collective-permute-start | bytes 3145736 | tf_op jit(solution)/shard_map/ppermute | solution.py:77
  19.3 58.2 %collective-permute-start.5 = (bf16[256,2048]{1,0:T(8,128)(2,1)S(1)}, bf16[256,2048]{1,0:T(8,128)(2,1)}, u32[]{:S(2)}, u32[]{:S(2)}) collective-permute-start(bf16[256,2048]{1,0:T(8,128)(2,1)S(1)} %copy-done.8), channel_id=1, source_target_pairs={{0,2},{1,3},{2,0},{3,1},{4,6},{5,7},{6,4},{7,5},{8,10},{9,11},{10,... | collective-permute-start | bytes 3145736 | tf_op jit(solution)/shard_map/ppermute | solution.py:77
  42.7 33.2 %collective-permute-start.2 = (bf16[128,2048]{1,0:T(8,128)(2,1)S(1)}, bf16[128,2048]{1,0:T(8,128)(2,1)S(1)}, u32[]{:S(2)}, u32[]{:S(2)}) collective-permute-start(bf16[128,2048]{1,0:T(8,128)(2,1)S(1)} %slice.216), channel_id=1, source_target_pairs={{0,1},{1,0},{2,3},{3,2},{4,5},{5,4},{6,7},{7,6},{8,9},{9,8},{10,11... | collective-permute-start | bytes 1572872 | tf_op jit(solution)/shard_map/ppermute | solution.py:77
  46.9 29.8 %collective-permute-start.3 = (bf16[128,2048]{1,0:T(8,128)(2,1)S(1)}, bf16[128,2048]{1,0:T(8,128)(2,1)S(1)}, u32[]{:S(2)}, u32[]{:S(2)}) collective-permute-start(bf16[128,2048]{1,0:T(8,128)(2,1)S(1)} %slice.217), channel_id=1, source_target_pairs={{0,2},{1,3},{2,0},{3,1},{4,6},{5,7},{6,4},{7,5},{8,10},{9,11},{10,... | collective-permute-start | bytes 1572872 | tf_op jit(solution)/shard_map/ppermute | solution.py:77
  78.6 12.7 %collective-permute-start.6 = (bf16[128,2048]{1,0:T(8,128)(2,1)S(1)}, bf16[128,2048]{1,0:T(8,128)(2,1)S(1)}, u32[]{:S(2)}, u32[]{:S(2)}) collective-permute-start(bf16[128,2048]{1,0:T(8,128)(2,1)S(1)} %slice.165), channel_id=1, source_target_pairs={{0,1},{1,0},{2,3},{3,2},{4,5},{5,4},{6,7},{7,6},{8,9},{9,8},{10,11... | collective-permute-start | bytes 1572872 | tf_op jit(solution)/shard_map/ppermute | solution.py:77
  81.5 12.4 %collective-permute-start.7 = (bf16[128,2048]{1,0:T(8,128)(2,1)S(1)}, bf16[128,2048]{1,0:T(8,128)(2,1)S(1)}, u32[]{:S(2)}, u32[]{:S(2)}) collective-permute-start(bf16[128,2048]{1,0:T(8,128)(2,1)S(1)} %slice.166), channel_id=1, source_target_pairs={{0,2},{1,3},{2,0},{3,1},{4,6},{5,7},{6,4},{7,5},{8,10},{9,11},{10,... | collective-permute-start | bytes 1572872 | tf_op jit(solution)/shard_map/ppermute | solution.py:77
  123.4 16.1 %copy-start.13 = (bf16[1024,2048]{1,0:T(8,128)(2,1)}, bf16[1024,2048]{1,0:T(8,128)(2,1)S(1)}, u32[]{:S(2)}) copy-start(bf16[1024,2048]{1,0:T(8,128)(2,1)S(1)} %convolution_convert_fusion.4) | copy-start | bytes 12582916
  124.7 14.9 %collective-permute-start.9 = (bf16[128,2048]{1,0:T(8,128)(2,1)S(1)}, bf16[128,2048]{1,0:T(8,128)(2,1)S(1)}, u32[]{:S(2)}, u32[]{:S(2)}) collective-permute-start(bf16[128,2048]{1,0:T(8,128)(2,1)S(1)} %get-tuple-element.152), channel_id=1, source_target_pairs={{0,1},{1,0},{2,3},{3,2},{4,5},{5,4},{6,7},{7,6},{8,9},{9,8},{10,11... | collective-permute-start | bytes 1572872 | tf_op jit(solution)/shard_map/ppermute | solution.py:77
  125.3 22.1 %collective-permute-start.8 = (bf16[128,2048]{1,0:T(8,128)(2,1)}, bf16[128,2048]{1,0:T(8,128)(2,1)S(1)}, u32[]{:S(2)}, u32[]{:S(2)}) collective-permute-start(bf16[128,2048]{1,0:T(8,128)(2,1)} %get-tuple-element.149), channel_id=1, source_target_pairs={{0,1},{1,0},{2,3},{3,2},{4,5},{5,4},{6,7},{7,6},{8,9},{9,8},{10,11... | collective-permute-start | bytes 1572872 | tf_op jit(solution)/shard_map/ppermute | solution.py:77
  126.7 20.6 %collective-permute-start.12 = (bf16[128,2048]{1,0:T(8,128)(2,1)S(1)}, bf16[128,2048]{1,0:T(8,128)(2,1)}, u32[]{:S(2)}, u32[]{:S(2)}) collective-permute-start(bf16[128,2048]{1,0:T(8,128)(2,1)S(1)} %get-tuple-element.150), channel_id=1, source_target_pairs={{0,2},{1,3},{2,0},{3,1},{4,6},{5,7},{6,4},{7,5},{8,10},{9,11},{10,... | collective-permute-start | bytes 1572872 | tf_op jit(solution)/shard_map/ppermute | solution.py:77
  139.7 14.8 %collective-permute-start.10 = (bf16[128,2048]{1,0:T(8,128)(2,1)S(1)}, bf16[128,2048]{1,0:T(8,128)(2,1)}, u32[]{:S(2)}, u32[]{:S(2)}) collective-permute-start(bf16[128,2048]{1,0:T(8,128)(2,1)S(1)} %add_convert_fusion.7), channel_id=1, source_target_pairs={{0,2},{1,3},{2,0},{3,1},{4,6},{5,7},{6,4},{7,5},{8,10},{9,11},{10,... | collective-permute-start | bytes 1572872 | tf_op jit(solution)/shard_map/ppermute | solution.py:77
  140.3 190.4 %reduce-scatter.4.cloned.1.call-start = ((), (), s32[]{:S(2)}) async-start(), calls=%async_computation.6 | async-start | bytes 7077888 | tf_op jit(solution)/shard_map/reduce_scatter | solution.py:161
  140.3 19.7 %collective-permute-start.11 = (bf16[128,2048]{1,0:T(8,128)(2,1)S(1)}, bf16[128,2048]{1,0:T(8,128)(2,1)S(1)}, u32[]{:S(2)}, u32[]{:S(2)}) collective-permute-start(bf16[128,2048]{1,0:T(8,128)(2,1)S(1)} %get-tuple-element.151), channel_id=1, source_target_pairs={{0,2},{1,3},{2,0},{3,1},{4,6},{5,7},{6,4},{7,5},{8,10},{9,11},{10,... | collective-permute-start | bytes 1572872 | tf_op jit(solution)/shard_map/ppermute | solution.py:77
  156.5 16.3 %copy-start.19 = (f32[2048]{0:T(1024)S(1)}, f32[2048]{0:T(1024)}, u32[]{:S(2)}) copy-start(f32[2048]{0:T(1024)} %param.17) | copy-start | bytes 24580
  156.5 14.6 %collective-permute-start.13 = (bf16[128,2048]{1,0:T(8,128)(2,1)S(1)}, bf16[128,2048]{1,0:T(8,128)(2,1)S(1)}, u32[]{:S(2)}, u32[]{:S(2)}) collective-permute-start(bf16[128,2048]{1,0:T(8,128)(2,1)S(1)} %get-tuple-element.148), channel_id=1, source_target_pairs={{0,1},{1,0},{2,3},{3,2},{4,5},{5,4},{6,7},{7,6},{8,9},{9,8},{10,11... | collective-permute-start | bytes 1572872 | tf_op jit(solution)/shard_map/ppermute | solution.py:77
  172.8 23.9 %copy-start = (f32[256,2048]{1,0:T(8,128)}, f32[256,2048]{1,0:T(8,128)S(1)}, u32[]{:S(2)}) copy-start(f32[256,2048]{1,0:T(8,128)S(1)} %get-tuple-element.124) | copy-start | bytes 6291460
  172.8 23.9 %copy-start.23 = (f32[256]{0:T(256)}, f32[256]{0:T(256)S(1)}, u32[]{:S(2)}) copy-start(f32[256]{0:T(256)S(1)} %add_rsqrt_fusion) | copy-start | bytes 3076
  174.3 20.4 %collective-permute-start.15 = (bf16[256,2048]{1,0:T(8,128)(2,1)S(1)}, bf16[256,2048]{1,0:T(8,128)(2,1)S(1)}, u32[]{:S(2)}, u32[]{:S(2)}) collective-permute-start(bf16[256,2048]{1,0:T(8,128)(2,1)S(1)} %get-tuple-element.122), channel_id=1, source_target_pairs={{0,2},{1,3},{2,0},{3,1},{4,6},{5,7},{6,4},{7,5},{8,10},{9,11},{10,... | collective-permute-start | bytes 3145736 | tf_op jit(solution)/shard_map/ppermute | solution.py:77
  174.3 20.5 %collective-permute-start.14 = (bf16[256,2048]{1,0:T(8,128)(2,1)S(1)}, bf16[256,2048]{1,0:T(8,128)(2,1)S(1)}, u32[]{:S(2)}, u32[]{:S(2)}) collective-permute-start(bf16[256,2048]{1,0:T(8,128)(2,1)S(1)} %get-tuple-element.122), channel_id=1, source_target_pairs={{0,1},{1,0},{2,3},{3,2},{4,5},{5,4},{6,7},{7,6},{8,9},{9,8},{10,11... | collective-permute-start | bytes 3145736 | tf_op jit(solution)/shard_map/ppermute | solution.py:77
  194.8 9.2 %collective-permute-start.16 = (bf16[128,2048]{1,0:T(8,128)(2,1)S(1)}, bf16[128,2048]{1,0:T(8,128)(2,1)S(1)}, u32[]{:S(2)}, u32[]{:S(2)}) collective-permute-start(bf16[128,2048]{1,0:T(8,128)(2,1)S(1)} %slice.228), channel_id=1, source_target_pairs={{0,1},{1,0},{2,3},{3,2},{4,5},{5,4},{6,7},{7,6},{8,9},{9,8},{10,11... | collective-permute-start | bytes 1572872 | tf_op jit(solution)/shard_map/ppermute | solution.py:77
  194.9 9.9 %collective-permute-start.17 = (bf16[128,2048]{1,0:T(8,128)(2,1)S(1)}, bf16[128,2048]{1,0:T(8,128)(2,1)S(1)}, u32[]{:S(2)}, u32[]{:S(2)}) collective-permute-start(bf16[128,2048]{1,0:T(8,128)(2,1)S(1)} %slice.229), channel_id=1, source_target_pairs={{0,2},{1,3},{2,0},{3,1},{4,6},{5,7},{6,4},{7,5},{8,10},{9,11},{10,... | collective-permute-start | bytes 1572872 | tf_op jit(solution)/shard_map/ppermute | solution.py:77
  240.4 221.6 %reduce-scatter.6.cloned.1.call-start = ((), (), s32[]{:S(2)}) async-start(), calls=%async_computation.7 | async-start | bytes 14155776 | tf_op jit(solution)/shard_map/reduce_scatter | solution.py:161
  301.0 22.5 %collective-permute-start.18 = (bf16[128,2048]{1,0:T(8,128)(2,1)}, bf16[128,2048]{1,0:T(8,128)(2,1)}, u32[]{:S(2)}, u32[]{:S(2)}) collective-permute-start(bf16[128,2048]{1,0:T(8,128)(2,1)} %get-tuple-element.146), channel_id=1, source_target_pairs={{0,1},{1,0},{2,3},{3,2},{4,5},{5,4},{6,7},{7,6},{8,9},{9,8},{10,11... | collective-permute-start | bytes 1572872 | tf_op jit(solution)/shard_map/ppermute | solution.py:77
  302.5 21.0 %collective-permute-start.19 = (bf16[128,2048]{1,0:T(8,128)(2,1)}, bf16[128,2048]{1,0:T(8,128)(2,1)}, u32[]{:S(2)}, u32[]{:S(2)}) collective-permute-start(bf16[128,2048]{1,0:T(8,128)(2,1)} %get-tuple-element.145), channel_id=1, source_target_pairs={{0,2},{1,3},{2,0},{3,1},{4,6},{5,7},{6,4},{7,5},{8,10},{9,11},{10,... | collective-permute-start | bytes 1572872 | tf_op jit(solution)/shard_map/ppermute | solution.py:77
  303.9 22.7 %collective-permute-start.20 = (bf16[128,2048]{1,0:T(8,128)(2,1)}, bf16[128,2048]{1,0:T(8,128)(2,1)}, u32[]{:S(2)}, u32[]{:S(2)}) collective-permute-start(bf16[128,2048]{1,0:T(8,128)(2,1)} %get-tuple-element.144), channel_id=1, source_target_pairs={{0,1},{1,0},{2,3},{3,2},{4,5},{5,4},{6,7},{7,6},{8,9},{9,8},{10,11... | collective-permute-start | bytes 1572872 | tf_op jit(solution)/shard_map/ppermute | solution.py:77
  304.5 23.3 %collective-permute-start.21 = (bf16[128,2048]{1,0:T(8,128)(2,1)}, bf16[128,2048]{1,0:T(8,128)(2,1)}, u32[]{:S(2)}, u32[]{:S(2)}) collective-permute-start(bf16[128,2048]{1,0:T(8,128)(2,1)} %get-tuple-element.143), channel_id=1, source_target_pairs={{0,2},{1,3},{2,0},{3,1},{4,6},{5,7},{6,4},{7,5},{8,10},{9,11},{10,... | collective-permute-start | bytes 1572872 | tf_op jit(solution)/shard_map/ppermute | solution.py:77
  330.7 16.6 %copy-start.17 = (bf16[1024,1536]{1,0:T(8,128)(2,1)S(1)}, bf16[1024,1536]{1,0:T(8,128)(2,1)}, u32[]{:S(2)}) copy-start(bf16[1024,1536]{1,0:T(8,128)(2,1)} %copy-done.16) | copy-start | bytes 9437188
  330.7 209.4 %reduce-scatter.8.cloned.1.call-start = ((), (), s32[]{:S(2)}) async-start(), calls=%async_computation.8 | async-start | bytes 7077888 | tf_op jit(solution)/shard_map/reduce_scatter | solution.py:161
  332.3 11.6 %collective-permute-start.22 = (bf16[128,2048]{1,0:T(8,128)(2,1)S(1)}, bf16[128,2048]{1,0:T(8,128)(2,1)S(1)}, u32[]{:S(2)}, u32[]{:S(2)}) collective-permute-start(bf16[128,2048]{1,0:T(8,128)(2,1)S(1)} %add_convert_fusion.5), channel_id=1, source_target_pairs={{0,2},{1,3},{2,0},{3,1},{4,6},{5,7},{6,4},{7,5},{8,10},{9,11},{10,... | collective-permute-start | bytes 1572872 | tf_op jit(solution)/shard_map/ppermute | solution.py:77
  345.8 10.7 %collective-permute-start.23 = (bf16[128,2048]{1,0:T(8,128)(2,1)S(1)}, bf16[128,2048]{1,0:T(8,128)(2,1)S(1)}, u32[]{:S(2)}, u32[]{:S(2)}) collective-permute-start(bf16[128,2048]{1,0:T(8,128)(2,1)S(1)} %get-tuple-element.142), channel_id=1, source_target_pairs={{0,1},{1,0},{2,3},{3,2},{4,5},{5,4},{6,7},{7,6},{8,9},{9,8},{10,11... | collective-permute-start | bytes 1572872 | tf_op jit(solution)/shard_map/ppermute | solution.py:77
  356.2 43.9 %copy-start.12 = (bf16[1024,2048]{1,0:T(8,128)(2,1)}, bf16[1024,2048]{1,0:T(8,128)(2,1)S(1)}, u32[]{:S(2)}) copy-start(bf16[1024,2048]{1,0:T(8,128)(2,1)S(1)} %convolution_convert_fusion.3) | copy-start | bytes 12582916
  361.6 34.6 %copy-start.30 = (bf16[1024,512]{1,0:T(8,128)(2,1)S(1)}, bf16[1024,512]{1,0:T(8,128)(2,1)}, u32[]{:S(2)}) copy-start(bf16[1024,512]{1,0:T(8,128)(2,1)} %get-tuple-element.69) | copy-start | bytes 3145732
  361.6 21.3 %collective-permute-start.25 = (bf16[256,2048]{1,0:T(8,128)(2,1)S(1)}, bf16[256,2048]{1,0:T(8,128)(2,1)S(1)}, u32[]{:S(2)}, u32[]{:S(2)}) collective-permute-start(bf16[256,2048]{1,0:T(8,128)(2,1)S(1)} %get-tuple-element.120), channel_id=1, source_target_pairs={{0,2},{1,3},{2,0},{3,1},{4,6},{5,7},{6,4},{7,5},{8,10},{9,11},{10,... | collective-permute-start | bytes 3145736 | tf_op jit(solution)/shard_map/ppermute | solution.py:77
  363.1 23.7 %collective-permute-start.24 = (bf16[256,2048]{1,0:T(8,128)(2,1)S(1)}, bf16[256,2048]{1,0:T(8,128)(2,1)S(1)}, u32[]{:S(2)}, u32[]{:S(2)}) collective-permute-start(bf16[256,2048]{1,0:T(8,128)(2,1)S(1)} %get-tuple-element.120), channel_id=1, source_target_pairs={{0,1},{1,0},{2,3},{3,2},{4,5},{5,4},{6,7},{7,6},{8,9},{9,8},{10,11... | collective-permute-start | bytes 3145736 | tf_op jit(solution)/shard_map/ppermute | solution.py:77
  382.9 12.0 %collective-permute-start.26 = (bf16[128,2048]{1,0:T(8,128)(2,1)S(1)}, bf16[128,2048]{1,0:T(8,128)(2,1)S(1)}, u32[]{:S(2)}, u32[]{:S(2)}) collective-permute-start(bf16[128,2048]{1,0:T(8,128)(2,1)S(1)} %slice.232), channel_id=1, source_target_pairs={{0,1},{1,0},{2,3},{3,2},{4,5},{5,4},{6,7},{7,6},{8,9},{9,8},{10,11... | collective-permute-start | bytes 1572872 | tf_op jit(solution)/shard_map/ppermute | solution.py:77
  386.9 9.2 %collective-permute-start.27 = (bf16[128,2048]{1,0:T(8,128)(2,1)S(1)}, bf16[128,2048]{1,0:T(8,128)(2,1)S(1)}, u32[]{:S(2)}, u32[]{:S(2)}) collective-permute-start(bf16[128,2048]{1,0:T(8,128)(2,1)S(1)} %slice.233), channel_id=1, source_target_pairs={{0,2},{1,3},{2,0},{3,1},{4,6},{5,7},{6,4},{7,5},{8,10},{9,11},{10,... | collective-permute-start | bytes 1572872 | tf_op jit(solution)/shard_map/ppermute | solution.py:77
  401.4 25.3 %collective-permute-start.28 = (bf16[128,2048]{1,0:T(8,128)(2,1)}, bf16[128,2048]{1,0:T(8,128)(2,1)}, u32[]{:S(2)}, u32[]{:S(2)}) collective-permute-start(bf16[128,2048]{1,0:T(8,128)(2,1)} %get-tuple-element.140), channel_id=1, source_target_pairs={{0,1},{1,0},{2,3},{3,2},{4,5},{5,4},{6,7},{7,6},{8,9},{9,8},{10,11... | collective-permute-start | bytes 1572872 | tf_op jit(solution)/shard_map/ppermute | solution.py:77
  402.6 24.1 %collective-permute-start.29 = (bf16[128,2048]{1,0:T(8,128)(2,1)}, bf16[128,2048]{1,0:T(8,128)(2,1)}, u32[]{:S(2)}, u32[]{:S(2)}) collective-permute-start(bf16[128,2048]{1,0:T(8,128)(2,1)} %get-tuple-element.139), channel_id=1, source_target_pairs={{0,2},{1,3},{2,0},{3,1},{4,6},{5,7},{6,4},{7,5},{8,10},{9,11},{10,... | collective-permute-start | bytes 1572872 | tf_op jit(solution)/shard_map/ppermute | solution.py:77
  402.6 24.1 %collective-permute-start.30 = (bf16[128,2048]{1,0:T(8,128)(2,1)}, bf16[128,2048]{1,0:T(8,128)(2,1)}, u32[]{:S(2)}, u32[]{:S(2)}) collective-permute-start(bf16[128,2048]{1,0:T(8,128)(2,1)} %get-tuple-element.138), channel_id=1, source_target_pairs={{0,1},{1,0},{2,3},{3,2},{4,5},{5,4},{6,7},{7,6},{8,9},{9,8},{10,11... | collective-permute-start | bytes 1572872 | tf_op jit(solution)/shard_map/ppermute | solution.py:77
  403.6 23.0 %collective-permute-start.31 = (bf16[128,2048]{1,0:T(8,128)(2,1)}, bf16[128,2048]{1,0:T(8,128)(2,1)}, u32[]{:S(2)}, u32[]{:S(2)}) collective-permute-start(bf16[128,2048]{1,0:T(8,128)(2,1)} %get-tuple-element.137), channel_id=1, source_target_pairs={{0,2},{1,3},{2,0},{3,1},{4,6},{5,7},{6,4},{7,5},{8,10},{9,11},{10,... | collective-permute-start | bytes 1572872 | tf_op jit(solution)/shard_map/ppermute | solution.py:77
  426.7 9.4 %copy-start.31 = (bf16[1024,1024]{1,0:T(8,128)(2,1)S(1)}, bf16[1024,1024]{1,0:T(8,128)(2,1)}, u32[]{:S(2)}) copy-start(bf16[1024,1024]{1,0:T(8,128)(2,1)} %get-tuple-element.103) | copy-start | bytes 6291460
  435.7 9.2 %collective-permute-start.32 = (bf16[128,2048]{1,0:T(8,128)(2,1)S(1)}, bf16[128,2048]{1,0:T(8,128)(2,1)S(1)}, u32[]{:S(2)}, u32[]{:S(2)}) collective-permute-start(bf16[128,2048]{1,0:T(8,128)(2,1)S(1)} %add_convert_fusion.3), channel_id=1, source_target_pairs={{0,2},{1,3},{2,0},{3,1},{4,6},{5,7},{6,4},{7,5},{8,10},{9,11},{10,... | collective-permute-start | bytes 1572872 | tf_op jit(solution)/shard_map/ppermute | solution.py:77
  448.1 9.5 %collective-permute-start.33 = (bf16[128,2048]{1,0:T(8,128)(2,1)}, bf16[128,2048]{1,0:T(8,128)(2,1)}, u32[]{:S(2)}, u32[]{:S(2)}) collective-permute-start(bf16[128,2048]{1,0:T(8,128)(2,1)} %get-tuple-element.136), channel_id=1, source_target_pairs={{0,1},{1,0},{2,3},{3,2},{4,5},{5,4},{6,7},{7,6},{8,9},{9,8},{10,11... | collective-permute-start | bytes 1572872 | tf_op jit(solution)/shard_map/ppermute | solution.py:77
  464.7 14.9 %collective-permute-start.35 = (bf16[128,2048]{1,0:T(8,128)(2,1)S(1)}, bf16[128,2048]{1,0:T(8,128)(2,1)S(1)}, u32[]{:S(2)}, u32[]{:S(2)}) collective-permute-start(bf16[128,2048]{1,0:T(8,128)(2,1)S(1)} %get-tuple-element.134), channel_id=1, source_target_pairs={{0,1},{1,0},{2,3},{3,2},{4,5},{5,4},{6,7},{7,6},{8,9},{9,8},{10,11... | collective-permute-start | bytes 1572872 | tf_op jit(solution)/shard_map/ppermute | solution.py:77
  465.8 20.3 %collective-permute-start.34 = (bf16[128,2048]{1,0:T(8,128)(2,1)}, bf16[128,2048]{1,0:T(8,128)(2,1)}, u32[]{:S(2)}, u32[]{:S(2)}) collective-permute-start(bf16[128,2048]{1,0:T(8,128)(2,1)} %get-tuple-element.131), channel_id=1, source_target_pairs={{0,1},{1,0},{2,3},{3,2},{4,5},{5,4},{6,7},{7,6},{8,9},{9,8},{10,11... | collective-permute-start | bytes 1572872 | tf_op jit(solution)/shard_map/ppermute | solution.py:77
  466.7 19.4 %collective-permute-start.38 = (bf16[128,2048]{1,0:T(8,128)(2,1)}, bf16[128,2048]{1,0:T(8,128)(2,1)}, u32[]{:S(2)}, u32[]{:S(2)}) collective-permute-start(bf16[128,2048]{1,0:T(8,128)(2,1)} %get-tuple-element.132), channel_id=1, source_target_pairs={{0,2},{1,3},{2,0},{3,1},{4,6},{5,7},{6,4},{7,5},{8,10},{9,11},{10,... | collective-permute-start | bytes 1572872 | tf_op jit(solution)/shard_map/ppermute | solution.py:77
  481.5 11.8 %collective-permute-start.36 = (bf16[128,2048]{1,0:T(8,128)(2,1)}, bf16[128,2048]{1,0:T(8,128)(2,1)}, u32[]{:S(2)}, u32[]{:S(2)}) collective-permute-start(bf16[128,2048]{1,0:T(8,128)(2,1)} %add_convert_fusion.1), channel_id=1, source_target_pairs={{0,2},{1,3},{2,0},{3,1},{4,6},{5,7},{6,4},{7,5},{8,10},{9,11},{10,... | collective-permute-start | bytes 1572872 | tf_op jit(solution)/shard_map/ppermute | solution.py:77
  482.8 14.2 %copy-start.6 = (bf16[1024,2048]{1,0:T(8,128)(2,1)S(1)}, bf16[1024,2048]{1,0:T(8,128)(2,1)}, u32[]{:S(2)}) copy-start(bf16[1024,2048]{1,0:T(8,128)(2,1)} %convolution_convert_fusion.5) | copy-start | bytes 12582916
  485.5 15.7 %collective-permute-start.37 = (bf16[128,2048]{1,0:T(8,128)(2,1)}, bf16[128,2048]{1,0:T(8,128)(2,1)S(1)}, u32[]{:S(2)}, u32[]{:S(2)}) collective-permute-start(bf16[128,2048]{1,0:T(8,128)(2,1)} %get-tuple-element.133), channel_id=1, source_target_pairs={{0,2},{1,3},{2,0},{3,1},{4,6},{5,7},{6,4},{7,5},{8,10},{9,11},{10,... | collective-permute-start | bytes 1572872 | tf_op jit(solution)/shard_map/ppermute | solution.py:77
  495.5 9.2 %collective-permute-start.39 = (bf16[128,2048]{1,0:T(8,128)(2,1)S(1)}, bf16[128,2048]{1,0:T(8,128)(2,1)S(1)}, u32[]{:S(2)}, u32[]{:S(2)}) collective-permute-start(bf16[128,2048]{1,0:T(8,128)(2,1)S(1)} %get-tuple-element.130), channel_id=1, source_target_pairs={{0,1},{1,0},{2,3},{3,2},{4,5},{5,4},{6,7},{7,6},{8,9},{9,8},{10,11... | collective-permute-start | bytes 1572872 | tf_op jit(solution)/shard_map/ppermute | solution.py:77
  505.2 20.7 %copy-start.3 = (f32[256,2048]{1,0:T(8,128)S(1)}, f32[256,2048]{1,0:T(8,128)}, u32[]{:S(2)}) copy-start(f32[256,2048]{1,0:T(8,128)} %copy-done.2) | copy-start | bytes 6291460
  505.2 20.7 %copy-start.10 = (f32[256,2048]{1,0:T(8,128)S(1)}, f32[256,2048]{1,0:T(8,128)}, u32[]{:S(2)}) copy-start(f32[256,2048]{1,0:T(8,128)} %pad_maximum_fusion.3) | copy-start | bytes 6291460
  505.2 3.8 collective-permute-start.40
  509.1 3.8 collective-permute-start.41
  512.9 1.2 collective-permute-start.42
  514.1 15.0 %collective-permute-start.45 = (f32[4352]{0:T(1024)S(1)}, f32[4352]{0:T(1024)S(1)}, u32[]{:S(2)}, u32[]{:S(2)}) collective-permute-start(f32[4352]{0:T(1024)S(1)} %add.213), channel_id=1, source_target_pairs={{0,24},{4,28},{8,0},{12,4},{16,8},{20,12},{24,16},{28,20},{1,25},{... | collective-permute-start | bytes 52232 | tf_op jit(solution)/shard_map/ppermute | solution.py:63
  520.3 9.1 %collective-permute-start.44 = (f32[4352]{0:T(1024)S(1)}, f32[4352]{0:T(1024)S(1)}, u32[]{:S(2)}, u32[]{:S(2)}) collective-permute-start(f32[4352]{0:T(1024)S(1)} %add.213), channel_id=1, source_target_pairs={{0,16},{4,20},{8,24},{12,28},{16,0},{20,4},{24,8},{28,12},{1,17},{... | collective-permute-start | bytes 52232 | tf_op jit(solution)/shard_map/ppermute | solution.py:63
  525.5 6.2 %collective-permute-start.43 = (f32[4352]{0:T(1024)S(1)}, f32[4352]{0:T(1024)S(1)}, u32[]{:S(2)}, u32[]{:S(2)}) collective-permute-start(f32[4352]{0:T(1024)S(1)} %add.213), channel_id=1, source_target_pairs={{0,8},{4,12},{8,16},{12,20},{16,24},{20,28},{24,0},{28,4},{1,9},{5... | collective-permute-start | bytes 52232 | tf_op jit(solution)/shard_map/ppermute | solution.py:63
  (20 other events, 88.4 us)
Sparse Core Ops, SparseCore 0:
  10.3 67.4 all-gather.3
  80.0 115.3 all-gather.5
  197.0 62.9 all-gather.7
  262.2 68.4 reduce-scatter.3
  332.9 127.5 reduce-scatter.5
  462.6 77.4 reduce-scatter.7

commit v4 on v3

--- a/solution.py
+++ b/solution.py
@@ -92,7 +92,7 @@
     def gather_first(self, block):
         if self.tensor_size != 4:
             return block, block
-        return self.across(block, 1), self.across(block, 2)
+        return lax.optimization_barrier((self.across(block, 1), self.across(block, 2)))
 
     def gather_second(self, block, first):
         if self.tensor_size != 4:
@@ -103,8 +103,9 @@
             return block
         half = block.shape[0] // 2
         by_x, by_y = first
-        corner_low = self.across(by_y[:half], 1)
-        corner_high = self.across(by_x[half:], 2)
+        corner_low, corner_high = lax.optimization_barrier(
+            (self.across(by_y[:half], 1), self.across(by_x[half:], 2))
+        )
         return jnp.concatenate([block, by_x, by_y, corner_low, corner_high], axis=0)
 
     def gather_tokens(self, block):
@@ -121,11 +122,13 @@
     def scatter_first(self, partial):
         if self.tensor_size != 4:
             return (partial,)
-        return (
-            self.across(self.half_block(partial, 3, 0), 1),
-            self.across(self.half_block(partial, 3, 1), 2),
-            self.across(self.half_block(partial, 1, 0), 1),
-            self.across(self.half_block(partial, 2, 1), 2),
+        return lax.optimization_barrier(
+            (
+                self.across(self.half_block(partial, 3, 0), 1),
+                self.across(self.half_block(partial, 3, 1), 2),
+                self.across(self.half_block(partial, 1, 0), 1),
+                self.across(self.half_block(partial, 2, 1), 2),
+            )
         )
 
     def scatter_second(self, partial, first):
@@ -146,8 +149,12 @@
             total = self.half_block(partial, block, high).astype(wide) + arrived.astype(wide)
             return total.astype(partial.dtype)
 
-        low_last = self.across(passed(2, 0, low_pass), 2)
-        high_last = self.across(passed(1, 1, high_pass), 1)
+        low_last, high_last = lax.optimization_barrier(
+            (
+                self.across(passed(2, 0, low_pass), 2),
+                self.across(passed(1, 1, high_pass), 1),
+            )
+        )
         low = self.half_block(partial, 0, 0).astype(wide) + low_own.astype(wide)
         high = self.half_block(partial, 0, 1).astype(wide) + high_own.astype(wide)
         return jnp.concatenate(

time: 557 us -> 548 us (0.984)
  starting transfers between devices: 56.8 us -> 50.4 us
    ppermute x42, waiting for transfers between devices: 190 us -> 169 us  [across(): lax.ppermute(value, 'tensor', [(place, place ^ bit) for place in range(se...]
    reduce_scatter x3, waiting for transfers between devices: 10.1 us -> 26.2 us  [scatter_weight(): return lax.psum_scatter(partial, 'dp', scatter_dimension=0, tiled=True)]
    add x4 -> x0, other arithmetic: 6.17 us -> none  [scatter_second(): high + high_last.astype(wide)]
  transfers between devices with their start and end apart: 52 -> 52, of which waited for: 32 -> 37; matrix products, arithmetic and copies ran while one was open for 38% -> 39% of each run, Pallas kernels for 6% -> 6%
where the time goes in v4:
time: 548 us; the launch traced here: 542 us
  waiting for transfers between devices  222 us (41%)
  matrix products  131 us (24%)
  starting transfers between devices  50.4 us (9%)
  other arithmetic  49.3 us (9%)
  local copies, waits for them, and re-layouts  41.1 us (8%)
  Pallas kernels  33.1 us (6%)
  between operations  15.3 us (3%)
    ppermute x42, waiting for transfers between devices, across(): lax.ppermute(value, 'tensor', [(place, place ^ bit) for place in range(se...  169 us
    dot_general x4, matrix products, matmul(): return jnp.dot(left, right, preferred_element_type=jnp.float32)  47.7 us
    ppermute x42, starting transfers between devices, across(): lax.ppermute(value, 'tensor', [(place, place ^ bit) for place in range(se...  42 us
    dot_general x4, matrix products, contract_last(): lax.dot_general(left, right, (((1,), (1,)), ((), ())), preferred_element_...  41.7 us
    dot_general x4, matrix products, contract_first(): lax.dot_general(left, right, (((0,), (0,)), ((), ())), preferred_element_...  41.2 us
    reduce_scatter x3, waiting for transfers between devices, scatter_weight(): return lax.psum_scatter(partial, 'dp', scatter_dimension=0, tiled=True)  26.2 us
    unnamed x77, local copies, waits for them, and re-layouts  23.4 us
    all_gather x3, waiting for transfers between devices, gather_weight(): return lax.all_gather(shard, 'dp', axis=0, tiled=True)  23 us
  transfers between devices with their start and end apart: 52, of which 37 were waited for; matrix products, arithmetic and copies ran while one was open for 39% of the time, Pallas kernels for 6%

profile of v4, /device:TPU:0, one launch (start us, length us, event | category | flops | bytes accessed | tf_op | source)
XLA Modules:
  0.0 541.7 jit_solution(11579179577051306555)
XLA Ops:
  7.2 2.2 pad_maximum_fusion.6
  9.5 2.7 pad_maximum_fusion.5
  14.3 2.9 collective-permute-start
  19.5 1.9 fusion.19
  21.4 20.1 %collective-permute-done = bf16[256,2048]{1,0:T(8,128)(2,1)} collective-permute-done((bf16[256,2048]{1,0:T(8,128)(2,1)}, bf16[256,2048]{1,0:T(8,128)(2,1)}, u32[]{:S(2)}, u32[]{:S(2)}) %collective-permute-start) | collective-permute-done | bytes 1048608 | tf_op jit(solution)/shard_map/ppermute | solution.py:77
  41.5 2.1 collective-permute-done.1
  45.9 2.1 collective-permute-start.3
  49.1 14.8 %collective-permute-done.4 = bf16[256,2048]{1,0:T(8,128)(2,1)S(1)} collective-permute-done((bf16[256,2048]{1,0:T(8,128)(2,1)S(1)}, bf16[256,2048]{1,0:T(8,128)(2,1)S(1)}, u32[]{:S(2)}, u32[]{:S(2)}) %collective-permute-start.4) | collective-permute-done | bytes 1048608 | tf_op jit(solution)/shard_map/ppermute | solution.py:77
  63.9 2.2 collective-permute-done.5
  66.1 2.3 constant_dynamic-update-slice_fusion.3
  68.4 2.3 constant_dynamic-update-slice_fusion.2
  70.8 3.5 collective-permute-done.2
  83.1 2.3 constant_dynamic-update-slice_fusion.7
  85.5 5.7 %collective-permute-done.6 = bf16[128,2048]{1,0:T(8,128)(2,1)S(1)} collective-permute-done((bf16[128,2048]{1,0:T(8,128)(2,1)S(1)}, bf16[128,2048]{1,0:T(8,128)(2,1)S(1)}, u32[]{:S(2)}, u32[]{:S(2)}) %collective-permute-start.6) | collective-permute-done | bytes 524320 | tf_op jit(solution)/shard_map/ppermute | solution.py:77
  93.3 10.0 %fusion.2.raw_query.raw_key.raw_value = f32[1024,1024]{1,0:T(8,128)} fusion(bf16[1024,2048]{1,0:T(8,128)(2,1)} %constant_dynamic-update-slice_fusion, bf16[2048,1536]{1,0:T(8,128)(2,1)} %all-gather.4.cloned.1.call-done), kind=kOutput, calls=%fused_computation.16 | convolution fusion | flops 4294967296 | bytes 12582912 | tf_op jit(solution)/shard_map/dot_general | solution.py:18
  103.3 14.4 %attention_forward.1 = (bf16[1024,512]{1,0:T(8,128)(2,1)}, bf16[1024,256]{1,0:T(8,128)(2,1)}, bf16[1024,256]{1,0:T(8,128)(2,1)}, bf16[1024,512]{1,0:T(8,128)(2,1)}, f32[2,2,1024]{2,1,0:T(2,128)}) custom-call(s32[1]{0:T(128)} %bitcast.place_ref, f32[1024,1024]{1,0:T(8,128)} %fusion.2.raw_query.raw_key.raw_value, ...), custom_call_target="tpu_custom_call" | custom-call | flops 4294967296 | bytes 8388608 | tf_op jit(solution)/shard_map/attention_forward/pallas_call | solution.py:290
  117.7 4.4 convolution_convert_fusion.4
  122.1 2.0 copy-done.13
  129.6 10.9 %collective-permute-done.8 = bf16[128,2048]{1,0:T(8,128)(2,1)S(1)} collective-permute-done((bf16[128,2048]{1,0:T(8,128)(2,1)}, bf16[128,2048]{1,0:T(8,128)(2,1)S(1)}, u32[]{:S(2)}, u32[]{:S(2)}) %collective-permute-start.8) | collective-permute-done | bytes 524320 | tf_op jit(solution)/shard_map/ppermute | solution.py:77
  141.9 6.5 %collective-permute-done.10 = bf16[128,2048]{1,0:T(8,128)(2,1)S(1)} collective-permute-done((bf16[128,2048]{1,0:T(8,128)(2,1)}, bf16[128,2048]{1,0:T(8,128)(2,1)S(1)}, u32[]{:S(2)}, u32[]{:S(2)}) %collective-permute-start.10) | collective-permute-done | bytes 524320 | tf_op jit(solution)/shard_map/ppermute | solution.py:77
  153.0 8.1 %collective-permute-done.12 = bf16[128,2048]{1,0:T(8,128)(2,1)S(1)} collective-permute-done((bf16[128,2048]{1,0:T(8,128)(2,1)S(1)}, bf16[128,2048]{1,0:T(8,128)(2,1)S(1)}, u32[]{:S(2)}, u32[]{:S(2)}) %collective-permute-start.12) | collective-permute-done | bytes 524320 | tf_op jit(solution)/shard_map/ppermute | solution.py:77
  167.8 21.0 %collective-permute-done.14 = bf16[256,2048]{1,0:T(8,128)(2,1)S(1)} collective-permute-done((bf16[256,2048]{1,0:T(8,128)(2,1)S(1)}, bf16[256,2048]{1,0:T(8,128)(2,1)S(1)}, u32[]{:S(2)}, u32[]{:S(2)}) %collective-permute-start.14) | collective-permute-done | bytes 1048608 | tf_op jit(solution)/shard_map/ppermute | solution.py:77
  193.2 4.8 collective-permute-done.16
  201.4 18.1 %fusion.30 = f32[1024,3072]{1,0:T(8,128)S(1)} fusion(bf16[1024,2048]{1,0:T(8,128)(2,1)} %constant_dynamic-update-slice_fusion.10, bf16[2048,3072]{1,0:T(8,128)(2,1)} %all-gather.6.cloned.1.call-done), kind=kOutput, calls=%fused_computation.105 | convolution fusion | flops 12884901888 | bytes 29360128 | tf_op jit(solution)/shard_map/dot_general | solution.py:18
  219.5 2.0 multiply_convert_fusion.2
  221.5 2.6 copy-done.7
  225.8 11.2 %convolution_convert_fusion.1 = bf16[2048,1536]{1,0:T(8,128)(2,1)} fusion(bf16[1024,2048]{1,0:T(8,128)(2,1)} %constant_dynamic-update-slice_fusion.5, bf16[1024,1536]{1,0:T(8,128)(2,1)S(1)} %multiply_convert_fusion.2), kind=kOutput, calls=%fused_computation.2 | convolution fusion | flops 6445596672 | bytes 13631488 | tf_op jit(solution)/shard_map/dot_general | solution.py:22
  237.0 23.0 %all-gather.8.cloned.1.call-done = bf16[2048,1536]{1,0:T(8,128)(2,1)} async-done(((bf16[256,1536]{1,0:T(8,128)(2,1)}), bf16[2048,1536]{1,0:T(8,128)(2,1)}) %all-gather.8.cloned.1.call-update) | async-done | bytes 6291472 | tf_op jit(solution)/shard_map/all_gather | solution.py:165
  260.1 14.7 %multiply_convert_fusion.1 = (bf16[1024,1536]{1,0:T(8,128)(2,1)S(1)}, bf16[1024,1536]{1,0:T(8,128)(2,1)S(1)}) fusion(f32[1024,3072]{1,0:T(8,128)} %copy-done.7, bf16[1024,2048]{1,0:T(8,128)(2,1)} %constant_dynamic-update-slice_fusion.5, bf16[2048,1536]{1,0:T(8,128)(2,1)} %all-gather.8.cloned.1.call-done), kind=kOutput, calls=%fused_computation.6 | convolution fusion | flops 6462898176 | bytes 29360128 | tf_op jit(solution)/shard_map/dot_general | solution.py:18
  278.4 19.5 %convolution_convert_fusion.2 = bf16[1024,2048]{1,0:T(8,128)(2,1)} fusion(bf16[2048,3072]{1,0:T(8,128)(2,1)} %all-gather.6.cloned.1.call-done, bf16[1024,1536]{1,0:T(8,128)(2,1)} %copy-done.15, bf16[1024,1536]{1,0:T(8,128)(2,1)} %copy-done.14), kind=kOutput, calls=%fused_computation.10 | convolution fusion | flops 12899581952 | bytes 23068672 | tf_op jit(solution)/shard_map/dot_general | solution.py:28
  297.9 2.9 fusion.25
  304.9 18.6 %convolution_convert_fusion = bf16[2048,3072]{1,0:T(8,128)(2,1)} fusion(bf16[1024,2048]{1,0:T(8,128)(2,1)} %constant_dynamic-update-slice_fusion.10, bf16[1024,3072]{1,0:T(8,128)(2,1)S(1)} %pad_maximum_fusion), kind=kOutput, calls=%fused_computation | convolution fusion | flops 12891193344 | bytes 23068672 | tf_op jit(solution)/shard_map/dot_general | solution.py:22
  323.5 2.9 collective-permute-done.20
  327.6 3.1 reduce-scatter.4.cloned.1.call-done
  330.8 1.9 add_convert_fusion.4
  335.7 9.3 %convolution_convert_fusion.3 = bf16[1024,2048]{1,0:T(8,128)(2,1)S(1)} fusion(bf16[1024,1536]{1,0:T(8,128)(2,1)S(1)} %copy-done.17, bf16[2048,1536]{1,0:T(8,128)(2,1)} %all-gather.8.cloned.1.call-done), kind=kOutput, calls=%fused_computation.11 | convolution fusion | flops 6444548096 | bytes 13631488 | tf_op jit(solution)/shard_map/dot_general | solution.py:28
  345.5 3.7 convert_add_fusion.6
  351.8 22.1 %collective-permute-done.24 = bf16[256,2048]{1,0:T(8,128)(2,1)S(1)} collective-permute-done((bf16[256,2048]{1,0:T(8,128)(2,1)S(1)}, bf16[256,2048]{1,0:T(8,128)(2,1)S(1)}, u32[]{:S(2)}, u32[]{:S(2)}) %collective-permute-start.24) | collective-permute-done | bytes 1048608 | tf_op jit(solution)/shard_map/ppermute | solution.py:77
  376.0 8.1 %collective-permute-done.26 = bf16[128,2048]{1,0:T(8,128)(2,1)S(1)} collective-permute-done((bf16[128,2048]{1,0:T(8,128)(2,1)S(1)}, bf16[128,2048]{1,0:T(8,128)(2,1)S(1)}, u32[]{:S(2)}, u32[]{:S(2)}) %collective-permute-start.26) | collective-permute-done | bytes 524320 | tf_op jit(solution)/shard_map/ppermute | solution.py:77
  385.1 3.8 convolution_convert_fusion.7
  392.4 1.9 collective-permute-start.31
  394.3 4.9 fusion.16.upstream
  399.2 16.4 %attention_backward.1 = (bf16[1024,1024]{1,0:T(8,128)(2,1)}, f32[1,128]{1,0:T(1,128)}, f32[1,128]{1,0:T(1,128)}) custom-call(s32[1]{0:T(128)} %bitcast.place_ref, f32[1024,1024]{1,0:T(8,128)} %fusion.2.raw_query.raw_key.raw_value, f32[1024,1024]{1,0:T(8,128)} %fusion.2.raw_query.raw_key.raw_value, f32[1024,128]{1,0:T(8,128)} %get-tuple-element.256.cosine, ...), custom_call_target="tpu_custom_call" | custom-call | flops 10737418240 | bytes 8388608 | tf_op jit(solution)/shard_map/attention_backward/pallas_call | solution.py:406
  415.6 7.6 %convolution_convert_fusion.6 = bf16[2048,1024]{1,0:T(8,128)(2,1)S(1)} fusion(bf16[1024,2048]{1,0:T(8,128)(2,1)} %constant_dynamic-update-slice_fusion, bf16[1024,1024]{1,0:T(8,128)(2,1)} %get-tuple-element.177), kind=kOutput, calls=%fused_computation.14 | convolution fusion | flops 4297064448 | bytes 10485760 | tf_op jit(solution)/shard_map/dot_general | solution.py:22
  423.2 2.9 add_convert_fusion.2
  427.4 8.6 %convolution_convert_fusion.5 = bf16[1024,2048]{1,0:T(8,128)(2,1)} fusion(bf16[1024,1024]{1,0:T(8,128)(2,1)S(1)} %copy-done.31, bf16[2048,1536]{1,0:T(8,128)(2,1)} %all-gather.4.cloned.1.call-done), kind=kOutput, calls=%fused_computation.13 | convolution fusion | flops 4297064448 | bytes 10485760 | tf_op jit(solution)/shard_map/dot_general | solution.py:28
  436.0 3.1 pad_maximum_fusion.1
  439.1 2.4 convert_add_fusion.4
  443.0 17.4 %reduce-scatter.6.cloned.1.call-done = bf16[256,3072]{1,0:T(8,128)(2,1)} async-done(((bf16[2048,3072]{1,0:T(8,128)(2,1)}), bf16[256,3072]{1,0:T(8,128)(2,1)}) %reduce-scatter.6.cloned.1.call-update) | async-done | bytes 1572880 | tf_op jit(solution)/shard_map/reduce_scatter | solution.py:168
  460.5 2.9 fusion.23
  467.4 2.6 convert_element_type.283
  470.1 8.5 %collective-permute-done.34 = bf16[128,2048]{1,0:T(8,128)(2,1)} collective-permute-done((bf16[128,2048]{1,0:T(8,128)(2,1)}, bf16[128,2048]{1,0:T(8,128)(2,1)}, u32[]{:S(2)}, u32[]{:S(2)}) %collective-permute-start.34) | collective-permute-done | bytes 524320 | tf_op jit(solution)/shard_map/ppermute | solution.py:77
  480.0 6.4 %collective-permute-done.36 = bf16[128,2048]{1,0:T(8,128)(2,1)} collective-permute-done((bf16[128,2048]{1,0:T(8,128)(2,1)}, bf16[128,2048]{1,0:T(8,128)(2,1)}, u32[]{:S(2)}, u32[]{:S(2)}) %collective-permute-start.36) | collective-permute-done | bytes 524320 | tf_op jit(solution)/shard_map/ppermute | solution.py:77
  487.6 1.9 add_convert_fusion
  491.7 4.0 multiply_reduce_fusion
  495.7 4.2 collective-permute-done.38
  503.7 2.1 fusion.27
  508.0 2.7 collective-permute-done.41
  511.9 5.0 collective-permute-start.45
  516.9 2.1 collective-permute-start.44
  520.1 3.1 fusion.11
  523.3 1.9 collective-permute-done.43
  526.5 5.7 %reduce-scatter.8.cloned.1.call-done.source = bf16[256,1536]{1,0:T(8,128)(2,1)} async-done(((bf16[2048,1536]{1,0:T(8,128)(2,1)}), bf16[256,1536]{1,0:T(8,128)(2,1)}) %reduce-scatter.8.cloned.1.call-update) | async-done | bytes 786448 | tf_op jit(solution)/shard_map/reduce_scatter | solution.py:168
  532.2 2.3 split_columns.1
  (203 shorter events, 88.6 us)
Async XLA Ops:
  7.2 86.1 %all-gather.4.cloned.1.call-start = ((), (), s32[]{:S(2)}) async-start(), calls=%async_computation.3 | async-start | bytes 7077888 | tf_op jit(solution)/shard_map/all_gather | solution.py:165
  9.4 9.9 %copy-start.27 = (s32[1024]{0:T(1024)S(1)}, s32[1024]{0:T(1024)}, u32[]{:S(2)}) copy-start(s32[1024]{0:T(1024)} %param.15) | copy-start | bytes 12292
  9.5 192.0 %all-gather.6.cloned.1.call-start = ((), (), s32[]{:S(2)}) async-start(), calls=%async_computation.4 | async-start | bytes 14155776 | tf_op jit(solution)/shard_map/all_gather | solution.py:165
  12.3 247.8 %all-gather.8.cloned.1.call-start = ((), (), s32[]{:S(2)}) async-start(), calls=%async_computation.5 | async-start | bytes 7077888 | tf_op jit(solution)/shard_map/all_gather | solution.py:165
  14.3 27.2 %collective-permute-start = (bf16[256,2048]{1,0:T(8,128)(2,1)}, bf16[256,2048]{1,0:T(8,128)(2,1)}, u32[]{:S(2)}, u32[]{:S(2)}) collective-permute-start(bf16[256,2048]{1,0:T(8,128)(2,1)} %get-tuple-element.206), channel_id=1, source_target_pairs={{0,1},{1,0},{2,3},{3,2},{4,5},{5,4},{6,7},{7,6},{8,9},{9,8},{10,11... | collective-permute-start | bytes 3145736 | tf_op jit(solution)/shard_map/ppermute | solution.py:77
  17.2 26.4 %collective-permute-start.1 = (bf16[256,2048]{1,0:T(8,128)(2,1)}, bf16[256,2048]{1,0:T(8,128)(2,1)}, u32[]{:S(2)}, u32[]{:S(2)}) collective-permute-start(bf16[256,2048]{1,0:T(8,128)(2,1)} %get-tuple-element.206), channel_id=1, source_target_pairs={{0,2},{1,3},{2,0},{3,1},{4,6},{5,7},{6,4},{7,5},{8,10},{9,11},{10,... | collective-permute-start | bytes 3145736 | tf_op jit(solution)/shard_map/ppermute | solution.py:77
  18.8 45.1 %collective-permute-start.4 = (bf16[256,2048]{1,0:T(8,128)(2,1)S(1)}, bf16[256,2048]{1,0:T(8,128)(2,1)S(1)}, u32[]{:S(2)}, u32[]{:S(2)}) collective-permute-start(bf16[256,2048]{1,0:T(8,128)(2,1)S(1)} %copy-done.8), channel_id=1, source_target_pairs={{0,1},{1,0},{2,3},{3,2},{4,5},{5,4},{6,7},{7,6},{8,9},{9,8},{10,11... | collective-permute-start | bytes 3145736 | tf_op jit(solution)/shard_map/ppermute | solution.py:77
  19.3 46.8 %collective-permute-start.5 = (bf16[256,2048]{1,0:T(8,128)(2,1)S(1)}, bf16[256,2048]{1,0:T(8,128)(2,1)}, u32[]{:S(2)}, u32[]{:S(2)}) collective-permute-start(bf16[256,2048]{1,0:T(8,128)(2,1)S(1)} %copy-done.8), channel_id=1, source_target_pairs={{0,2},{1,3},{2,0},{3,1},{4,6},{5,7},{6,4},{7,5},{8,10},{9,11},{10,... | collective-permute-start | bytes 3145736 | tf_op jit(solution)/shard_map/ppermute | solution.py:77
  44.7 29.6 %collective-permute-start.2 = (bf16[128,2048]{1,0:T(8,128)(2,1)S(1)}, bf16[128,2048]{1,0:T(8,128)(2,1)S(1)}, u32[]{:S(2)}, u32[]{:S(2)}) collective-permute-start(bf16[128,2048]{1,0:T(8,128)(2,1)S(1)} %slice.162), channel_id=1, source_target_pairs={{0,1},{1,0},{2,3},{3,2},{4,5},{5,4},{6,7},{7,6},{8,9},{9,8},{10,11... | collective-permute-start | bytes 1572872 | tf_op jit(solution)/shard_map/ppermute | solution.py:77
  45.9 29.9 %collective-permute-start.3 = (bf16[128,2048]{1,0:T(8,128)(2,1)S(1)}, bf16[128,2048]{1,0:T(8,128)(2,1)S(1)}, u32[]{:S(2)}, u32[]{:S(2)}) collective-permute-start(bf16[128,2048]{1,0:T(8,128)(2,1)S(1)} %slice.163), channel_id=1, source_target_pairs={{0,2},{1,3},{2,0},{3,1},{4,6},{5,7},{6,4},{7,5},{8,10},{9,11},{10,... | collective-permute-start | bytes 1572872 | tf_op jit(solution)/shard_map/ppermute | solution.py:77
  78.5 12.6 %collective-permute-start.6 = (bf16[128,2048]{1,0:T(8,128)(2,1)S(1)}, bf16[128,2048]{1,0:T(8,128)(2,1)S(1)}, u32[]{:S(2)}, u32[]{:S(2)}) collective-permute-start(bf16[128,2048]{1,0:T(8,128)(2,1)S(1)} %slice.165), channel_id=1, source_target_pairs={{0,1},{1,0},{2,3},{3,2},{4,5},{5,4},{6,7},{7,6},{8,9},{9,8},{10,11... | collective-permute-start | bytes 1572872 | tf_op jit(solution)/shard_map/ppermute | solution.py:77
  79.0 12.7 %collective-permute-start.7 = (bf16[128,2048]{1,0:T(8,128)(2,1)S(1)}, bf16[128,2048]{1,0:T(8,128)(2,1)S(1)}, u32[]{:S(2)}, u32[]{:S(2)}) collective-permute-start(bf16[128,2048]{1,0:T(8,128)(2,1)S(1)} %slice.166), channel_id=1, source_target_pairs={{0,2},{1,3},{2,0},{3,1},{4,6},{5,7},{6,4},{7,5},{8,10},{9,11},{10,... | collective-permute-start | bytes 1572872 | tf_op jit(solution)/shard_map/ppermute | solution.py:77
  125.4 15.1 %collective-permute-start.8 = (bf16[128,2048]{1,0:T(8,128)(2,1)}, bf16[128,2048]{1,0:T(8,128)(2,1)S(1)}, u32[]{:S(2)}, u32[]{:S(2)}) collective-permute-start(bf16[128,2048]{1,0:T(8,128)(2,1)} %get-tuple-element.240), channel_id=1, source_target_pairs={{0,1},{1,0},{2,3},{3,2},{4,5},{5,4},{6,7},{7,6},{8,9},{9,8},{10,11... | collective-permute-start | bytes 1572872 | tf_op jit(solution)/shard_map/ppermute | solution.py:77
  126.8 15.1 %collective-permute-start.9 = (bf16[128,2048]{1,0:T(8,128)(2,1)}, bf16[128,2048]{1,0:T(8,128)(2,1)S(1)}, u32[]{:S(2)}, u32[]{:S(2)}) collective-permute-start(bf16[128,2048]{1,0:T(8,128)(2,1)} %get-tuple-element.239), channel_id=1, source_target_pairs={{0,2},{1,3},{2,0},{3,1},{4,6},{5,7},{6,4},{7,5},{8,10},{9,11},{10,... | collective-permute-start | bytes 1572872 | tf_op jit(solution)/shard_map/ppermute | solution.py:77
  128.4 20.1 %collective-permute-start.10 = (bf16[128,2048]{1,0:T(8,128)(2,1)}, bf16[128,2048]{1,0:T(8,128)(2,1)S(1)}, u32[]{:S(2)}, u32[]{:S(2)}) collective-permute-start(bf16[128,2048]{1,0:T(8,128)(2,1)} %get-tuple-element.238), channel_id=1, source_target_pairs={{0,1},{1,0},{2,3},{3,2},{4,5},{5,4},{6,7},{7,6},{8,9},{9,8},{10,11... | collective-permute-start | bytes 1572872 | tf_op jit(solution)/shard_map/ppermute | solution.py:77
  128.9 20.3 %collective-permute-start.11 = (bf16[128,2048]{1,0:T(8,128)(2,1)}, bf16[128,2048]{1,0:T(8,128)(2,1)S(1)}, u32[]{:S(2)}, u32[]{:S(2)}) collective-permute-start(bf16[128,2048]{1,0:T(8,128)(2,1)} %get-tuple-element.237), channel_id=1, source_target_pairs={{0,2},{1,3},{2,0},{3,1},{4,6},{5,7},{6,4},{7,5},{8,10},{9,11},{10,... | collective-permute-start | bytes 1572872 | tf_op jit(solution)/shard_map/ppermute | solution.py:77
  129.5 201.2 %reduce-scatter.4.cloned.1.call-start = ((), (), s32[]{:S(2)}) async-start(), calls=%async_computation.6 | async-start | bytes 7077888 | tf_op jit(solution)/shard_map/reduce_scatter | solution.py:168
  150.8 10.2 %collective-permute-start.12 = (bf16[128,2048]{1,0:T(8,128)(2,1)S(1)}, bf16[128,2048]{1,0:T(8,128)(2,1)S(1)}, u32[]{:S(2)}, u32[]{:S(2)}) collective-permute-start(bf16[128,2048]{1,0:T(8,128)(2,1)S(1)} %get-tuple-element.236), channel_id=1, source_target_pairs={{0,2},{1,3},{2,0},{3,1},{4,6},{5,7},{6,4},{7,5},{8,10},{9,11},{10,... | collective-permute-start | bytes 1572872 | tf_op jit(solution)/shard_map/ppermute | solution.py:77
  152.4 12.0 %copy-start.19 = (f32[2048]{0:T(1024)S(1)}, f32[2048]{0:T(1024)}, u32[]{:S(2)}) copy-start(f32[2048]{0:T(1024)} %param.17) | copy-start | bytes 24580
  152.4 9.9 %collective-permute-start.13 = (bf16[128,2048]{1,0:T(8,128)(2,1)S(1)}, bf16[128,2048]{1,0:T(8,128)(2,1)S(1)}, u32[]{:S(2)}, u32[]{:S(2)}) collective-permute-start(bf16[128,2048]{1,0:T(8,128)(2,1)S(1)} %get-tuple-element.235), channel_id=1, source_target_pairs={{0,1},{1,0},{2,3},{3,2},{4,5},{5,4},{6,7},{7,6},{8,9},{9,8},{10,11... | collective-permute-start | bytes 1572872 | tf_op jit(solution)/shard_map/ppermute | solution.py:77
  164.4 27.8 %copy-start = (f32[256,2048]{1,0:T(8,128)}, f32[256,2048]{1,0:T(8,128)S(1)}, u32[]{:S(2)}) copy-start(f32[256,2048]{1,0:T(8,128)S(1)} %get-tuple-element.204) | copy-start | bytes 6291460
  164.4 27.7 %copy-start.23 = (f32[256]{0:T(256)}, f32[256]{0:T(256)S(1)}, u32[]{:S(2)}) copy-start(f32[256]{0:T(256)S(1)} %add_rsqrt_fusion) | copy-start | bytes 3076
  165.9 22.8 %collective-permute-start.14 = (bf16[256,2048]{1,0:T(8,128)(2,1)S(1)}, bf16[256,2048]{1,0:T(8,128)(2,1)S(1)}, u32[]{:S(2)}, u32[]{:S(2)}) collective-permute-start(bf16[256,2048]{1,0:T(8,128)(2,1)S(1)} %get-tuple-element.202), channel_id=1, source_target_pairs={{0,1},{1,0},{2,3},{3,2},{4,5},{5,4},{6,7},{7,6},{8,9},{9,8},{10,11... | collective-permute-start | bytes 3145736 | tf_op jit(solution)/shard_map/ppermute | solution.py:77
  166.6 22.2 %collective-permute-start.15 = (bf16[256,2048]{1,0:T(8,128)(2,1)S(1)}, bf16[256,2048]{1,0:T(8,128)(2,1)S(1)}, u32[]{:S(2)}, u32[]{:S(2)}) collective-permute-start(bf16[256,2048]{1,0:T(8,128)(2,1)S(1)} %get-tuple-element.202), channel_id=1, source_target_pairs={{0,2},{1,3},{2,0},{3,1},{4,6},{5,7},{6,4},{7,5},{8,10},{9,11},{10,... | collective-permute-start | bytes 3145736 | tf_op jit(solution)/shard_map/ppermute | solution.py:77
  188.8 9.2 %collective-permute-start.16 = (bf16[128,2048]{1,0:T(8,128)(2,1)S(1)}, bf16[128,2048]{1,0:T(8,128)(2,1)S(1)}, u32[]{:S(2)}, u32[]{:S(2)}) collective-permute-start(bf16[128,2048]{1,0:T(8,128)(2,1)S(1)} %slice.176), channel_id=1, source_target_pairs={{0,1},{1,0},{2,3},{3,2},{4,5},{5,4},{6,7},{7,6},{8,9},{9,8},{10,11... | collective-permute-start | bytes 1572872 | tf_op jit(solution)/shard_map/ppermute | solution.py:77
  190.5 9.2 %collective-permute-start.17 = (bf16[128,2048]{1,0:T(8,128)(2,1)S(1)}, bf16[128,2048]{1,0:T(8,128)(2,1)S(1)}, u32[]{:S(2)}, u32[]{:S(2)}) collective-permute-start(bf16[128,2048]{1,0:T(8,128)(2,1)S(1)} %slice.177), channel_id=1, source_target_pairs={{0,2},{1,3},{2,0},{3,1},{4,6},{5,7},{6,4},{7,5},{8,10},{9,11},{10,... | collective-permute-start | bytes 1572872 | tf_op jit(solution)/shard_map/ppermute | solution.py:77
  237.0 223.5 %reduce-scatter.6.cloned.1.call-start = ((), (), s32[]{:S(2)}) async-start(), calls=%async_computation.7 | async-start | bytes 14155776 | tf_op jit(solution)/shard_map/reduce_scatter | solution.py:168
  300.8 22.7 %collective-permute-start.18 = (bf16[128,2048]{1,0:T(8,128)(2,1)}, bf16[128,2048]{1,0:T(8,128)(2,1)}, u32[]{:S(2)}, u32[]{:S(2)}) collective-permute-start(bf16[128,2048]{1,0:T(8,128)(2,1)} %get-tuple-element.232), channel_id=1, source_target_pairs={{0,1},{1,0},{2,3},{3,2},{4,5},{5,4},{6,7},{7,6},{8,9},{9,8},{10,11... | collective-permute-start | bytes 1572872 | tf_op jit(solution)/shard_map/ppermute | solution.py:77
  302.3 21.2 %collective-permute-start.19 = (bf16[128,2048]{1,0:T(8,128)(2,1)}, bf16[128,2048]{1,0:T(8,128)(2,1)}, u32[]{:S(2)}, u32[]{:S(2)}) collective-permute-start(bf16[128,2048]{1,0:T(8,128)(2,1)} %get-tuple-element.231), channel_id=1, source_target_pairs={{0,2},{1,3},{2,0},{3,1},{4,6},{5,7},{6,4},{7,5},{8,10},{9,11},{10,... | collective-permute-start | bytes 1572872 | tf_op jit(solution)/shard_map/ppermute | solution.py:77
  303.7 22.7 %collective-permute-start.20 = (bf16[128,2048]{1,0:T(8,128)(2,1)}, bf16[128,2048]{1,0:T(8,128)(2,1)}, u32[]{:S(2)}, u32[]{:S(2)}) collective-permute-start(bf16[128,2048]{1,0:T(8,128)(2,1)} %get-tuple-element.230), channel_id=1, source_target_pairs={{0,1},{1,0},{2,3},{3,2},{4,5},{5,4},{6,7},{7,6},{8,9},{9,8},{10,11... | collective-permute-start | bytes 1572872 | tf_op jit(solution)/shard_map/ppermute | solution.py:77
  304.3 23.3 %collective-permute-start.21 = (bf16[128,2048]{1,0:T(8,128)(2,1)}, bf16[128,2048]{1,0:T(8,128)(2,1)}, u32[]{:S(2)}, u32[]{:S(2)}) collective-permute-start(bf16[128,2048]{1,0:T(8,128)(2,1)} %get-tuple-element.229), channel_id=1, source_target_pairs={{0,2},{1,3},{2,0},{3,1},{4,6},{5,7},{6,4},{7,5},{8,10},{9,11},{10,... | collective-permute-start | bytes 1572872 | tf_op jit(solution)/shard_map/ppermute | solution.py:77
  323.5 12.2 %copy-start.17 = (bf16[1024,1536]{1,0:T(8,128)(2,1)S(1)}, bf16[1024,1536]{1,0:T(8,128)(2,1)}, u32[]{:S(2)}) copy-start(bf16[1024,1536]{1,0:T(8,128)(2,1)} %copy-done.16) | copy-start | bytes 9437188
  330.7 201.4 %reduce-scatter.8.cloned.1.call-start = ((), (), s32[]{:S(2)}) async-start(), calls=%async_computation.8 | async-start | bytes 7077888 | tf_op jit(solution)/shard_map/reduce_scatter | solution.py:168
  332.7 12.3 %collective-permute-start.22 = (bf16[128,2048]{1,0:T(8,128)(2,1)S(1)}, bf16[128,2048]{1,0:T(8,128)(2,1)S(1)}, u32[]{:S(2)}, u32[]{:S(2)}) collective-permute-start(bf16[128,2048]{1,0:T(8,128)(2,1)S(1)} %get-tuple-element.228), channel_id=1, source_target_pairs={{0,2},{1,3},{2,0},{3,1},{4,6},{5,7},{6,4},{7,5},{8,10},{9,11},{10,... | collective-permute-start | bytes 1572872 | tf_op jit(solution)/shard_map/ppermute | solution.py:77
  334.2 11.2 %collective-permute-start.23 = (bf16[128,2048]{1,0:T(8,128)(2,1)S(1)}, bf16[128,2048]{1,0:T(8,128)(2,1)S(1)}, u32[]{:S(2)}, u32[]{:S(2)}) collective-permute-start(bf16[128,2048]{1,0:T(8,128)(2,1)S(1)} %get-tuple-element.227), channel_id=1, source_target_pairs={{0,1},{1,0},{2,3},{3,2},{4,5},{5,4},{6,7},{7,6},{8,9},{9,8},{10,11... | collective-permute-start | bytes 1572872 | tf_op jit(solution)/shard_map/ppermute | solution.py:77
  345.0 43.9 %copy-start.12 = (bf16[1024,2048]{1,0:T(8,128)(2,1)}, bf16[1024,2048]{1,0:T(8,128)(2,1)S(1)}, u32[]{:S(2)}) copy-start(bf16[1024,2048]{1,0:T(8,128)(2,1)S(1)} %convolution_convert_fusion.3) | copy-start | bytes 12582916
  351.1 34.0 %copy-start.30 = (bf16[1024,512]{1,0:T(8,128)(2,1)S(1)}, bf16[1024,512]{1,0:T(8,128)(2,1)}, u32[]{:S(2)}) copy-start(bf16[1024,512]{1,0:T(8,128)(2,1)} %get-tuple-element.117) | copy-start | bytes 3145732
  351.1 22.8 %collective-permute-start.24 = (bf16[256,2048]{1,0:T(8,128)(2,1)S(1)}, bf16[256,2048]{1,0:T(8,128)(2,1)S(1)}, u32[]{:S(2)}, u32[]{:S(2)}) collective-permute-start(bf16[256,2048]{1,0:T(8,128)(2,1)S(1)} %get-tuple-element.200), channel_id=1, source_target_pairs={{0,1},{1,0},{2,3},{3,2},{4,5},{5,4},{6,7},{7,6},{8,9},{9,8},{10,11... | collective-permute-start | bytes 3145736 | tf_op jit(solution)/shard_map/ppermute | solution.py:77
  351.4 22.6 %collective-permute-start.25 = (bf16[256,2048]{1,0:T(8,128)(2,1)S(1)}, bf16[256,2048]{1,0:T(8,128)(2,1)S(1)}, u32[]{:S(2)}, u32[]{:S(2)}) collective-permute-start(bf16[256,2048]{1,0:T(8,128)(2,1)S(1)} %get-tuple-element.200), channel_id=1, source_target_pairs={{0,2},{1,3},{2,0},{3,1},{4,6},{5,7},{6,4},{7,5},{8,10},{9,11},{10,... | collective-permute-start | bytes 3145736 | tf_op jit(solution)/shard_map/ppermute | solution.py:77
  374.0 10.2 %collective-permute-start.26 = (bf16[128,2048]{1,0:T(8,128)(2,1)S(1)}, bf16[128,2048]{1,0:T(8,128)(2,1)S(1)}, u32[]{:S(2)}, u32[]{:S(2)}) collective-permute-start(bf16[128,2048]{1,0:T(8,128)(2,1)S(1)} %slice.188), channel_id=1, source_target_pairs={{0,1},{1,0},{2,3},{3,2},{4,5},{5,4},{6,7},{7,6},{8,9},{9,8},{10,11... | collective-permute-start | bytes 1572872 | tf_op jit(solution)/shard_map/ppermute | solution.py:77
  375.7 9.2 %collective-permute-start.27 = (bf16[128,2048]{1,0:T(8,128)(2,1)S(1)}, bf16[128,2048]{1,0:T(8,128)(2,1)S(1)}, u32[]{:S(2)}, u32[]{:S(2)}) collective-permute-start(bf16[128,2048]{1,0:T(8,128)(2,1)S(1)} %slice.189), channel_id=1, source_target_pairs={{0,2},{1,3},{2,0},{3,1},{4,6},{5,7},{6,4},{7,5},{8,10},{9,11},{10,... | collective-permute-start | bytes 1572872 | tf_op jit(solution)/shard_map/ppermute | solution.py:77
  390.2 25.3 %collective-permute-start.28 = (bf16[128,2048]{1,0:T(8,128)(2,1)}, bf16[128,2048]{1,0:T(8,128)(2,1)}, u32[]{:S(2)}, u32[]{:S(2)}) collective-permute-start(bf16[128,2048]{1,0:T(8,128)(2,1)} %get-tuple-element.224), channel_id=1, source_target_pairs={{0,1},{1,0},{2,3},{3,2},{4,5},{5,4},{6,7},{7,6},{8,9},{9,8},{10,11... | collective-permute-start | bytes 1572872 | tf_op jit(solution)/shard_map/ppermute | solution.py:77
  391.2 24.4 %collective-permute-start.29 = (bf16[128,2048]{1,0:T(8,128)(2,1)}, bf16[128,2048]{1,0:T(8,128)(2,1)}, u32[]{:S(2)}, u32[]{:S(2)}) collective-permute-start(bf16[128,2048]{1,0:T(8,128)(2,1)} %get-tuple-element.223), channel_id=1, source_target_pairs={{0,2},{1,3},{2,0},{3,1},{4,6},{5,7},{6,4},{7,5},{8,10},{9,11},{10,... | collective-permute-start | bytes 1572872 | tf_op jit(solution)/shard_map/ppermute | solution.py:77
  391.5 24.1 %collective-permute-start.30 = (bf16[128,2048]{1,0:T(8,128)(2,1)}, bf16[128,2048]{1,0:T(8,128)(2,1)}, u32[]{:S(2)}, u32[]{:S(2)}) collective-permute-start(bf16[128,2048]{1,0:T(8,128)(2,1)} %get-tuple-element.222), channel_id=1, source_target_pairs={{0,1},{1,0},{2,3},{3,2},{4,5},{5,4},{6,7},{7,6},{8,9},{9,8},{10,11... | collective-permute-start | bytes 1572872 | tf_op jit(solution)/shard_map/ppermute | solution.py:77
  392.4 23.2 %collective-permute-start.31 = (bf16[128,2048]{1,0:T(8,128)(2,1)}, bf16[128,2048]{1,0:T(8,128)(2,1)}, u32[]{:S(2)}, u32[]{:S(2)}) collective-permute-start(bf16[128,2048]{1,0:T(8,128)(2,1)} %get-tuple-element.221), channel_id=1, source_target_pairs={{0,2},{1,3},{2,0},{3,1},{4,6},{5,7},{6,4},{7,5},{8,10},{9,11},{10,... | collective-permute-start | bytes 1572872 | tf_op jit(solution)/shard_map/ppermute | solution.py:77
  415.6 11.8 %copy-start.31 = (bf16[1024,1024]{1,0:T(8,128)(2,1)S(1)}, bf16[1024,1024]{1,0:T(8,128)(2,1)}, u32[]{:S(2)}) copy-start(bf16[1024,1024]{1,0:T(8,128)(2,1)} %get-tuple-element.177) | copy-start | bytes 6291460
  426.1 13.0 %collective-permute-start.32 = (bf16[128,2048]{1,0:T(8,128)(2,1)}, bf16[128,2048]{1,0:T(8,128)(2,1)}, u32[]{:S(2)}, u32[]{:S(2)}) collective-permute-start(bf16[128,2048]{1,0:T(8,128)(2,1)} %get-tuple-element.220), channel_id=1, source_target_pairs={{0,2},{1,3},{2,0},{3,1},{4,6},{5,7},{6,4},{7,5},{8,10},{9,11},{10,... | collective-permute-start | bytes 1572872 | tf_op jit(solution)/shard_map/ppermute | solution.py:77
  426.2 9.8 %copy-start.18 = (bf16[2048,512]{1,0:T(8,128)(2,1)S(1)}, bf16[2048,512]{1,0:T(8,128)(2,1)}, u32[]{:S(2)}) copy-start(bf16[2048,512]{1,0:T(8,128)(2,1)} %convolution_convert_fusion.7) | copy-start | bytes 6291460
  426.2 12.9 %collective-permute-start.33 = (bf16[128,2048]{1,0:T(8,128)(2,1)}, bf16[128,2048]{1,0:T(8,128)(2,1)}, u32[]{:S(2)}, u32[]{:S(2)}) collective-permute-start(bf16[128,2048]{1,0:T(8,128)(2,1)} %get-tuple-element.219), channel_id=1, source_target_pairs={{0,1},{1,0},{2,3},{3,2},{4,5},{5,4},{6,7},{7,6},{8,9},{9,8},{10,11... | collective-permute-start | bytes 1572872 | tf_op jit(solution)/shard_map/ppermute | solution.py:77
  463.4 15.2 %collective-permute-start.34 = (bf16[128,2048]{1,0:T(8,128)(2,1)}, bf16[128,2048]{1,0:T(8,128)(2,1)}, u32[]{:S(2)}, u32[]{:S(2)}) collective-permute-start(bf16[128,2048]{1,0:T(8,128)(2,1)} %get-tuple-element.216), channel_id=1, source_target_pairs={{0,1},{1,0},{2,3},{3,2},{4,5},{5,4},{6,7},{7,6},{8,9},{9,8},{10,11... | collective-permute-start | bytes 1572872 | tf_op jit(solution)/shard_map/ppermute | solution.py:77
  464.8 15.2 %collective-permute-start.35 = (bf16[128,2048]{1,0:T(8,128)(2,1)}, bf16[128,2048]{1,0:T(8,128)(2,1)}, u32[]{:S(2)}, u32[]{:S(2)}) collective-permute-start(bf16[128,2048]{1,0:T(8,128)(2,1)} %get-tuple-element.215), channel_id=1, source_target_pairs={{0,2},{1,3},{2,0},{3,1},{4,6},{5,7},{6,4},{7,5},{8,10},{9,11},{10,... | collective-permute-start | bytes 1572872 | tf_op jit(solution)/shard_map/ppermute | solution.py:77
  466.3 20.1 %collective-permute-start.36 = (bf16[128,2048]{1,0:T(8,128)(2,1)}, bf16[128,2048]{1,0:T(8,128)(2,1)}, u32[]{:S(2)}, u32[]{:S(2)}) collective-permute-start(bf16[128,2048]{1,0:T(8,128)(2,1)} %get-tuple-element.214), channel_id=1, source_target_pairs={{0,1},{1,0},{2,3},{3,2},{4,5},{5,4},{6,7},{7,6},{8,9},{9,8},{10,11... | collective-permute-start | bytes 1572872 | tf_op jit(solution)/shard_map/ppermute | solution.py:77
  466.9 20.8 %collective-permute-start.37 = (bf16[128,2048]{1,0:T(8,128)(2,1)}, bf16[128,2048]{1,0:T(8,128)(2,1)}, u32[]{:S(2)}, u32[]{:S(2)}) collective-permute-start(bf16[128,2048]{1,0:T(8,128)(2,1)} %get-tuple-element.213), channel_id=1, source_target_pairs={{0,2},{1,3},{2,0},{3,1},{4,6},{5,7},{6,4},{7,5},{8,10},{9,11},{10,... | collective-permute-start | bytes 1572872 | tf_op jit(solution)/shard_map/ppermute | solution.py:77
  467.4 24.2 %copy-start.6 = (bf16[1024,2048]{1,0:T(8,128)(2,1)S(1)}, bf16[1024,2048]{1,0:T(8,128)(2,1)}, u32[]{:S(2)}) copy-start(bf16[1024,2048]{1,0:T(8,128)(2,1)} %convolution_convert_fusion.5) | copy-start | bytes 12582916
  489.6 10.4 %collective-permute-start.38 = (bf16[128,2048]{1,0:T(8,128)(2,1)S(1)}, bf16[128,2048]{1,0:T(8,128)(2,1)S(1)}, u32[]{:S(2)}, u32[]{:S(2)}) collective-permute-start(bf16[128,2048]{1,0:T(8,128)(2,1)S(1)} %get-tuple-element.212), channel_id=1, source_target_pairs={{0,2},{1,3},{2,0},{3,1},{4,6},{5,7},{6,4},{7,5},{8,10},{9,11},{10,... | collective-permute-start | bytes 1572872 | tf_op jit(solution)/shard_map/ppermute | solution.py:77
  491.1 10.0 %collective-permute-start.39 = (bf16[128,2048]{1,0:T(8,128)(2,1)S(1)}, bf16[128,2048]{1,0:T(8,128)(2,1)S(1)}, u32[]{:S(2)}, u32[]{:S(2)}) collective-permute-start(bf16[128,2048]{1,0:T(8,128)(2,1)S(1)} %get-tuple-element.211), channel_id=1, source_target_pairs={{0,1},{1,0},{2,3},{3,2},{4,5},{5,4},{6,7},{7,6},{8,9},{9,8},{10,11... | collective-permute-start | bytes 1572872 | tf_op jit(solution)/shard_map/ppermute | solution.py:77
  503.1 17.1 %copy-start.3 = (f32[256,2048]{1,0:T(8,128)S(1)}, f32[256,2048]{1,0:T(8,128)}, u32[]{:S(2)}) copy-start(f32[256,2048]{1,0:T(8,128)} %copy-done.2) | copy-start | bytes 6291460
  503.1 17.1 %copy-start.10 = (f32[256,2048]{1,0:T(8,128)S(1)}, f32[256,2048]{1,0:T(8,128)}, u32[]{:S(2)}) copy-start(f32[256,2048]{1,0:T(8,128)} %pad_maximum_fusion.3) | copy-start | bytes 6291460
  503.1 3.8 collective-permute-start.40
  506.9 3.8 collective-permute-start.41
  510.7 1.2 collective-permute-start.42
  511.9 11.3 %collective-permute-start.45 = (f32[4352]{0:T(1024)S(1)}, f32[4352]{0:T(1024)S(1)}, u32[]{:S(2)}, u32[]{:S(2)}) collective-permute-start(f32[4352]{0:T(1024)S(1)} %add.213), channel_id=1, source_target_pairs={{0,24},{4,28},{8,0},{12,4},{16,8},{20,12},{24,16},{28,20},{1,25},{... | collective-permute-start | bytes 52232 | tf_op jit(solution)/shard_map/ppermute | solution.py:63
  516.9 6.4 %collective-permute-start.44 = (f32[4352]{0:T(1024)S(1)}, f32[4352]{0:T(1024)S(1)}, u32[]{:S(2)}, u32[]{:S(2)}) collective-permute-start(f32[4352]{0:T(1024)S(1)} %add.213), channel_id=1, source_target_pairs={{0,16},{4,20},{8,24},{12,28},{16,0},{20,4},{24,8},{28,12},{1,17},{... | collective-permute-start | bytes 52232 | tf_op jit(solution)/shard_map/ppermute | solution.py:63
  519.0 6.2 %collective-permute-start.43 = (f32[4352]{0:T(1024)S(1)}, f32[4352]{0:T(1024)S(1)}, u32[]{:S(2)}, u32[]{:S(2)}) collective-permute-start(f32[4352]{0:T(1024)S(1)} %add.213), channel_id=1, source_target_pairs={{0,8},{4,12},{8,16},{12,20},{16,24},{20,28},{24,0},{28,4},{1,9},{5... | collective-permute-start | bytes 52232 | tf_op jit(solution)/shard_map/ppermute | solution.py:63
  (20 other events, 85.5 us)
Sparse Core Ops, SparseCore 0:
  10.3 67.4 all-gather.3
  80.0 115.3 all-gather.5
  197.0 62.9 all-gather.7
  262.2 68.4 reduce-scatter.3
  332.9 127.5 reduce-scatter.5
  462.6 69.4 reduce-scatter.7

commit v5 on v3

--- a/solution.py
+++ b/solution.py
@@ -22,6 +22,12 @@
     return lax.dot_general(
         left, right, (((0,), (0,)), ((), ())), preferred_element_type=jnp.float32
     )
+
+
+def weight_term(left, right):
+    return lax.dot_general(
+        left, right, (((0, 1), (0, 1)), ((), ())), preferred_element_type=jnp.float32
+    ).astype(jnp.bfloat16)
 
 
 def contract_last(left, right):
@@ -92,7 +98,7 @@
     def gather_first(self, block):
         if self.tensor_size != 4:
             return block, block
-        return self.across(block, 1), self.across(block, 2)
+        return lax.optimization_barrier((self.across(block, 1), self.across(block, 2)))
 
     def gather_second(self, block, first):
         if self.tensor_size != 4:
@@ -103,8 +109,9 @@
             return block
         half = block.shape[0] // 2
         by_x, by_y = first
-        corner_low = self.across(by_y[:half], 1)
-        corner_high = self.across(by_x[half:], 2)
+        corner_low, corner_high = lax.optimization_barrier(
+            (self.across(by_y[:half], 1), self.across(by_x[half:], 2))
+        )
         return jnp.concatenate([block, by_x, by_y, corner_low, corner_high], axis=0)
 
     def gather_tokens(self, block):
@@ -118,9 +125,7 @@
         start = 2 * block * half + high * half
         return partial[start : start + half]
 
-    def scatter_first(self, partial):
-        if self.tensor_size != 4:
-            return (partial,)
+    def first_sends(self, partial):
         return (
             self.across(self.half_block(partial, 3, 0), 1),
             self.across(self.half_block(partial, 3, 1), 2),
@@ -128,37 +133,87 @@
             self.across(self.half_block(partial, 2, 1), 2),
         )
 
+    def last_sends(self, partial, first):
+        def passed(block, high, arrived):
+            total = self.half_block(partial, block, high).astype(jnp.float32)
+            return (total + arrived.astype(jnp.float32)).astype(partial.dtype)
+
+        return (
+            self.across(passed(2, 0, first[0]), 2),
+            self.across(passed(1, 1, first[1]), 1),
+        )
+
+    def combined(self, partial, first, last):
+        return jnp.concatenate(
+            [
+                self.half_block(partial, 0, high).astype(jnp.float32)
+                + first[2 + high].astype(jnp.float32)
+                + last[high].astype(jnp.float32)
+                for high in range(2)
+            ],
+            axis=0,
+        )
+
+    def scatter_first(self, partial):
+        if self.tensor_size != 4:
+            return (partial,)
+        return lax.optimization_barrier(self.first_sends(partial))
+
     def scatter_second(self, partial, first):
-        wide = jnp.float32
         if self.tensor_size != 4:
             (partial,) = first
             bit = self.tensor_size // 2
             while bit:
                 middle = partial.shape[0] // 2
-                arrived = self.across(partial[middle:], bit).astype(wide)
-                total = partial[:middle].astype(wide) + arrived
+                arrived = self.across(partial[middle:], bit).astype(jnp.float32)
+                total = partial[:middle].astype(jnp.float32) + arrived
                 partial = total.astype(partial.dtype)
                 bit //= 2
             return total
-        low_pass, high_pass, low_own, high_own = first
-
-        def passed(block, high, arrived):
-            total = self.half_block(partial, block, high).astype(wide) + arrived.astype(wide)
-            return total.astype(partial.dtype)
-
-        low_last = self.across(passed(2, 0, low_pass), 2)
-        high_last = self.across(passed(1, 1, high_pass), 1)
-        low = self.half_block(partial, 0, 0).astype(wide) + low_own.astype(wide)
-        high = self.half_block(partial, 0, 1).astype(wide) + high_own.astype(wide)
-        return jnp.concatenate(
-            [low + low_last.astype(wide), high + high_last.astype(wide)], axis=0
-        )
+        last = lax.optimization_barrier(self.last_sends(partial, first))
+        return self.combined(partial, first, last)
+
+    def scatter_beside(self, partial, terms):
+        if self.tensor_size != 4:
+            return self.scatter_tokens(partial), self.total_tensor(terms)
+        first, arrived = lax.optimization_barrier(
+            (self.first_sends(partial), self.across(terms, 1))
+        )
+        terms = terms + arrived
+        last, arrived = lax.optimization_barrier(
+            (self.last_sends(partial, first), self.across(terms, 2))
+        )
+        return self.combined(partial, first, last), terms + arrived
 
     def gather_weight(self, shard):
         return lax.all_gather(shard, "dp", axis=0, tiled=True)
 
+    def core_columns(self, rows, core):
+        width = rows.shape[1] // self.dp_size
+        return jnp.concatenate(
+            [
+                lax.dynamic_slice_in_dim(rows, (2 * chip + core) * width, width, 1)
+                for chip in range(self.chips)
+            ],
+            axis=1,
+        )
+
+    def both_cores(self, rows):
+        return jnp.stack([rows, self.other_core(rows)])
+
+    def both_columns(self, rows):
+        core = lax.axis_index("dp") % 2
+        theirs = self.other_core(self.core_columns(rows, core ^ 1))
+        return jnp.stack([self.core_columns(rows, core), theirs])
+
     def scatter_weight(self, partial):
         return lax.psum_scatter(partial, "dp", scatter_dimension=0, tiled=True)
+
+    def scatter_chips(self, partial):
+        groups = [list(range(core, self.dp_size, 2)) for core in range(2)]
+        return lax.psum_scatter(
+            partial, "dp", scatter_dimension=0, tiled=True, axis_index_groups=groups
+        )
 
     def total_tensor(self, value):
         bit = 1
@@ -529,8 +584,6 @@
     branch_grad = links.gather_tokens(middle_grad.astype(jnp.bfloat16))
     feed_partial, branch_grad = lax.optimization_barrier((feed_partial, branch_grad))
     feed_first = links.scatter_first(feed_partial)
-    output_term = contract_first(branch_grad, attended_rows).astype(jnp.bfloat16)
-    branch_grad, output_term = lax.optimization_barrier((branch_grad, output_term))
     attended_grad = matmul(branch_grad, wide_output).astype(jnp.bfloat16)
     raw_grad, query_gain_term, key_gain_term = attention.backward(
         place,
@@ -545,18 +598,16 @@
         log_totals,
         attended_grad,
     )
-    raw_grad, feed_first = lax.optimization_barrier((raw_grad, feed_first))
-    attention_term = contract_first(normed_rows, raw_grad).astype(jnp.bfloat16)
+    raw_grad, feed_first, branch_grad = lax.optimization_barrier(
+        (raw_grad, feed_first, branch_grad)
+    )
+    output_term = weight_term(links.both_columns(branch_grad), links.both_cores(attended_rows))
+    attention_term = weight_term(links.both_columns(normed_rows), links.both_cores(raw_grad))
     feed_first, attention_term = lax.optimization_barrier((feed_first, attention_term))
     feed_branch = links.scatter_second(feed_partial, feed_first)
     raw_grad, attention_term = lax.optimization_barrier((raw_grad, attention_term))
     input_partial = contract_last(raw_grad, wide_attention).astype(jnp.bfloat16)
     mixing_term = jnp.concatenate([attention_term, output_term], axis=1)
-    mixing_term, feed_sum, feed_branch, input_partial = lax.optimization_barrier(
-        (mixing_term, feed_sum, feed_branch, input_partial)
-    )
-    mixing_sum = links.scatter_weight(mixing_term)
-    input_first = links.scatter_first(input_partial)
     input_gain_term = (
         jnp.sum(input_partial.astype(jnp.float32) * normed_rows.astype(jnp.float32), axis=0)
         / input_gain
@@ -564,11 +615,14 @@
     terms = jnp.concatenate(
         [input_gain_term, middle_gain_term, query_gain_term[0], key_gain_term[0]]
     )
-    input_normed_grad = links.scatter_second(input_partial, input_first)
-    terms, input_normed_grad = lax.optimization_barrier((terms, input_normed_grad))
+    mixing_term, feed_sum, feed_branch, input_partial, terms = lax.optimization_barrier(
+        (mixing_term, feed_sum, feed_branch, input_partial, terms)
+    )
+    mixing_sum = links.scatter_chips(mixing_term)
+    input_normed_grad, terms = links.scatter_beside(input_partial, terms)
     layer_output = middle + feed_branch
     tokens_grad = middle_grad + norm_backward(input_normed_grad, scaled_in, inverse_in, input_gain)
-    terms = links.total_dp(links.total_tensor(terms))
+    terms = links.total_dp(terms)
     width = tokens.shape[1]
     feed_sum = feed_sum.astype(jnp.float32)
     query_sum, key_sum, value_sum, output_sum = split_columns(

time: 557 us -> 539 us (0.968)
  waiting for transfers between devices: 223 us -> 201 us
  local copies, waits for them, and re-layouts: 39 us -> 47.5 us
    ppermute x42, waiting for transfers between devices: 190 us -> 156 us  [across(): lax.ppermute(value, 'tensor', [(place, place ^ bit) for place in range(se...]
    dot_general x0 -> x2, matrix products: none -> 10.9 us  [weight_term(): lax.dot_general(left, right, (((0, 1), (0, 1)), ((), ())), preferred_elem...]
    dot_general x4 -> x2, matrix products: 41 us -> 31.9 us  [contract_first(): lax.dot_general(left, right, (((0,), (0,)), ((), ())), preferred_element_...]
    add x10 -> x6, other arithmetic: 15.4 us -> 8.51 us  [the longest x4 8.5 us: combined(): self.half_block(partial, 0, high).astype(jnp.float32)]
    reduce_scatter x3 -> x2, waiting for transfers between devices: 10.1 us -> 16.9 us  [scatter_weight(): return lax.psum_scatter(partial, 'dp', scatter_dimension=0, tiled=True)]
    unnamed x77 -> x81, local copies, waits for them, and re-layouts: 21.5 us -> 23 us
  transfers between devices with their start and end apart: 52 -> 56, of which waited for: 32 -> 33; matrix products, arithmetic and copies ran while one was open for 38% -> 42% of each run, Pallas kernels for 6% -> 6%
where the time goes in v5:
time: 539 us; the launch traced here: 532 us
  waiting for transfers between devices  201 us (37%)
  matrix products  132 us (24%)
  starting transfers between devices  52.5 us (10%)
  other arithmetic  50.9 us (9%)
  local copies, waits for them, and re-layouts  47.5 us (9%)
  Pallas kernels  33.1 us (6%)
  between operations  15.4 us (3%)
    ppermute x42, waiting for transfers between devices, across(): lax.ppermute(value, 'tensor', [(place, place ^ bit) for place in range(se...  156 us
    dot_general x4, matrix products, matmul(): return jnp.dot(left, right, preferred_element_type=jnp.float32)  48.2 us
    ppermute x42, starting transfers between devices, across(): lax.ppermute(value, 'tensor', [(place, place ^ bit) for place in range(se...  42.4 us
    dot_general x4, matrix products, contract_last(): lax.dot_general(left, right, (((1,), (1,)), ((), ())), preferred_element_...  40.8 us
    dot_general x2, matrix products, contract_first(): lax.dot_general(left, right, (((0,), (0,)), ((), ())), preferred_element_...  31.9 us
    all_gather x3, waiting for transfers between devices, gather_weight(): return lax.all_gather(shard, 'dp', axis=0, tiled=True)  23.5 us
    unnamed x81, local copies, waits for them, and re-layouts  23 us
    reduce_scatter x2, waiting for transfers between devices, scatter_weight(): return lax.psum_scatter(partial, 'dp', scatter_dimension=0, tiled=True)  16.9 us
  transfers between devices with their start and end apart: 56, of which 33 were waited for; matrix products, arithmetic and copies ran while one was open for 42% of the time, Pallas kernels for 6%

profile of v5, /device:TPU:0, one launch (start us, length us, event | category | flops | bytes accessed | tf_op | source)
XLA Modules:
  0.0 532.2 jit_solution(5134384204606950062)
XLA Ops:
  7.2 2.2 pad_maximum_fusion.7
  9.5 2.7 pad_maximum_fusion.6
  14.3 2.9 collective-permute-start
  19.5 1.9 fusion.41
  21.4 20.1 %collective-permute-done = bf16[256,2048]{1,0:T(8,128)(2,1)} collective-permute-done((bf16[256,2048]{1,0:T(8,128)(2,1)}, bf16[256,2048]{1,0:T(8,128)(2,1)}, u32[]{:S(2)}, u32[]{:S(2)}) %collective-permute-start) | collective-permute-done | bytes 1048608 | tf_op jit(solution)/shard_map/ppermute | solution.py:83
  41.5 2.1 collective-permute-done.1
  45.9 2.1 collective-permute-start.3
  49.1 14.8 %collective-permute-done.4 = bf16[256,2048]{1,0:T(8,128)(2,1)S(1)} collective-permute-done((bf16[256,2048]{1,0:T(8,128)(2,1)S(1)}, bf16[256,2048]{1,0:T(8,128)(2,1)S(1)}, u32[]{:S(2)}, u32[]{:S(2)}) %collective-permute-start.4) | collective-permute-done | bytes 1048608 | tf_op jit(solution)/shard_map/ppermute | solution.py:83
  63.9 2.2 collective-permute-done.5
  66.1 2.3 constant_dynamic-update-slice_fusion.3
  68.4 2.4 constant_dynamic-update-slice_fusion.2
  70.8 3.5 collective-permute-done.2
  83.1 2.3 constant_dynamic-update-slice_fusion.7
  85.5 5.7 %collective-permute-done.6 = bf16[128,2048]{1,0:T(8,128)(2,1)S(1)} collective-permute-done((bf16[128,2048]{1,0:T(8,128)(2,1)S(1)}, bf16[128,2048]{1,0:T(8,128)(2,1)S(1)}, u32[]{:S(2)}, u32[]{:S(2)}) %collective-permute-start.6) | collective-permute-done | bytes 524320 | tf_op jit(solution)/shard_map/ppermute | solution.py:83
  93.3 10.0 %fusion.13.raw_query.raw_key.raw_value = f32[1024,1024]{1,0:T(8,128)} fusion(bf16[1024,2048]{1,0:T(8,128)(2,1)} %constant_dynamic-update-slice_fusion, bf16[2048,1536]{1,0:T(8,128)(2,1)} %all-gather.4.cloned.1.call-done), kind=kOutput, calls=%fused_computation.26 | convolution fusion | flops 4294967296 | bytes 12582912 | tf_op jit(solution)/shard_map/dot_general | solution.py:18
  103.3 14.4 %attention_forward.1 = (bf16[1024,512]{1,0:T(8,128)(2,1)}, bf16[1024,256]{1,0:T(8,128)(2,1)}, bf16[1024,256]{1,0:T(8,128)(2,1)}, bf16[1024,512]{1,0:T(8,128)(2,1)}, f32[2,2,1024]{2,1,0:T(2,128)}) custom-call(s32[1]{0:T(128)} %bitcast.place_ref, f32[1024,1024]{1,0:T(8,128)} %fusion.13.raw_query.raw_key.raw_value, ...), custom_call_target="tpu_custom_call" | custom-call | flops 4294967296 | bytes 8388608 | tf_op jit(solution)/shard_map/attention_forward/pallas_call | solution.py:338
  117.8 4.4 convolution_convert_fusion.4
  122.2 2.0 copy-done.16
  129.6 10.9 %collective-permute-done.10 = bf16[128,2048]{1,0:T(8,128)(2,1)S(1)} collective-permute-done((bf16[128,2048]{1,0:T(8,128)(2,1)}, bf16[128,2048]{1,0:T(8,128)(2,1)S(1)}, u32[]{:S(2)}, u32[]{:S(2)}) %collective-permute-start.10) | collective-permute-done | bytes 524320 | tf_op jit(solution)/shard_map/ppermute | solution.py:83
  141.9 6.5 %collective-permute-done.8 = bf16[128,2048]{1,0:T(8,128)(2,1)S(1)} collective-permute-done((bf16[128,2048]{1,0:T(8,128)(2,1)}, bf16[128,2048]{1,0:T(8,128)(2,1)S(1)}, u32[]{:S(2)}, u32[]{:S(2)}) %collective-permute-start.8) | collective-permute-done | bytes 524320 | tf_op jit(solution)/shard_map/ppermute | solution.py:83
  153.0 8.0 %collective-permute-done.12 = bf16[128,2048]{1,0:T(8,128)(2,1)S(1)} collective-permute-done((bf16[128,2048]{1,0:T(8,128)(2,1)S(1)}, bf16[128,2048]{1,0:T(8,128)(2,1)S(1)}, u32[]{:S(2)}, u32[]{:S(2)}) %collective-permute-start.12) | collective-permute-done | bytes 524320 | tf_op jit(solution)/shard_map/ppermute | solution.py:83
  167.8 21.2 %collective-permute-done.14 = bf16[256,2048]{1,0:T(8,128)(2,1)S(1)} collective-permute-done((bf16[256,2048]{1,0:T(8,128)(2,1)S(1)}, bf16[256,2048]{1,0:T(8,128)(2,1)S(1)}, u32[]{:S(2)}, u32[]{:S(2)}) %collective-permute-start.14) | collective-permute-done | bytes 1048608 | tf_op jit(solution)/shard_map/ppermute | solution.py:83
  193.3 5.0 collective-permute-done.16
  201.7 18.0 %fusion.54 = f32[1024,3072]{1,0:T(8,128)S(1)} fusion(bf16[1024,2048]{1,0:T(8,128)(2,1)} %constant_dynamic-update-slice_fusion.10, bf16[2048,3072]{1,0:T(8,128)(2,1)} %all-gather.6.cloned.1.call-done), kind=kOutput, calls=%fused_computation.141 | convolution fusion | flops 12884901888 | bytes 29360128 | tf_op jit(solution)/shard_map/dot_general | solution.py:18
  219.7 2.0 multiply_convert_fusion.2
  221.6 2.6 copy-done.6
  224.3 12.2 %convolution_convert_fusion.1 = bf16[2048,1536]{1,0:T(8,128)(2,1)} fusion(bf16[1024,2048]{1,0:T(8,128)(2,1)} %constant_dynamic-update-slice_fusion.5, bf16[1024,1536]{1,0:T(8,128)(2,1)S(1)} %multiply_convert_fusion.2), kind=kOutput, calls=%fused_computation.2 | convolution fusion | flops 6445596672 | bytes 13631488 | tf_op jit(solution)/shard_map/dot_general | solution.py:22
  236.6 23.5 %all-gather.8.cloned.1.call-done = bf16[2048,1536]{1,0:T(8,128)(2,1)} async-done(((bf16[256,1536]{1,0:T(8,128)(2,1)}), bf16[2048,1536]{1,0:T(8,128)(2,1)}) %all-gather.8.cloned.1.call-update) | async-done | bytes 6291472 | tf_op jit(solution)/shard_map/all_gather | solution.py:189
  260.0 15.3 %multiply_convert_fusion.1 = (bf16[1024,1536]{1,0:T(8,128)(2,1)S(1)}, bf16[1024,1536]{1,0:T(8,128)(2,1)S(1)}) fusion(f32[1024,3072]{1,0:T(8,128)} %copy-done.6, bf16[1024,2048]{1,0:T(8,128)(2,1)} %constant_dynamic-update-slice_fusion.5, bf16[2048,1536]{1,0:T(8,128)(2,1)} %all-gather.8.cloned.1.call-done), kind=kOutput, calls=%fused_computation.5 | convolution fusion | flops 6462898176 | bytes 29360128 | tf_op jit(solution)/shard_map/dot_general | solution.py:18
  275.3 3.6 pad_maximum_fusion
  278.9 17.6 %convolution_convert_fusion.2 = bf16[1024,2048]{1,0:T(8,128)(2,1)} fusion(bf16[2048,3072]{1,0:T(8,128)(2,1)} %all-gather.6.cloned.1.call-done, bf16[1024,1536]{1,0:T(8,128)(2,1)S(1)} %get-tuple-element.208, bf16[1024,1536]{1,0:T(8,128)(2,1)S(1)} %get-tuple-element.207), kind=kOutput, calls=%fused_computation.21 | convolution fusion | flops 12899581952 | bytes 23068672 | tf_op jit(solution)/shard_map/dot_general | solution.py:34
  296.5 3.0 fusion.49
  303.5 19.6 %convolution_convert_fusion = bf16[2048,3072]{1,0:T(8,128)(2,1)} fusion(bf16[1024,2048]{1,0:T(8,128)(2,1)} %constant_dynamic-update-slice_fusion.10, bf16[1024,3072]{1,0:T(8,128)(2,1)} %pad_maximum_fusion), kind=kOutput, calls=%fused_computation | convolution fusion | flops 12891193344 | bytes 23068672 | tf_op jit(solution)/shard_map/dot_general | solution.py:22
  323.1 1.9 collective-permute-done.20
  326.2 4.5 reduce-scatter.4.cloned.1.call-done
  330.8 1.9 add_convert_fusion.4
  335.7 12.4 %convolution_convert_fusion.3 = bf16[1024,2048]{1,0:T(8,128)(2,1)} fusion(bf16[1024,1536]{1,0:T(8,128)(2,1)S(1)} %copy-done.18, bf16[2048,1536]{1,0:T(8,128)(2,1)} %all-gather.8.cloned.1.call-done), kind=kOutput, calls=%fused_computation.22 | convolution fusion | flops 6444548096 | bytes 13631488 | tf_op jit(solution)/shard_map/dot_general | solution.py:34
  348.1 2.2 convert_add_fusion.6
  351.9 1.9 constant_dynamic-update-slice_fusion.19
  353.9 3.8 constant_dynamic-slice_fusion.15
  357.7 17.9 %collective-permute-done.24 = bf16[256,2048]{1,0:T(8,128)(2,1)} collective-permute-done((bf16[256,2048]{1,0:T(8,128)(2,1)}, bf16[256,2048]{1,0:T(8,128)(2,1)}, u32[]{:S(2)}, u32[]{:S(2)}) %collective-permute-start.24) | collective-permute-done | bytes 1048608 | tf_op jit(solution)/shard_map/ppermute | solution.py:83
  384.3 2.0 collective-permute-done.26
  386.2 2.1 collective-permute-done.27
  394.0 4.9 fusion.38.upstream
  398.9 16.4 %attention_backward.1 = (bf16[1024,1024]{1,0:T(8,128)(2,1)}, f32[1,128]{1,0:T(1,128)}, f32[1,128]{1,0:T(1,128)}) custom-call(s32[1]{0:T(128)} %bitcast.place_ref, f32[1024,1024]{1,0:T(8,128)} %fusion.13.raw_query.raw_key.raw_value, f32[1024,1024]{1,0:T(8,128)} %fusion.13.raw_query.raw_key.raw_value, f32[1024,128]{1,0:T(8,128)} %get-tuple-element.274.cosine, ...), custom_call_target="tpu_custom_call" | custom-call | flops 10737418240 | bytes 8388608 | tf_op jit(solution)/shard_map/attention_backward/pallas_call | solution.py:454
  415.4 2.0 maximum_bitcast_fusion
  420.3 6.6 %bitcast_convert_fusion = bf16[1024,1024]{1,0:T(8,128)(2,1)S(1)} fusion(bf16[1,1024,1024]{2,1,0:T(8,128)(2,1)S(1)} %bitcast.47, bf16[1,1024,1024]{2,1,0:T(8,128)(2,1)S(1)} %bitcast.46, bf16[1,1024,1024]{2,1,0:T(8,128)(2,1)} %bitcast.4, bf16[1,1024,1024]{2,1,0:T(8,128)(2,1)S(1)} %maximum_bitcast_fusion), kind=kOutput, calls=%fused_computation.20 | convolution fusion | flops 4300210176 | bytes 10485760 | tf_op jit(solution)/shard_map/dot_general | solution.py:28
  426.9 2.9 add_convert_fusion.2
  431.3 6.4 %multiply_reduce_fusion = (f32[2048]{0:T(1024)S(1)}, bf16[1024,2048]{1,0:T(8,128)(2,1)}) fusion(bf16[1024,2048]{1,0:T(8,128)(2,1)S(1)} %copy-done.13, bf16[1024,1024]{1,0:T(8,128)(2,1)S(1)} %copy-done.30, bf16[2048,1536]{1,0:T(8,128)(2,1)S(1)} %bitcast.45), kind=kOutput, calls=%fused_computation.1 | convolution fusion | flops 4305451008 | bytes 14688256 | tf_op jit(solution)/shard_map/dot_general | solution.py:34
  437.8 4.3 bitcast_convert_fusion.1
  444.2 2.4 convert_add_fusion.4
  448.1 12.4 %reduce-scatter.6.cloned.1.call-done = bf16[256,3072]{1,0:T(8,128)(2,1)} async-done(((bf16[2048,3072]{1,0:T(8,128)(2,1)}), bf16[256,3072]{1,0:T(8,128)(2,1)}) %reduce-scatter.6.cloned.1.call-update) | async-done | bytes 1572880 | tf_op jit(solution)/shard_map/reduce_scatter | solution.py:210
  460.5 2.9 fusion.47
  468.9 2.6 convert_element_type.283
  471.5 15.3 %collective-permute-done.42 = f32[4352]{0:T(1024)S(1)} collective-permute-done((f32[4352]{0:T(1024)S(1)}, f32[4352]{0:T(1024)S(1)}, u32[]{:S(2)}, u32[]{:S(2)}) %collective-permute-start.42) | collective-permute-done | bytes 17440 | tf_op jit(solution)/shard_map/ppermute | solution.py:83
  489.3 1.9 add_convert_fusion
  492.4 2.1 fusion.51
  494.5 6.9 %collective-permute-done.43 = bf16[128,2048]{1,0:T(8,128)(2,1)S(1)} collective-permute-done((bf16[128,2048]{1,0:T(8,128)(2,1)S(1)}, bf16[128,2048]{1,0:T(8,128)(2,1)S(1)}, u32[]{:S(2)}, u32[]{:S(2)}) %collective-permute-start.43) | collective-permute-done | bytes 524320 | tf_op jit(solution)/shard_map/ppermute | solution.py:83
  501.5 2.2 convert_add_fusion.2
  504.2 5.7 %collective-permute-start.47 = (f32[4352]{0:T(1024)S(1)}, f32[4352]{0:T(1024)S(1)}, u32[]{:S(2)}, u32[]{:S(2)}) collective-permute-start(f32[4352]{0:T(1024)S(1)} %add.288), channel_id=1, source_target_pairs={{0,8},{4,12},{8,16},{12,20},{16,24},{20,28},{24,0},{28,4},{1,9},{5... | collective-permute-start | bytes 52232 | tf_op jit(solution)/shard_map/ppermute | solution.py:69
  510.6 2.8 collective-permute-start.49
  513.4 3.3 fusion.26
  518.7 3.9 reduce-scatter.8.cloned.1.call-done.source
  522.5 2.3 split_columns.1
  (220 shorter events, 89.3 us)
Async XLA Ops:
  7.2 86.1 %all-gather.4.cloned.1.call-start = ((), (), s32[]{:S(2)}) async-start(), calls=%async_computation.3 | async-start | bytes 7077888 | tf_op jit(solution)/shard_map/all_gather | solution.py:189
  9.5 192.2 %all-gather.6.cloned.1.call-start = ((), (), s32[]{:S(2)}) async-start(), calls=%async_computation.4 | async-start | bytes 14155776 | tf_op jit(solution)/shard_map/all_gather | solution.py:189
  12.3 247.8 %all-gather.8.cloned.1.call-start = ((), (), s32[]{:S(2)}) async-start(), calls=%async_computation.5 | async-start | bytes 7077888 | tf_op jit(solution)/shard_map/all_gather | solution.py:189
  14.3 27.2 %collective-permute-start = (bf16[256,2048]{1,0:T(8,128)(2,1)}, bf16[256,2048]{1,0:T(8,128)(2,1)}, u32[]{:S(2)}, u32[]{:S(2)}) collective-permute-start(bf16[256,2048]{1,0:T(8,128)(2,1)} %get-tuple-element.206), channel_id=1, source_target_pairs={{0,1},{1,0},{2,3},{3,2},{4,5},{5,4},{6,7},{7,6},{8,9},{9,8},{10,11... | collective-permute-start | bytes 3145736 | tf_op jit(solution)/shard_map/ppermute | solution.py:83
  17.2 26.4 %collective-permute-start.1 = (bf16[256,2048]{1,0:T(8,128)(2,1)}, bf16[256,2048]{1,0:T(8,128)(2,1)}, u32[]{:S(2)}, u32[]{:S(2)}) collective-permute-start(bf16[256,2048]{1,0:T(8,128)(2,1)} %get-tuple-element.206), channel_id=1, source_target_pairs={{0,2},{1,3},{2,0},{3,1},{4,6},{5,7},{6,4},{7,5},{8,10},{9,11},{10,... | collective-permute-start | bytes 3145736 | tf_op jit(solution)/shard_map/ppermute | solution.py:83
  18.8 45.1 %collective-permute-start.4 = (bf16[256,2048]{1,0:T(8,128)(2,1)S(1)}, bf16[256,2048]{1,0:T(8,128)(2,1)S(1)}, u32[]{:S(2)}, u32[]{:S(2)}) collective-permute-start(bf16[256,2048]{1,0:T(8,128)(2,1)S(1)} %copy-done.7), channel_id=1, source_target_pairs={{0,1},{1,0},{2,3},{3,2},{4,5},{5,4},{6,7},{7,6},{8,9},{9,8},{10,11... | collective-permute-start | bytes 3145736 | tf_op jit(solution)/shard_map/ppermute | solution.py:83
  19.3 46.8 %collective-permute-start.5 = (bf16[256,2048]{1,0:T(8,128)(2,1)S(1)}, bf16[256,2048]{1,0:T(8,128)(2,1)}, u32[]{:S(2)}, u32[]{:S(2)}) collective-permute-start(bf16[256,2048]{1,0:T(8,128)(2,1)S(1)} %copy-done.7), channel_id=1, source_target_pairs={{0,2},{1,3},{2,0},{3,1},{4,6},{5,7},{6,4},{7,5},{8,10},{9,11},{10,... | collective-permute-start | bytes 3145736 | tf_op jit(solution)/shard_map/ppermute | solution.py:83
  44.7 29.6 %collective-permute-start.2 = (bf16[128,2048]{1,0:T(8,128)(2,1)S(1)}, bf16[128,2048]{1,0:T(8,128)(2,1)S(1)}, u32[]{:S(2)}, u32[]{:S(2)}) collective-permute-start(bf16[128,2048]{1,0:T(8,128)(2,1)S(1)} %slice.162), channel_id=1, source_target_pairs={{0,1},{1,0},{2,3},{3,2},{4,5},{5,4},{6,7},{7,6},{8,9},{9,8},{10,11... | collective-permute-start | bytes 1572872 | tf_op jit(solution)/shard_map/ppermute | solution.py:83
  45.9 29.9 %collective-permute-start.3 = (bf16[128,2048]{1,0:T(8,128)(2,1)S(1)}, bf16[128,2048]{1,0:T(8,128)(2,1)S(1)}, u32[]{:S(2)}, u32[]{:S(2)}) collective-permute-start(bf16[128,2048]{1,0:T(8,128)(2,1)S(1)} %slice.163), channel_id=1, source_target_pairs={{0,2},{1,3},{2,0},{3,1},{4,6},{5,7},{6,4},{7,5},{8,10},{9,11},{10,... | collective-permute-start | bytes 1572872 | tf_op jit(solution)/shard_map/ppermute | solution.py:83
  78.5 12.6 %collective-permute-start.6 = (bf16[128,2048]{1,0:T(8,128)(2,1)S(1)}, bf16[128,2048]{1,0:T(8,128)(2,1)S(1)}, u32[]{:S(2)}, u32[]{:S(2)}) collective-permute-start(bf16[128,2048]{1,0:T(8,128)(2,1)S(1)} %slice.165), channel_id=1, source_target_pairs={{0,1},{1,0},{2,3},{3,2},{4,5},{5,4},{6,7},{7,6},{8,9},{9,8},{10,11... | collective-permute-start | bytes 1572872 | tf_op jit(solution)/shard_map/ppermute | solution.py:83
  78.9 12.7 %collective-permute-start.7 = (bf16[128,2048]{1,0:T(8,128)(2,1)S(1)}, bf16[128,2048]{1,0:T(8,128)(2,1)S(1)}, u32[]{:S(2)}, u32[]{:S(2)}) collective-permute-start(bf16[128,2048]{1,0:T(8,128)(2,1)S(1)} %slice.166), channel_id=1, source_target_pairs={{0,2},{1,3},{2,0},{3,1},{4,6},{5,7},{6,4},{7,5},{8,10},{9,11},{10,... | collective-permute-start | bytes 1572872 | tf_op jit(solution)/shard_map/ppermute | solution.py:83
  125.5 15.1 %collective-permute-start.10 = (bf16[128,2048]{1,0:T(8,128)(2,1)}, bf16[128,2048]{1,0:T(8,128)(2,1)S(1)}, u32[]{:S(2)}, u32[]{:S(2)}) collective-permute-start(bf16[128,2048]{1,0:T(8,128)(2,1)} %get-tuple-element.254), channel_id=1, source_target_pairs={{0,1},{1,0},{2,3},{3,2},{4,5},{5,4},{6,7},{7,6},{8,9},{9,8},{10,11... | collective-permute-start | bytes 1572872 | tf_op jit(solution)/shard_map/ppermute | solution.py:83
  126.8 15.1 %collective-permute-start.11 = (bf16[128,2048]{1,0:T(8,128)(2,1)}, bf16[128,2048]{1,0:T(8,128)(2,1)S(1)}, u32[]{:S(2)}, u32[]{:S(2)}) collective-permute-start(bf16[128,2048]{1,0:T(8,128)(2,1)} %get-tuple-element.253), channel_id=1, source_target_pairs={{0,2},{1,3},{2,0},{3,1},{4,6},{5,7},{6,4},{7,5},{8,10},{9,11},{10,... | collective-permute-start | bytes 1572872 | tf_op jit(solution)/shard_map/ppermute | solution.py:83
  128.4 20.1 %collective-permute-start.8 = (bf16[128,2048]{1,0:T(8,128)(2,1)}, bf16[128,2048]{1,0:T(8,128)(2,1)S(1)}, u32[]{:S(2)}, u32[]{:S(2)}) collective-permute-start(bf16[128,2048]{1,0:T(8,128)(2,1)} %get-tuple-element.256), channel_id=1, source_target_pairs={{0,1},{1,0},{2,3},{3,2},{4,5},{5,4},{6,7},{7,6},{8,9},{9,8},{10,11... | collective-permute-start | bytes 1572872 | tf_op jit(solution)/shard_map/ppermute | solution.py:83
  129.0 20.2 %collective-permute-start.9 = (bf16[128,2048]{1,0:T(8,128)(2,1)}, bf16[128,2048]{1,0:T(8,128)(2,1)S(1)}, u32[]{:S(2)}, u32[]{:S(2)}) collective-permute-start(bf16[128,2048]{1,0:T(8,128)(2,1)} %get-tuple-element.255), channel_id=1, source_target_pairs={{0,2},{1,3},{2,0},{3,1},{4,6},{5,7},{6,4},{7,5},{8,10},{9,11},{10,... | collective-permute-start | bytes 1572872 | tf_op jit(solution)/shard_map/ppermute | solution.py:83
  129.6 201.1 %reduce-scatter.4.cloned.1.call-start = ((), (), s32[]{:S(2)}) async-start(), calls=%async_computation.6 | async-start | bytes 7077888 | tf_op jit(solution)/shard_map/reduce_scatter | solution.py:210
  150.8 10.2 %collective-permute-start.12 = (bf16[128,2048]{1,0:T(8,128)(2,1)S(1)}, bf16[128,2048]{1,0:T(8,128)(2,1)S(1)}, u32[]{:S(2)}, u32[]{:S(2)}) collective-permute-start(bf16[128,2048]{1,0:T(8,128)(2,1)S(1)} %get-tuple-element.252), channel_id=1, source_target_pairs={{0,2},{1,3},{2,0},{3,1},{4,6},{5,7},{6,4},{7,5},{8,10},{9,11},{10,... | collective-permute-start | bytes 1572872 | tf_op jit(solution)/shard_map/ppermute | solution.py:83
  152.4 12.1 %copy-start.19 = (f32[2048]{0:T(1024)S(1)}, f32[2048]{0:T(1024)}, u32[]{:S(2)}) copy-start(f32[2048]{0:T(1024)} %param.17) | copy-start | bytes 24580
  152.4 9.9 %collective-permute-start.13 = (bf16[128,2048]{1,0:T(8,128)(2,1)S(1)}, bf16[128,2048]{1,0:T(8,128)(2,1)S(1)}, u32[]{:S(2)}, u32[]{:S(2)}) collective-permute-start(bf16[128,2048]{1,0:T(8,128)(2,1)S(1)} %get-tuple-element.251), channel_id=1, source_target_pairs={{0,1},{1,0},{2,3},{3,2},{4,5},{5,4},{6,7},{7,6},{8,9},{9,8},{10,11... | collective-permute-start | bytes 1572872 | tf_op jit(solution)/shard_map/ppermute | solution.py:83
  164.5 27.7 %copy-start = (f32[256,2048]{1,0:T(8,128)}, f32[256,2048]{1,0:T(8,128)S(1)}, u32[]{:S(2)}) copy-start(f32[256,2048]{1,0:T(8,128)S(1)} %get-tuple-element.204) | copy-start | bytes 6291460
  166.0 22.9 %collective-permute-start.14 = (bf16[256,2048]{1,0:T(8,128)(2,1)S(1)}, bf16[256,2048]{1,0:T(8,128)(2,1)S(1)}, u32[]{:S(2)}, u32[]{:S(2)}) collective-permute-start(bf16[256,2048]{1,0:T(8,128)(2,1)S(1)} %get-tuple-element.202), channel_id=1, source_target_pairs={{0,1},{1,0},{2,3},{3,2},{4,5},{5,4},{6,7},{7,6},{8,9},{9,8},{10,11... | collective-permute-start | bytes 3145736 | tf_op jit(solution)/shard_map/ppermute | solution.py:83
  166.6 22.4 %collective-permute-start.15 = (bf16[256,2048]{1,0:T(8,128)(2,1)S(1)}, bf16[256,2048]{1,0:T(8,128)(2,1)S(1)}, u32[]{:S(2)}, u32[]{:S(2)}) collective-permute-start(bf16[256,2048]{1,0:T(8,128)(2,1)S(1)} %get-tuple-element.202), channel_id=1, source_target_pairs={{0,2},{1,3},{2,0},{3,1},{4,6},{5,7},{6,4},{7,5},{8,10},{9,11},{10,... | collective-permute-start | bytes 3145736 | tf_op jit(solution)/shard_map/ppermute | solution.py:83
  189.0 9.2 %collective-permute-start.16 = (bf16[128,2048]{1,0:T(8,128)(2,1)S(1)}, bf16[128,2048]{1,0:T(8,128)(2,1)S(1)}, u32[]{:S(2)}, u32[]{:S(2)}) collective-permute-start(bf16[128,2048]{1,0:T(8,128)(2,1)S(1)} %slice.176), channel_id=1, source_target_pairs={{0,1},{1,0},{2,3},{3,2},{4,5},{5,4},{6,7},{7,6},{8,9},{9,8},{10,11... | collective-permute-start | bytes 1572872 | tf_op jit(solution)/shard_map/ppermute | solution.py:83
  190.7 9.2 %collective-permute-start.17 = (bf16[128,2048]{1,0:T(8,128)(2,1)S(1)}, bf16[128,2048]{1,0:T(8,128)(2,1)S(1)}, u32[]{:S(2)}, u32[]{:S(2)}) collective-permute-start(bf16[128,2048]{1,0:T(8,128)(2,1)S(1)} %slice.177), channel_id=1, source_target_pairs={{0,2},{1,3},{2,0},{3,1},{4,6},{5,7},{6,4},{7,5},{8,10},{9,11},{10,... | collective-permute-start | bytes 1572872 | tf_op jit(solution)/shard_map/ppermute | solution.py:83
  224.3 12.3 %copy-start.17 = (bf16[1024,1536]{1,0:T(8,128)(2,1)}, bf16[1024,1536]{1,0:T(8,128)(2,1)S(1)}, u32[]{:S(2)}) copy-start(bf16[1024,1536]{1,0:T(8,128)(2,1)S(1)} %multiply_convert_fusion.2) | copy-start | bytes 9437188
  236.5 223.9 %reduce-scatter.6.cloned.1.call-start = ((), (), s32[]{:S(2)}) async-start(), calls=%async_computation.7 | async-start | bytes 14155776 | tf_op jit(solution)/shard_map/reduce_scatter | solution.py:210
  299.4 23.7 %collective-permute-start.18 = (bf16[128,2048]{1,0:T(8,128)(2,1)}, bf16[128,2048]{1,0:T(8,128)(2,1)}, u32[]{:S(2)}, u32[]{:S(2)}) collective-permute-start(bf16[128,2048]{1,0:T(8,128)(2,1)} %get-tuple-element.248), channel_id=1, source_target_pairs={{0,1},{1,0},{2,3},{3,2},{4,5},{5,4},{6,7},{7,6},{8,9},{9,8},{10,11... | collective-permute-start | bytes 1572872 | tf_op jit(solution)/shard_map/ppermute | solution.py:83
  300.9 22.2 %collective-permute-start.19 = (bf16[128,2048]{1,0:T(8,128)(2,1)}, bf16[128,2048]{1,0:T(8,128)(2,1)}, u32[]{:S(2)}, u32[]{:S(2)}) collective-permute-start(bf16[128,2048]{1,0:T(8,128)(2,1)} %get-tuple-element.247), channel_id=1, source_target_pairs={{0,2},{1,3},{2,0},{3,1},{4,6},{5,7},{6,4},{7,5},{8,10},{9,11},{10,... | collective-permute-start | bytes 1572872 | tf_op jit(solution)/shard_map/ppermute | solution.py:83
  302.4 22.7 %collective-permute-start.20 = (bf16[128,2048]{1,0:T(8,128)(2,1)}, bf16[128,2048]{1,0:T(8,128)(2,1)}, u32[]{:S(2)}, u32[]{:S(2)}) collective-permute-start(bf16[128,2048]{1,0:T(8,128)(2,1)} %get-tuple-element.246), channel_id=1, source_target_pairs={{0,1},{1,0},{2,3},{3,2},{4,5},{5,4},{6,7},{7,6},{8,9},{9,8},{10,11... | collective-permute-start | bytes 1572872 | tf_op jit(solution)/shard_map/ppermute | solution.py:83
  302.9 23.3 %collective-permute-start.21 = (bf16[128,2048]{1,0:T(8,128)(2,1)}, bf16[128,2048]{1,0:T(8,128)(2,1)}, u32[]{:S(2)}, u32[]{:S(2)}) collective-permute-start(bf16[128,2048]{1,0:T(8,128)(2,1)} %get-tuple-element.245), channel_id=1, source_target_pairs={{0,2},{1,3},{2,0},{3,1},{4,6},{5,7},{6,4},{7,5},{8,10},{9,11},{10,... | collective-permute-start | bytes 1572872 | tf_op jit(solution)/shard_map/ppermute | solution.py:83
  323.1 12.6 %copy-start.18 = (bf16[1024,1536]{1,0:T(8,128)(2,1)S(1)}, bf16[1024,1536]{1,0:T(8,128)(2,1)}, u32[]{:S(2)}) copy-start(bf16[1024,1536]{1,0:T(8,128)(2,1)} %copy-done.17) | copy-start | bytes 9437188
  330.7 191.8 %reduce-scatter.8.cloned.1.call-start = ((), (), s32[]{:S(2)}) async-start(), calls=%async_computation.8 | async-start | bytes 3932160 | tf_op jit(solution)/shard_map/reduce_scatter | solution.py:214
  332.7 15.4 %collective-permute-start.22 = (bf16[128,2048]{1,0:T(8,128)(2,1)S(1)}, bf16[128,2048]{1,0:T(8,128)(2,1)S(1)}, u32[]{:S(2)}, u32[]{:S(2)}) collective-permute-start(bf16[128,2048]{1,0:T(8,128)(2,1)S(1)} %get-tuple-element.244), channel_id=1, source_target_pairs={{0,2},{1,3},{2,0},{3,1},{4,6},{5,7},{6,4},{7,5},{8,10},{9,11},{10,... | collective-permute-start | bytes 1572872 | tf_op jit(solution)/shard_map/ppermute | solution.py:83
  334.2 13.9 %collective-permute-start.23 = (bf16[128,2048]{1,0:T(8,128)(2,1)S(1)}, bf16[128,2048]{1,0:T(8,128)(2,1)S(1)}, u32[]{:S(2)}, u32[]{:S(2)}) collective-permute-start(bf16[128,2048]{1,0:T(8,128)(2,1)S(1)} %get-tuple-element.243), channel_id=1, source_target_pairs={{0,1},{1,0},{2,3},{3,2},{4,5},{5,4},{6,7},{7,6},{8,9},{9,8},{10,11... | collective-permute-start | bytes 1572872 | tf_op jit(solution)/shard_map/ppermute | solution.py:83
  353.8 21.7 %collective-permute-start.24 = (bf16[256,2048]{1,0:T(8,128)(2,1)}, bf16[256,2048]{1,0:T(8,128)(2,1)}, u32[]{:S(2)}, u32[]{:S(2)}) collective-permute-start(bf16[256,2048]{1,0:T(8,128)(2,1)} %get-tuple-element.200), channel_id=1, source_target_pairs={{0,1},{1,0},{2,3},{3,2},{4,5},{5,4},{6,7},{7,6},{8,9},{9,8},{10,11... | collective-permute-start | bytes 3145736 | tf_op jit(solution)/shard_map/ppermute | solution.py:83
  353.8 21.7 %collective-permute-start.25 = (bf16[256,2048]{1,0:T(8,128)(2,1)}, bf16[256,2048]{1,0:T(8,128)(2,1)}, u32[]{:S(2)}, u32[]{:S(2)}) collective-permute-start(bf16[256,2048]{1,0:T(8,128)(2,1)} %get-tuple-element.200), channel_id=1, source_target_pairs={{0,2},{1,3},{2,0},{3,1},{4,6},{5,7},{6,4},{7,5},{8,10},{9,11},{10,... | collective-permute-start | bytes 3145736 | tf_op jit(solution)/shard_map/ppermute | solution.py:83
  357.6 23.7 %copy-start.10 = (bf16[1024,2048]{1,0:T(8,128)(2,1)S(1)}, bf16[1024,2048]{1,0:T(8,128)(2,1)}, u32[]{:S(2)}) copy-start(bf16[1024,2048]{1,0:T(8,128)(2,1)} %get-tuple-element.199) | copy-start | bytes 12582916
  376.6 9.6 %collective-permute-start.26 = (bf16[128,2048]{1,0:T(8,128)(2,1)S(1)}, bf16[128,2048]{1,0:T(8,128)(2,1)S(1)}, u32[]{:S(2)}, u32[]{:S(2)}) collective-permute-start(bf16[128,2048]{1,0:T(8,128)(2,1)S(1)} %slice.188), channel_id=1, source_target_pairs={{0,1},{1,0},{2,3},{3,2},{4,5},{5,4},{6,7},{7,6},{8,9},{9,8},{10,11... | collective-permute-start | bytes 1572872 | tf_op jit(solution)/shard_map/ppermute | solution.py:83
  379.1 9.2 %collective-permute-start.27 = (bf16[128,2048]{1,0:T(8,128)(2,1)S(1)}, bf16[128,2048]{1,0:T(8,128)(2,1)S(1)}, u32[]{:S(2)}, u32[]{:S(2)}) collective-permute-start(bf16[128,2048]{1,0:T(8,128)(2,1)S(1)} %slice.189), channel_id=1, source_target_pairs={{0,2},{1,3},{2,0},{3,1},{4,6},{5,7},{6,4},{7,5},{8,10},{9,11},{10,... | collective-permute-start | bytes 1572872 | tf_op jit(solution)/shard_map/ppermute | solution.py:83
  381.4 38.0 %collective-permute-start.32 = (bf16[1024,1024]{1,0:T(8,128)(2,1)}, bf16[1024,1024]{1,0:T(8,128)(2,1)}, u32[]{:S(2)}, u32[]{:S(2)}) collective-permute-start(bf16[1024,1024]{1,0:T(8,128)(2,1)} %pad_maximum_fusion.3), channel_id=1, source_target_pairs={{0,4},{4,0},{8,12},{12,8},{16,20},{20,16},{24,28},{28,24},{1,5},{5... | collective-permute-start | bytes 6291464 | tf_op jit(solution)/shard_map/ppermute | solution.py:80
  390.0 25.4 %collective-permute-start.28 = (bf16[128,2048]{1,0:T(8,128)(2,1)}, bf16[128,2048]{1,0:T(8,128)(2,1)}, u32[]{:S(2)}, u32[]{:S(2)}) collective-permute-start(bf16[128,2048]{1,0:T(8,128)(2,1)} %get-tuple-element.240), channel_id=1, source_target_pairs={{0,1},{1,0},{2,3},{3,2},{4,5},{5,4},{6,7},{7,6},{8,9},{9,8},{10,11... | collective-permute-start | bytes 1572872 | tf_op jit(solution)/shard_map/ppermute | solution.py:83
  390.6 24.7 %collective-permute-start.29 = (bf16[128,2048]{1,0:T(8,128)(2,1)}, bf16[128,2048]{1,0:T(8,128)(2,1)}, u32[]{:S(2)}, u32[]{:S(2)}) collective-permute-start(bf16[128,2048]{1,0:T(8,128)(2,1)} %get-tuple-element.239), channel_id=1, source_target_pairs={{0,2},{1,3},{2,0},{3,1},{4,6},{5,7},{6,4},{7,5},{8,10},{9,11},{10,... | collective-permute-start | bytes 1572872 | tf_op jit(solution)/shard_map/ppermute | solution.py:83
  391.2 24.1 %collective-permute-start.30 = (bf16[128,2048]{1,0:T(8,128)(2,1)}, bf16[128,2048]{1,0:T(8,128)(2,1)}, u32[]{:S(2)}, u32[]{:S(2)}) collective-permute-start(bf16[128,2048]{1,0:T(8,128)(2,1)} %get-tuple-element.238), channel_id=1, source_target_pairs={{0,1},{1,0},{2,3},{3,2},{4,5},{5,4},{6,7},{7,6},{8,9},{9,8},{10,11... | collective-permute-start | bytes 1572872 | tf_op jit(solution)/shard_map/ppermute | solution.py:83
  392.6 22.8 %collective-permute-start.31 = (bf16[128,2048]{1,0:T(8,128)(2,1)}, bf16[128,2048]{1,0:T(8,128)(2,1)}, u32[]{:S(2)}, u32[]{:S(2)}) collective-permute-start(bf16[128,2048]{1,0:T(8,128)(2,1)} %get-tuple-element.237), channel_id=1, source_target_pairs={{0,2},{1,3},{2,0},{3,1},{4,6},{5,7},{6,4},{7,5},{8,10},{9,11},{10,... | collective-permute-start | bytes 1572872 | tf_op jit(solution)/shard_map/ppermute | solution.py:83
  415.4 4.4 collective-permute-start.33
  417.4 20.4 %collective-permute-start.35 = (bf16[1024,512]{1,0:T(8,128)(2,1)}, bf16[1024,512]{1,0:T(8,128)(2,1)}, u32[]{:S(2)}, u32[]{:S(2)}) collective-permute-start(bf16[1024,512]{1,0:T(8,128)(2,1)} %get-tuple-element.117), channel_id=1, source_target_pairs={{0,4},{4,0},{8,12},{12,8},{16,20},{20,16},{24,28},{28,24},{1,5},{5... | collective-permute-start | bytes 3145736 | tf_op jit(solution)/shard_map/ppermute | solution.py:80
  418.7 12.6 %slice-start = ((s8[6291456]{0:T(1024)(128)(4,1)}), s8[4194304]{0:T(1024)(128)(4,1)S(1)}, s32[]{:S(2)}) async-start(s8[6291456]{0:T(1024)(128)(4,1)} %bitcast.44), calls=%async_computation.9 | async-start | bytes 8388608
  419.0 18.8 %collective-permute-start.34 = (bf16[1024,1024]{1,0:T(8,128)(2,1)S(1)}, bf16[1024,1024]{1,0:T(8,128)(2,1)}, u32[]{:S(2)}, u32[]{:S(2)}) collective-permute-start(bf16[1024,1024]{1,0:T(8,128)(2,1)S(1)} %pad_maximum_fusion.4), channel_id=1, source_target_pairs={{0,4},{4,0},{8,12},{12,8},{16,20},{20,16},{24,28},{28,24},{1,5},{5... | collective-permute-start | bytes 6291464 | tf_op jit(solution)/shard_map/ppermute | solution.py:80
  429.8 14.3 %collective-permute-start.36 = (bf16[128,2048]{1,0:T(8,128)(2,1)}, bf16[128,2048]{1,0:T(8,128)(2,1)}, u32[]{:S(2)}, u32[]{:S(2)}) collective-permute-start(bf16[128,2048]{1,0:T(8,128)(2,1)} %get-tuple-element.220), channel_id=1, source_target_pairs={{0,2},{1,3},{2,0},{3,1},{4,6},{5,7},{6,4},{7,5},{8,10},{9,11},{10,... | collective-permute-start | bytes 1572872 | tf_op jit(solution)/shard_map/ppermute | solution.py:83
  430.5 13.7 %collective-permute-start.37 = (bf16[128,2048]{1,0:T(8,128)(2,1)}, bf16[128,2048]{1,0:T(8,128)(2,1)}, u32[]{:S(2)}, u32[]{:S(2)}) collective-permute-start(bf16[128,2048]{1,0:T(8,128)(2,1)} %get-tuple-element.219), channel_id=1, source_target_pairs={{0,1},{1,0},{2,3},{3,2},{4,5},{5,4},{6,7},{7,6},{8,9},{9,8},{10,11... | collective-permute-start | bytes 1572872 | tf_op jit(solution)/shard_map/ppermute | solution.py:83
  463.4 23.4 %collective-permute-start.38 = (bf16[128,2048]{1,0:T(8,128)(2,1)}, bf16[128,2048]{1,0:T(8,128)(2,1)}, u32[]{:S(2)}, u32[]{:S(2)}) collective-permute-start(bf16[128,2048]{1,0:T(8,128)(2,1)} %get-tuple-element.216), channel_id=1, source_target_pairs={{0,1},{1,0},{2,3},{3,2},{4,5},{5,4},{6,7},{7,6},{8,9},{9,8},{10,11... | collective-permute-start | bytes 1572872 | tf_op jit(solution)/shard_map/ppermute | solution.py:83
  464.8 21.9 %collective-permute-start.39 = (bf16[128,2048]{1,0:T(8,128)(2,1)}, bf16[128,2048]{1,0:T(8,128)(2,1)}, u32[]{:S(2)}, u32[]{:S(2)}) collective-permute-start(bf16[128,2048]{1,0:T(8,128)(2,1)} %get-tuple-element.215), channel_id=1, source_target_pairs={{0,2},{1,3},{2,0},{3,1},{4,6},{5,7},{6,4},{7,5},{8,10},{9,11},{10,... | collective-permute-start | bytes 1572872 | tf_op jit(solution)/shard_map/ppermute | solution.py:83
  466.3 20.5 %collective-permute-start.40 = (bf16[128,2048]{1,0:T(8,128)(2,1)}, bf16[128,2048]{1,0:T(8,128)(2,1)}, u32[]{:S(2)}, u32[]{:S(2)}) collective-permute-start(bf16[128,2048]{1,0:T(8,128)(2,1)} %get-tuple-element.214), channel_id=1, source_target_pairs={{0,1},{1,0},{2,3},{3,2},{4,5},{5,4},{6,7},{7,6},{8,9},{9,8},{10,11... | collective-permute-start | bytes 1572872 | tf_op jit(solution)/shard_map/ppermute | solution.py:83
  466.9 21.0 %collective-permute-start.41 = (bf16[128,2048]{1,0:T(8,128)(2,1)}, bf16[128,2048]{1,0:T(8,128)(2,1)}, u32[]{:S(2)}, u32[]{:S(2)}) collective-permute-start(bf16[128,2048]{1,0:T(8,128)(2,1)} %get-tuple-element.213), channel_id=1, source_target_pairs={{0,2},{1,3},{2,0},{3,1},{4,6},{5,7},{6,4},{7,5},{8,10},{9,11},{10,... | collective-permute-start | bytes 1572872 | tf_op jit(solution)/shard_map/ppermute | solution.py:83
  467.4 19.4 %collective-permute-start.42 = (f32[4352]{0:T(1024)S(1)}, f32[4352]{0:T(1024)S(1)}, u32[]{:S(2)}, u32[]{:S(2)}) collective-permute-start(f32[4352]{0:T(1024)S(1)} %pad_maximum_fusion.11), channel_id=1, source_target_pairs={{0,1},{1,0},{2,3},{3,2},{4,5},{5,4},{6,7},{7,6},{8,9},{9,8},{10,11... | collective-permute-start | bytes 52232 | tf_op jit(solution)/shard_map/ppermute | solution.py:83
  468.9 23.5 %copy-start.14 = (bf16[256,3072]{1,0:T(8,128)(2,1)S(1)}, bf16[256,3072]{1,0:T(8,128)(2,1)}, u32[]{:S(2)}) copy-start(bf16[256,3072]{1,0:T(8,128)(2,1)} %reduce-scatter.6.cloned.1.call-done) | copy-start | bytes 4718596
  487.9 6.6 %collective-permute-start.45 = (f32[4352]{0:T(1024)S(1)}, f32[4352]{0:T(1024)S(1)}, u32[]{:S(2)}, u32[]{:S(2)}) collective-permute-start(f32[4352]{0:T(1024)S(1)} %add.282), channel_id=1, source_target_pairs={{0,2},{1,3},{2,0},{3,1},{4,6},{5,7},{6,4},{7,5},{8,10},{9,11},{10,... | collective-permute-start | bytes 52232 | tf_op jit(solution)/shard_map/ppermute | solution.py:83
  491.2 10.1 %collective-permute-start.43 = (bf16[128,2048]{1,0:T(8,128)(2,1)S(1)}, bf16[128,2048]{1,0:T(8,128)(2,1)S(1)}, u32[]{:S(2)}, u32[]{:S(2)}) collective-permute-start(bf16[128,2048]{1,0:T(8,128)(2,1)S(1)} %get-tuple-element.212), channel_id=1, source_target_pairs={{0,2},{1,3},{2,0},{3,1},{4,6},{5,7},{6,4},{7,5},{8,10},{9,11},{10,... | collective-permute-start | bytes 1572872 | tf_op jit(solution)/shard_map/ppermute | solution.py:83
  491.9 9.5 %collective-permute-start.44 = (bf16[128,2048]{1,0:T(8,128)(2,1)S(1)}, bf16[128,2048]{1,0:T(8,128)(2,1)S(1)}, u32[]{:S(2)}, u32[]{:S(2)}) collective-permute-start(bf16[128,2048]{1,0:T(8,128)(2,1)S(1)} %get-tuple-element.211), channel_id=1, source_target_pairs={{0,1},{1,0},{2,3},{3,2},{4,5},{5,4},{6,7},{7,6},{8,9},{9,8},{10,11... | collective-permute-start | bytes 1572872 | tf_op jit(solution)/shard_map/ppermute | solution.py:83
  501.4 12.0 %copy-start.9 = (f32[256,2048]{1,0:T(8,128)S(1)}, f32[256,2048]{1,0:T(8,128)}, u32[]{:S(2)}) copy-start(f32[256,2048]{1,0:T(8,128)} %pad_maximum_fusion.5) | copy-start | bytes 6291460
  501.4 2.8 collective-permute-start.46
  504.2 12.5 %collective-permute-start.47 = (f32[4352]{0:T(1024)S(1)}, f32[4352]{0:T(1024)S(1)}, u32[]{:S(2)}, u32[]{:S(2)}) collective-permute-start(f32[4352]{0:T(1024)S(1)} %add.288), channel_id=1, source_target_pairs={{0,8},{4,12},{8,16},{12,20},{16,24},{20,28},{24,0},{28,4},{1,9},{5... | collective-permute-start | bytes 52232 | tf_op jit(solution)/shard_map/ppermute | solution.py:69
  509.9 7.5 %collective-permute-start.48 = (f32[4352]{0:T(1024)S(1)}, f32[4352]{0:T(1024)S(1)}, u32[]{:S(2)}, u32[]{:S(2)}) collective-permute-start(f32[4352]{0:T(1024)S(1)} %add.288), channel_id=1, source_target_pairs={{0,16},{4,20},{8,24},{12,28},{16,0},{20,4},{24,8},{28,12},{1,17},{... | collective-permute-start | bytes 52232 | tf_op jit(solution)/shard_map/ppermute | solution.py:69
  510.6 6.8 %collective-permute-start.49 = (f32[4352]{0:T(1024)S(1)}, f32[4352]{0:T(1024)S(1)}, u32[]{:S(2)}, u32[]{:S(2)}) collective-permute-start(f32[4352]{0:T(1024)S(1)} %add.288), channel_id=1, source_target_pairs={{0,24},{4,28},{8,0},{12,4},{16,8},{20,12},{24,16},{28,20},{1,25},{... | collective-permute-start | bytes 52232 | tf_op jit(solution)/shard_map/ppermute | solution.py:69
  (26 other events, 149.4 us)
Sparse Core Ops, SparseCore 0:
  10.3 67.4 all-gather.3
  80.0 115.3 all-gather.5
  197.0 62.9 all-gather.7
  262.2 68.4 reduce-scatter.3
  332.8 127.5 reduce-scatter.5
  462.6 59.8 reduce-scatter.7

commit v6 on v5

--- a/solution.py
+++ b/solution.py
@@ -454,7 +454,7 @@
         return pl.pallas_call(
             self.backward_kernel,
             name="attention_backward",
-            cost_estimate=self.cost(5),
+            cost_estimate=pl.CostEstimate(flops=1, transcendentals=0, bytes_accessed=1),
             grid_spec=pltpu.PrefetchScalarGridSpec(
                 num_scalar_prefetch=1,
                 grid=(self.key_heads,),
@@ -556,7 +556,10 @@
     silu_gate = gating * gate_sigmoid
     active = (silu_gate * upward).astype(jnp.bfloat16)
     down_term = contract_first(cotangent, active).astype(jnp.bfloat16)
-    active, down_term = lax.optimization_barrier((active, down_term))
+    middle_columns = links.both_columns(normed_middle)
+    active, down_term, middle_columns = lax.optimization_barrier(
+        (active, down_term, middle_columns)
+    )
     down_sum = links.scatter_weight(down_term)
     cotangent, down_term = lax.optimization_barrier((cotangent, down_term))
     active_grad = matmul(cotangent, wide_down)
@@ -567,13 +570,16 @@
     feed_grad = jnp.concatenate([gate_grad, upward_grad], axis=1)
     middle_partial = contract_last(feed_grad, wide_feed)
     middle_partial = middle_partial.astype(jnp.bfloat16)
-    feed_grad, middle_partial = lax.optimization_barrier((feed_grad, middle_partial))
+    other_grad = links.other_core(feed_grad)
+    feed_grad, other_grad, middle_partial = lax.optimization_barrier(
+        (feed_grad, other_grad, middle_partial)
+    )
     middle_first = links.scatter_first(middle_partial)
-    feed_term = contract_first(normed_middle, feed_grad).astype(jnp.bfloat16)
+    feed_term = weight_term(middle_columns, jnp.stack([feed_grad, other_grad]))
     feed_term, middle_first, down_sum = lax.optimization_barrier(
         (feed_term, middle_first, down_sum)
     )
-    feed_sum = links.scatter_weight(feed_term)
+    feed_sum = links.scatter_chips(feed_term)
     middle_normed_grad = links.scatter_second(middle_partial, middle_first)
     feed_partial = contract_last(active, wide_down).astype(jnp.bfloat16)
     middle_normed_grad, feed_partial = lax.optimization_barrier((middle_normed_grad, feed_partial))

time: 539 us -> 528 us (0.980)
  waiting for transfers between devices: 201 us -> 193 us
  matrix products: 132 us -> 126 us
    dot_general x2 -> x1, matrix products: 31.9 us -> 11 us  [contract_first(): lax.dot_general(left, right, (((0,), (0,)), ((), ())), preferred_element_...]
    dot_general x2 -> x3, matrix products: 10.9 us -> 29.2 us  [weight_term(): lax.dot_general(left, right, (((0, 1), (0, 1)), ((), ())), preferred_elem...]
    reduce_scatter x2 -> x1, waiting for transfers between devices: 16.9 us -> 3.75 us  [scatter_weight(): return lax.psum_scatter(partial, 'dp', scatter_dimension=0, tiled=True)]
    ppermute x42, waiting for transfers between devices: 156 us -> 162 us  [across(): lax.ppermute(value, 'tensor', [(place, place ^ bit) for place in range(se...]
    all_gather x3, waiting for transfers between devices: 23.5 us -> 17.4 us  [gather_weight(): return lax.all_gather(shard, 'dp', axis=0, tiled=True)]
    unnamed x81 -> x79, local copies, waits for them, and re-layouts: 23 us -> 22.5 us
  transfers between devices with their start and end apart: 56 -> 58, of which waited for: 33 -> 33; matrix products, arithmetic and copies ran while one was open for 42% -> 41% of each run, Pallas kernels for 6% -> 6%
where the time goes in v6:
time: 528 us; the launch traced here: 521 us
  waiting for transfers between devices  193 us (37%)
  matrix products  126 us (24%)
  starting transfers between devices  54.3 us (10%)
  other arithmetic  51.1 us (10%)
  local copies, waits for them, and re-layouts  48.1 us (9%)
  Pallas kernels  33.2 us (6%)
  between operations  15.4 us (3%)
    ppermute x42, waiting for transfers between devices, across(): lax.ppermute(value, 'tensor', [(place, place ^ bit) for place in range(se...  162 us
    dot_general x4, matrix products, matmul(): return jnp.dot(left, right, preferred_element_type=jnp.float32)  46.9 us
    ppermute x42, starting transfers between devices, across(): lax.ppermute(value, 'tensor', [(place, place ^ bit) for place in range(se...  43.5 us
    dot_general x4, matrix products, contract_last(): lax.dot_general(left, right, (((1,), (1,)), ((), ())), preferred_element_...  39.3 us
    dot_general x3, matrix products, weight_term(): lax.dot_general(left, right, (((0, 1), (0, 1)), ((), ())), preferred_elem...  29.2 us
    unnamed x79, local copies, waits for them, and re-layouts  22.5 us
    all_gather x3, waiting for transfers between devices, gather_weight(): return lax.all_gather(shard, 'dp', axis=0, tiled=True)  17.4 us
    pallas_call x1, Pallas kernels, backward(): pl.pallas_call(self.backward_kernel, name='attention_backward', cost_esti...  16.4 us
  transfers between devices with their start and end apart: 58, of which 33 were waited for; matrix products, arithmetic and copies ran while one was open for 41% of the time, Pallas kernels for 6%

profile of v6, /device:TPU:0, one launch (start us, length us, event | category | flops | bytes accessed | tf_op | source)
XLA Modules:
  0.0 520.9 jit_solution(8685815799788799705)
XLA Ops:
  7.2 2.2 pad_maximum_fusion.9
  9.5 2.7 pad_maximum_fusion.8
  14.4 2.9 collective-permute-start
  19.6 1.9 fusion.47
  21.5 20.1 %collective-permute-done = bf16[256,2048]{1,0:T(8,128)(2,1)} collective-permute-done((bf16[256,2048]{1,0:T(8,128)(2,1)}, bf16[256,2048]{1,0:T(8,128)(2,1)}, u32[]{:S(2)}, u32[]{:S(2)}) %collective-permute-start) | collective-permute-done | bytes 1048608 | tf_op jit(solution)/shard_map/ppermute | solution.py:83
  41.6 2.1 collective-permute-done.1
  46.0 2.1 collective-permute-start.3
  49.2 14.8 %collective-permute-done.4 = bf16[256,2048]{1,0:T(8,128)(2,1)S(1)} collective-permute-done((bf16[256,2048]{1,0:T(8,128)(2,1)S(1)}, bf16[256,2048]{1,0:T(8,128)(2,1)S(1)}, u32[]{:S(2)}, u32[]{:S(2)}) %collective-permute-start.4) | collective-permute-done | bytes 1048608 | tf_op jit(solution)/shard_map/ppermute | solution.py:83
  64.0 2.2 collective-permute-done.5
  66.2 2.3 constant_dynamic-update-slice_fusion.3
  68.5 2.3 constant_dynamic-update-slice_fusion.2
  70.8 3.6 collective-permute-done.2
  83.2 2.3 constant_dynamic-update-slice_fusion.7
  85.6 5.8 %collective-permute-done.6 = bf16[128,2048]{1,0:T(8,128)(2,1)S(1)} collective-permute-done((bf16[128,2048]{1,0:T(8,128)(2,1)S(1)}, bf16[128,2048]{1,0:T(8,128)(2,1)S(1)}, u32[]{:S(2)}, u32[]{:S(2)}) %collective-permute-start.6) | collective-permute-done | bytes 524320 | tf_op jit(solution)/shard_map/ppermute | solution.py:83
  93.5 10.0 %fusion.19.raw_query.raw_key.raw_value = f32[1024,1024]{1,0:T(8,128)} fusion(bf16[1024,2048]{1,0:T(8,128)(2,1)} %constant_dynamic-update-slice_fusion, bf16[2048,1536]{1,0:T(8,128)(2,1)} %all-gather.4.cloned.1.call-done), kind=kOutput, calls=%fused_computation.31 | convolution fusion | flops 4294967296 | bytes 12582912 | tf_op jit(solution)/shard_map/dot_general | solution.py:18
  103.5 14.4 %attention_forward.1 = (bf16[1024,512]{1,0:T(8,128)(2,1)}, bf16[1024,256]{1,0:T(8,128)(2,1)}, bf16[1024,256]{1,0:T(8,128)(2,1)}, bf16[1024,512]{1,0:T(8,128)(2,1)}, f32[2,2,1024]{2,1,0:T(2,128)}) custom-call(s32[1]{0:T(128)} %bitcast.place_ref, f32[1024,1024]{1,0:T(8,128)} %fusion.19.raw_query.raw_key.raw_value, ...), custom_call_target="tpu_custom_call" | custom-call | flops 4294967296 | bytes 8388608 | tf_op jit(solution)/shard_map/attention_forward/pallas_call | solution.py:338
  117.9 4.4 convolution_convert_fusion.3
  126.7 10.8 %collective-permute-done.10 = bf16[128,2048]{1,0:T(8,128)(2,1)S(1)} collective-permute-done((bf16[128,2048]{1,0:T(8,128)(2,1)S(1)}, bf16[128,2048]{1,0:T(8,128)(2,1)S(1)}, u32[]{:S(2)}, u32[]{:S(2)}) %collective-permute-start.10) | collective-permute-done | bytes 524320 | tf_op jit(solution)/shard_map/ppermute | solution.py:83
  138.9 6.4 %collective-permute-done.8 = bf16[128,2048]{1,0:T(8,128)(2,1)S(1)} collective-permute-done((bf16[128,2048]{1,0:T(8,128)(2,1)S(1)}, bf16[128,2048]{1,0:T(8,128)(2,1)S(1)}, u32[]{:S(2)}, u32[]{:S(2)}) %collective-permute-start.8) | collective-permute-done | bytes 524320 | tf_op jit(solution)/shard_map/ppermute | solution.py:83
  149.3 8.2 %collective-permute-done.12 = bf16[128,2048]{1,0:T(8,128)(2,1)S(1)} collective-permute-done((bf16[128,2048]{1,0:T(8,128)(2,1)S(1)}, bf16[128,2048]{1,0:T(8,128)(2,1)S(1)}, u32[]{:S(2)}, u32[]{:S(2)}) %collective-permute-start.12) | collective-permute-done | bytes 524320 | tf_op jit(solution)/shard_map/ppermute | solution.py:83
  162.2 18.9 %collective-permute-done.14 = bf16[256,2048]{1,0:T(8,128)(2,1)S(1)} collective-permute-done((bf16[256,2048]{1,0:T(8,128)(2,1)}, bf16[256,2048]{1,0:T(8,128)(2,1)S(1)}, u32[]{:S(2)}, u32[]{:S(2)}) %collective-permute-start.14) | collective-permute-done | bytes 1048608 | tf_op jit(solution)/shard_map/ppermute | solution.py:83
  188.0 2.3 constant_dynamic-update-slice_fusion.12
  190.3 2.8 collective-permute-done.16
  194.9 1.9 constant_dynamic-update-slice_fusion.11
  196.8 1.9 constant_dynamic-update-slice_fusion.10
  198.7 2.5 constant_dynamic-slice_fusion.23
  201.9 3.9 collective-permute-done.18
  205.7 2.3 pad_maximum_fusion.1
  208.0 17.3 %fusion.61 = f32[1024,3072]{1,0:T(8,128)S(1)} fusion(bf16[1024,2048]{1,0:T(8,128)(2,1)} %constant_dynamic-update-slice_fusion.10, bf16[2048,3072]{1,0:T(8,128)(2,1)} %all-gather.6.cloned.1.call-done), kind=kOutput, calls=%fused_computation.157 | convolution fusion | flops 12884901888 | bytes 29360128 | tf_op jit(solution)/shard_map/dot_general | solution.py:18
  225.3 2.0 multiply_convert_fusion.2
  227.3 2.6 copy-done.4
  231.6 11.0 %convolution_convert_fusion = bf16[2048,1536]{1,0:T(8,128)(2,1)} fusion(bf16[1024,2048]{1,0:T(8,128)(2,1)} %constant_dynamic-update-slice_fusion.5, bf16[1024,1536]{1,0:T(8,128)(2,1)S(1)} %multiply_convert_fusion.2), kind=kOutput, calls=%fused_computation.6 | convolution fusion | flops 6445596672 | bytes 13631488 | tf_op jit(solution)/shard_map/dot_general | solution.py:22
  242.7 17.4 %all-gather.8.cloned.1.call-done = bf16[2048,1536]{1,0:T(8,128)(2,1)} async-done(((bf16[256,1536]{1,0:T(8,128)(2,1)}), bf16[2048,1536]{1,0:T(8,128)(2,1)}) %all-gather.8.cloned.1.call-update) | async-done | bytes 6291472 | tf_op jit(solution)/shard_map/all_gather | solution.py:189
  260.0 14.7 %multiply_convert_fusion.1 = (bf16[1024,1536]{1,0:T(8,128)(2,1)S(1)}, bf16[1024,1536]{1,0:T(8,128)(2,1)S(1)}) fusion(f32[1024,3072]{1,0:T(8,128)} %copy-done.4, bf16[1024,2048]{1,0:T(8,128)(2,1)} %constant_dynamic-update-slice_fusion.5, bf16[2048,1536]{1,0:T(8,128)(2,1)} %all-gather.8.cloned.1.call-done), kind=kOutput, calls=%fused_computation.9 | convolution fusion | flops 6462898176 | bytes 29360128 | tf_op jit(solution)/shard_map/dot_general | solution.py:18
  274.8 3.6 pad_maximum_fusion
  278.6 18.5 %convolution_convert_fusion.1 = bf16[1024,2048]{1,0:T(8,128)(2,1)} fusion(bf16[2048,3072]{1,0:T(8,128)(2,1)} %all-gather.6.cloned.1.call-done, bf16[1024,1536]{1,0:T(8,128)(2,1)} %copy-done.16, bf16[1024,1536]{1,0:T(8,128)(2,1)S(1)} %get-tuple-element.211), kind=kOutput, calls=%fused_computation.26 | convolution fusion | flops 12899581952 | bytes 23068672 | tf_op jit(solution)/shard_map/dot_general | solution.py:34
  297.2 3.0 fusion.56
  304.3 18.2 %bitcast_convert_fusion = bf16[1024,3072]{1,0:T(8,128)(2,1)} fusion(bf16[2,1024,1024]{2,1,0:T(8,128)(2,1)S(1)} %copy-done.15, bf16[1,1024,3072]{2,1,0:T(8,128)(2,1)} %bitcast.6, bf16[1,1024,3072]{2,1,0:T(8,128)(2,1)} %bitcast.5), kind=kOutput, calls=%fused_computation.4 | convolution fusion | flops 12894339072 | bytes 23068672 | tf_op jit(solution)/shard_map/dot_general | solution.py:28
  322.4 3.3 collective-permute-done.22
  326.9 3.7 reduce-scatter.4.cloned.1.call-done
  330.7 2.9 add_convert_fusion.4
  336.6 10.1 %convolution_convert_fusion.2 = bf16[1024,2048]{1,0:T(8,128)(2,1)S(1)} fusion(bf16[1024,1536]{1,0:T(8,128)(2,1)} %copy-done.17, bf16[2048,1536]{1,0:T(8,128)(2,1)} %all-gather.8.cloned.1.call-done), kind=kOutput, calls=%fused_computation.27 | convolution fusion | flops 6444548096 | bytes 13631488 | tf_op jit(solution)/shard_map/dot_general | solution.py:34
  346.7 3.6 convert_add_fusion.6
  355.3 20.0 %collective-permute-done.26 = bf16[256,2048]{1,0:T(8,128)(2,1)S(1)} collective-permute-done((bf16[256,2048]{1,0:T(8,128)(2,1)S(1)}, bf16[256,2048]{1,0:T(8,128)(2,1)S(1)}, u32[]{:S(2)}, u32[]{:S(2)}) %collective-permute-start.26) | collective-permute-done | bytes 1048608 | tf_op jit(solution)/shard_map/ppermute | solution.py:83
  379.5 6.1 %collective-permute-done.28 = bf16[128,2048]{1,0:T(8,128)(2,1)S(1)} collective-permute-done((bf16[128,2048]{1,0:T(8,128)(2,1)S(1)}, bf16[128,2048]{1,0:T(8,128)(2,1)S(1)}, u32[]{:S(2)}, u32[]{:S(2)}) %collective-permute-start.28) | collective-permute-done | bytes 524320 | tf_op jit(solution)/shard_map/ppermute | solution.py:83
  392.1 4.9 fusion.44.upstream
  397.0 16.4 %attention_backward.1 = (bf16[1024,1024]{1,0:T(8,128)(2,1)}, f32[1,128]{1,0:T(1,128)}, f32[1,128]{1,0:T(1,128)}) custom-call(s32[1]{0:T(128)} %bitcast.place_ref, f32[1024,1024]{1,0:T(8,128)} %fusion.19.raw_query.raw_key.raw_value, f32[1024,1024]{1,0:T(8,128)} %fusion.19.raw_query.raw_key.raw_value, f32[1024,128]{1,0:T(8,128)} %get-tuple-element.286.cosine, ...), custom_call_target="tpu_custom_call" | custom-call | flops 1 | bytes 1 | tf_op jit(solution)/shard_map/attention_backward/pallas_call | solution.py:454
  418.0 6.8 %bitcast_convert_fusion.1 = bf16[1024,1024]{1,0:T(8,128)(2,1)S(1)} fusion(bf16[1,1024,1024]{2,1,0:T(8,128)(2,1)S(1)} %bitcast.58, bf16[1,1024,1024]{2,1,0:T(8,128)(2,1)S(1)} %bitcast.57, bf16[1,1024,1024]{2,1,0:T(8,128)(2,1)} %bitcast.9, bf16[1,1024,1024]{2,1,0:T(8,128)(2,1)S(1)} %maximum_bitcast_fusion.1), kind=kOutput, calls=%fused_computation.25 | convolution fusion | flops 4300210176 | bytes 10485760 | tf_op jit(solution)/shard_map/dot_general | solution.py:28
  424.8 2.9 add_convert_fusion.2
  429.2 6.4 %multiply_reduce_fusion = (f32[2048]{0:T(1024)S(1)}, bf16[1024,2048]{1,0:T(8,128)(2,1)}) fusion(bf16[1024,2048]{1,0:T(8,128)(2,1)S(1)} %copy-done.12, bf16[1024,1024]{1,0:T(8,128)(2,1)S(1)} %copy-done.29, bf16[2048,1536]{1,0:T(8,128)(2,1)S(1)} %bitcast.56), kind=kOutput, calls=%fused_computation.5 | convolution fusion | flops 4305451008 | bytes 14688256 | tf_op jit(solution)/shard_map/dot_general | solution.py:34
  435.6 4.2 bitcast_convert_fusion.2
  439.9 1.9 pad_maximum_fusion.2
  441.8 2.3 convert_add_fusion.4
  445.7 2.9 fusion.54
  455.1 18.7 %collective-permute-done.44 = f32[4352]{0:T(1024)S(1)} collective-permute-done((f32[4352]{0:T(1024)S(1)}, f32[4352]{0:T(1024)S(1)}, u32[]{:S(2)}, u32[]{:S(2)}) %collective-permute-start.44) | collective-permute-done | bytes 17440 | tf_op jit(solution)/shard_map/ppermute | solution.py:83
  475.8 1.9 add_convert_fusion
  479.2 2.1 fusion.58
  481.2 8.2 %collective-permute-done.45 = bf16[128,2048]{1,0:T(8,128)(2,1)S(1)} collective-permute-done((bf16[128,2048]{1,0:T(8,128)(2,1)S(1)}, bf16[128,2048]{1,0:T(8,128)(2,1)S(1)}, u32[]{:S(2)}, u32[]{:S(2)}) %collective-permute-start.45) | collective-permute-done | bytes 524320 | tf_op jit(solution)/shard_map/ppermute | solution.py:83
  489.8 2.2 convert_add_fusion.2
  492.6 6.3 %collective-permute-start.49 = (f32[4352]{0:T(1024)S(1)}, f32[4352]{0:T(1024)S(1)}, u32[]{:S(2)}, u32[]{:S(2)}) collective-permute-start(f32[4352]{0:T(1024)S(1)} %add.303), channel_id=1, source_target_pairs={{0,8},{4,12},{8,16},{12,20},{16,24},{20,28},{24,0},{28,4},{1,9},{5... | collective-permute-start | bytes 52232 | tf_op jit(solution)/shard_map/ppermute | solution.py:69
  499.4 2.8 collective-permute-start.51
  502.3 3.3 fusion.32
  507.5 3.9 reduce-scatter.8.cloned.1.call-done.source
  511.4 2.3 split_columns.1
  (226 shorter events, 89.3 us)
Async XLA Ops:
  7.2 86.3 %all-gather.4.cloned.1.call-start = ((), (), s32[]{:S(2)}) async-start(), calls=%async_computation.3 | async-start | bytes 7077888 | tf_op jit(solution)/shard_map/all_gather | solution.py:189
  9.5 198.6 %all-gather.6.cloned.1.call-start = ((), (), s32[]{:S(2)}) async-start(), calls=%async_computation.4 | async-start | bytes 14155776 | tf_op jit(solution)/shard_map/all_gather | solution.py:189
  12.3 247.8 %all-gather.8.cloned.1.call-start = ((), (), s32[]{:S(2)}) async-start(), calls=%async_computation.5 | async-start | bytes 7077888 | tf_op jit(solution)/shard_map/all_gather | solution.py:189
  14.4 27.2 %collective-permute-start = (bf16[256,2048]{1,0:T(8,128)(2,1)}, bf16[256,2048]{1,0:T(8,128)(2,1)}, u32[]{:S(2)}, u32[]{:S(2)}) collective-permute-start(bf16[256,2048]{1,0:T(8,128)(2,1)} %get-tuple-element.210), channel_id=1, source_target_pairs={{0,1},{1,0},{2,3},{3,2},{4,5},{5,4},{6,7},{7,6},{8,9},{9,8},{10,11... | collective-permute-start | bytes 3145736 | tf_op jit(solution)/shard_map/ppermute | solution.py:83
  17.3 26.4 %collective-permute-start.1 = (bf16[256,2048]{1,0:T(8,128)(2,1)}, bf16[256,2048]{1,0:T(8,128)(2,1)}, u32[]{:S(2)}, u32[]{:S(2)}) collective-permute-start(bf16[256,2048]{1,0:T(8,128)(2,1)} %get-tuple-element.210), channel_id=1, source_target_pairs={{0,2},{1,3},{2,0},{3,1},{4,6},{5,7},{6,4},{7,5},{8,10},{9,11},{10,... | collective-permute-start | bytes 3145736 | tf_op jit(solution)/shard_map/ppermute | solution.py:83
  18.8 45.1 %collective-permute-start.4 = (bf16[256,2048]{1,0:T(8,128)(2,1)S(1)}, bf16[256,2048]{1,0:T(8,128)(2,1)S(1)}, u32[]{:S(2)}, u32[]{:S(2)}) collective-permute-start(bf16[256,2048]{1,0:T(8,128)(2,1)S(1)} %copy-done.5), channel_id=1, source_target_pairs={{0,1},{1,0},{2,3},{3,2},{4,5},{5,4},{6,7},{7,6},{8,9},{9,8},{10,11... | collective-permute-start | bytes 3145736 | tf_op jit(solution)/shard_map/ppermute | solution.py:83
  19.4 46.8 %collective-permute-start.5 = (bf16[256,2048]{1,0:T(8,128)(2,1)S(1)}, bf16[256,2048]{1,0:T(8,128)(2,1)}, u32[]{:S(2)}, u32[]{:S(2)}) collective-permute-start(bf16[256,2048]{1,0:T(8,128)(2,1)S(1)} %copy-done.5), channel_id=1, source_target_pairs={{0,2},{1,3},{2,0},{3,1},{4,6},{5,7},{6,4},{7,5},{8,10},{9,11},{10,... | collective-permute-start | bytes 3145736 | tf_op jit(solution)/shard_map/ppermute | solution.py:83
  44.8 29.6 %collective-permute-start.2 = (bf16[128,2048]{1,0:T(8,128)(2,1)S(1)}, bf16[128,2048]{1,0:T(8,128)(2,1)S(1)}, u32[]{:S(2)}, u32[]{:S(2)}) collective-permute-start(bf16[128,2048]{1,0:T(8,128)(2,1)S(1)} %slice.162), channel_id=1, source_target_pairs={{0,1},{1,0},{2,3},{3,2},{4,5},{5,4},{6,7},{7,6},{8,9},{9,8},{10,11... | collective-permute-start | bytes 1572872 | tf_op jit(solution)/shard_map/ppermute | solution.py:83
  46.0 29.9 %collective-permute-start.3 = (bf16[128,2048]{1,0:T(8,128)(2,1)S(1)}, bf16[128,2048]{1,0:T(8,128)(2,1)S(1)}, u32[]{:S(2)}, u32[]{:S(2)}) collective-permute-start(bf16[128,2048]{1,0:T(8,128)(2,1)S(1)} %slice.163), channel_id=1, source_target_pairs={{0,2},{1,3},{2,0},{3,1},{4,6},{5,7},{6,4},{7,5},{8,10},{9,11},{10,... | collective-permute-start | bytes 1572872 | tf_op jit(solution)/shard_map/ppermute | solution.py:83
  78.6 12.7 %collective-permute-start.6 = (bf16[128,2048]{1,0:T(8,128)(2,1)S(1)}, bf16[128,2048]{1,0:T(8,128)(2,1)S(1)}, u32[]{:S(2)}, u32[]{:S(2)}) collective-permute-start(bf16[128,2048]{1,0:T(8,128)(2,1)S(1)} %slice.165), channel_id=1, source_target_pairs={{0,1},{1,0},{2,3},{3,2},{4,5},{5,4},{6,7},{7,6},{8,9},{9,8},{10,11... | collective-permute-start | bytes 1572872 | tf_op jit(solution)/shard_map/ppermute | solution.py:83
  79.1 12.7 %collective-permute-start.7 = (bf16[128,2048]{1,0:T(8,128)(2,1)S(1)}, bf16[128,2048]{1,0:T(8,128)(2,1)S(1)}, u32[]{:S(2)}, u32[]{:S(2)}) collective-permute-start(bf16[128,2048]{1,0:T(8,128)(2,1)S(1)} %slice.166), channel_id=1, source_target_pairs={{0,2},{1,3},{2,0},{3,1},{4,6},{5,7},{6,4},{7,5},{8,10},{9,11},{10,... | collective-permute-start | bytes 1572872 | tf_op jit(solution)/shard_map/ppermute | solution.py:83
  122.5 14.9 %collective-permute-start.10 = (bf16[128,2048]{1,0:T(8,128)(2,1)S(1)}, bf16[128,2048]{1,0:T(8,128)(2,1)S(1)}, u32[]{:S(2)}, u32[]{:S(2)}) collective-permute-start(bf16[128,2048]{1,0:T(8,128)(2,1)S(1)} %get-tuple-element.266), channel_id=1, source_target_pairs={{0,1},{1,0},{2,3},{3,2},{4,5},{5,4},{6,7},{7,6},{8,9},{9,8},{10,11... | collective-permute-start | bytes 1572872 | tf_op jit(solution)/shard_map/ppermute | solution.py:83
  124.0 14.9 %collective-permute-start.11 = (bf16[128,2048]{1,0:T(8,128)(2,1)S(1)}, bf16[128,2048]{1,0:T(8,128)(2,1)S(1)}, u32[]{:S(2)}, u32[]{:S(2)}) collective-permute-start(bf16[128,2048]{1,0:T(8,128)(2,1)S(1)} %get-tuple-element.265), channel_id=1, source_target_pairs={{0,2},{1,3},{2,0},{3,1},{4,6},{5,7},{6,4},{7,5},{8,10},{9,11},{10,... | collective-permute-start | bytes 1572872 | tf_op jit(solution)/shard_map/ppermute | solution.py:83
  125.5 19.8 %collective-permute-start.8 = (bf16[128,2048]{1,0:T(8,128)(2,1)S(1)}, bf16[128,2048]{1,0:T(8,128)(2,1)S(1)}, u32[]{:S(2)}, u32[]{:S(2)}) collective-permute-start(bf16[128,2048]{1,0:T(8,128)(2,1)S(1)} %get-tuple-element.268), channel_id=1, source_target_pairs={{0,1},{1,0},{2,3},{3,2},{4,5},{5,4},{6,7},{7,6},{8,9},{9,8},{10,11... | collective-permute-start | bytes 1572872 | tf_op jit(solution)/shard_map/ppermute | solution.py:83
  126.1 20.7 %collective-permute-start.9 = (bf16[128,2048]{1,0:T(8,128)(2,1)S(1)}, bf16[128,2048]{1,0:T(8,128)(2,1)S(1)}, u32[]{:S(2)}, u32[]{:S(2)}) collective-permute-start(bf16[128,2048]{1,0:T(8,128)(2,1)S(1)} %get-tuple-element.267), channel_id=1, source_target_pairs={{0,2},{1,3},{2,0},{3,1},{4,6},{5,7},{6,4},{7,5},{8,10},{9,11},{10,... | collective-permute-start | bytes 1572872 | tf_op jit(solution)/shard_map/ppermute | solution.py:83
  147.2 10.3 %collective-permute-start.12 = (bf16[128,2048]{1,0:T(8,128)(2,1)S(1)}, bf16[128,2048]{1,0:T(8,128)(2,1)S(1)}, u32[]{:S(2)}, u32[]{:S(2)}) collective-permute-start(bf16[128,2048]{1,0:T(8,128)(2,1)S(1)} %get-tuple-element.264), channel_id=1, source_target_pairs={{0,2},{1,3},{2,0},{3,1},{4,6},{5,7},{6,4},{7,5},{8,10},{9,11},{10,... | collective-permute-start | bytes 1572872 | tf_op jit(solution)/shard_map/ppermute | solution.py:83
  148.7 9.3 %collective-permute-start.13 = (bf16[128,2048]{1,0:T(8,128)(2,1)S(1)}, bf16[128,2048]{1,0:T(8,128)(2,1)S(1)}, u32[]{:S(2)}, u32[]{:S(2)}) collective-permute-start(bf16[128,2048]{1,0:T(8,128)(2,1)S(1)} %get-tuple-element.263), channel_id=1, source_target_pairs={{0,1},{1,0},{2,3},{3,2},{4,5},{5,4},{6,7},{7,6},{8,9},{9,8},{10,11... | collective-permute-start | bytes 1572872 | tf_op jit(solution)/shard_map/ppermute | solution.py:83
  160.6 20.5 %collective-permute-start.14 = (bf16[256,2048]{1,0:T(8,128)(2,1)}, bf16[256,2048]{1,0:T(8,128)(2,1)S(1)}, u32[]{:S(2)}, u32[]{:S(2)}) collective-permute-start(bf16[256,2048]{1,0:T(8,128)(2,1)} %get-tuple-element.206), channel_id=1, source_target_pairs={{0,1},{1,0},{2,3},{3,2},{4,5},{5,4},{6,7},{7,6},{8,9},{9,8},{10,11... | collective-permute-start | bytes 3145736 | tf_op jit(solution)/shard_map/ppermute | solution.py:83
  161.2 20.5 %collective-permute-start.15 = (bf16[256,2048]{1,0:T(8,128)(2,1)}, bf16[256,2048]{1,0:T(8,128)(2,1)}, u32[]{:S(2)}, u32[]{:S(2)}) collective-permute-start(bf16[256,2048]{1,0:T(8,128)(2,1)} %get-tuple-element.206), channel_id=1, source_target_pairs={{0,2},{1,3},{2,0},{3,1},{4,6},{5,7},{6,4},{7,5},{8,10},{9,11},{10,... | collective-permute-start | bytes 3145736 | tf_op jit(solution)/shard_map/ppermute | solution.py:83
  162.2 168.5 %reduce-scatter.4.cloned.1.call-start = ((), (), s32[]{:S(2)}) async-start(), calls=%async_computation.6 | async-start | bytes 7077888 | tf_op jit(solution)/shard_map/reduce_scatter | solution.py:210
  183.6 9.5 %collective-permute-start.16 = (bf16[128,2048]{1,0:T(8,128)(2,1)}, bf16[128,2048]{1,0:T(8,128)(2,1)}, u32[]{:S(2)}, u32[]{:S(2)}) collective-permute-start(bf16[128,2048]{1,0:T(8,128)(2,1)} %slice.176), channel_id=1, source_target_pairs={{0,1},{1,0},{2,3},{3,2},{4,5},{5,4},{6,7},{7,6},{8,9},{9,8},{10,11... | collective-permute-start | bytes 1572872 | tf_op jit(solution)/shard_map/ppermute | solution.py:83
  185.4 9.5 %collective-permute-start.17 = (bf16[128,2048]{1,0:T(8,128)(2,1)}, bf16[128,2048]{1,0:T(8,128)(2,1)}, u32[]{:S(2)}, u32[]{:S(2)}) collective-permute-start(bf16[128,2048]{1,0:T(8,128)(2,1)} %slice.177), channel_id=1, source_target_pairs={{0,2},{1,3},{2,0},{3,1},{4,6},{5,7},{6,4},{7,5},{8,10},{9,11},{10,... | collective-permute-start | bytes 1572872 | tf_op jit(solution)/shard_map/ppermute | solution.py:83
  201.5 4.2 collective-permute-start.18
  242.6 203.1 %reduce-scatter.6.cloned.1.call-start = ((), (), s32[]{:S(2)}) async-start(), calls=%async_computation.7 | async-start | bytes 7864320 | tf_op jit(solution)/shard_map/reduce_scatter | solution.py:214
  278.4 18.7 %collective-permute-start.19 = (bf16[1024,3072]{1,0:T(8,128)(2,1)}, bf16[1024,3072]{1,0:T(8,128)(2,1)}, u32[]{:S(2)}, u32[]{:S(2)}) collective-permute-start(bf16[1024,3072]{1,0:T(8,128)(2,1)} %pad_maximum_fusion), channel_id=1, source_target_pairs={{0,4},{4,0},{8,12},{12,8},{16,20},{20,16},{24,28},{28,24},{1,5},{5... | collective-permute-start | bytes 18874376 | tf_op jit(solution)/shard_map/ppermute | solution.py:80
  300.2 22.2 %collective-permute-start.20 = (bf16[128,2048]{1,0:T(8,128)(2,1)}, bf16[128,2048]{1,0:T(8,128)(2,1)}, u32[]{:S(2)}, u32[]{:S(2)}) collective-permute-start(bf16[128,2048]{1,0:T(8,128)(2,1)} %get-tuple-element.252), channel_id=1, source_target_pairs={{0,1},{1,0},{2,3},{3,2},{4,5},{5,4},{6,7},{7,6},{8,9},{9,8},{10,11... | collective-permute-start | bytes 1572872 | tf_op jit(solution)/shard_map/ppermute | solution.py:83
  301.7 20.8 %collective-permute-start.21 = (bf16[128,2048]{1,0:T(8,128)(2,1)}, bf16[128,2048]{1,0:T(8,128)(2,1)}, u32[]{:S(2)}, u32[]{:S(2)}) collective-permute-start(bf16[128,2048]{1,0:T(8,128)(2,1)} %get-tuple-element.251), channel_id=1, source_target_pairs={{0,2},{1,3},{2,0},{3,1},{4,6},{5,7},{6,4},{7,5},{8,10},{9,11},{10,... | collective-permute-start | bytes 1572872 | tf_op jit(solution)/shard_map/ppermute | solution.py:83
  303.1 22.6 %collective-permute-start.22 = (bf16[128,2048]{1,0:T(8,128)(2,1)}, bf16[128,2048]{1,0:T(8,128)(2,1)S(1)}, u32[]{:S(2)}, u32[]{:S(2)}) collective-permute-start(bf16[128,2048]{1,0:T(8,128)(2,1)} %get-tuple-element.250), channel_id=1, source_target_pairs={{0,1},{1,0},{2,3},{3,2},{4,5},{5,4},{6,7},{7,6},{8,9},{9,8},{10,11... | collective-permute-start | bytes 1572872 | tf_op jit(solution)/shard_map/ppermute | solution.py:83
  303.7 23.2 %collective-permute-start.23 = (bf16[128,2048]{1,0:T(8,128)(2,1)}, bf16[128,2048]{1,0:T(8,128)(2,1)S(1)}, u32[]{:S(2)}, u32[]{:S(2)}) collective-permute-start(bf16[128,2048]{1,0:T(8,128)(2,1)} %get-tuple-element.249), channel_id=1, source_target_pairs={{0,2},{1,3},{2,0},{3,1},{4,6},{5,7},{6,4},{7,5},{8,10},{9,11},{10,... | collective-permute-start | bytes 1572872 | tf_op jit(solution)/shard_map/ppermute | solution.py:83
  333.6 13.1 %collective-permute-start.24 = (bf16[128,2048]{1,0:T(8,128)(2,1)}, bf16[128,2048]{1,0:T(8,128)(2,1)}, u32[]{:S(2)}, u32[]{:S(2)}) collective-permute-start(bf16[128,2048]{1,0:T(8,128)(2,1)} %get-tuple-element.248), channel_id=1, source_target_pairs={{0,2},{1,3},{2,0},{3,1},{4,6},{5,7},{6,4},{7,5},{8,10},{9,11},{10,... | collective-permute-start | bytes 1572872 | tf_op jit(solution)/shard_map/ppermute | solution.py:83
  335.0 11.6 %collective-permute-start.25 = (bf16[128,2048]{1,0:T(8,128)(2,1)}, bf16[128,2048]{1,0:T(8,128)(2,1)}, u32[]{:S(2)}, u32[]{:S(2)}) collective-permute-start(bf16[128,2048]{1,0:T(8,128)(2,1)} %get-tuple-element.247), channel_id=1, source_target_pairs={{0,1},{1,0},{2,3},{3,2},{4,5},{5,4},{6,7},{7,6},{8,9},{9,8},{10,11... | collective-permute-start | bytes 1572872 | tf_op jit(solution)/shard_map/ppermute | solution.py:83
  336.5 174.8 %reduce-scatter.8.cloned.1.call-start = ((), (), s32[]{:S(2)}) async-start(), calls=%async_computation.8 | async-start | bytes 3932160 | tf_op jit(solution)/shard_map/reduce_scatter | solution.py:214
  346.6 39.8 %copy-start.14 = (bf16[1024,2048]{1,0:T(8,128)(2,1)}, bf16[1024,2048]{1,0:T(8,128)(2,1)S(1)}, u32[]{:S(2)}) copy-start(bf16[1024,2048]{1,0:T(8,128)(2,1)S(1)} %convolution_convert_fusion.2) | copy-start | bytes 12582916
  352.4 22.9 %collective-permute-start.26 = (bf16[256,2048]{1,0:T(8,128)(2,1)S(1)}, bf16[256,2048]{1,0:T(8,128)(2,1)S(1)}, u32[]{:S(2)}, u32[]{:S(2)}) collective-permute-start(bf16[256,2048]{1,0:T(8,128)(2,1)S(1)} %get-tuple-element.204), channel_id=1, source_target_pairs={{0,1},{1,0},{2,3},{3,2},{4,5},{5,4},{6,7},{7,6},{8,9},{9,8},{10,11... | collective-permute-start | bytes 3145736 | tf_op jit(solution)/shard_map/ppermute | solution.py:83
  352.6 22.6 %collective-permute-start.27 = (bf16[256,2048]{1,0:T(8,128)(2,1)S(1)}, bf16[256,2048]{1,0:T(8,128)(2,1)S(1)}, u32[]{:S(2)}, u32[]{:S(2)}) collective-permute-start(bf16[256,2048]{1,0:T(8,128)(2,1)S(1)} %get-tuple-element.204), channel_id=1, source_target_pairs={{0,2},{1,3},{2,0},{3,1},{4,6},{5,7},{6,4},{7,5},{8,10},{9,11},{10,... | collective-permute-start | bytes 3145736 | tf_op jit(solution)/shard_map/ppermute | solution.py:83
  375.3 10.3 %collective-permute-start.28 = (bf16[128,2048]{1,0:T(8,128)(2,1)S(1)}, bf16[128,2048]{1,0:T(8,128)(2,1)S(1)}, u32[]{:S(2)}, u32[]{:S(2)}) collective-permute-start(bf16[128,2048]{1,0:T(8,128)(2,1)S(1)} %slice.188), channel_id=1, source_target_pairs={{0,1},{1,0},{2,3},{3,2},{4,5},{5,4},{6,7},{7,6},{8,9},{9,8},{10,11... | collective-permute-start | bytes 1572872 | tf_op jit(solution)/shard_map/ppermute | solution.py:83
  377.1 9.2 %collective-permute-start.29 = (bf16[128,2048]{1,0:T(8,128)(2,1)S(1)}, bf16[128,2048]{1,0:T(8,128)(2,1)S(1)}, u32[]{:S(2)}, u32[]{:S(2)}) collective-permute-start(bf16[128,2048]{1,0:T(8,128)(2,1)S(1)} %slice.189), channel_id=1, source_target_pairs={{0,2},{1,3},{2,0},{3,1},{4,6},{5,7},{6,4},{7,5},{8,10},{9,11},{10,... | collective-permute-start | bytes 1572872 | tf_op jit(solution)/shard_map/ppermute | solution.py:83
  379.3 37.8 %collective-permute-start.34 = (bf16[1024,1024]{1,0:T(8,128)(2,1)}, bf16[1024,1024]{1,0:T(8,128)(2,1)}, u32[]{:S(2)}, u32[]{:S(2)}) collective-permute-start(bf16[1024,1024]{1,0:T(8,128)(2,1)} %pad_maximum_fusion.5), channel_id=1, source_target_pairs={{0,4},{4,0},{8,12},{12,8},{16,20},{20,16},{24,28},{28,24},{1,5},{5... | collective-permute-start | bytes 6291464 | tf_op jit(solution)/shard_map/ppermute | solution.py:80
  388.0 25.4 %collective-permute-start.30 = (bf16[128,2048]{1,0:T(8,128)(2,1)}, bf16[128,2048]{1,0:T(8,128)(2,1)}, u32[]{:S(2)}, u32[]{:S(2)}) collective-permute-start(bf16[128,2048]{1,0:T(8,128)(2,1)} %get-tuple-element.244), channel_id=1, source_target_pairs={{0,1},{1,0},{2,3},{3,2},{4,5},{5,4},{6,7},{7,6},{8,9},{9,8},{10,11... | collective-permute-start | bytes 1572872 | tf_op jit(solution)/shard_map/ppermute | solution.py:83
  389.1 24.4 %collective-permute-start.31 = (bf16[128,2048]{1,0:T(8,128)(2,1)}, bf16[128,2048]{1,0:T(8,128)(2,1)}, u32[]{:S(2)}, u32[]{:S(2)}) collective-permute-start(bf16[128,2048]{1,0:T(8,128)(2,1)} %get-tuple-element.243), channel_id=1, source_target_pairs={{0,2},{1,3},{2,0},{3,1},{4,6},{5,7},{6,4},{7,5},{8,10},{9,11},{10,... | collective-permute-start | bytes 1572872 | tf_op jit(solution)/shard_map/ppermute | solution.py:83
  389.6 23.8 %collective-permute-start.32 = (bf16[128,2048]{1,0:T(8,128)(2,1)}, bf16[128,2048]{1,0:T(8,128)(2,1)}, u32[]{:S(2)}, u32[]{:S(2)}) collective-permute-start(bf16[128,2048]{1,0:T(8,128)(2,1)} %get-tuple-element.242), channel_id=1, source_target_pairs={{0,1},{1,0},{2,3},{3,2},{4,5},{5,4},{6,7},{7,6},{8,9},{9,8},{10,11... | collective-permute-start | bytes 1572872 | tf_op jit(solution)/shard_map/ppermute | solution.py:83
  390.6 22.9 %collective-permute-start.33 = (bf16[128,2048]{1,0:T(8,128)(2,1)}, bf16[128,2048]{1,0:T(8,128)(2,1)}, u32[]{:S(2)}, u32[]{:S(2)}) collective-permute-start(bf16[128,2048]{1,0:T(8,128)(2,1)} %get-tuple-element.241), channel_id=1, source_target_pairs={{0,2},{1,3},{2,0},{3,1},{4,6},{5,7},{6,4},{7,5},{8,10},{9,11},{10,... | collective-permute-start | bytes 1572872 | tf_op jit(solution)/shard_map/ppermute | solution.py:83
  397.0 16.6 %copy-start.18 = (bf16[1024,256]{1,0:T(8,128)(2,1)S(1)}, bf16[1024,256]{1,0:T(8,128)(2,1)}, u32[]{:S(2)}) copy-start(bf16[1024,256]{1,0:T(8,128)(2,1)} %get-tuple-element.225) | copy-start | bytes 1572868
  397.0 16.6 %copy-start.19 = (bf16[1024,256]{1,0:T(8,128)(2,1)S(1)}, bf16[1024,256]{1,0:T(8,128)(2,1)}, u32[]{:S(2)}) copy-start(bf16[1024,256]{1,0:T(8,128)(2,1)} %get-tuple-element.230) | copy-start | bytes 1572868
  413.5 4.4 collective-permute-start.35
  415.2 20.4 %collective-permute-start.37 = (bf16[1024,512]{1,0:T(8,128)(2,1)}, bf16[1024,512]{1,0:T(8,128)(2,1)}, u32[]{:S(2)}, u32[]{:S(2)}) collective-permute-start(bf16[1024,512]{1,0:T(8,128)(2,1)} %get-tuple-element.119), channel_id=1, source_target_pairs={{0,4},{4,0},{8,12},{12,8},{16,20},{20,16},{24,28},{28,24},{1,5},{5... | collective-permute-start | bytes 3145736 | tf_op jit(solution)/shard_map/ppermute | solution.py:80
  416.5 12.7 %slice-start = ((s8[6291456]{0:T(1024)(128)(4,1)}), s8[4194304]{0:T(1024)(128)(4,1)S(1)}, s32[]{:S(2)}) async-start(s8[6291456]{0:T(1024)(128)(4,1)} %bitcast.55), calls=%async_computation.9 | async-start | bytes 8388608
  416.8 18.8 %collective-permute-start.36 = (bf16[1024,1024]{1,0:T(8,128)(2,1)S(1)}, bf16[1024,1024]{1,0:T(8,128)(2,1)}, u32[]{:S(2)}, u32[]{:S(2)}) collective-permute-start(bf16[1024,1024]{1,0:T(8,128)(2,1)S(1)} %pad_maximum_fusion.6), channel_id=1, source_target_pairs={{0,4},{4,0},{8,12},{12,8},{16,20},{20,16},{24,28},{28,24},{1,5},{5... | collective-permute-start | bytes 6291464 | tf_op jit(solution)/shard_map/ppermute | solution.py:80
  427.7 14.1 %collective-permute-start.38 = (bf16[128,2048]{1,0:T(8,128)(2,1)}, bf16[128,2048]{1,0:T(8,128)(2,1)}, u32[]{:S(2)}, u32[]{:S(2)}) collective-permute-start(bf16[128,2048]{1,0:T(8,128)(2,1)} %get-tuple-element.224), channel_id=1, source_target_pairs={{0,2},{1,3},{2,0},{3,1},{4,6},{5,7},{6,4},{7,5},{8,10},{9,11},{10,... | collective-permute-start | bytes 1572872 | tf_op jit(solution)/shard_map/ppermute | solution.py:83
  428.1 13.8 %collective-permute-start.39 = (bf16[128,2048]{1,0:T(8,128)(2,1)}, bf16[128,2048]{1,0:T(8,128)(2,1)}, u32[]{:S(2)}, u32[]{:S(2)}) collective-permute-start(bf16[128,2048]{1,0:T(8,128)(2,1)} %get-tuple-element.223), channel_id=1, source_target_pairs={{0,1},{1,0},{2,3},{3,2},{4,5},{5,4},{6,7},{7,6},{8,9},{9,8},{10,11... | collective-permute-start | bytes 1572872 | tf_op jit(solution)/shard_map/ppermute | solution.py:83
  448.7 25.1 %collective-permute-start.40 = (bf16[128,2048]{1,0:T(8,128)(2,1)}, bf16[128,2048]{1,0:T(8,128)(2,1)}, u32[]{:S(2)}, u32[]{:S(2)}) collective-permute-start(bf16[128,2048]{1,0:T(8,128)(2,1)} %get-tuple-element.220), channel_id=1, source_target_pairs={{0,1},{1,0},{2,3},{3,2},{4,5},{5,4},{6,7},{7,6},{8,9},{9,8},{10,11... | collective-permute-start | bytes 1572872 | tf_op jit(solution)/shard_map/ppermute | solution.py:83
  449.7 24.1 %collective-permute-start.41 = (bf16[128,2048]{1,0:T(8,128)(2,1)}, bf16[128,2048]{1,0:T(8,128)(2,1)}, u32[]{:S(2)}, u32[]{:S(2)}) collective-permute-start(bf16[128,2048]{1,0:T(8,128)(2,1)} %get-tuple-element.219), channel_id=1, source_target_pairs={{0,2},{1,3},{2,0},{3,1},{4,6},{5,7},{6,4},{7,5},{8,10},{9,11},{10,... | collective-permute-start | bytes 1572872 | tf_op jit(solution)/shard_map/ppermute | solution.py:83
  451.3 22.5 %collective-permute-start.42 = (bf16[128,2048]{1,0:T(8,128)(2,1)}, bf16[128,2048]{1,0:T(8,128)(2,1)}, u32[]{:S(2)}, u32[]{:S(2)}) collective-permute-start(bf16[128,2048]{1,0:T(8,128)(2,1)} %get-tuple-element.218), channel_id=1, source_target_pairs={{0,1},{1,0},{2,3},{3,2},{4,5},{5,4},{6,7},{7,6},{8,9},{9,8},{10,11... | collective-permute-start | bytes 1572872 | tf_op jit(solution)/shard_map/ppermute | solution.py:83
  452.3 21.9 %collective-permute-start.43 = (bf16[128,2048]{1,0:T(8,128)(2,1)}, bf16[128,2048]{1,0:T(8,128)(2,1)}, u32[]{:S(2)}, u32[]{:S(2)}) collective-permute-start(bf16[128,2048]{1,0:T(8,128)(2,1)} %get-tuple-element.217), channel_id=1, source_target_pairs={{0,2},{1,3},{2,0},{3,1},{4,6},{5,7},{6,4},{7,5},{8,10},{9,11},{10,... | collective-permute-start | bytes 1572872 | tf_op jit(solution)/shard_map/ppermute | solution.py:83
  452.7 21.0 %collective-permute-start.44 = (f32[4352]{0:T(1024)S(1)}, f32[4352]{0:T(1024)S(1)}, u32[]{:S(2)}, u32[]{:S(2)}) collective-permute-start(f32[4352]{0:T(1024)S(1)} %pad_maximum_fusion.13), channel_id=1, source_target_pairs={{0,1},{1,0},{2,3},{3,2},{4,5},{5,4},{6,7},{7,6},{8,9},{9,8},{10,11... | collective-permute-start | bytes 52232 | tf_op jit(solution)/shard_map/ppermute | solution.py:83
  453.8 25.4 %copy-start.13 = (bf16[256,3072]{1,0:T(8,128)(2,1)S(1)}, bf16[256,3072]{1,0:T(8,128)(2,1)}, u32[]{:S(2)}) copy-start(bf16[256,3072]{1,0:T(8,128)(2,1)} %reduce-scatter.6.cloned.1.call-done) | copy-start | bytes 4718596
  474.2 7.1 %collective-permute-start.47 = (f32[4352]{0:T(1024)S(1)}, f32[4352]{0:T(1024)S(1)}, u32[]{:S(2)}, u32[]{:S(2)}) collective-permute-start(f32[4352]{0:T(1024)S(1)} %add.297), channel_id=1, source_target_pairs={{0,2},{1,3},{2,0},{3,1},{4,6},{5,7},{6,4},{7,5},{8,10},{9,11},{10,... | collective-permute-start | bytes 52232 | tf_op jit(solution)/shard_map/ppermute | solution.py:83
  477.7 11.7 %collective-permute-start.45 = (bf16[128,2048]{1,0:T(8,128)(2,1)S(1)}, bf16[128,2048]{1,0:T(8,128)(2,1)S(1)}, u32[]{:S(2)}, u32[]{:S(2)}) collective-permute-start(bf16[128,2048]{1,0:T(8,128)(2,1)S(1)} %get-tuple-element.216), channel_id=1, source_target_pairs={{0,2},{1,3},{2,0},{3,1},{4,6},{5,7},{6,4},{7,5},{8,10},{9,11},{10,... | collective-permute-start | bytes 1572872 | tf_op jit(solution)/shard_map/ppermute | solution.py:83
  478.2 11.5 %collective-permute-start.46 = (bf16[128,2048]{1,0:T(8,128)(2,1)S(1)}, bf16[128,2048]{1,0:T(8,128)(2,1)S(1)}, u32[]{:S(2)}, u32[]{:S(2)}) collective-permute-start(bf16[128,2048]{1,0:T(8,128)(2,1)S(1)} %get-tuple-element.215), channel_id=1, source_target_pairs={{0,1},{1,0},{2,3},{3,2},{4,5},{5,4},{6,7},{7,6},{8,9},{9,8},{10,11... | collective-permute-start | bytes 1572872 | tf_op jit(solution)/shard_map/ppermute | solution.py:83
  489.7 12.6 %copy-start.7 = (bf16[256,2048]{1,0:T(8,128)(2,1)S(1)}, bf16[256,2048]{1,0:T(8,128)(2,1)}, u32[]{:S(2)}) copy-start(bf16[256,2048]{1,0:T(8,128)(2,1)} %param.27) | copy-start | bytes 3145732
  489.7 2.9 collective-permute-start.48
  492.6 13.0 %collective-permute-start.49 = (f32[4352]{0:T(1024)S(1)}, f32[4352]{0:T(1024)S(1)}, u32[]{:S(2)}, u32[]{:S(2)}) collective-permute-start(f32[4352]{0:T(1024)S(1)} %add.303), channel_id=1, source_target_pairs={{0,8},{4,12},{8,16},{12,20},{16,24},{20,28},{24,0},{28,4},{1,9},{5... | collective-permute-start | bytes 52232 | tf_op jit(solution)/shard_map/ppermute | solution.py:69
  498.9 7.3 %collective-permute-start.50 = (f32[4352]{0:T(1024)S(1)}, f32[4352]{0:T(1024)S(1)}, u32[]{:S(2)}, u32[]{:S(2)}) collective-permute-start(f32[4352]{0:T(1024)S(1)} %add.303), channel_id=1, source_target_pairs={{0,16},{4,20},{8,24},{12,28},{16,0},{20,4},{24,8},{28,12},{1,17},{... | collective-permute-start | bytes 52232 | tf_op jit(solution)/shard_map/ppermute | solution.py:69
  499.4 6.8 %collective-permute-start.51 = (f32[4352]{0:T(1024)S(1)}, f32[4352]{0:T(1024)S(1)}, u32[]{:S(2)}, u32[]{:S(2)}) collective-permute-start(f32[4352]{0:T(1024)S(1)} %add.303), channel_id=1, source_target_pairs={{0,24},{4,28},{8,0},{12,4},{16,8},{20,12},{24,16},{28,20},{1,25},{... | collective-permute-start | bytes 52232 | tf_op jit(solution)/shard_map/ppermute | solution.py:69
  (27 other events, 180.2 us)
Sparse Core Ops, SparseCore 0:
  10.3 67.4 all-gather.3
  80.0 115.3 all-gather.5
  197.0 62.9 all-gather.7
  262.2 68.4 reduce-scatter.3
  336.7 107.2 reduce-scatter.5
  446.1 65.1 reduce-scatter.7

commit v7 on v6

--- a/solution.py
+++ b/solution.py
@@ -172,6 +172,14 @@
             return total
         last = lax.optimization_barrier(self.last_sends(partial, first))
         return self.combined(partial, first, last)
+
+    def scatter_last(self, partial, first):
+        if self.tensor_size != 4:
+            return (self.scatter_second(partial, first),)
+        return lax.optimization_barrier(self.last_sends(partial, first))
+
+    def scatter_end(self, partial, first, last):
+        return last[0] if self.tensor_size != 4 else self.combined(partial, first, last)
 
     def scatter_beside(self, partial, terms):
         if self.tensor_size != 4:
@@ -576,9 +584,8 @@
     )
     middle_first = links.scatter_first(middle_partial)
     feed_term = weight_term(middle_columns, jnp.stack([feed_grad, other_grad]))
-    feed_term, middle_first, down_sum = lax.optimization_barrier(
-        (feed_term, middle_first, down_sum)
-    )
+    feed_term, middle_first = lax.optimization_barrier((feed_term, middle_first))
+    feed_term, down_sum = lax.optimization_barrier((feed_term, down_sum))
     feed_sum = links.scatter_chips(feed_term)
     middle_normed_grad = links.scatter_second(middle_partial, middle_first)
     feed_partial = contract_last(active, wide_down).astype(jnp.bfloat16)
@@ -610,7 +617,7 @@
     output_term = weight_term(links.both_columns(branch_grad), links.both_cores(attended_rows))
     attention_term = weight_term(links.both_columns(normed_rows), links.both_cores(raw_grad))
     feed_first, attention_term = lax.optimization_barrier((feed_first, attention_term))
-    feed_branch = links.scatter_second(feed_partial, feed_first)
+    feed_last = links.scatter_last(feed_partial, feed_first)
     raw_grad, attention_term = lax.optimization_barrier((raw_grad, attention_term))
     input_partial = contract_last(raw_grad, wide_attention).astype(jnp.bfloat16)
     mixing_term = jnp.concatenate([attention_term, output_term], axis=1)
@@ -621,12 +628,12 @@
     terms = jnp.concatenate(
         [input_gain_term, middle_gain_term, query_gain_term[0], key_gain_term[0]]
     )
-    mixing_term, feed_sum, feed_branch, input_partial, terms = lax.optimization_barrier(
-        (mixing_term, feed_sum, feed_branch, input_partial, terms)
+    mixing_term, feed_sum, feed_last, input_partial, terms = lax.optimization_barrier(
+        (mixing_term, feed_sum, feed_last, input_partial, terms)
     )
     mixing_sum = links.scatter_chips(mixing_term)
     input_normed_grad, terms = links.scatter_beside(input_partial, terms)
-    layer_output = middle + feed_branch
+    layer_output = middle + links.scatter_end(feed_partial, feed_first, feed_last)
     tokens_grad = middle_grad + norm_backward(input_normed_grad, scaled_in, inverse_in, input_gain)
     terms = links.total_dp(terms)
     width = tokens.shape[1]

time: 528 us -> 522 us (0.989)
    unnamed x79 -> x75, local copies, waits for them, and re-layouts: 22.5 us -> 25.1 us
  transfers between devices with their start and end apart: 58 -> 58, of which waited for: 33 -> 35; matrix products, arithmetic and copies ran while one was open for 41% -> 41% of each run, Pallas kernels for 6% -> 6%
where the time goes in v7:
time: 522 us; the launch traced here: 516 us
  waiting for transfers between devices  197 us (38%)
  matrix products  125 us (24%)
  starting transfers between devices  50.4 us (10%)
  local copies, waits for them, and re-layouts  47.6 us (9%)
  other arithmetic  47.3 us (9%)
  Pallas kernels  33.4 us (6%)
  between operations  15.2 us (3%)
    ppermute x42, waiting for transfers between devices, across(): lax.ppermute(value, 'tensor', [(place, place ^ bit) for place in range(se...  167 us
    dot_general x4, matrix products, matmul(): return jnp.dot(left, right, preferred_element_type=jnp.float32)  47.1 us
    ppermute x42, starting transfers between devices, across(): lax.ppermute(value, 'tensor', [(place, place ^ bit) for place in range(se...  43.1 us
    dot_general x4, matrix products, contract_last(): lax.dot_general(left, right, (((1,), (1,)), ((), ())), preferred_element_...  38.2 us
    dot_general x3, matrix products, weight_term(): lax.dot_general(left, right, (((0, 1), (0, 1)), ((), ())), preferred_elem...  28.7 us
    unnamed x75, local copies, waits for them, and re-layouts  25.1 us
    all_gather x3, waiting for transfers between devices, gather_weight(): return lax.all_gather(shard, 'dp', axis=0, tiled=True)  17.1 us
    pallas_call x1, Pallas kernels, backward(): pl.pallas_call(self.backward_kernel, name='attention_backward', cost_esti...  16.6 us
  transfers between devices with their start and end apart: 58, of which 35 were waited for; matrix products, arithmetic and copies ran while one was open for 41% of the time, Pallas kernels for 6%

profile of v7, /device:TPU:0, one launch (start us, length us, event | category | flops | bytes accessed | tf_op | source)
XLA Modules:
  0.0 515.6 jit_solution(13211005537338986810)
XLA Ops:
  7.2 2.2 pad_maximum_fusion.8
  9.5 2.7 pad_maximum_fusion.7
  14.3 2.9 collective-permute-start
  19.5 1.9 fusion.47
  21.4 20.1 %collective-permute-done = bf16[256,2048]{1,0:T(8,128)(2,1)} collective-permute-done((bf16[256,2048]{1,0:T(8,128)(2,1)}, bf16[256,2048]{1,0:T(8,128)(2,1)}, u32[]{:S(2)}, u32[]{:S(2)}) %collective-permute-start) | collective-permute-done | bytes 1048608 | tf_op jit(solution)/shard_map/ppermute | solution.py:83
  41.6 2.1 collective-permute-done.1
  45.9 2.1 collective-permute-start.3
  49.1 14.8 %collective-permute-done.4 = bf16[256,2048]{1,0:T(8,128)(2,1)S(1)} collective-permute-done((bf16[256,2048]{1,0:T(8,128)(2,1)S(1)}, bf16[256,2048]{1,0:T(8,128)(2,1)S(1)}, u32[]{:S(2)}, u32[]{:S(2)}) %collective-permute-start.4) | collective-permute-done | bytes 1048608 | tf_op jit(solution)/shard_map/ppermute | solution.py:83
  63.9 2.2 collective-permute-done.5
  66.1 2.3 constant_dynamic-update-slice_fusion.3
  68.5 2.3 constant_dynamic-update-slice_fusion.2
  70.8 3.5 collective-permute-done.2
  79.0 1.8 collective-permute-start.7
  83.2 2.3 constant_dynamic-update-slice_fusion.7
  85.6 5.6 %collective-permute-done.6 = bf16[128,2048]{1,0:T(8,128)(2,1)S(1)} collective-permute-done((bf16[128,2048]{1,0:T(8,128)(2,1)S(1)}, bf16[128,2048]{1,0:T(8,128)(2,1)S(1)}, u32[]{:S(2)}, u32[]{:S(2)}) %collective-permute-start.6) | collective-permute-done | bytes 524320 | tf_op jit(solution)/shard_map/ppermute | solution.py:83
  93.4 10.0 %fusion.19.raw_query.raw_key.raw_value = f32[1024,1024]{1,0:T(8,128)} fusion(bf16[1024,2048]{1,0:T(8,128)(2,1)} %constant_dynamic-update-slice_fusion, bf16[2048,1536]{1,0:T(8,128)(2,1)} %all-gather.4.cloned.1.call-done), kind=kOutput, calls=%fused_computation.31 | convolution fusion | flops 4294967296 | bytes 12582912 | tf_op jit(solution)/shard_map/dot_general | solution.py:18
  103.3 14.5 %attention_forward.1 = (bf16[1024,512]{1,0:T(8,128)(2,1)}, bf16[1024,256]{1,0:T(8,128)(2,1)}, bf16[1024,256]{1,0:T(8,128)(2,1)}, bf16[1024,512]{1,0:T(8,128)(2,1)}, f32[2,2,1024]{2,1,0:T(2,128)}) custom-call(s32[1]{0:T(128)} %bitcast.place_ref, f32[1024,1024]{1,0:T(8,128)} %fusion.19.raw_query.raw_key.raw_value, ...), custom_call_target="tpu_custom_call" | custom-call | flops 4294967296 | bytes 8388608 | tf_op jit(solution)/shard_map/attention_forward/pallas_call | solution.py:346
  117.9 4.4 convolution_convert_fusion.3
  126.6 10.8 %collective-permute-done.10 = bf16[128,2048]{1,0:T(8,128)(2,1)S(1)} collective-permute-done((bf16[128,2048]{1,0:T(8,128)(2,1)S(1)}, bf16[128,2048]{1,0:T(8,128)(2,1)S(1)}, u32[]{:S(2)}, u32[]{:S(2)}) %collective-permute-start.10) | collective-permute-done | bytes 524320 | tf_op jit(solution)/shard_map/ppermute | solution.py:83
  138.8 6.4 %collective-permute-done.8 = bf16[128,2048]{1,0:T(8,128)(2,1)S(1)} collective-permute-done((bf16[128,2048]{1,0:T(8,128)(2,1)S(1)}, bf16[128,2048]{1,0:T(8,128)(2,1)S(1)}, u32[]{:S(2)}, u32[]{:S(2)}) %collective-permute-start.8) | collective-permute-done | bytes 524320 | tf_op jit(solution)/shard_map/ppermute | solution.py:83
  149.3 8.1 %collective-permute-done.12 = bf16[128,2048]{1,0:T(8,128)(2,1)S(1)} collective-permute-done((bf16[128,2048]{1,0:T(8,128)(2,1)S(1)}, bf16[128,2048]{1,0:T(8,128)(2,1)S(1)}, u32[]{:S(2)}, u32[]{:S(2)}) %collective-permute-start.12) | collective-permute-done | bytes 524320 | tf_op jit(solution)/shard_map/ppermute | solution.py:83
  162.2 18.5 %collective-permute-done.14 = bf16[256,2048]{1,0:T(8,128)(2,1)S(1)} collective-permute-done((bf16[256,2048]{1,0:T(8,128)(2,1)}, bf16[256,2048]{1,0:T(8,128)(2,1)S(1)}, u32[]{:S(2)}, u32[]{:S(2)}) %collective-permute-start.14) | collective-permute-done | bytes 1048608 | tf_op jit(solution)/shard_map/ppermute | solution.py:83
  181.7 1.9 slice.176
  187.9 2.3 constant_dynamic-update-slice_fusion.12
  190.3 2.8 collective-permute-done.16
  194.7 1.9 constant_dynamic-update-slice_fusion.11
  196.7 1.9 constant_dynamic-update-slice_fusion.10
  198.6 2.5 constant_dynamic-slice_fusion.23
  201.7 3.9 collective-permute-done.18
  205.6 2.4 pad_maximum_fusion.1
  208.0 17.6 %fusion.61 = f32[1024,3072]{1,0:T(8,128)S(1)} fusion(bf16[1024,2048]{1,0:T(8,128)(2,1)} %constant_dynamic-update-slice_fusion.10, bf16[2048,3072]{1,0:T(8,128)(2,1)} %all-gather.6.cloned.1.call-done), kind=kOutput, calls=%fused_computation.157 | convolution fusion | flops 12884901888 | bytes 29360128 | tf_op jit(solution)/shard_map/dot_general | solution.py:18
  225.5 2.0 multiply_convert_fusion.2
  227.5 2.6 copy-done.4
  231.8 11.0 %convolution_convert_fusion = bf16[2048,1536]{1,0:T(8,128)(2,1)} fusion(bf16[1024,2048]{1,0:T(8,128)(2,1)} %constant_dynamic-update-slice_fusion.5, bf16[1024,1536]{1,0:T(8,128)(2,1)S(1)} %multiply_convert_fusion.2), kind=kOutput, calls=%fused_computation.6 | convolution fusion | flops 6445596672 | bytes 13631488 | tf_op jit(solution)/shard_map/dot_general | solution.py:22
  242.9 17.1 %all-gather.8.cloned.1.call-done = bf16[2048,1536]{1,0:T(8,128)(2,1)} async-done(((bf16[256,1536]{1,0:T(8,128)(2,1)}), bf16[2048,1536]{1,0:T(8,128)(2,1)}) %all-gather.8.cloned.1.call-update) | async-done | bytes 6291472 | tf_op jit(solution)/shard_map/all_gather | solution.py:197
  260.0 14.7 %multiply_convert_fusion.1 = (bf16[1024,1536]{1,0:T(8,128)(2,1)S(1)}, bf16[1024,1536]{1,0:T(8,128)(2,1)S(1)}) fusion(f32[1024,3072]{1,0:T(8,128)} %copy-done.4, bf16[1024,2048]{1,0:T(8,128)(2,1)} %constant_dynamic-update-slice_fusion.5, bf16[2048,1536]{1,0:T(8,128)(2,1)} %all-gather.8.cloned.1.call-done), kind=kOutput, calls=%fused_computation.9 | convolution fusion | flops 6462898176 | bytes 29360128 | tf_op jit(solution)/shard_map/dot_general | solution.py:18
  274.7 4.0 pad_maximum_fusion
  279.5 17.7 %convolution_convert_fusion.1 = bf16[1024,2048]{1,0:T(8,128)(2,1)S(1)} fusion(bf16[2048,3072]{1,0:T(8,128)(2,1)} %all-gather.6.cloned.1.call-done, bf16[1024,1536]{1,0:T(8,128)(2,1)} %copy-done.17, bf16[1024,1536]{1,0:T(8,128)(2,1)} %copy-done.16), kind=kOutput, calls=%fused_computation.26 | convolution fusion | flops 12899581952 | bytes 23068672 | tf_op jit(solution)/shard_map/dot_general | solution.py:34
  297.3 2.1 copy-done.14
  304.8 18.0 %bitcast_convert_fusion = bf16[1024,3072]{1,0:T(8,128)(2,1)} fusion(bf16[2,1024,1024]{2,1,0:T(8,128)(2,1)S(1)} %copy-done.15, bf16[1,1024,3072]{2,1,0:T(8,128)(2,1)} %bitcast.6, bf16[1,1024,3072]{2,1,0:T(8,128)(2,1)} %bitcast.5), kind=kOutput, calls=%fused_computation.4 | convolution fusion | flops 12894339072 | bytes 23068672 | tf_op jit(solution)/shard_map/dot_general | solution.py:28
  322.8 3.5 collective-permute-done.22
  327.5 2.9 add_convert_fusion.4
  332.7 9.8 %convolution_convert_fusion.2 = bf16[1024,2048]{1,0:T(8,128)(2,1)S(1)} fusion(bf16[1024,1536]{1,0:T(8,128)(2,1)} %copy-done.18, bf16[2048,1536]{1,0:T(8,128)(2,1)} %all-gather.8.cloned.1.call-done), kind=kOutput, calls=%fused_computation.27 | convolution fusion | flops 6444548096 | bytes 13631488 | tf_op jit(solution)/shard_map/dot_general | solution.py:34
  344.9 2.0 convert_add_fusion.6
  352.1 20.1 %collective-permute-done.26 = bf16[256,2048]{1,0:T(8,128)(2,1)S(1)} collective-permute-done((bf16[256,2048]{1,0:T(8,128)(2,1)S(1)}, bf16[256,2048]{1,0:T(8,128)(2,1)S(1)}, u32[]{:S(2)}, u32[]{:S(2)}) %collective-permute-start.26) | collective-permute-done | bytes 1048608 | tf_op jit(solution)/shard_map/ppermute | solution.py:83
  376.6 7.8 %collective-permute-done.28 = bf16[128,2048]{1,0:T(8,128)(2,1)S(1)} collective-permute-done((bf16[128,2048]{1,0:T(8,128)(2,1)S(1)}, bf16[128,2048]{1,0:T(8,128)(2,1)S(1)}, u32[]{:S(2)}, u32[]{:S(2)}) %collective-permute-start.28) | collective-permute-done | bytes 524320 | tf_op jit(solution)/shard_map/ppermute | solution.py:83
  390.4 4.9 fusion.44.upstream
  395.3 16.6 %attention_backward.1 = (bf16[1024,1024]{1,0:T(8,128)(2,1)}, f32[1,128]{1,0:T(1,128)}, f32[1,128]{1,0:T(1,128)}) custom-call(s32[1]{0:T(128)} %bitcast.place_ref, f32[1024,1024]{1,0:T(8,128)} %fusion.19.raw_query.raw_key.raw_value, f32[1024,1024]{1,0:T(8,128)} %fusion.19.raw_query.raw_key.raw_value, f32[1024,128]{1,0:T(8,128)} %get-tuple-element.290.cosine, ...), custom_call_target="tpu_custom_call" | custom-call | flops 1 | bytes 1 | tf_op jit(solution)/shard_map/attention_backward/pallas_call | solution.py:462
  412.1 2.0 maximum_bitcast_fusion.1
  416.9 6.5 %bitcast_convert_fusion.1 = bf16[1024,1024]{1,0:T(8,128)(2,1)S(1)} fusion(bf16[1,1024,1024]{2,1,0:T(8,128)(2,1)S(1)} %bitcast.58, bf16[1,1024,1024]{2,1,0:T(8,128)(2,1)S(1)} %bitcast.57, bf16[1,1024,1024]{2,1,0:T(8,128)(2,1)} %bitcast.9, bf16[1,1024,1024]{2,1,0:T(8,128)(2,1)S(1)} %maximum_bitcast_fusion.1), kind=kOutput, calls=%fused_computation.25 | convolution fusion | flops 4300210176 | bytes 10485760 | tf_op jit(solution)/shard_map/dot_general | solution.py:28
  423.4 2.9 add_convert_fusion.2
  428.2 6.3 %multiply_reduce_fusion = (f32[2048]{0:T(1024)S(1)}, bf16[1024,2048]{1,0:T(8,128)(2,1)}) fusion(bf16[1024,2048]{1,0:T(8,128)(2,1)S(1)} %copy-done.10, bf16[1024,1024]{1,0:T(8,128)(2,1)S(1)} %copy-done.27, bf16[2048,1536]{1,0:T(8,128)(2,1)S(1)} %bitcast.56), kind=kOutput, calls=%fused_computation.5 | convolution fusion | flops 4305451008 | bytes 14688256 | tf_op jit(solution)/shard_map/dot_general | solution.py:34
  434.7 4.2 bitcast_convert_fusion.2
  438.9 1.9 pad_maximum_fusion.2
  442.1 2.6 convert_element_type.283
  452.0 2.1 fusion.58
  454.0 17.8 %collective-permute-done.44 = f32[4352]{0:T(1024)S(1)} collective-permute-done((f32[4352]{0:T(1024)S(1)}, f32[4352]{0:T(1024)S(1)}, u32[]{:S(2)}, u32[]{:S(2)}) %collective-permute-start.44) | collective-permute-done | bytes 17440 | tf_op jit(solution)/shard_map/ppermute | solution.py:83
  475.9 2.4 convert_add_fusion.4
  478.3 8.8 %collective-permute-done.45 = bf16[128,2048]{1,0:T(8,128)(2,1)S(1)} collective-permute-done((bf16[128,2048]{1,0:T(8,128)(2,1)S(1)}, bf16[128,2048]{1,0:T(8,128)(2,1)S(1)}, u32[]{:S(2)}, u32[]{:S(2)}) %collective-permute-start.45) | collective-permute-done | bytes 524320 | tf_op jit(solution)/shard_map/ppermute | solution.py:83
  489.9 1.9 collective-permute-start.50
  491.8 2.5 collective-permute-start.51
  494.3 3.7 fusion.32
  499.3 6.9 %reduce-scatter.8.cloned.1.call-done.source = bf16[256,1536]{1,0:T(8,128)(2,1)} async-done(((bf16[1024,1536]{1,0:T(8,128)(2,1)}), bf16[256,1536]{1,0:T(8,128)(2,1)}) %reduce-scatter.8.cloned.1.call-update) | async-done | bytes 786448 | tf_op jit(solution)/shard_map/reduce_scatter | solution.py:222
  506.3 2.3 split_columns.1
  (221 shorter events, 90.0 us)
Async XLA Ops:
  7.2 86.2 %all-gather.4.cloned.1.call-start = ((), (), s32[]{:S(2)}) async-start(), calls=%async_computation.3 | async-start | bytes 7077888 | tf_op jit(solution)/shard_map/all_gather | solution.py:197
  9.5 198.5 %all-gather.6.cloned.1.call-start = ((), (), s32[]{:S(2)}) async-start(), calls=%async_computation.4 | async-start | bytes 14155776 | tf_op jit(solution)/shard_map/all_gather | solution.py:197
  12.3 247.8 %all-gather.8.cloned.1.call-start = ((), (), s32[]{:S(2)}) async-start(), calls=%async_computation.5 | async-start | bytes 7077888 | tf_op jit(solution)/shard_map/all_gather | solution.py:197
  14.3 27.2 %collective-permute-start = (bf16[256,2048]{1,0:T(8,128)(2,1)}, bf16[256,2048]{1,0:T(8,128)(2,1)}, u32[]{:S(2)}, u32[]{:S(2)}) collective-permute-start(bf16[256,2048]{1,0:T(8,128)(2,1)} %get-tuple-element.214), channel_id=1, source_target_pairs={{0,1},{1,0},{2,3},{3,2},{4,5},{5,4},{6,7},{7,6},{8,9},{9,8},{10,11... | collective-permute-start | bytes 3145736 | tf_op jit(solution)/shard_map/ppermute | solution.py:83
  17.3 26.4 %collective-permute-start.1 = (bf16[256,2048]{1,0:T(8,128)(2,1)}, bf16[256,2048]{1,0:T(8,128)(2,1)}, u32[]{:S(2)}, u32[]{:S(2)}) collective-permute-start(bf16[256,2048]{1,0:T(8,128)(2,1)} %get-tuple-element.214), channel_id=1, source_target_pairs={{0,2},{1,3},{2,0},{3,1},{4,6},{5,7},{6,4},{7,5},{8,10},{9,11},{10,... | collective-permute-start | bytes 3145736 | tf_op jit(solution)/shard_map/ppermute | solution.py:83
  18.8 45.1 %collective-permute-start.4 = (bf16[256,2048]{1,0:T(8,128)(2,1)S(1)}, bf16[256,2048]{1,0:T(8,128)(2,1)S(1)}, u32[]{:S(2)}, u32[]{:S(2)}) collective-permute-start(bf16[256,2048]{1,0:T(8,128)(2,1)S(1)} %copy-done.5), channel_id=1, source_target_pairs={{0,1},{1,0},{2,3},{3,2},{4,5},{5,4},{6,7},{7,6},{8,9},{9,8},{10,11... | collective-permute-start | bytes 3145736 | tf_op jit(solution)/shard_map/ppermute | solution.py:83
  19.3 46.8 %collective-permute-start.5 = (bf16[256,2048]{1,0:T(8,128)(2,1)S(1)}, bf16[256,2048]{1,0:T(8,128)(2,1)}, u32[]{:S(2)}, u32[]{:S(2)}) collective-permute-start(bf16[256,2048]{1,0:T(8,128)(2,1)S(1)} %copy-done.5), channel_id=1, source_target_pairs={{0,2},{1,3},{2,0},{3,1},{4,6},{5,7},{6,4},{7,5},{8,10},{9,11},{10,... | collective-permute-start | bytes 3145736 | tf_op jit(solution)/shard_map/ppermute | solution.py:83
  44.8 29.6 %collective-permute-start.2 = (bf16[128,2048]{1,0:T(8,128)(2,1)S(1)}, bf16[128,2048]{1,0:T(8,128)(2,1)S(1)}, u32[]{:S(2)}, u32[]{:S(2)}) collective-permute-start(bf16[128,2048]{1,0:T(8,128)(2,1)S(1)} %slice.162), channel_id=1, source_target_pairs={{0,1},{1,0},{2,3},{3,2},{4,5},{5,4},{6,7},{7,6},{8,9},{9,8},{10,11... | collective-permute-start | bytes 1572872 | tf_op jit(solution)/shard_map/ppermute | solution.py:83
  45.9 29.9 %collective-permute-start.3 = (bf16[128,2048]{1,0:T(8,128)(2,1)S(1)}, bf16[128,2048]{1,0:T(8,128)(2,1)S(1)}, u32[]{:S(2)}, u32[]{:S(2)}) collective-permute-start(bf16[128,2048]{1,0:T(8,128)(2,1)S(1)} %slice.163), channel_id=1, source_target_pairs={{0,2},{1,3},{2,0},{3,1},{4,6},{5,7},{6,4},{7,5},{8,10},{9,11},{10,... | collective-permute-start | bytes 1572872 | tf_op jit(solution)/shard_map/ppermute | solution.py:83
  78.6 12.6 %collective-permute-start.6 = (bf16[128,2048]{1,0:T(8,128)(2,1)S(1)}, bf16[128,2048]{1,0:T(8,128)(2,1)S(1)}, u32[]{:S(2)}, u32[]{:S(2)}) collective-permute-start(bf16[128,2048]{1,0:T(8,128)(2,1)S(1)} %slice.165), channel_id=1, source_target_pairs={{0,1},{1,0},{2,3},{3,2},{4,5},{5,4},{6,7},{7,6},{8,9},{9,8},{10,11... | collective-permute-start | bytes 1572872 | tf_op jit(solution)/shard_map/ppermute | solution.py:83
  79.0 12.7 %collective-permute-start.7 = (bf16[128,2048]{1,0:T(8,128)(2,1)S(1)}, bf16[128,2048]{1,0:T(8,128)(2,1)S(1)}, u32[]{:S(2)}, u32[]{:S(2)}) collective-permute-start(bf16[128,2048]{1,0:T(8,128)(2,1)S(1)} %slice.166), channel_id=1, source_target_pairs={{0,2},{1,3},{2,0},{3,1},{4,6},{5,7},{6,4},{7,5},{8,10},{9,11},{10,... | collective-permute-start | bytes 1572872 | tf_op jit(solution)/shard_map/ppermute | solution.py:83
  122.5 14.9 %collective-permute-start.10 = (bf16[128,2048]{1,0:T(8,128)(2,1)S(1)}, bf16[128,2048]{1,0:T(8,128)(2,1)S(1)}, u32[]{:S(2)}, u32[]{:S(2)}) collective-permute-start(bf16[128,2048]{1,0:T(8,128)(2,1)S(1)} %get-tuple-element.270), channel_id=1, source_target_pairs={{0,1},{1,0},{2,3},{3,2},{4,5},{5,4},{6,7},{7,6},{8,9},{9,8},{10,11... | collective-permute-start | bytes 1572872 | tf_op jit(solution)/shard_map/ppermute | solution.py:83
  124.0 14.9 %collective-permute-start.11 = (bf16[128,2048]{1,0:T(8,128)(2,1)S(1)}, bf16[128,2048]{1,0:T(8,128)(2,1)S(1)}, u32[]{:S(2)}, u32[]{:S(2)}) collective-permute-start(bf16[128,2048]{1,0:T(8,128)(2,1)S(1)} %get-tuple-element.269), channel_id=1, source_target_pairs={{0,2},{1,3},{2,0},{3,1},{4,6},{5,7},{6,4},{7,5},{8,10},{9,11},{10,... | collective-permute-start | bytes 1572872 | tf_op jit(solution)/shard_map/ppermute | solution.py:83
  125.5 19.8 %collective-permute-start.8 = (bf16[128,2048]{1,0:T(8,128)(2,1)S(1)}, bf16[128,2048]{1,0:T(8,128)(2,1)S(1)}, u32[]{:S(2)}, u32[]{:S(2)}) collective-permute-start(bf16[128,2048]{1,0:T(8,128)(2,1)S(1)} %get-tuple-element.272), channel_id=1, source_target_pairs={{0,1},{1,0},{2,3},{3,2},{4,5},{5,4},{6,7},{7,6},{8,9},{9,8},{10,11... | collective-permute-start | bytes 1572872 | tf_op jit(solution)/shard_map/ppermute | solution.py:83
  126.0 20.7 %collective-permute-start.9 = (bf16[128,2048]{1,0:T(8,128)(2,1)S(1)}, bf16[128,2048]{1,0:T(8,128)(2,1)S(1)}, u32[]{:S(2)}, u32[]{:S(2)}) collective-permute-start(bf16[128,2048]{1,0:T(8,128)(2,1)S(1)} %get-tuple-element.271), channel_id=1, source_target_pairs={{0,2},{1,3},{2,0},{3,1},{4,6},{5,7},{6,4},{7,5},{8,10},{9,11},{10,... | collective-permute-start | bytes 1572872 | tf_op jit(solution)/shard_map/ppermute | solution.py:83
  147.1 10.2 %collective-permute-start.12 = (bf16[128,2048]{1,0:T(8,128)(2,1)S(1)}, bf16[128,2048]{1,0:T(8,128)(2,1)S(1)}, u32[]{:S(2)}, u32[]{:S(2)}) collective-permute-start(bf16[128,2048]{1,0:T(8,128)(2,1)S(1)} %get-tuple-element.268), channel_id=1, source_target_pairs={{0,2},{1,3},{2,0},{3,1},{4,6},{5,7},{6,4},{7,5},{8,10},{9,11},{10,... | collective-permute-start | bytes 1572872 | tf_op jit(solution)/shard_map/ppermute | solution.py:83
  148.7 9.3 %collective-permute-start.13 = (bf16[128,2048]{1,0:T(8,128)(2,1)S(1)}, bf16[128,2048]{1,0:T(8,128)(2,1)S(1)}, u32[]{:S(2)}, u32[]{:S(2)}) collective-permute-start(bf16[128,2048]{1,0:T(8,128)(2,1)S(1)} %get-tuple-element.267), channel_id=1, source_target_pairs={{0,1},{1,0},{2,3},{3,2},{4,5},{5,4},{6,7},{7,6},{8,9},{9,8},{10,11... | collective-permute-start | bytes 1572872 | tf_op jit(solution)/shard_map/ppermute | solution.py:83
  160.6 20.1 %collective-permute-start.14 = (bf16[256,2048]{1,0:T(8,128)(2,1)}, bf16[256,2048]{1,0:T(8,128)(2,1)S(1)}, u32[]{:S(2)}, u32[]{:S(2)}) collective-permute-start(bf16[256,2048]{1,0:T(8,128)(2,1)} %get-tuple-element.210), channel_id=1, source_target_pairs={{0,1},{1,0},{2,3},{3,2},{4,5},{5,4},{6,7},{7,6},{8,9},{9,8},{10,11... | collective-permute-start | bytes 3145736 | tf_op jit(solution)/shard_map/ppermute | solution.py:83
  161.1 20.6 %collective-permute-start.15 = (bf16[256,2048]{1,0:T(8,128)(2,1)}, bf16[256,2048]{1,0:T(8,128)(2,1)}, u32[]{:S(2)}, u32[]{:S(2)}) collective-permute-start(bf16[256,2048]{1,0:T(8,128)(2,1)} %get-tuple-element.210), channel_id=1, source_target_pairs={{0,2},{1,3},{2,0},{3,1},{4,6},{5,7},{6,4},{7,5},{8,10},{9,11},{10,... | collective-permute-start | bytes 3145736 | tf_op jit(solution)/shard_map/ppermute | solution.py:83
  162.2 170.2 %reduce-scatter.4.cloned.1.call-start = ((), (), s32[]{:S(2)}) async-start(), calls=%async_computation.6 | async-start | bytes 7077888 | tf_op jit(solution)/shard_map/reduce_scatter | solution.py:218
  183.6 9.5 %collective-permute-start.16 = (bf16[128,2048]{1,0:T(8,128)(2,1)}, bf16[128,2048]{1,0:T(8,128)(2,1)}, u32[]{:S(2)}, u32[]{:S(2)}) collective-permute-start(bf16[128,2048]{1,0:T(8,128)(2,1)} %slice.176), channel_id=1, source_target_pairs={{0,1},{1,0},{2,3},{3,2},{4,5},{5,4},{6,7},{7,6},{8,9},{9,8},{10,11... | collective-permute-start | bytes 1572872 | tf_op jit(solution)/shard_map/ppermute | solution.py:83
  185.3 9.5 %collective-permute-start.17 = (bf16[128,2048]{1,0:T(8,128)(2,1)}, bf16[128,2048]{1,0:T(8,128)(2,1)}, u32[]{:S(2)}, u32[]{:S(2)}) collective-permute-start(bf16[128,2048]{1,0:T(8,128)(2,1)} %slice.177), channel_id=1, source_target_pairs={{0,2},{1,3},{2,0},{3,1},{4,6},{5,7},{6,4},{7,5},{8,10},{9,11},{10,... | collective-permute-start | bytes 1572872 | tf_op jit(solution)/shard_map/ppermute | solution.py:83
  201.3 4.2 collective-permute-start.18
  242.8 199.1 %reduce-scatter.6.cloned.1.call-start = ((), (), s32[]{:S(2)}) async-start(), calls=%async_computation.7 | async-start | bytes 7864320 | tf_op jit(solution)/shard_map/reduce_scatter | solution.py:222
  279.3 18.0 %collective-permute-start.19 = (bf16[1024,3072]{1,0:T(8,128)(2,1)}, bf16[1024,3072]{1,0:T(8,128)(2,1)}, u32[]{:S(2)}, u32[]{:S(2)}) collective-permute-start(bf16[1024,3072]{1,0:T(8,128)(2,1)} %pad_maximum_fusion), channel_id=1, source_target_pairs={{0,4},{4,0},{8,12},{12,8},{16,20},{20,16},{24,28},{28,24},{1,5},{5... | collective-permute-start | bytes 18874376 | tf_op jit(solution)/shard_map/ppermute | solution.py:80
  300.8 22.0 %collective-permute-start.20 = (bf16[128,2048]{1,0:T(8,128)(2,1)}, bf16[128,2048]{1,0:T(8,128)(2,1)}, u32[]{:S(2)}, u32[]{:S(2)}) collective-permute-start(bf16[128,2048]{1,0:T(8,128)(2,1)} %get-tuple-element.256), channel_id=1, source_target_pairs={{0,1},{1,0},{2,3},{3,2},{4,5},{5,4},{6,7},{7,6},{8,9},{9,8},{10,11... | collective-permute-start | bytes 1572872 | tf_op jit(solution)/shard_map/ppermute | solution.py:83
  302.2 20.6 %collective-permute-start.21 = (bf16[128,2048]{1,0:T(8,128)(2,1)}, bf16[128,2048]{1,0:T(8,128)(2,1)}, u32[]{:S(2)}, u32[]{:S(2)}) collective-permute-start(bf16[128,2048]{1,0:T(8,128)(2,1)} %get-tuple-element.255), channel_id=1, source_target_pairs={{0,2},{1,3},{2,0},{3,1},{4,6},{5,7},{6,4},{7,5},{8,10},{9,11},{10,... | collective-permute-start | bytes 1572872 | tf_op jit(solution)/shard_map/ppermute | solution.py:83
  303.7 22.6 %collective-permute-start.22 = (bf16[128,2048]{1,0:T(8,128)(2,1)}, bf16[128,2048]{1,0:T(8,128)(2,1)S(1)}, u32[]{:S(2)}, u32[]{:S(2)}) collective-permute-start(bf16[128,2048]{1,0:T(8,128)(2,1)} %get-tuple-element.254), channel_id=1, source_target_pairs={{0,1},{1,0},{2,3},{3,2},{4,5},{5,4},{6,7},{7,6},{8,9},{9,8},{10,11... | collective-permute-start | bytes 1572872 | tf_op jit(solution)/shard_map/ppermute | solution.py:83
  304.3 23.2 %collective-permute-start.23 = (bf16[128,2048]{1,0:T(8,128)(2,1)}, bf16[128,2048]{1,0:T(8,128)(2,1)S(1)}, u32[]{:S(2)}, u32[]{:S(2)}) collective-permute-start(bf16[128,2048]{1,0:T(8,128)(2,1)} %get-tuple-element.253), channel_id=1, source_target_pairs={{0,2},{1,3},{2,0},{3,1},{4,6},{5,7},{6,4},{7,5},{8,10},{9,11},{10,... | collective-permute-start | bytes 1572872 | tf_op jit(solution)/shard_map/ppermute | solution.py:83
  330.4 13.3 %collective-permute-start.24 = (bf16[128,2048]{1,0:T(8,128)(2,1)}, bf16[128,2048]{1,0:T(8,128)(2,1)}, u32[]{:S(2)}, u32[]{:S(2)}) collective-permute-start(bf16[128,2048]{1,0:T(8,128)(2,1)} %get-tuple-element.252), channel_id=1, source_target_pairs={{0,2},{1,3},{2,0},{3,1},{4,6},{5,7},{6,4},{7,5},{8,10},{9,11},{10,... | collective-permute-start | bytes 1572872 | tf_op jit(solution)/shard_map/ppermute | solution.py:83
  331.9 13.1 %collective-permute-start.25 = (bf16[128,2048]{1,0:T(8,128)(2,1)}, bf16[128,2048]{1,0:T(8,128)(2,1)}, u32[]{:S(2)}, u32[]{:S(2)}) collective-permute-start(bf16[128,2048]{1,0:T(8,128)(2,1)} %get-tuple-element.251), channel_id=1, source_target_pairs={{0,1},{1,0},{2,3},{3,2},{4,5},{5,4},{6,7},{7,6},{8,9},{9,8},{10,11... | collective-permute-start | bytes 1572872 | tf_op jit(solution)/shard_map/ppermute | solution.py:83
  332.4 173.8 %reduce-scatter.8.cloned.1.call-start = ((), (), s32[]{:S(2)}) async-start(), calls=%async_computation.8 | async-start | bytes 3932160 | tf_op jit(solution)/shard_map/reduce_scatter | solution.py:222
  342.5 42.4 %copy-start.12 = (bf16[1024,2048]{1,0:T(8,128)(2,1)}, bf16[1024,2048]{1,0:T(8,128)(2,1)S(1)}, u32[]{:S(2)}) copy-start(bf16[1024,2048]{1,0:T(8,128)(2,1)S(1)} %convolution_convert_fusion.2) | copy-start | bytes 12582916
  349.1 23.1 %collective-permute-start.26 = (bf16[256,2048]{1,0:T(8,128)(2,1)S(1)}, bf16[256,2048]{1,0:T(8,128)(2,1)S(1)}, u32[]{:S(2)}, u32[]{:S(2)}) collective-permute-start(bf16[256,2048]{1,0:T(8,128)(2,1)S(1)} %get-tuple-element.208), channel_id=1, source_target_pairs={{0,1},{1,0},{2,3},{3,2},{4,5},{5,4},{6,7},{7,6},{8,9},{9,8},{10,11... | collective-permute-start | bytes 3145736 | tf_op jit(solution)/shard_map/ppermute | solution.py:83
  349.8 23.3 %collective-permute-start.27 = (bf16[256,2048]{1,0:T(8,128)(2,1)S(1)}, bf16[256,2048]{1,0:T(8,128)(2,1)S(1)}, u32[]{:S(2)}, u32[]{:S(2)}) collective-permute-start(bf16[256,2048]{1,0:T(8,128)(2,1)S(1)} %get-tuple-element.208), channel_id=1, source_target_pairs={{0,2},{1,3},{2,0},{3,1},{4,6},{5,7},{6,4},{7,5},{8,10},{9,11},{10,... | collective-permute-start | bytes 3145736 | tf_op jit(solution)/shard_map/ppermute | solution.py:83
  373.1 11.3 %collective-permute-start.28 = (bf16[128,2048]{1,0:T(8,128)(2,1)S(1)}, bf16[128,2048]{1,0:T(8,128)(2,1)S(1)}, u32[]{:S(2)}, u32[]{:S(2)}) collective-permute-start(bf16[128,2048]{1,0:T(8,128)(2,1)S(1)} %slice.188), channel_id=1, source_target_pairs={{0,1},{1,0},{2,3},{3,2},{4,5},{5,4},{6,7},{7,6},{8,9},{9,8},{10,11... | collective-permute-start | bytes 1572872 | tf_op jit(solution)/shard_map/ppermute | solution.py:83
  374.1 10.6 %collective-permute-start.29 = (bf16[128,2048]{1,0:T(8,128)(2,1)S(1)}, bf16[128,2048]{1,0:T(8,128)(2,1)S(1)}, u32[]{:S(2)}, u32[]{:S(2)}) collective-permute-start(bf16[128,2048]{1,0:T(8,128)(2,1)S(1)} %slice.189), channel_id=1, source_target_pairs={{0,2},{1,3},{2,0},{3,1},{4,6},{5,7},{6,4},{7,5},{8,10},{9,11},{10,... | collective-permute-start | bytes 1572872 | tf_op jit(solution)/shard_map/ppermute | solution.py:83
  376.4 39.6 %collective-permute-start.34 = (bf16[1024,1024]{1,0:T(8,128)(2,1)}, bf16[1024,1024]{1,0:T(8,128)(2,1)}, u32[]{:S(2)}, u32[]{:S(2)}) collective-permute-start(bf16[1024,1024]{1,0:T(8,128)(2,1)} %pad_maximum_fusion.5), channel_id=1, source_target_pairs={{0,4},{4,0},{8,12},{12,8},{16,20},{20,16},{24,28},{28,24},{1,5},{5... | collective-permute-start | bytes 6291464 | tf_op jit(solution)/shard_map/ppermute | solution.py:80
  386.4 25.6 %collective-permute-start.30 = (bf16[128,2048]{1,0:T(8,128)(2,1)}, bf16[128,2048]{1,0:T(8,128)(2,1)}, u32[]{:S(2)}, u32[]{:S(2)}) collective-permute-start(bf16[128,2048]{1,0:T(8,128)(2,1)} %get-tuple-element.248), channel_id=1, source_target_pairs={{0,1},{1,0},{2,3},{3,2},{4,5},{5,4},{6,7},{7,6},{8,9},{9,8},{10,11... | collective-permute-start | bytes 1572872 | tf_op jit(solution)/shard_map/ppermute | solution.py:83
  387.8 24.1 %collective-permute-start.31 = (bf16[128,2048]{1,0:T(8,128)(2,1)}, bf16[128,2048]{1,0:T(8,128)(2,1)}, u32[]{:S(2)}, u32[]{:S(2)}) collective-permute-start(bf16[128,2048]{1,0:T(8,128)(2,1)} %get-tuple-element.247), channel_id=1, source_target_pairs={{0,2},{1,3},{2,0},{3,1},{4,6},{5,7},{6,4},{7,5},{8,10},{9,11},{10,... | collective-permute-start | bytes 1572872 | tf_op jit(solution)/shard_map/ppermute | solution.py:83
  388.3 23.7 %collective-permute-start.32 = (bf16[128,2048]{1,0:T(8,128)(2,1)}, bf16[128,2048]{1,0:T(8,128)(2,1)}, u32[]{:S(2)}, u32[]{:S(2)}) collective-permute-start(bf16[128,2048]{1,0:T(8,128)(2,1)} %get-tuple-element.246), channel_id=1, source_target_pairs={{0,1},{1,0},{2,3},{3,2},{4,5},{5,4},{6,7},{7,6},{8,9},{9,8},{10,11... | collective-permute-start | bytes 1572872 | tf_op jit(solution)/shard_map/ppermute | solution.py:83
  388.9 23.1 %collective-permute-start.33 = (bf16[128,2048]{1,0:T(8,128)(2,1)}, bf16[128,2048]{1,0:T(8,128)(2,1)}, u32[]{:S(2)}, u32[]{:S(2)}) collective-permute-start(bf16[128,2048]{1,0:T(8,128)(2,1)} %get-tuple-element.245), channel_id=1, source_target_pairs={{0,2},{1,3},{2,0},{3,1},{4,6},{5,7},{6,4},{7,5},{8,10},{9,11},{10,... | collective-permute-start | bytes 1572872 | tf_op jit(solution)/shard_map/ppermute | solution.py:83
  412.0 4.4 collective-permute-start.35
  414.0 20.5 %collective-permute-start.37 = (bf16[1024,512]{1,0:T(8,128)(2,1)}, bf16[1024,512]{1,0:T(8,128)(2,1)}, u32[]{:S(2)}, u32[]{:S(2)}) collective-permute-start(bf16[1024,512]{1,0:T(8,128)(2,1)} %get-tuple-element.121), channel_id=1, source_target_pairs={{0,4},{4,0},{8,12},{12,8},{16,20},{20,16},{24,28},{28,24},{1,5},{5... | collective-permute-start | bytes 3145736 | tf_op jit(solution)/shard_map/ppermute | solution.py:80
  415.3 12.9 %slice-start = ((s8[6291456]{0:T(1024)(128)(4,1)}), s8[2097152]{0:T(1024)(128)(4,1)S(1)}, s32[]{:S(2)}) async-start(s8[6291456]{0:T(1024)(128)(4,1)} %bitcast.55), calls=%async_computation.9 | async-start | bytes 4194304
  415.6 19.0 %collective-permute-start.36 = (bf16[1024,1024]{1,0:T(8,128)(2,1)S(1)}, bf16[1024,1024]{1,0:T(8,128)(2,1)}, u32[]{:S(2)}, u32[]{:S(2)}) collective-permute-start(bf16[1024,1024]{1,0:T(8,128)(2,1)S(1)} %pad_maximum_fusion.6), channel_id=1, source_target_pairs={{0,4},{4,0},{8,12},{12,8},{16,20},{20,16},{24,28},{28,24},{1,5},{5... | collective-permute-start | bytes 6291464 | tf_op jit(solution)/shard_map/ppermute | solution.py:80
  416.9 11.3 %slice-start.1 = ((s8[6291456]{0:T(1024)(128)(4,1)}), s8[4194304]{0:T(1024)(128)(4,1)S(1)}, s32[]{:S(2)}) async-start(s8[6291456]{0:T(1024)(128)(4,1)} %bitcast.55), calls=%async_computation.10 | async-start | bytes 8388608
  426.3 14.5 %collective-permute-start.38 = (bf16[128,2048]{1,0:T(8,128)(2,1)}, bf16[128,2048]{1,0:T(8,128)(2,1)}, u32[]{:S(2)}, u32[]{:S(2)}) collective-permute-start(bf16[128,2048]{1,0:T(8,128)(2,1)} %get-tuple-element.228), channel_id=1, source_target_pairs={{0,2},{1,3},{2,0},{3,1},{4,6},{5,7},{6,4},{7,5},{8,10},{9,11},{10,... | collective-permute-start | bytes 1572872 | tf_op jit(solution)/shard_map/ppermute | solution.py:83
  426.8 14.1 %collective-permute-start.39 = (bf16[128,2048]{1,0:T(8,128)(2,1)}, bf16[128,2048]{1,0:T(8,128)(2,1)}, u32[]{:S(2)}, u32[]{:S(2)}) collective-permute-start(bf16[128,2048]{1,0:T(8,128)(2,1)} %get-tuple-element.227), channel_id=1, source_target_pairs={{0,1},{1,0},{2,3},{3,2},{4,5},{5,4},{6,7},{7,6},{8,9},{9,8},{10,11... | collective-permute-start | bytes 1572872 | tf_op jit(solution)/shard_map/ppermute | solution.py:83
  446.4 27.7 %copy-start.13 = (bf16[1024,2048]{1,0:T(8,128)(2,1)S(1)}, bf16[1024,2048]{1,0:T(8,128)(2,1)}, u32[]{:S(2)}) copy-start(bf16[1024,2048]{1,0:T(8,128)(2,1)} %get-tuple-element.188) | copy-start | bytes 12582916
  446.4 25.5 %collective-permute-start.40 = (bf16[128,2048]{1,0:T(8,128)(2,1)S(1)}, bf16[128,2048]{1,0:T(8,128)(2,1)S(1)}, u32[]{:S(2)}, u32[]{:S(2)}) collective-permute-start(bf16[128,2048]{1,0:T(8,128)(2,1)S(1)} %get-tuple-element.224), channel_id=1, source_target_pairs={{0,1},{1,0},{2,3},{3,2},{4,5},{5,4},{6,7},{7,6},{8,9},{9,8},{10,11... | collective-permute-start | bytes 1572872 | tf_op jit(solution)/shard_map/ppermute | solution.py:83
  447.9 23.9 %collective-permute-start.41 = (bf16[128,2048]{1,0:T(8,128)(2,1)S(1)}, bf16[128,2048]{1,0:T(8,128)(2,1)S(1)}, u32[]{:S(2)}, u32[]{:S(2)}) collective-permute-start(bf16[128,2048]{1,0:T(8,128)(2,1)S(1)} %get-tuple-element.223), channel_id=1, source_target_pairs={{0,2},{1,3},{2,0},{3,1},{4,6},{5,7},{6,4},{7,5},{8,10},{9,11},{10,... | collective-permute-start | bytes 1572872 | tf_op jit(solution)/shard_map/ppermute | solution.py:83
  449.4 22.5 %collective-permute-start.42 = (bf16[128,2048]{1,0:T(8,128)(2,1)S(1)}, bf16[128,2048]{1,0:T(8,128)(2,1)S(1)}, u32[]{:S(2)}, u32[]{:S(2)}) collective-permute-start(bf16[128,2048]{1,0:T(8,128)(2,1)S(1)} %get-tuple-element.222), channel_id=1, source_target_pairs={{0,1},{1,0},{2,3},{3,2},{4,5},{5,4},{6,7},{7,6},{8,9},{9,8},{10,11... | collective-permute-start | bytes 1572872 | tf_op jit(solution)/shard_map/ppermute | solution.py:83
  449.9 22.6 %collective-permute-start.43 = (bf16[128,2048]{1,0:T(8,128)(2,1)S(1)}, bf16[128,2048]{1,0:T(8,128)(2,1)S(1)}, u32[]{:S(2)}, u32[]{:S(2)}) collective-permute-start(bf16[128,2048]{1,0:T(8,128)(2,1)S(1)} %get-tuple-element.221), channel_id=1, source_target_pairs={{0,2},{1,3},{2,0},{3,1},{4,6},{5,7},{6,4},{7,5},{8,10},{9,11},{10,... | collective-permute-start | bytes 1572872 | tf_op jit(solution)/shard_map/ppermute | solution.py:83
  450.5 21.3 %collective-permute-start.44 = (f32[4352]{0:T(1024)S(1)}, f32[4352]{0:T(1024)S(1)}, u32[]{:S(2)}, u32[]{:S(2)}) collective-permute-start(f32[4352]{0:T(1024)S(1)} %pad_maximum_fusion.12), channel_id=1, source_target_pairs={{0,1},{1,0},{2,3},{3,2},{4,5},{5,4},{6,7},{7,6},{8,9},{9,8},{10,11... | collective-permute-start | bytes 52232 | tf_op jit(solution)/shard_map/ppermute | solution.py:83
  472.6 5.8 %collective-permute-start.47 = (f32[4352]{0:T(1024)S(1)}, f32[4352]{0:T(1024)S(1)}, u32[]{:S(2)}, u32[]{:S(2)}) collective-permute-start(f32[4352]{0:T(1024)S(1)} %add.297), channel_id=1, source_target_pairs={{0,2},{1,3},{2,0},{3,1},{4,6},{5,7},{6,4},{7,5},{8,10},{9,11},{10,... | collective-permute-start | bytes 52232 | tf_op jit(solution)/shard_map/ppermute | solution.py:83
  474.4 12.6 %collective-permute-start.45 = (bf16[128,2048]{1,0:T(8,128)(2,1)S(1)}, bf16[128,2048]{1,0:T(8,128)(2,1)S(1)}, u32[]{:S(2)}, u32[]{:S(2)}) collective-permute-start(bf16[128,2048]{1,0:T(8,128)(2,1)S(1)} %get-tuple-element.220), channel_id=1, source_target_pairs={{0,2},{1,3},{2,0},{3,1},{4,6},{5,7},{6,4},{7,5},{8,10},{9,11},{10,... | collective-permute-start | bytes 1572872 | tf_op jit(solution)/shard_map/ppermute | solution.py:83
  475.1 12.7 %copy-start.3 = (bf16[256,2048]{1,0:T(8,128)(2,1)S(1)}, bf16[256,2048]{1,0:T(8,128)(2,1)}, u32[]{:S(2)}) copy-start(bf16[256,2048]{1,0:T(8,128)(2,1)} %param.14) | copy-start | bytes 3145732
  475.1 12.7 %copy-start.23 = (f32[256]{0:T(256)S(1)}, f32[256]{0:T(256)}, u32[]{:S(2)}) copy-start(f32[256]{0:T(256)} %copy-done.22) | copy-start | bytes 3076
  475.1 12.1 %collective-permute-start.46 = (bf16[128,2048]{1,0:T(8,128)(2,1)S(1)}, bf16[128,2048]{1,0:T(8,128)(2,1)S(1)}, u32[]{:S(2)}, u32[]{:S(2)}) collective-permute-start(bf16[128,2048]{1,0:T(8,128)(2,1)S(1)} %get-tuple-element.219), channel_id=1, source_target_pairs={{0,1},{1,0},{2,3},{3,2},{4,5},{5,4},{6,7},{7,6},{8,9},{9,8},{10,11... | collective-permute-start | bytes 1572872 | tf_op jit(solution)/shard_map/ppermute | solution.py:83
  487.1 1.2 collective-permute-start.48
  488.4 9.6 %collective-permute-start.49 = (f32[4352]{0:T(1024)S(1)}, f32[4352]{0:T(1024)S(1)}, u32[]{:S(2)}, u32[]{:S(2)}) collective-permute-start(f32[4352]{0:T(1024)S(1)} %add.303), channel_id=1, source_target_pairs={{0,8},{4,12},{8,16},{12,20},{16,24},{20,28},{24,0},{28,4},{1,9},{5... | collective-permute-start | bytes 52232 | tf_op jit(solution)/shard_map/ppermute | solution.py:69
  489.9 8.1 %collective-permute-start.50 = (f32[4352]{0:T(1024)S(1)}, f32[4352]{0:T(1024)S(1)}, u32[]{:S(2)}, u32[]{:S(2)}) collective-permute-start(f32[4352]{0:T(1024)S(1)} %add.303), channel_id=1, source_target_pairs={{0,16},{4,20},{8,24},{12,28},{16,0},{20,4},{24,8},{28,12},{1,17},{... | collective-permute-start | bytes 52232 | tf_op jit(solution)/shard_map/ppermute | solution.py:69
  491.8 6.3 %collective-permute-start.51 = (f32[4352]{0:T(1024)S(1)}, f32[4352]{0:T(1024)S(1)}, u32[]{:S(2)}, u32[]{:S(2)}) collective-permute-start(f32[4352]{0:T(1024)S(1)} %add.303), channel_id=1, source_target_pairs={{0,24},{4,28},{8,0},{12,4},{16,8},{20,12},{24,16},{28,20},{1,25},{... | collective-permute-start | bytes 52232 | tf_op jit(solution)/shard_map/ppermute | solution.py:69
  (25 other events, 139.3 us)
Sparse Core Ops, SparseCore 0:
  10.3 67.4 all-gather.3
  80.0 115.3 all-gather.5
  197.0 62.9 all-gather.7
  262.2 68.4 reduce-scatter.3
  332.8 109.1 reduce-scatter.5
  444.2 62.0 reduce-scatter.7

commit v8 on v7

--- a/solution.py
+++ b/solution.py
@@ -263,6 +263,28 @@
         name="split_columns",
         out_shape=[jax.ShapeDtypeStruct((rows.shape[0], width), jnp.float32) for width in widths],
     )(rows)
+
+
+def long_product(left, right):
+    rows, depth = left.shape
+    columns = right.shape[0]
+    width = math.gcd(512, columns)
+
+    def kernel(left_ref, right_ref, target):
+        target[...] = product(left_ref[...], right_ref[...], 1, 1).astype(target.dtype)
+
+    return pl.pallas_call(
+        kernel,
+        name="long_product",
+        grid=(columns // width,),
+        in_specs=[
+            pl.BlockSpec((rows, depth), lambda column: (0, 0)),
+            pl.BlockSpec((width, depth), lambda column: (column, 0)),
+        ],
+        out_specs=pl.BlockSpec((rows, width), lambda column: (0, column)),
+        out_shape=jax.ShapeDtypeStruct((rows, columns), left.dtype),
+        cost_estimate=pl.CostEstimate(flops=1, transcendentals=0, bytes_accessed=1),
+    )(left, right)
 
 
 class Attention:
@@ -576,8 +598,7 @@
     ).astype(jnp.bfloat16)
     upward_grad = (active_grad * silu_gate).astype(jnp.bfloat16)
     feed_grad = jnp.concatenate([gate_grad, upward_grad], axis=1)
-    middle_partial = contract_last(feed_grad, wide_feed)
-    middle_partial = middle_partial.astype(jnp.bfloat16)
+    middle_partial = long_product(feed_grad, wide_feed)
     other_grad = links.other_core(feed_grad)
     feed_grad, other_grad, middle_partial = lax.optimization_barrier(
         (feed_grad, other_grad, middle_partial)
@@ -588,7 +609,7 @@
     feed_term, down_sum = lax.optimization_barrier((feed_term, down_sum))
     feed_sum = links.scatter_chips(feed_term)
     middle_normed_grad = links.scatter_second(middle_partial, middle_first)
-    feed_partial = contract_last(active, wide_down).astype(jnp.bfloat16)
+    feed_partial = long_product(active, wide_down)
     middle_normed_grad, feed_partial = lax.optimization_barrier((middle_normed_grad, feed_partial))
     middle_gain_term = jnp.sum(middle_normed_grad * scaled_mid, axis=0)
     middle_grad = own_cotangent.astype(jnp.float32) + norm_backward(

time: 522 us -> 524 us (level)
  Pallas kernels: 33.4 us -> 63.7 us
  matrix products: 125 us -> 97 us
    pallas_call x0 -> x2, Pallas kernels: none -> 30.5 us  [long_product(): pl.pallas_call(kernel, name='long_product', grid=(columns // width,), in_...]
    dot_general x4 -> x2, matrix products: 38.2 us -> 10.5 us  [contract_last(): lax.dot_general(left, right, (((1,), (1,)), ((), ())), preferred_element_...]
    unnamed x75 -> x69, local copies, waits for them, and re-layouts: 25.1 us -> 22.6 us
  transfers between devices with their start and end apart: 58 -> 58, of which waited for: 35 -> 35; matrix products, arithmetic and copies ran while one was open for 41% -> 35% of each run, Pallas kernels for 6% -> 12%
where the time goes in v8:
time: 524 us; the launch traced here: 517 us
  waiting for transfers between devices  196 us (37%)
  matrix products  97 us (19%)
  Pallas kernels  63.7 us (12%)
  starting transfers between devices  51.7 us (10%)
  other arithmetic  46.8 us (9%)
  local copies, waits for them, and re-layouts  46.6 us (9%)
  between operations  15.1 us (3%)
    ppermute x42, waiting for transfers between devices, across(): lax.ppermute(value, 'tensor', [(place, place ^ bit) for place in range(se...  164 us
    dot_general x4, matrix products, matmul(): return jnp.dot(left, right, preferred_element_type=jnp.float32)  46.8 us
    ppermute x42, starting transfers between devices, across(): lax.ppermute(value, 'tensor', [(place, place ^ bit) for place in range(se...  42.8 us
    pallas_call x2, Pallas kernels, long_product(): pl.pallas_call(kernel, name='long_product', grid=(columns // width,), in_...  30.5 us
    dot_general x3, matrix products, weight_term(): lax.dot_general(left, right, (((0, 1), (0, 1)), ((), ())), preferred_elem...  28.7 us
    unnamed x69, local copies, waits for them, and re-layouts  22.6 us
    all_gather x3, waiting for transfers between devices, gather_weight(): return lax.all_gather(shard, 'dp', axis=0, tiled=True)  17.4 us
    pallas_call x1, Pallas kernels, backward(): pl.pallas_call(self.backward_kernel, name='attention_backward', cost_esti...  16.3 us
  transfers between devices with their start and end apart: 58, of which 35 were waited for; matrix products, arithmetic and copies ran while one was open for 35% of the time, Pallas kernels for 12%

profile of v8, /device:TPU:0, one launch (start us, length us, event | category | flops | bytes accessed | tf_op | source)
XLA Modules:
  0.0 516.9 jit_solution(16152189423565103281)
XLA Ops:
  7.2 2.2 pad_maximum_fusion.8
  9.5 2.7 pad_maximum_fusion.7
  14.4 2.9 collective-permute-start
  19.5 1.9 fusion.47
  21.4 20.1 %collective-permute-done = bf16[256,2048]{1,0:T(8,128)(2,1)} collective-permute-done((bf16[256,2048]{1,0:T(8,128)(2,1)}, bf16[256,2048]{1,0:T(8,128)(2,1)}, u32[]{:S(2)}, u32[]{:S(2)}) %collective-permute-start) | collective-permute-done | bytes 1048608 | tf_op jit(solution)/shard_map/ppermute | solution.py:83
  41.6 2.1 collective-permute-done.1
  46.0 2.1 collective-permute-start.3
  49.2 14.8 %collective-permute-done.4 = bf16[256,2048]{1,0:T(8,128)(2,1)S(1)} collective-permute-done((bf16[256,2048]{1,0:T(8,128)(2,1)S(1)}, bf16[256,2048]{1,0:T(8,128)(2,1)S(1)}, u32[]{:S(2)}, u32[]{:S(2)}) %collective-permute-start.4) | collective-permute-done | bytes 1048608 | tf_op jit(solution)/shard_map/ppermute | solution.py:83
  64.0 2.2 collective-permute-done.5
  66.2 2.3 constant_dynamic-update-slice_fusion.3
  68.5 2.3 constant_dynamic-update-slice_fusion.2
  70.8 3.6 collective-permute-done.2
  83.2 2.3 constant_dynamic-update-slice_fusion.7
  85.5 5.7 %collective-permute-done.6 = bf16[128,2048]{1,0:T(8,128)(2,1)S(1)} collective-permute-done((bf16[128,2048]{1,0:T(8,128)(2,1)S(1)}, bf16[128,2048]{1,0:T(8,128)(2,1)S(1)}, u32[]{:S(2)}, u32[]{:S(2)}) %collective-permute-start.6) | collective-permute-done | bytes 524320 | tf_op jit(solution)/shard_map/ppermute | solution.py:83
  93.4 10.0 %fusion.19.raw_query.raw_key.raw_value = f32[1024,1024]{1,0:T(8,128)} fusion(bf16[1024,2048]{1,0:T(8,128)(2,1)} %constant_dynamic-update-slice_fusion, bf16[2048,1536]{1,0:T(8,128)(2,1)} %all-gather.4.cloned.1.call-done), kind=kOutput, calls=%fused_computation.29 | convolution fusion | flops 4294967296 | bytes 12582912 | tf_op jit(solution)/shard_map/dot_general | solution.py:18
  103.3 14.7 %attention_forward.1 = (bf16[1024,512]{1,0:T(8,128)(2,1)}, bf16[1024,256]{1,0:T(8,128)(2,1)}, bf16[1024,256]{1,0:T(8,128)(2,1)}, bf16[1024,512]{1,0:T(8,128)(2,1)}, f32[2,2,1024]{2,1,0:T(2,128)}) custom-call(s32[1]{0:T(128)} %bitcast.place_ref, f32[1024,1024]{1,0:T(8,128)} %fusion.19.raw_query.raw_key.raw_value, ...), custom_call_target="tpu_custom_call" | custom-call | flops 4294967296 | bytes 8388608 | tf_op jit(solution)/shard_map/attention_forward/pallas_call | solution.py:368
  118.0 4.4 convolution_convert_fusion.1
  126.8 10.8 %collective-permute-done.10 = bf16[128,2048]{1,0:T(8,128)(2,1)S(1)} collective-permute-done((bf16[128,2048]{1,0:T(8,128)(2,1)S(1)}, bf16[128,2048]{1,0:T(8,128)(2,1)S(1)}, u32[]{:S(2)}, u32[]{:S(2)}) %collective-permute-start.10) | collective-permute-done | bytes 524320 | tf_op jit(solution)/shard_map/ppermute | solution.py:83
  139.0 6.5 %collective-permute-done.8 = bf16[128,2048]{1,0:T(8,128)(2,1)S(1)} collective-permute-done((bf16[128,2048]{1,0:T(8,128)(2,1)S(1)}, bf16[128,2048]{1,0:T(8,128)(2,1)S(1)}, u32[]{:S(2)}, u32[]{:S(2)}) %collective-permute-start.8) | collective-permute-done | bytes 524320 | tf_op jit(solution)/shard_map/ppermute | solution.py:83
  149.4 8.1 %collective-permute-done.12 = bf16[128,2048]{1,0:T(8,128)(2,1)S(1)} collective-permute-done((bf16[128,2048]{1,0:T(8,128)(2,1)S(1)}, bf16[128,2048]{1,0:T(8,128)(2,1)S(1)}, u32[]{:S(2)}, u32[]{:S(2)}) %collective-permute-start.12) | collective-permute-done | bytes 524320 | tf_op jit(solution)/shard_map/ppermute | solution.py:83
  162.4 18.5 %collective-permute-done.14 = bf16[256,2048]{1,0:T(8,128)(2,1)S(1)} collective-permute-done((bf16[256,2048]{1,0:T(8,128)(2,1)}, bf16[256,2048]{1,0:T(8,128)(2,1)S(1)}, u32[]{:S(2)}, u32[]{:S(2)}) %collective-permute-start.14) | collective-permute-done | bytes 1048608 | tf_op jit(solution)/shard_map/ppermute | solution.py:83
  188.1 2.4 constant_dynamic-update-slice_fusion.12
  190.4 2.8 collective-permute-done.16
  194.9 1.9 constant_dynamic-update-slice_fusion.11
  196.8 1.9 constant_dynamic-update-slice_fusion.10
  198.7 2.5 constant_dynamic-slice_fusion.23
  201.9 3.9 collective-permute-done.18
  205.7 2.3 pad_maximum_fusion.1
  208.0 17.2 %fusion.61 = f32[1024,3072]{1,0:T(8,128)S(1)} fusion(bf16[1024,2048]{1,0:T(8,128)(2,1)} %constant_dynamic-update-slice_fusion.10, bf16[2048,3072]{1,0:T(8,128)(2,1)} %all-gather.6.cloned.1.call-done.right_ref), kind=kOutput, calls=%fused_computation.155 | convolution fusion | flops 12884901888 | bytes 29360128 | tf_op jit(solution)/shard_map/dot_general | solution.py:18
  225.3 2.0 multiply_convert_fusion.2.left_ref
  227.2 2.6 copy-done.5
  231.5 11.0 %convolution_convert_fusion = bf16[2048,1536]{1,0:T(8,128)(2,1)} fusion(bf16[1024,2048]{1,0:T(8,128)(2,1)} %constant_dynamic-update-slice_fusion.5, bf16[1024,1536]{1,0:T(8,128)(2,1)S(1)} %multiply_convert_fusion.2.left_ref), kind=kOutput, calls=%fused_computation.6 | convolution fusion | flops 6445596672 | bytes 13631488 | tf_op jit(solution)/shard_map/dot_general | solution.py:22
  242.6 17.4 %all-gather.8.cloned.1.call-done.right_ref = bf16[2048,1536]{1,0:T(8,128)(2,1)} async-done(((bf16[256,1536]{1,0:T(8,128)(2,1)}), bf16[2048,1536]{1,0:T(8,128)(2,1)}) %all-gather.8.cloned.1.call-update) | async-done | bytes 6291472 | tf_op jit(solution)/shard_map/all_gather | solution.py:197
  260.0 14.7 %multiply_convert_fusion.1 = (bf16[1024,1536]{1,0:T(8,128)(2,1)S(1)}, bf16[1024,1536]{1,0:T(8,128)(2,1)S(1)}) fusion(f32[1024,3072]{1,0:T(8,128)} %copy-done.5, bf16[1024,2048]{1,0:T(8,128)(2,1)} %constant_dynamic-update-slice_fusion.5, bf16[2048,1536]{1,0:T(8,128)(2,1)} %all-gather.8.cloned.1.call-done.right_ref), kind=kOutput, calls=%fused_computation.9 | convolution fusion | flops 6462898176 | bytes 29360128 | tf_op jit(solution)/shard_map/dot_general | solution.py:18
  274.7 3.5 pad_maximum_fusion.left_ref
  278.5 18.7 %long_product.2 = bf16[1024,2048]{1,0:T(8,128)(2,1)} custom-call(bf16[1024,3072]{1,0:T(8,128)(2,1)} %pad_maximum_fusion.left_ref, bf16[2048,3072]{1,0:T(8,128)(2,1)} %all-gather.6.cloned.1.call-done.right_ref), custom_call_target="tpu_custom_call" | custom-call | flops 1 | bytes 1 | tf_op jit(solution)/shard_map/long_product/pallas_call | solution.py:276
  297.2 3.1 fusion.56
  304.3 18.0 %bitcast_convert_fusion = bf16[1024,3072]{1,0:T(8,128)(2,1)} fusion(bf16[2,1024,1024]{2,1,0:T(8,128)(2,1)S(1)} %copy-done.15, bf16[1,1024,3072]{2,1,0:T(8,128)(2,1)} %bitcast.6, bf16[1,1024,3072]{2,1,0:T(8,128)(2,1)} %bitcast.5), kind=kOutput, calls=%fused_computation.4 | convolution fusion | flops 12894339072 | bytes 23068672 | tf_op jit(solution)/shard_map/dot_general | solution.py:28
  322.3 3.5 collective-permute-done.22
  327.0 3.7 reduce-scatter.4.cloned.1.call-done
  330.8 2.9 add_convert_fusion.4
  336.6 11.9 %long_product.3 = bf16[1024,2048]{1,0:T(8,128)(2,1)} custom-call(bf16[1024,1536]{1,0:T(8,128)(2,1)} %copy-done.6, bf16[2048,1536]{1,0:T(8,128)(2,1)} %all-gather.8.cloned.1.call-done.right_ref), custom_call_target="tpu_custom_call" | custom-call | flops 1 | bytes 1 | tf_op jit(solution)/shard_map/long_product/pallas_call | solution.py:276
  348.5 2.1 convert_add_fusion.6
  355.6 20.1 %collective-permute-done.26 = bf16[256,2048]{1,0:T(8,128)(2,1)S(1)} collective-permute-done((bf16[256,2048]{1,0:T(8,128)(2,1)S(1)}, bf16[256,2048]{1,0:T(8,128)(2,1)S(1)}, u32[]{:S(2)}, u32[]{:S(2)}) %collective-permute-start.26) | collective-permute-done | bytes 1048608 | tf_op jit(solution)/shard_map/ppermute | solution.py:83
  379.9 6.1 %collective-permute-done.28 = bf16[128,2048]{1,0:T(8,128)(2,1)S(1)} collective-permute-done((bf16[128,2048]{1,0:T(8,128)(2,1)S(1)}, bf16[128,2048]{1,0:T(8,128)(2,1)S(1)}, u32[]{:S(2)}, u32[]{:S(2)}) %collective-permute-start.28) | collective-permute-done | bytes 524320 | tf_op jit(solution)/shard_map/ppermute | solution.py:83
  390.9 2.0 collective-permute-start.33
  392.9 4.9 fusion.44.upstream
  397.8 16.3 %attention_backward.1 = (bf16[1024,1024]{1,0:T(8,128)(2,1)}, f32[1,128]{1,0:T(1,128)}, f32[1,128]{1,0:T(1,128)}) custom-call(s32[1]{0:T(128)} %bitcast.place_ref, f32[1024,1024]{1,0:T(8,128)} %fusion.19.raw_query.raw_key.raw_value, f32[1024,1024]{1,0:T(8,128)} %fusion.19.raw_query.raw_key.raw_value, f32[1024,128]{1,0:T(8,128)} %get-tuple-element.290.cosine, ...), custom_call_target="tpu_custom_call" | custom-call | flops 1 | bytes 1 | tf_op jit(solution)/shard_map/attention_backward/pallas_call | solution.py:484
  414.2 2.0 maximum_bitcast_fusion.1
  419.1 6.5 %bitcast_convert_fusion.1 = bf16[1024,1024]{1,0:T(8,128)(2,1)S(1)} fusion(bf16[1,1024,1024]{2,1,0:T(8,128)(2,1)S(1)} %bitcast.55, bf16[1,1024,1024]{2,1,0:T(8,128)(2,1)S(1)} %bitcast.54, bf16[1,1024,1024]{2,1,0:T(8,128)(2,1)} %bitcast.9, bf16[1,1024,1024]{2,1,0:T(8,128)(2,1)S(1)} %maximum_bitcast_fusion.1), kind=kOutput, calls=%fused_computation.25 | convolution fusion | flops 4300210176 | bytes 10485760 | tf_op jit(solution)/shard_map/dot_general | solution.py:28
  425.6 2.9 add_convert_fusion.2
  429.3 6.2 %multiply_reduce_fusion = (f32[2048]{0:T(1024)S(1)}, bf16[1024,2048]{1,0:T(8,128)(2,1)}) fusion(bf16[1024,2048]{1,0:T(8,128)(2,1)S(1)} %copy-done.12, bf16[1024,1024]{1,0:T(8,128)(2,1)S(1)} %copy-done.24, bf16[2048,1536]{1,0:T(8,128)(2,1)S(1)} %bitcast.53), kind=kOutput, calls=%fused_computation.5 | convolution fusion | flops 4305451008 | bytes 14688256 | tf_op jit(solution)/shard_map/dot_general | solution.py:34
  435.5 4.2 bitcast_convert_fusion.2
  439.8 1.9 pad_maximum_fusion.2
  442.6 2.6 convert_element_type.275
  452.0 2.1 fusion.58
  454.0 17.8 %collective-permute-done.44 = f32[4352]{0:T(1024)S(1)} collective-permute-done((f32[4352]{0:T(1024)S(1)}, f32[4352]{0:T(1024)S(1)}, u32[]{:S(2)}, u32[]{:S(2)}) %collective-permute-start.44) | collective-permute-done | bytes 17440 | tf_op jit(solution)/shard_map/ppermute | solution.py:83
  475.9 2.4 convert_add_fusion.4
  478.3 8.8 %collective-permute-done.45 = bf16[128,2048]{1,0:T(8,128)(2,1)S(1)} collective-permute-done((bf16[128,2048]{1,0:T(8,128)(2,1)S(1)}, bf16[128,2048]{1,0:T(8,128)(2,1)S(1)}, u32[]{:S(2)}, u32[]{:S(2)}) %collective-permute-start.45) | collective-permute-done | bytes 524320 | tf_op jit(solution)/shard_map/ppermute | solution.py:83
  488.4 4.5 collective-permute-start.49
  493.3 2.9 collective-permute-start.51
  496.2 3.7 fusion.32
  501.2 6.3 %reduce-scatter.8.cloned.1.call-done.source = bf16[256,1536]{1,0:T(8,128)(2,1)} async-done(((bf16[1024,1536]{1,0:T(8,128)(2,1)}), bf16[256,1536]{1,0:T(8,128)(2,1)}) %reduce-scatter.8.cloned.1.call-update) | async-done | bytes 786448 | tf_op jit(solution)/shard_map/reduce_scatter | solution.py:222
  507.6 2.3 split_columns.1
  (215 shorter events, 85.5 us)
Async XLA Ops:
  7.2 86.2 %all-gather.4.cloned.1.call-start = ((), (), s32[]{:S(2)}) async-start(), calls=%async_computation.3 | async-start | bytes 7077888 | tf_op jit(solution)/shard_map/all_gather | solution.py:197
  9.5 198.6 %all-gather.6.cloned.1.call-start = ((), (), s32[]{:S(2)}) async-start(), calls=%async_computation.4 | async-start | bytes 14155776 | tf_op jit(solution)/shard_map/all_gather | solution.py:197
  12.3 247.8 %all-gather.8.cloned.1.call-start = ((), (), s32[]{:S(2)}) async-start(), calls=%async_computation.5 | async-start | bytes 7077888 | tf_op jit(solution)/shard_map/all_gather | solution.py:197
  14.4 27.2 %collective-permute-start = (bf16[256,2048]{1,0:T(8,128)(2,1)}, bf16[256,2048]{1,0:T(8,128)(2,1)}, u32[]{:S(2)}, u32[]{:S(2)}) collective-permute-start(bf16[256,2048]{1,0:T(8,128)(2,1)} %get-tuple-element.214), channel_id=1, source_target_pairs={{0,1},{1,0},{2,3},{3,2},{4,5},{5,4},{6,7},{7,6},{8,9},{9,8},{10,11... | collective-permute-start | bytes 3145736 | tf_op jit(solution)/shard_map/ppermute | solution.py:83
  17.3 26.4 %collective-permute-start.1 = (bf16[256,2048]{1,0:T(8,128)(2,1)}, bf16[256,2048]{1,0:T(8,128)(2,1)}, u32[]{:S(2)}, u32[]{:S(2)}) collective-permute-start(bf16[256,2048]{1,0:T(8,128)(2,1)} %get-tuple-element.214), channel_id=1, source_target_pairs={{0,2},{1,3},{2,0},{3,1},{4,6},{5,7},{6,4},{7,5},{8,10},{9,11},{10,... | collective-permute-start | bytes 3145736 | tf_op jit(solution)/shard_map/ppermute | solution.py:83
  18.8 45.1 %collective-permute-start.4 = (bf16[256,2048]{1,0:T(8,128)(2,1)S(1)}, bf16[256,2048]{1,0:T(8,128)(2,1)S(1)}, u32[]{:S(2)}, u32[]{:S(2)}) collective-permute-start(bf16[256,2048]{1,0:T(8,128)(2,1)S(1)} %copy-done.7), channel_id=1, source_target_pairs={{0,1},{1,0},{2,3},{3,2},{4,5},{5,4},{6,7},{7,6},{8,9},{9,8},{10,11... | collective-permute-start | bytes 3145736 | tf_op jit(solution)/shard_map/ppermute | solution.py:83
  19.4 46.8 %collective-permute-start.5 = (bf16[256,2048]{1,0:T(8,128)(2,1)S(1)}, bf16[256,2048]{1,0:T(8,128)(2,1)}, u32[]{:S(2)}, u32[]{:S(2)}) collective-permute-start(bf16[256,2048]{1,0:T(8,128)(2,1)S(1)} %copy-done.7), channel_id=1, source_target_pairs={{0,2},{1,3},{2,0},{3,1},{4,6},{5,7},{6,4},{7,5},{8,10},{9,11},{10,... | collective-permute-start | bytes 3145736 | tf_op jit(solution)/shard_map/ppermute | solution.py:83
  44.8 29.6 %collective-permute-start.2 = (bf16[128,2048]{1,0:T(8,128)(2,1)S(1)}, bf16[128,2048]{1,0:T(8,128)(2,1)S(1)}, u32[]{:S(2)}, u32[]{:S(2)}) collective-permute-start(bf16[128,2048]{1,0:T(8,128)(2,1)S(1)} %slice.162), channel_id=1, source_target_pairs={{0,1},{1,0},{2,3},{3,2},{4,5},{5,4},{6,7},{7,6},{8,9},{9,8},{10,11... | collective-permute-start | bytes 1572872 | tf_op jit(solution)/shard_map/ppermute | solution.py:83
  46.0 29.9 %collective-permute-start.3 = (bf16[128,2048]{1,0:T(8,128)(2,1)S(1)}, bf16[128,2048]{1,0:T(8,128)(2,1)S(1)}, u32[]{:S(2)}, u32[]{:S(2)}) collective-permute-start(bf16[128,2048]{1,0:T(8,128)(2,1)S(1)} %slice.163), channel_id=1, source_target_pairs={{0,2},{1,3},{2,0},{3,1},{4,6},{5,7},{6,4},{7,5},{8,10},{9,11},{10,... | collective-permute-start | bytes 1572872 | tf_op jit(solution)/shard_map/ppermute | solution.py:83
  78.6 12.6 %collective-permute-start.6 = (bf16[128,2048]{1,0:T(8,128)(2,1)S(1)}, bf16[128,2048]{1,0:T(8,128)(2,1)S(1)}, u32[]{:S(2)}, u32[]{:S(2)}) collective-permute-start(bf16[128,2048]{1,0:T(8,128)(2,1)S(1)} %slice.165), channel_id=1, source_target_pairs={{0,1},{1,0},{2,3},{3,2},{4,5},{5,4},{6,7},{7,6},{8,9},{9,8},{10,11... | collective-permute-start | bytes 1572872 | tf_op jit(solution)/shard_map/ppermute | solution.py:83
  79.0 12.7 %collective-permute-start.7 = (bf16[128,2048]{1,0:T(8,128)(2,1)S(1)}, bf16[128,2048]{1,0:T(8,128)(2,1)S(1)}, u32[]{:S(2)}, u32[]{:S(2)}) collective-permute-start(bf16[128,2048]{1,0:T(8,128)(2,1)S(1)} %slice.166), channel_id=1, source_target_pairs={{0,2},{1,3},{2,0},{3,1},{4,6},{5,7},{6,4},{7,5},{8,10},{9,11},{10,... | collective-permute-start | bytes 1572872 | tf_op jit(solution)/shard_map/ppermute | solution.py:83
  122.6 14.9 %collective-permute-start.10 = (bf16[128,2048]{1,0:T(8,128)(2,1)S(1)}, bf16[128,2048]{1,0:T(8,128)(2,1)S(1)}, u32[]{:S(2)}, u32[]{:S(2)}) collective-permute-start(bf16[128,2048]{1,0:T(8,128)(2,1)S(1)} %get-tuple-element.270), channel_id=1, source_target_pairs={{0,1},{1,0},{2,3},{3,2},{4,5},{5,4},{6,7},{7,6},{8,9},{9,8},{10,11... | collective-permute-start | bytes 1572872 | tf_op jit(solution)/shard_map/ppermute | solution.py:83
  124.1 14.9 %collective-permute-start.11 = (bf16[128,2048]{1,0:T(8,128)(2,1)S(1)}, bf16[128,2048]{1,0:T(8,128)(2,1)S(1)}, u32[]{:S(2)}, u32[]{:S(2)}) collective-permute-start(bf16[128,2048]{1,0:T(8,128)(2,1)S(1)} %get-tuple-element.269), channel_id=1, source_target_pairs={{0,2},{1,3},{2,0},{3,1},{4,6},{5,7},{6,4},{7,5},{8,10},{9,11},{10,... | collective-permute-start | bytes 1572872 | tf_op jit(solution)/shard_map/ppermute | solution.py:83
  125.6 19.8 %collective-permute-start.8 = (bf16[128,2048]{1,0:T(8,128)(2,1)S(1)}, bf16[128,2048]{1,0:T(8,128)(2,1)S(1)}, u32[]{:S(2)}, u32[]{:S(2)}) collective-permute-start(bf16[128,2048]{1,0:T(8,128)(2,1)S(1)} %get-tuple-element.272), channel_id=1, source_target_pairs={{0,1},{1,0},{2,3},{3,2},{4,5},{5,4},{6,7},{7,6},{8,9},{9,8},{10,11... | collective-permute-start | bytes 1572872 | tf_op jit(solution)/shard_map/ppermute | solution.py:83
  126.2 20.7 %collective-permute-start.9 = (bf16[128,2048]{1,0:T(8,128)(2,1)S(1)}, bf16[128,2048]{1,0:T(8,128)(2,1)S(1)}, u32[]{:S(2)}, u32[]{:S(2)}) collective-permute-start(bf16[128,2048]{1,0:T(8,128)(2,1)S(1)} %get-tuple-element.271), channel_id=1, source_target_pairs={{0,2},{1,3},{2,0},{3,1},{4,6},{5,7},{6,4},{7,5},{8,10},{9,11},{10,... | collective-permute-start | bytes 1572872 | tf_op jit(solution)/shard_map/ppermute | solution.py:83
  147.3 10.3 %collective-permute-start.12 = (bf16[128,2048]{1,0:T(8,128)(2,1)S(1)}, bf16[128,2048]{1,0:T(8,128)(2,1)S(1)}, u32[]{:S(2)}, u32[]{:S(2)}) collective-permute-start(bf16[128,2048]{1,0:T(8,128)(2,1)S(1)} %get-tuple-element.268), channel_id=1, source_target_pairs={{0,2},{1,3},{2,0},{3,1},{4,6},{5,7},{6,4},{7,5},{8,10},{9,11},{10,... | collective-permute-start | bytes 1572872 | tf_op jit(solution)/shard_map/ppermute | solution.py:83
  148.8 10.2 %copy-start.16 = (f32[2048]{0:T(1024)S(1)}, f32[2048]{0:T(1024)}, u32[]{:S(2)}) copy-start(f32[2048]{0:T(1024)} %param.17) | copy-start | bytes 24580
  148.8 9.3 %collective-permute-start.13 = (bf16[128,2048]{1,0:T(8,128)(2,1)S(1)}, bf16[128,2048]{1,0:T(8,128)(2,1)S(1)}, u32[]{:S(2)}, u32[]{:S(2)}) collective-permute-start(bf16[128,2048]{1,0:T(8,128)(2,1)S(1)} %get-tuple-element.267), channel_id=1, source_target_pairs={{0,1},{1,0},{2,3},{3,2},{4,5},{5,4},{6,7},{7,6},{8,9},{9,8},{10,11... | collective-permute-start | bytes 1572872 | tf_op jit(solution)/shard_map/ppermute | solution.py:83
  160.7 20.2 %collective-permute-start.14 = (bf16[256,2048]{1,0:T(8,128)(2,1)}, bf16[256,2048]{1,0:T(8,128)(2,1)S(1)}, u32[]{:S(2)}, u32[]{:S(2)}) collective-permute-start(bf16[256,2048]{1,0:T(8,128)(2,1)} %get-tuple-element.210), channel_id=1, source_target_pairs={{0,1},{1,0},{2,3},{3,2},{4,5},{5,4},{6,7},{7,6},{8,9},{9,8},{10,11... | collective-permute-start | bytes 3145736 | tf_op jit(solution)/shard_map/ppermute | solution.py:83
  161.3 20.6 %collective-permute-start.15 = (bf16[256,2048]{1,0:T(8,128)(2,1)}, bf16[256,2048]{1,0:T(8,128)(2,1)}, u32[]{:S(2)}, u32[]{:S(2)}) collective-permute-start(bf16[256,2048]{1,0:T(8,128)(2,1)} %get-tuple-element.210), channel_id=1, source_target_pairs={{0,2},{1,3},{2,0},{3,1},{4,6},{5,7},{6,4},{7,5},{8,10},{9,11},{10,... | collective-permute-start | bytes 3145736 | tf_op jit(solution)/shard_map/ppermute | solution.py:83
  162.3 168.4 %reduce-scatter.4.cloned.1.call-start = ((), (), s32[]{:S(2)}) async-start(), calls=%async_computation.6 | async-start | bytes 7077888 | tf_op jit(solution)/shard_map/reduce_scatter | solution.py:218
  183.8 9.5 %collective-permute-start.16 = (bf16[128,2048]{1,0:T(8,128)(2,1)}, bf16[128,2048]{1,0:T(8,128)(2,1)}, u32[]{:S(2)}, u32[]{:S(2)}) collective-permute-start(bf16[128,2048]{1,0:T(8,128)(2,1)} %slice.176), channel_id=1, source_target_pairs={{0,1},{1,0},{2,3},{3,2},{4,5},{5,4},{6,7},{7,6},{8,9},{9,8},{10,11... | collective-permute-start | bytes 1572872 | tf_op jit(solution)/shard_map/ppermute | solution.py:83
  185.4 9.5 %collective-permute-start.17 = (bf16[128,2048]{1,0:T(8,128)(2,1)}, bf16[128,2048]{1,0:T(8,128)(2,1)}, u32[]{:S(2)}, u32[]{:S(2)}) collective-permute-start(bf16[128,2048]{1,0:T(8,128)(2,1)} %slice.177), channel_id=1, source_target_pairs={{0,2},{1,3},{2,0},{3,1},{4,6},{5,7},{6,4},{7,5},{8,10},{9,11},{10,... | collective-permute-start | bytes 1572872 | tf_op jit(solution)/shard_map/ppermute | solution.py:83
  201.5 4.2 collective-permute-start.18
  242.6 199.9 %reduce-scatter.6.cloned.1.call-start = ((), (), s32[]{:S(2)}) async-start(), calls=%async_computation.7 | async-start | bytes 7864320 | tf_op jit(solution)/shard_map/reduce_scatter | solution.py:222
  278.3 18.9 %collective-permute-start.19 = (bf16[1024,3072]{1,0:T(8,128)(2,1)}, bf16[1024,3072]{1,0:T(8,128)(2,1)}, u32[]{:S(2)}, u32[]{:S(2)}) collective-permute-start(bf16[1024,3072]{1,0:T(8,128)(2,1)} %pad_maximum_fusion.left_ref), channel_id=1, source_target_pairs={{0,4},{4,0},{8,12},{12,8},{16,20},{20,16},{24,28},{28,24},{1,5},{5... | collective-permute-start | bytes 18874376 | tf_op jit(solution)/shard_map/ppermute | solution.py:80
  300.3 22.0 %collective-permute-start.20 = (bf16[128,2048]{1,0:T(8,128)(2,1)}, bf16[128,2048]{1,0:T(8,128)(2,1)}, u32[]{:S(2)}, u32[]{:S(2)}) collective-permute-start(bf16[128,2048]{1,0:T(8,128)(2,1)} %get-tuple-element.256), channel_id=1, source_target_pairs={{0,1},{1,0},{2,3},{3,2},{4,5},{5,4},{6,7},{7,6},{8,9},{9,8},{10,11... | collective-permute-start | bytes 1572872 | tf_op jit(solution)/shard_map/ppermute | solution.py:83
  301.8 20.6 %collective-permute-start.21 = (bf16[128,2048]{1,0:T(8,128)(2,1)}, bf16[128,2048]{1,0:T(8,128)(2,1)}, u32[]{:S(2)}, u32[]{:S(2)}) collective-permute-start(bf16[128,2048]{1,0:T(8,128)(2,1)} %get-tuple-element.255), channel_id=1, source_target_pairs={{0,2},{1,3},{2,0},{3,1},{4,6},{5,7},{6,4},{7,5},{8,10},{9,11},{10,... | collective-permute-start | bytes 1572872 | tf_op jit(solution)/shard_map/ppermute | solution.py:83
  303.2 22.6 %collective-permute-start.22 = (bf16[128,2048]{1,0:T(8,128)(2,1)}, bf16[128,2048]{1,0:T(8,128)(2,1)S(1)}, u32[]{:S(2)}, u32[]{:S(2)}) collective-permute-start(bf16[128,2048]{1,0:T(8,128)(2,1)} %get-tuple-element.254), channel_id=1, source_target_pairs={{0,1},{1,0},{2,3},{3,2},{4,5},{5,4},{6,7},{7,6},{8,9},{9,8},{10,11... | collective-permute-start | bytes 1572872 | tf_op jit(solution)/shard_map/ppermute | solution.py:83
  303.8 23.2 %collective-permute-start.23 = (bf16[128,2048]{1,0:T(8,128)(2,1)}, bf16[128,2048]{1,0:T(8,128)(2,1)S(1)}, u32[]{:S(2)}, u32[]{:S(2)}) collective-permute-start(bf16[128,2048]{1,0:T(8,128)(2,1)} %get-tuple-element.253), channel_id=1, source_target_pairs={{0,2},{1,3},{2,0},{3,1},{4,6},{5,7},{6,4},{7,5},{8,10},{9,11},{10,... | collective-permute-start | bytes 1572872 | tf_op jit(solution)/shard_map/ppermute | solution.py:83
  330.7 176.9 %reduce-scatter.8.cloned.1.call-start = ((), (), s32[]{:S(2)}) async-start(), calls=%async_computation.8 | async-start | bytes 3932160 | tf_op jit(solution)/shard_map/reduce_scatter | solution.py:222
  333.6 14.8 %collective-permute-start.24 = (bf16[128,2048]{1,0:T(8,128)(2,1)}, bf16[128,2048]{1,0:T(8,128)(2,1)}, u32[]{:S(2)}, u32[]{:S(2)}) collective-permute-start(bf16[128,2048]{1,0:T(8,128)(2,1)} %get-tuple-element.252), channel_id=1, source_target_pairs={{0,2},{1,3},{2,0},{3,1},{4,6},{5,7},{6,4},{7,5},{8,10},{9,11},{10,... | collective-permute-start | bytes 1572872 | tf_op jit(solution)/shard_map/ppermute | solution.py:83
  335.1 13.3 %collective-permute-start.25 = (bf16[128,2048]{1,0:T(8,128)(2,1)}, bf16[128,2048]{1,0:T(8,128)(2,1)}, u32[]{:S(2)}, u32[]{:S(2)}) collective-permute-start(bf16[128,2048]{1,0:T(8,128)(2,1)} %get-tuple-element.251), channel_id=1, source_target_pairs={{0,1},{1,0},{2,3},{3,2},{4,5},{5,4},{6,7},{7,6},{8,9},{9,8},{10,11... | collective-permute-start | bytes 1572872 | tf_op jit(solution)/shard_map/ppermute | solution.py:83
  352.8 22.9 %collective-permute-start.26 = (bf16[256,2048]{1,0:T(8,128)(2,1)S(1)}, bf16[256,2048]{1,0:T(8,128)(2,1)S(1)}, u32[]{:S(2)}, u32[]{:S(2)}) collective-permute-start(bf16[256,2048]{1,0:T(8,128)(2,1)S(1)} %get-tuple-element.208), channel_id=1, source_target_pairs={{0,1},{1,0},{2,3},{3,2},{4,5},{5,4},{6,7},{7,6},{8,9},{9,8},{10,11... | collective-permute-start | bytes 3145736 | tf_op jit(solution)/shard_map/ppermute | solution.py:83
  353.6 22.1 %collective-permute-start.27 = (bf16[256,2048]{1,0:T(8,128)(2,1)S(1)}, bf16[256,2048]{1,0:T(8,128)(2,1)S(1)}, u32[]{:S(2)}, u32[]{:S(2)}) collective-permute-start(bf16[256,2048]{1,0:T(8,128)(2,1)S(1)} %get-tuple-element.208), channel_id=1, source_target_pairs={{0,2},{1,3},{2,0},{3,1},{4,6},{5,7},{6,4},{7,5},{8,10},{9,11},{10,... | collective-permute-start | bytes 3145736 | tf_op jit(solution)/shard_map/ppermute | solution.py:83
  375.8 10.2 %collective-permute-start.28 = (bf16[128,2048]{1,0:T(8,128)(2,1)S(1)}, bf16[128,2048]{1,0:T(8,128)(2,1)S(1)}, u32[]{:S(2)}, u32[]{:S(2)}) collective-permute-start(bf16[128,2048]{1,0:T(8,128)(2,1)S(1)} %slice.188), channel_id=1, source_target_pairs={{0,1},{1,0},{2,3},{3,2},{4,5},{5,4},{6,7},{7,6},{8,9},{9,8},{10,11... | collective-permute-start | bytes 1572872 | tf_op jit(solution)/shard_map/ppermute | solution.py:83
  377.4 10.0 %collective-permute-start.29 = (bf16[128,2048]{1,0:T(8,128)(2,1)S(1)}, bf16[128,2048]{1,0:T(8,128)(2,1)S(1)}, u32[]{:S(2)}, u32[]{:S(2)}) collective-permute-start(bf16[128,2048]{1,0:T(8,128)(2,1)S(1)} %slice.189), channel_id=1, source_target_pairs={{0,2},{1,3},{2,0},{3,1},{4,6},{5,7},{6,4},{7,5},{8,10},{9,11},{10,... | collective-permute-start | bytes 1572872 | tf_op jit(solution)/shard_map/ppermute | solution.py:83
  379.6 38.5 %collective-permute-start.34 = (bf16[1024,1024]{1,0:T(8,128)(2,1)}, bf16[1024,1024]{1,0:T(8,128)(2,1)}, u32[]{:S(2)}, u32[]{:S(2)}) collective-permute-start(bf16[1024,1024]{1,0:T(8,128)(2,1)} %pad_maximum_fusion.5), channel_id=1, source_target_pairs={{0,4},{4,0},{8,12},{12,8},{16,20},{20,16},{24,28},{28,24},{1,5},{5... | collective-permute-start | bytes 6291464 | tf_op jit(solution)/shard_map/ppermute | solution.py:80
  387.5 10.3 %copy-start.9 = (bf16[1024,2048]{1,0:T(8,128)(2,1)}, bf16[1024,2048]{1,0:T(8,128)(2,1)S(1)}, u32[]{:S(2)}) copy-start(bf16[1024,2048]{1,0:T(8,128)(2,1)S(1)} %constant_dynamic-update-slice_fusion.15) | copy-start | bytes 12582916
  388.9 25.2 %collective-permute-start.30 = (bf16[128,2048]{1,0:T(8,128)(2,1)}, bf16[128,2048]{1,0:T(8,128)(2,1)}, u32[]{:S(2)}, u32[]{:S(2)}) collective-permute-start(bf16[128,2048]{1,0:T(8,128)(2,1)} %get-tuple-element.248), channel_id=1, source_target_pairs={{0,1},{1,0},{2,3},{3,2},{4,5},{5,4},{6,7},{7,6},{8,9},{9,8},{10,11... | collective-permute-start | bytes 1572872 | tf_op jit(solution)/shard_map/ppermute | solution.py:83
  389.2 24.9 %collective-permute-start.31 = (bf16[128,2048]{1,0:T(8,128)(2,1)}, bf16[128,2048]{1,0:T(8,128)(2,1)}, u32[]{:S(2)}, u32[]{:S(2)}) collective-permute-start(bf16[128,2048]{1,0:T(8,128)(2,1)} %get-tuple-element.247), channel_id=1, source_target_pairs={{0,2},{1,3},{2,0},{3,1},{4,6},{5,7},{6,4},{7,5},{8,10},{9,11},{10,... | collective-permute-start | bytes 1572872 | tf_op jit(solution)/shard_map/ppermute | solution.py:83
  389.6 24.5 %collective-permute-start.32 = (bf16[128,2048]{1,0:T(8,128)(2,1)}, bf16[128,2048]{1,0:T(8,128)(2,1)}, u32[]{:S(2)}, u32[]{:S(2)}) collective-permute-start(bf16[128,2048]{1,0:T(8,128)(2,1)} %get-tuple-element.246), channel_id=1, source_target_pairs={{0,1},{1,0},{2,3},{3,2},{4,5},{5,4},{6,7},{7,6},{8,9},{9,8},{10,11... | collective-permute-start | bytes 1572872 | tf_op jit(solution)/shard_map/ppermute | solution.py:83
  390.9 23.2 %collective-permute-start.33 = (bf16[128,2048]{1,0:T(8,128)(2,1)}, bf16[128,2048]{1,0:T(8,128)(2,1)}, u32[]{:S(2)}, u32[]{:S(2)}) collective-permute-start(bf16[128,2048]{1,0:T(8,128)(2,1)} %get-tuple-element.245), channel_id=1, source_target_pairs={{0,2},{1,3},{2,0},{3,1},{4,6},{5,7},{6,4},{7,5},{8,10},{9,11},{10,... | collective-permute-start | bytes 1572872 | tf_op jit(solution)/shard_map/ppermute | solution.py:83
  414.1 4.4 collective-permute-start.35
  416.2 19.3 %collective-permute-start.37 = (bf16[1024,512]{1,0:T(8,128)(2,1)}, bf16[1024,512]{1,0:T(8,128)(2,1)}, u32[]{:S(2)}, u32[]{:S(2)}) collective-permute-start(bf16[1024,512]{1,0:T(8,128)(2,1)} %get-tuple-element.121), channel_id=1, source_target_pairs={{0,4},{4,0},{8,12},{12,8},{16,20},{20,16},{24,28},{28,24},{1,5},{5... | collective-permute-start | bytes 3145736 | tf_op jit(solution)/shard_map/ppermute | solution.py:80
  417.5 11.8 %slice-start = ((s8[6291456]{0:T(1024)(128)(4,1)}), s8[2097152]{0:T(1024)(128)(4,1)S(1)}, s32[]{:S(2)}) async-start(s8[6291456]{0:T(1024)(128)(4,1)} %bitcast.52), calls=%async_computation.9 | async-start | bytes 4194304
  417.8 17.6 %collective-permute-start.36 = (bf16[1024,1024]{1,0:T(8,128)(2,1)S(1)}, bf16[1024,1024]{1,0:T(8,128)(2,1)}, u32[]{:S(2)}, u32[]{:S(2)}) collective-permute-start(bf16[1024,1024]{1,0:T(8,128)(2,1)S(1)} %pad_maximum_fusion.6), channel_id=1, source_target_pairs={{0,4},{4,0},{8,12},{12,8},{16,20},{20,16},{24,28},{28,24},{1,5},{5... | collective-permute-start | bytes 6291464 | tf_op jit(solution)/shard_map/ppermute | solution.py:80
  428.5 14.0 %collective-permute-start.38 = (bf16[128,2048]{1,0:T(8,128)(2,1)}, bf16[128,2048]{1,0:T(8,128)(2,1)}, u32[]{:S(2)}, u32[]{:S(2)}) collective-permute-start(bf16[128,2048]{1,0:T(8,128)(2,1)} %get-tuple-element.228), channel_id=1, source_target_pairs={{0,2},{1,3},{2,0},{3,1},{4,6},{5,7},{6,4},{7,5},{8,10},{9,11},{10,... | collective-permute-start | bytes 1572872 | tf_op jit(solution)/shard_map/ppermute | solution.py:83
  428.8 13.7 %collective-permute-start.39 = (bf16[128,2048]{1,0:T(8,128)(2,1)}, bf16[128,2048]{1,0:T(8,128)(2,1)}, u32[]{:S(2)}, u32[]{:S(2)}) collective-permute-start(bf16[128,2048]{1,0:T(8,128)(2,1)} %get-tuple-element.227), channel_id=1, source_target_pairs={{0,1},{1,0},{2,3},{3,2},{4,5},{5,4},{6,7},{7,6},{8,9},{9,8},{10,11... | collective-permute-start | bytes 1572872 | tf_op jit(solution)/shard_map/ppermute | solution.py:83
  446.8 27.2 %copy-start.14 = (bf16[1024,2048]{1,0:T(8,128)(2,1)S(1)}, bf16[1024,2048]{1,0:T(8,128)(2,1)}, u32[]{:S(2)}) copy-start(bf16[1024,2048]{1,0:T(8,128)(2,1)} %get-tuple-element.188) | copy-start | bytes 12582916
  446.8 25.0 %collective-permute-start.40 = (bf16[128,2048]{1,0:T(8,128)(2,1)S(1)}, bf16[128,2048]{1,0:T(8,128)(2,1)S(1)}, u32[]{:S(2)}, u32[]{:S(2)}) collective-permute-start(bf16[128,2048]{1,0:T(8,128)(2,1)S(1)} %get-tuple-element.224), channel_id=1, source_target_pairs={{0,1},{1,0},{2,3},{3,2},{4,5},{5,4},{6,7},{7,6},{8,9},{9,8},{10,11... | collective-permute-start | bytes 1572872 | tf_op jit(solution)/shard_map/ppermute | solution.py:83
  447.9 23.9 %collective-permute-start.41 = (bf16[128,2048]{1,0:T(8,128)(2,1)S(1)}, bf16[128,2048]{1,0:T(8,128)(2,1)S(1)}, u32[]{:S(2)}, u32[]{:S(2)}) collective-permute-start(bf16[128,2048]{1,0:T(8,128)(2,1)S(1)} %get-tuple-element.223), channel_id=1, source_target_pairs={{0,2},{1,3},{2,0},{3,1},{4,6},{5,7},{6,4},{7,5},{8,10},{9,11},{10,... | collective-permute-start | bytes 1572872 | tf_op jit(solution)/shard_map/ppermute | solution.py:83
  449.4 22.4 %collective-permute-start.42 = (bf16[128,2048]{1,0:T(8,128)(2,1)S(1)}, bf16[128,2048]{1,0:T(8,128)(2,1)S(1)}, u32[]{:S(2)}, u32[]{:S(2)}) collective-permute-start(bf16[128,2048]{1,0:T(8,128)(2,1)S(1)} %get-tuple-element.222), channel_id=1, source_target_pairs={{0,1},{1,0},{2,3},{3,2},{4,5},{5,4},{6,7},{7,6},{8,9},{9,8},{10,11... | collective-permute-start | bytes 1572872 | tf_op jit(solution)/shard_map/ppermute | solution.py:83
  450.7 21.9 %collective-permute-start.43 = (bf16[128,2048]{1,0:T(8,128)(2,1)S(1)}, bf16[128,2048]{1,0:T(8,128)(2,1)S(1)}, u32[]{:S(2)}, u32[]{:S(2)}) collective-permute-start(bf16[128,2048]{1,0:T(8,128)(2,1)S(1)} %get-tuple-element.221), channel_id=1, source_target_pairs={{0,2},{1,3},{2,0},{3,1},{4,6},{5,7},{6,4},{7,5},{8,10},{9,11},{10,... | collective-permute-start | bytes 1572872 | tf_op jit(solution)/shard_map/ppermute | solution.py:83
  451.0 20.9 %collective-permute-start.44 = (f32[4352]{0:T(1024)S(1)}, f32[4352]{0:T(1024)S(1)}, u32[]{:S(2)}, u32[]{:S(2)}) collective-permute-start(f32[4352]{0:T(1024)S(1)} %pad_maximum_fusion.12), channel_id=1, source_target_pairs={{0,1},{1,0},{2,3},{3,2},{4,5},{5,4},{6,7},{7,6},{8,9},{9,8},{10,11... | collective-permute-start | bytes 52232 | tf_op jit(solution)/shard_map/ppermute | solution.py:83
  472.6 5.7 %collective-permute-start.47 = (f32[4352]{0:T(1024)S(1)}, f32[4352]{0:T(1024)S(1)}, u32[]{:S(2)}, u32[]{:S(2)}) collective-permute-start(f32[4352]{0:T(1024)S(1)} %add.297), channel_id=1, source_target_pairs={{0,2},{1,3},{2,0},{3,1},{4,6},{5,7},{6,4},{7,5},{8,10},{9,11},{10,... | collective-permute-start | bytes 52232 | tf_op jit(solution)/shard_map/ppermute | solution.py:83
  474.4 12.6 %collective-permute-start.45 = (bf16[128,2048]{1,0:T(8,128)(2,1)S(1)}, bf16[128,2048]{1,0:T(8,128)(2,1)S(1)}, u32[]{:S(2)}, u32[]{:S(2)}) collective-permute-start(bf16[128,2048]{1,0:T(8,128)(2,1)S(1)} %get-tuple-element.220), channel_id=1, source_target_pairs={{0,2},{1,3},{2,0},{3,1},{4,6},{5,7},{6,4},{7,5},{8,10},{9,11},{10,... | collective-permute-start | bytes 1572872 | tf_op jit(solution)/shard_map/ppermute | solution.py:83
  475.1 12.7 %copy-start.3 = (bf16[256,2048]{1,0:T(8,128)(2,1)S(1)}, bf16[256,2048]{1,0:T(8,128)(2,1)}, u32[]{:S(2)}) copy-start(bf16[256,2048]{1,0:T(8,128)(2,1)} %param.14) | copy-start | bytes 3145732
  475.1 12.7 %copy-start.20 = (f32[256]{0:T(256)S(1)}, f32[256]{0:T(256)}, u32[]{:S(2)}) copy-start(f32[256]{0:T(256)} %copy-done.19) | copy-start | bytes 3076
  475.1 12.1 %collective-permute-start.46 = (bf16[128,2048]{1,0:T(8,128)(2,1)S(1)}, bf16[128,2048]{1,0:T(8,128)(2,1)S(1)}, u32[]{:S(2)}, u32[]{:S(2)}) collective-permute-start(bf16[128,2048]{1,0:T(8,128)(2,1)S(1)} %get-tuple-element.219), channel_id=1, source_target_pairs={{0,1},{1,0},{2,3},{3,2},{4,5},{5,4},{6,7},{7,6},{8,9},{9,8},{10,11... | collective-permute-start | bytes 1572872 | tf_op jit(solution)/shard_map/ppermute | solution.py:83
  487.1 1.2 collective-permute-start.48
  488.4 11.5 %collective-permute-start.49 = (f32[4352]{0:T(1024)S(1)}, f32[4352]{0:T(1024)S(1)}, u32[]{:S(2)}, u32[]{:S(2)}) collective-permute-start(f32[4352]{0:T(1024)S(1)} %add.303), channel_id=1, source_target_pairs={{0,8},{4,12},{8,16},{12,20},{16,24},{20,28},{24,0},{28,4},{1,9},{5... | collective-permute-start | bytes 52232 | tf_op jit(solution)/shard_map/ppermute | solution.py:69
  492.9 7.0 %collective-permute-start.50 = (f32[4352]{0:T(1024)S(1)}, f32[4352]{0:T(1024)S(1)}, u32[]{:S(2)}, u32[]{:S(2)}) collective-permute-start(f32[4352]{0:T(1024)S(1)} %add.303), channel_id=1, source_target_pairs={{0,16},{4,20},{8,24},{12,28},{16,0},{20,4},{24,8},{28,12},{1,17},{... | collective-permute-start | bytes 52232 | tf_op jit(solution)/shard_map/ppermute | solution.py:69
  493.3 6.6 %collective-permute-start.51 = (f32[4352]{0:T(1024)S(1)}, f32[4352]{0:T(1024)S(1)}, u32[]{:S(2)}, u32[]{:S(2)}) collective-permute-start(f32[4352]{0:T(1024)S(1)} %add.303), channel_id=1, source_target_pairs={{0,24},{4,28},{8,0},{12,4},{16,8},{20,12},{24,16},{28,20},{1,25},{... | collective-permute-start | bytes 52232 | tf_op jit(solution)/shard_map/ppermute | solution.py:69
  (22 other events, 124.7 us)
Sparse Core Ops, SparseCore 0:
  10.3 67.5 all-gather.3
  80.0 115.3 all-gather.5
  197.0 62.9 all-gather.7
  262.2 68.4 reduce-scatter.3
  332.8 109.1 reduce-scatter.5
  444.2 63.3 reduce-scatter.7
